TPU v7x, 128 devices: a whole 4x4x4 slice. The times are simulated.
128 devices in a mesh: req: 4 (over z_hi, core), tile: 32 (over y, z_lo, x).
Axes of the slice: x: 4, y: 4, z: 4 (z_hi: 2, z_lo: 2; z = z_hi * 2 + z_lo), core: 2. Of those that a mesh axis runs over, the one named last changes fastest.
Arguments:
- latents: bfloat16 [4, 3840, 1536], P('req', 'tile'), may hold values from -6 to 6
- modulation: bfloat16 [4, 6, 1536], P('req'), may hold values from -2.5 to 2.5
- kv_cache: bfloat16 [4, 3840, 3072], P('req', 'tile'), may hold values from -6 to 6
- text_kv: bfloat16 [4, 154, 3072], P('req'), as said below
- lengths: int32 [4], P('req'), may hold values from 960 to 3840, as said below
- refresh: int32 [4, 4], P('req'), may hold values from 0 to 31, as said below
- w_qkv: bfloat16 [1536, 4608], replicated, may hold values from -0.15625 to 0.15625
- w_out: bfloat16 [1536, 1536], P('req'), may hold values from -6 to 6
- w_up: bfloat16 [1536, 6144], P(None, 'req'), may hold values from -0.15625 to 0.15625
- w_down: bfloat16 [6144, 1536], P('req'), may hold values from -0.078125 to 0.078125
Outputs:
- block_out: bfloat16 [4, 3840, 1536], P('req', 'tile')
Inputs may be any that keep to these rules, and one draw needn't show every extreme that they name: `lengths`: some request has exactly 3840 live tokens and another exactly 960. `refresh`: each row holds 4 different tile indices; the first and the last tile each appear in some row. `text_kv`: keys in the first 1536 columns, values in the last 1536.
All inputs are finite; a program needn't handle non-finite values.
Results may differ from a plain program's by a relative error of at most 0.017.
Values may be sent and summed in bfloat16 or wider, within the bound.
No kernel may reach another device: no remote copies, remote signals or barrier semaphores. Data moves between devices by JAX's collectives and lax.ppermute only.
A program may use at most 192 MiB of HBM per device.

v0:
```python
import math

import jax
import jax.numpy as jnp
from jax import lax
from jax.sharding import PartitionSpec as P


def layer_norm(values):
    average = jnp.mean(values, -1, keepdims=True)
    centred = values - average
    spread = jnp.mean(centred * centred, -1, keepdims=True)
    return centred * lax.rsqrt(spread + 1e-06)


def attend(queries, key_rows, text_rows, live_keys):
    model_width = queries.shape[1]
    row_count = queries.shape[0]
    head_size = 64
    head_count = model_width // head_size
    head_group = math.gcd(head_count, 4)
    outputs = []
    for head_start in range(0, head_count, head_group):
        col_low = head_start * head_size
        col_high = (head_start + head_group) * head_size
        q_part = queries[:, col_low:col_high].reshape(row_count, head_group, head_size)
        img_keys = key_rows[:, col_low:col_high].reshape(-1, head_group, head_size)
        img_vals = key_rows[:, model_width + col_low : model_width + col_high].reshape(
            -1, head_group, head_size
        )
        txt_keys = text_rows[:, col_low:col_high].reshape(-1, head_group, head_size)
        txt_vals = text_rows[:, model_width + col_low : model_width + col_high].reshape(
            -1, head_group, head_size
        )
        img_scores = (
            jnp.einsum("qhe,khe->hqk", q_part, img_keys, preferred_element_type=jnp.float32) * 0.125
        )
        img_scores = jnp.where(live_keys[None, None, :], img_scores, -1e30)
        txt_scores = (
            jnp.einsum("qhe,khe->hqk", q_part, txt_keys, preferred_element_type=jnp.float32) * 0.125
        )
        row_max = jnp.maximum(
            jnp.max(img_scores, -1, keepdims=True), jnp.max(txt_scores, -1, keepdims=True)
        )
        img_probs = jnp.exp(img_scores - row_max)
        txt_probs = jnp.exp(txt_scores - row_max)
        total_weight = jnp.sum(img_probs, -1, keepdims=True) + jnp.sum(txt_probs, -1, keepdims=True)
        img_weights = (img_probs / total_weight).astype(jnp.bfloat16)
        txt_weights = (txt_probs / total_weight).astype(jnp.bfloat16)
        mixed_part = jnp.einsum(
            "hqk,khe->qhe", img_weights, img_vals, preferred_element_type=jnp.float32
        )
        mixed_part = mixed_part + jnp.einsum(
            "hqk,khe->qhe", txt_weights, txt_vals, preferred_element_type=jnp.float32
        )
        outputs.append(mixed_part.reshape(row_count, head_group * head_size))
    return jnp.concatenate(outputs, axis=1).astype(jnp.bfloat16)


def per_device(
    latents, modulation, kv_cache, text_kv, lengths, refresh, w_qkv, w_out, w_up, w_down
):
    tokens = latents[0]
    row_count = tokens.shape[0]
    model_width = tokens.shape[1]
    modulate = modulation[0].astype(jnp.float32)
    tile_index = lax.axis_index("tile")
    tile_count = lax.axis_size("tile")
    length = lengths[0]
    refreshed = refresh[0]
    normed = (layer_norm(tokens.astype(jnp.float32)) * (1.0 + modulate[1]) + modulate[0]).astype(
        jnp.bfloat16
    )
    projections = jnp.dot(normed, w_qkv, preferred_element_type=jnp.float32).astype(jnp.bfloat16)
    queries = projections[:, :model_width]
    fresh_rows = projections[:, model_width:]
    flagged = jnp.any(refreshed == tile_index)
    outgoing = jnp.where(flagged, fresh_rows, kv_cache[0])
    key_rows = lax.all_gather(outgoing, "tile", axis=0, tiled=True)
    key_rows = lax.dynamic_update_slice_in_dim(key_rows, fresh_rows, tile_index * row_count, 0)
    total_rows = row_count * tile_count
    live_keys = jnp.arange(total_rows, dtype=jnp.int32) < length
    attended = attend(queries, key_rows, text_kv[0], live_keys)
    feature_rows = lax.all_to_all(attended, "req", split_axis=1, concat_axis=0, tiled=True)
    part_rows = feature_rows
    projected = lax.psum_scatter(
        jnp.dot(part_rows, w_out, preferred_element_type=jnp.float32).astype(jnp.bfloat16),
        "req",
        scatter_dimension=0,
        tiled=True,
    ).astype(jnp.float32)
    mixed = tokens.astype(jnp.float32) + modulate[2] * projected
    mlp_input = (layer_norm(mixed) * (1.0 + modulate[4]) + modulate[3]).astype(jnp.bfloat16)
    hidden = jax.nn.gelu(
        jnp.dot(
            lax.all_gather(mlp_input, "req", axis=0, tiled=True),
            w_up,
            preferred_element_type=jnp.float32,
        ),
        approximate=True,
    ).astype(jnp.bfloat16)
    part_rows = hidden
    mlp_out = lax.psum_scatter(
        jnp.dot(part_rows, w_down, preferred_element_type=jnp.float32).astype(jnp.bfloat16),
        "req",
        scatter_dimension=0,
        tiled=True,
    ).astype(jnp.float32)
    positions = tile_index * row_count + jnp.arange(row_count, dtype=jnp.int32)
    live_rows = positions < length
    finished = jnp.where(live_rows[:, None], mixed + modulate[5] * mlp_out, 0.0)
    return finished.astype(jnp.bfloat16)[None]


def solution(mesh):
    return jax.shard_map(
        per_device,
        mesh=mesh,
        in_specs=(
            P("req", "tile", None),
            P("req", None, None),
            P("req", "tile", None),
            P("req", None, None),
            P("req"),
            P("req", None),
            P(),
            P("req", None),
            P(None, "req"),
            P("req", None),
        ),
        out_specs=P("req", "tile", None),
        check_vma=False,
    )
```

profile of v0, /device:TPU:1, one launch (start us, length us, event | category | flops | bytes accessed | tf_op | source)
XLA Modules:
  0.0 574.7 jit_solution(11674869932821956748)
XLA Ops:
  11.8 7.4 %convolution_convert_fusion = bf16[120,4608]{1,0:T(8,128)(2,1)S(1)} fusion(bf16[1536,4608]{1,0:T(8,128)(2,1)} %param.16, bf16[1,120,1536]{2,1,0:T(8,128)(2,1)} %param.10, f32[1536]{0:T(1024)S(1)} %get-tuple-element.8, f32[1536]{0:T(1024)S(1)} %get-tuple-element.9, f32[120]{0:T(128)S(1)} %add_rsqrt_fusion.1, f32[120]{0:T(128)S(1)} %broadcast_multiply_fusion.1), kind=kOutput, calls=%fused_computation.24 | convolution fusion | flops 1700352000 | bytes 15643584 | tf_op jit(solution)/shard_map/dot_general | solution.py:74
  44.0 2.4 fusion.103
  46.5 2.5 fusion.105
  53.9 231.7 %all-gather.3.cloned.1.call-done = bf16[3840,3072]{1,0:T(8,128)(2,1)} async-done(((bf16[120,3072]{1,0:T(8,128)(2,1)}), bf16[3840,3072]{1,0:T(8,128)(2,1)}) %all-gather.3.cloned.1.call-update) | async-done | bytes 23592976 | tf_op jit(solution)/shard_map/all_gather | solution.py:79
  286.5 17.4 %fusion.100 = (bf16[3840,256]{1,0:T(8,128)(2,1)}, bf16[3840,256]{1,0:T(8,128)(2,1)}, bf16[3840,256]{1,0:T(8,128)(2,1)}, bf16[3840,256]{1,0:T(8,128)(2,1)}, bf16[...) fusion(bf16[3840,3072]{1,0:T(8,128)(2,1)} %slice_dynamic-update, ...), kind=kLoop, calls=%fused_computation.171 | loop fusion | bytes 47185920 | tf_op jit(solution)/shard_map/slice | solution.py:28
  304.0 2.7 copy.116
  306.7 4.1 fusion.111
  310.8 4.1 copy.141
  314.9 2.7 copy.126
  317.6 4.2 fusion.112
  321.8 2.7 copy.131
  324.5 5.0 fusion.113
  329.5 2.7 copy.136
  332.1 4.1 fusion.114
  336.3 4.1 copy.121
  340.4 4.0 copy.139
  344.5 6.2 %fusion.5 = (f32[4,120]{1,0:T(4,128)S(1)}, f32[4,120]{1,0:T(4,128)S(1)}, f32[4,120,3840]{2,1,0:T(8,128)}) fusion(pred[3840]{0:T(1024)(128)(4,1)S(1)} %iota_compare_fusion, f32[4,120,3840]{2,1,0:T(8,128)} %fusion.111, bf16[120,4,64]{0,2,1:T(8,128)(2,1)S(1)} %bitcast.194, bf16[3840,4,64]{0,2,1:T(8,128)(2,1)S(1)} %bitcast.174), kind=kOutput, calls=%fused_computation.23 | convolution fusion | flops 246987840 | bytes 16780800 | tf_op jit(solution)/shard_map/qhe,khe->hqk/dot_general | solution.py:36
  350.9 18.8 %fusion.11 = (f32[4,120]{1,0:T(4,128)S(1)}, f32[4,120]{1,0:T(4,128)}, f32[4,120]{1,0:T(4,128)}, f32[4,120]{1,0:T(4,128)}, f32[4,120]{1,0:T(4,128)}, /*index=5*/f32[4,120]{1,0:T(4,128)}, f32[4,120,3840]{2,1,0:T(8,128)}) fusion(f32[4,120,3840]{2,1,0:T(8,128)} %get-tuple-element.53, f32[4,120]{1,0:T(4,128)S(1)} %max.53, ...), kind=kOutput, calls=%fused_computation.30 | convolution fusion | flops 272790720 | bytes 46283520 | tf_op jit(solution)/shard_map/qhe,khe->hqk/dot_general | solution.py:36
  369.8 4.7 fusion.37
  376.3 2.4 copy.134
  382.5 13.4 %fusion.10 = (f32[4,120]{1,0:T(4,128)S(1)}, f32[4,120]{1,0:T(4,128)}, f32[4,120]{1,0:T(4,128)}, f32[4,120]{1,0:T(4,128)}) fusion(f32[4,120,3840]{2,1,0:T(8,128)} %fusion.114, f32[4,120]{1,0:T(4,128)S(1)} %max.52, pred[3840]{0:T(1024)(128)(4,1)S(1)} %iota_compare_fusion, f32[4,120]{1,0:T(4,128)S(1)} %max.49, f32[4,120,3840]{2,1,0:T(8,128)} %get-tuple-element.58, ...), kind=kLoop, calls=%fused_computation.29 | loop fusion | flops 29489280 | bytes 29510400 | tf_op jit(solution)/shard_map/reduce_sum | solution.py:47
  395.9 4.5 fusion.38
  407.6 5.9 %fusion.39 = f32[120,4,64]{0,2,1:T(8,128)S(1)} fusion(bf16[3840,4,64]{0,2,1:T(8,128)(2,1)} %bitcast.180, f32[4,120,3840]{2,1,0:T(8,128)} %fusion.113, f32[4,120]{1,0:T(4,128)S(1)} %add.158, f32[4,120]{1,0:T(4,128)} %copy-done.39, pred[3840]{0:T(1024)(128)(4,1)S(1)} %iota_compare_fusion), kind=kOutput, calls=%fused_computation.72 | convolution fusion | flops 245145600 | bytes 9469440 | tf_op jit(solution)/shard_map/hqk,khe->qhe/dot_general | solution.py:50
  420.5 5.9 %fusion.40 = f32[120,4,64]{0,2,1:T(8,128)S(1)} fusion(bf16[3840,4,64]{0,2,1:T(8,128)(2,1)} %bitcast.181, f32[4,120,3840]{2,1,0:T(8,128)} %fusion.112, f32[4,120]{1,0:T(4,128)S(1)} %add.156, f32[4,120]{1,0:T(4,128)S(1)} %max.50, pred[3840]{0:T(1024)(128)(4,1)S(1)} %iota_compare_fusion), kind=kOutput, calls=%fused_computation.73 | convolution fusion | flops 245145600 | bytes 9469440 | tf_op jit(solution)/shard_map/hqk,khe->qhe/dot_general | solution.py:50
  429.9 2.5 copy.119
  433.1 5.9 %fusion.41 = f32[120,4,64]{0,2,1:T(8,128)S(1)} fusion(bf16[3840,4,64]{0,2,1:T(8,128)(2,1)} %bitcast.179, f32[4,120,3840]{2,1,0:T(8,128)} %get-tuple-element.58, f32[4,120]{1,0:T(4,128)S(1)} %add.154, f32[4,120]{1,0:T(4,128)S(1)} %max.49, pred[3840]{0:T(1024)(128)(4,1)S(1)} %iota_compare_fusion), kind=kOutput, calls=%fused_computation.74 | convolution fusion | flops 245145600 | bytes 9469440 | tf_op jit(solution)/shard_map/hqk,khe->qhe/dot_general | solution.py:50
  444.5 5.8 %fusion.42 = f32[120,4,64]{0,2,1:T(8,128)S(1)} fusion(bf16[3840,4,64]{0,2,1:T(8,128)(2,1)} %bitcast.178, f32[4,120,3840]{2,1,0:T(8,128)} %fusion.111, f32[4,120]{1,0:T(4,128)S(1)} %add.152, f32[4,120]{1,0:T(4,128)S(1)} %copy-done.45, pred[3840]{0:T(1024)(128)(4,1)S(1)} %iota_compare_fusion), kind=kOutput, calls=%fused_computation.75 | convolution fusion | flops 245145600 | bytes 9469440 | tf_op jit(solution)/shard_map/hqk,khe->qhe/dot_general | solution.py:50
  450.9 12.3 %all_to_all.16 = bf16[120,4,384]{2,0,1:T(8,128)(2,1)S(1)} all-to-all(bf16[120,4,384]{2,0,1:T(8,128)(2,1)S(1)} %bitcast.183), channel_id=1, replica_groups=mesh['req'=4,'tile'=32] {'req'}, dimensions={1} | all-to-all | bytes 737280 | tf_op jit(solution)/shard_map/all_to_all | solution.py:84
  465.4 29.3 %reduce-scatter.3.cloned.1.call-done = bf16[120,1536]{1,0:T(8,128)(2,1)} async-done(((bf16[480,1536]{1,0:T(8,128)(2,1)}), bf16[120,1536]{1,0:T(8,128)(2,1)}) %reduce-scatter.3.cloned.1.call-update) | async-done | bytes 368656 | tf_op jit(solution)/shard_map/reduce_scatter | solution.py:86
  499.3 23.0 %all-gather.5.cloned.1.call-done = bf16[480,1536]{1,0:T(8,128)(2,1)} async-done(((bf16[120,1536]{1,0:T(8,128)(2,1)}), bf16[480,1536]{1,0:T(8,128)(2,1)}) %all-gather.5.cloned.1.call-update) | async-done | bytes 1474576 | tf_op jit(solution)/shard_map/all_gather | solution.py:96
  522.3 10.1 %convolution_convert_fusion.1 = bf16[480,1536]{1,0:T(8,128)(2,1)} fusion(bf16[1536,1536]{1,0:T(8,128)(2,1)} %param.19, bf16[480,1536]{1,0:T(8,128)(2,1)} %all-gather.5.cloned.1.call-done, bf16[1536,1536]{1,0:T(8,128)(2,1)} %param.18), kind=kOutput, calls=%fused_computation.46 | convolution fusion | flops 4537221120 | bytes 12386304 | tf_op jit(solution)/shard_map/dot_general | solution.py:104
  532.4 33.5 %reduce-scatter.5.cloned.1.call-done = bf16[120,1536]{1,0:T(8,128)(2,1)} async-done(((bf16[480,1536]{1,0:T(8,128)(2,1)}), bf16[120,1536]{1,0:T(8,128)(2,1)}) %reduce-scatter.5.cloned.1.call-update) | async-done | bytes 368656 | tf_op jit(solution)/shard_map/reduce_scatter | solution.py:103
  (182 shorter events, 73.6 us)
Async XLA Ops:
  6.5 456.7 %copy-start = (bf16[384,1536]{1,0:T(8,128)(2,1)S(1)}, bf16[384,1536]{1,0:T(8,128)(2,1)}, u32[]{:S(2)}) copy-start(bf16[384,1536]{1,0:T(8,128)(2,1)} %param.17) | copy-start | bytes 3538948
  6.5 279.1 %all-gather.3.cloned.1.call-start = ((), (), s32[]{:S(2)}) async-start(), calls=%async_computation.3 | async-start | bytes 24330240 | tf_op jit(solution)/shard_map/all_gather | solution.py:79
  11.8 7.4 %copy-start.23 = (bf16[1,120,3072]{2,1,0:T(8,128)(2,1)S(1)}, bf16[1,120,3072]{2,1,0:T(8,128)(2,1)}, u32[]{:S(2)}) copy-start(bf16[1,120,3072]{2,1,0:T(8,128)(2,1)} %param.12) | copy-start | bytes 2211844
  11.8 11.3 %copy-start.17 = (bf16[1,154,3072]{2,1,0:T(8,128)(2,1)S(1)}, bf16[1,154,3072]{2,1,0:T(8,128)(2,1)}, u32[]{:S(2)}) copy-start(bf16[1,154,3072]{2,1,0:T(8,128)(2,1)} %param.13) | copy-start | bytes 2838532
  20.9 473.8 %reduce-scatter.3.cloned.1.call-start = ((), (), s32[]{:S(2)}) async-start(), calls=%async_computation.4 | async-start | bytes 1843200 | tf_op jit(solution)/shard_map/reduce_scatter | solution.py:86
  27.0 277.0 %copy-start.21 = (bf16[120,256]{0,1:T(8,128)(2,1)}, bf16[120,256]{0,1:T(8,128)(2,1)S(1)}, u32[]{:S(2)}) copy-start(bf16[120,256]{0,1:T(8,128)(2,1)S(1)} %copy.125) | copy-start | bytes 184324
  27.9 276.0 %copy-start.20 = (bf16[120,256]{0,1:T(8,128)(2,1)}, bf16[120,256]{0,1:T(8,128)(2,1)S(1)}, u32[]{:S(2)}) copy-start(bf16[120,256]{0,1:T(8,128)(2,1)S(1)} %copy.130) | copy-start | bytes 184324
  28.9 275.1 %copy-start.18 = (bf16[120,256]{0,1:T(8,128)(2,1)}, bf16[120,256]{0,1:T(8,128)(2,1)S(1)}, u32[]{:S(2)}) copy-start(bf16[120,256]{0,1:T(8,128)(2,1)S(1)} %copy.135) | copy-start | bytes 184324
  310.8 6.8 %copy-start.22 = (bf16[120,256]{0,1:T(8,128)(2,1)S(1)}, bf16[120,256]{0,1:T(8,128)(2,1)}, u32[]{:S(2)}) copy-start(bf16[120,256]{0,1:T(8,128)(2,1)} %copy-done.21) | copy-start | bytes 184324
  324.5 7.7 %copy-start.19 = (bf16[120,256]{0,1:T(8,128)(2,1)S(1)}, bf16[120,256]{0,1:T(8,128)(2,1)}, u32[]{:S(2)}) copy-start(bf16[120,256]{0,1:T(8,128)(2,1)} %copy-done.18) | copy-start | bytes 184324
  336.3 8.2 %copy-start.7 = (bf16[3840,256]{0,1:T(8,128)(2,1)S(1)}, bf16[3840,256]{0,1:T(8,128)(2,1)}, u32[]{:S(2)}) copy-start(bf16[3840,256]{0,1:T(8,128)(2,1)} %copy.141) | copy-start | bytes 5898244
  336.3 8.2 %copy-start.24 = (bf16[120,256]{0,1:T(8,128)(2,1)S(1)}, bf16[120,256]{0,1:T(8,128)(2,1)}, u32[]{:S(2)}) copy-start(bf16[120,256]{0,1:T(8,128)(2,1)} %copy.140) | copy-start | bytes 184324
  344.5 6.4 %copy-start.10 = (bf16[3840,256]{0,1:T(8,128)(2,1)S(1)}, bf16[3840,256]{0,1:T(8,128)(2,1)}, u32[]{:S(2)}) copy-start(bf16[3840,256]{0,1:T(8,128)(2,1)} %copy.121) | copy-start | bytes 5898244
  344.5 6.4 %copy-start.25 = (bf16[120,256]{0,1:T(8,128)(2,1)S(1)}, bf16[120,256]{0,1:T(8,128)(2,1)}, u32[]{:S(2)}) copy-start(bf16[120,256]{0,1:T(8,128)(2,1)} %copy.120) | copy-start | bytes 184324
  350.8 19.0 %copy-start.44 = (f32[4,120]{1,0:T(4,128)}, f32[4,120]{1,0:T(4,128)S(1)}, u32[]{:S(2)}) copy-start(f32[4,120]{1,0:T(4,128)S(1)} %max.48) | copy-start | bytes 5764
  350.9 18.8 %copy-start.9 = (bf16[3840,256]{0,1:T(8,128)(2,1)S(1)}, bf16[3840,256]{0,1:T(8,128)(2,1)}, u32[]{:S(2)}) copy-start(bf16[3840,256]{0,1:T(8,128)(2,1)} %copy.139) | copy-start | bytes 5898244
  369.7 6.5 %copy-start.6 = (bf16[3840,256]{1,0:T(8,128)(2,1)S(1)}, bf16[3840,256]{1,0:T(8,128)(2,1)}, u32[]{:S(2)}) copy-start(bf16[3840,256]{1,0:T(8,128)(2,1)} %get-tuple-element.26) | copy-start | bytes 5898244
  369.7 9.0 %copy-start.41 = (f32[4,120]{1,0:T(4,128)S(1)}, f32[4,120]{1,0:T(4,128)}, u32[]{:S(2)}) copy-start(f32[4,120]{1,0:T(4,128)} %get-tuple-element.59) | copy-start | bytes 5764
  382.5 13.4 %copy-start.39 = (f32[4,120]{1,0:T(4,128)}, f32[4,120]{1,0:T(4,128)S(1)}, u32[]{:S(2)}) copy-start(f32[4,120]{1,0:T(4,128)S(1)} %max.51) | copy-start | bytes 5764
  382.5 13.4 %copy-start.11 = (bf16[3840,256]{0,1:T(8,128)(2,1)S(1)}, bf16[3840,256]{0,1:T(8,128)(2,1)}, u32[]{:S(2)}) copy-start(bf16[3840,256]{0,1:T(8,128)(2,1)} %copy.134) | copy-start | bytes 5898244
  395.9 8.6 %copy-start.5 = (bf16[3840,256]{1,0:T(8,128)(2,1)S(1)}, bf16[3840,256]{1,0:T(8,128)(2,1)}, u32[]{:S(2)}) copy-start(bf16[3840,256]{1,0:T(8,128)(2,1)} %get-tuple-element.28) | copy-start | bytes 5898244
  407.5 9.9 %copy-start.4 = (bf16[3840,256]{1,0:T(8,128)(2,1)S(1)}, bf16[3840,256]{1,0:T(8,128)(2,1)}, u32[]{:S(2)}) copy-start(bf16[3840,256]{1,0:T(8,128)(2,1)} %get-tuple-element.30) | copy-start | bytes 5898244
  420.5 9.4 %copy-start.3 = (bf16[3840,256]{1,0:T(8,128)(2,1)S(1)}, bf16[3840,256]{1,0:T(8,128)(2,1)}, u32[]{:S(2)}) copy-start(bf16[3840,256]{1,0:T(8,128)(2,1)} %get-tuple-element.32) | copy-start | bytes 5898244
  433.1 8.4 %copy-start.45 = (f32[4,120]{1,0:T(4,128)S(1)}, f32[4,120]{1,0:T(4,128)}, u32[]{:S(2)}) copy-start(f32[4,120]{1,0:T(4,128)} %copy-done.44) | copy-start | bytes 5764
  433.1 8.4 %copy-start.2 = (bf16[3840,256]{1,0:T(8,128)(2,1)S(1)}, bf16[3840,256]{1,0:T(8,128)(2,1)}, u32[]{:S(2)}) copy-start(bf16[3840,256]{1,0:T(8,128)(2,1)} %get-tuple-element.34) | copy-start | bytes 5898244
  450.4 44.4 %copy-start.1 = (bf16[1,120,1536]{2,1,0:T(8,128)(2,1)S(1)}, bf16[1,120,1536]{2,1,0:T(8,128)(2,1)}, u32[]{:S(2)}) copy-start(bf16[1,120,1536]{2,1,0:T(8,128)(2,1)} %param.10) | copy-start | bytes 1105924
  450.4 46.8 %copy-start.37 = (f32[1536]{0:T(1024)S(1)}, f32[1536]{0:T(1024)}, u32[]{:S(2)}) copy-start(f32[1536]{0:T(1024)} %get-tuple-element.6) | copy-start | bytes 18436
  450.4 46.8 %copy-start.38 = (f32[1536]{0:T(1024)S(1)}, f32[1536]{0:T(1024)}, u32[]{:S(2)}) copy-start(f32[1536]{0:T(1024)} %get-tuple-element.7) | copy-start | bytes 18436
  465.3 57.0 %all-gather.5.cloned.1.call-start = ((), (), s32[]{:S(2)}) async-start(), calls=%async_computation.5 | async-start | bytes 1843200 | tf_op jit(solution)/shard_map/all_gather | solution.py:96
  499.2 66.7 %copy-start.8 = (bf16[120,1536]{1,0:T(8,128)(2,1)S(1)}, bf16[120,1536]{1,0:T(8,128)(2,1)}, u32[]{:S(2)}) copy-start(bf16[120,1536]{1,0:T(8,128)(2,1)} %reduce-scatter.3.cloned.1.call-done) | copy-start | bytes 1105924
  499.2 66.7 %copy-start.36 = (f32[1536]{0:T(1024)S(1)}, f32[1536]{0:T(1024)}, u32[]{:S(2)}) copy-start(f32[1536]{0:T(1024)} %get-tuple-element.5) | copy-start | bytes 18436
  499.2 66.7 %reduce-scatter.5.cloned.1.call-start = ((), (), s32[]{:S(2)}) async-start(), calls=%async_computation.6 | async-start | bytes 1843200 | tf_op jit(solution)/shard_map/reduce_scatter | solution.py:103
  (18 other events, 105.1 us)
Sparse Core Ops, SparseCore 0:
  21.0 264.5 all-gather.2
  465.4 29.2 reduce-scatter.2
  499.3 22.8 all-gather.4
  532.5 33.3 reduce-scatter.4
where the time goes:
time: 581 us; the launch traced here: 575 us
  waiting for transfers between devices  318 us (55%)
  matrix products  110 us (19%)
  local copies, waits for them, and re-layouts  82.4 us (14%)
  other arithmetic  37.5 us (6%)
  between operations  14.8 us (3%)
  blocking collectives  12.3 us (2%)
    all_gather x1, waiting for transfers between devices, per_device(): key_rows = lax.all_gather(outgoing, 'tile', axis=0, tiled=True)  232 us
    dot_general x6, matrix products, attend(): jnp.einsum('qhe,khe->hqk', q_part, img_keys, preferred_element_type=jnp.f...  42.5 us
    reduce_scatter x1, waiting for transfers between devices, per_device(): lax.psum_scatter(jnp.dot(part_rows, w_down, preferred_element_type=jnp.fl...  33.5 us
    slice x7, local copies, waits for them, and re-layouts, attend(): key_rows[:, model_width + col_low:model_width + col_high]  33.5 us
    dot_general x6, matrix products, attend(): jnp.einsum('hqk,khe->qhe', img_weights, img_vals, preferred_element_type=...  32.8 us
    reduce_scatter x1, waiting for transfers between devices, per_device(): lax.psum_scatter(jnp.dot(part_rows, w_out, preferred_element_type=jnp.flo...  29.3 us
    all_gather x1, waiting for transfers between devices, per_device(): lax.all_gather(mlp_input, 'req', axis=0, tiled=True)  23 us
    slice x6, local copies, waits for them, and re-layouts, attend(): img_keys = key_rows[:, col_low:col_high].reshape(-1, head_group, head_size)  18.9 us
  transfers between devices with their start and end apart: 4, of which 4 were waited for; matrix products, arithmetic and copies ran while one was open for 6% of the time, Pallas kernels for 0%

commit v1 on v0

v1 whole, which is shorter than its diff:
```python
import functools

import jax
import jax.numpy as jnp
from jax import lax
from jax.experimental import pallas as pl
from jax.experimental.pallas import tpu as pltpu
from jax.sharding import Mesh
from jax.sharding import PartitionSpec as P

REQ = ("zh", "co")
TILE = ("y", "zl", "x")
HEAD = 64
BIG = 1e30
F32 = jnp.float32
BF16 = jnp.bfloat16


def layer_norm(values):
    average = jnp.mean(values, -1, keepdims=True)
    centred = values - average
    spread = jnp.mean(centred * centred, -1, keepdims=True)
    return centred * lax.rsqrt(spread + 1e-06)


def lane_iota(shape):
    return lax.broadcasted_iota(jnp.int32, shape, len(shape) - 1)


def row_iota(shape):
    return lax.broadcasted_iota(jnp.int32, shape, len(shape) - 2)


def swap_halves(values):
    return pltpu.roll(values, HEAD, axis=1)


def project_kernel(
    flag_ref, tokens_ref, mod_ref, wq_ref, wk_ref, wv_ref, ck_ref, cv_ref, send_ref, own_ref, normed_ref
):
    step = pl.program_id(0)
    rows = tokens_ref.shape[0]
    half = send_ref.shape[1] - rows

    @pl.when(step == 0)
    def _():
        shift = mod_ref[0:1, :].astype(F32)
        scale = mod_ref[1:2, :].astype(F32)
        normed = layer_norm(tokens_ref[...].astype(F32)) * (1.0 + scale) + shift
        normed_ref[...] = normed.astype(BF16)

    normed = normed_ref[...]
    wide = wq_ref.shape[1]
    heads = wide // HEAD
    queries = jnp.dot(normed, wq_ref[...], preferred_element_type=F32) * 0.125
    keys = jnp.dot(normed, wk_ref[...], preferred_element_type=F32)
    values = jnp.dot(normed, wv_ref[...], preferred_element_type=F32)
    flagged = flag_ref[0] != 0
    low = lane_iota((rows, 2 * HEAD)) < HEAD
    low_q = lane_iota((half, 2 * HEAD)) < HEAD
    pad = jnp.zeros((2 * half - rows, 2 * HEAD), F32)
    for pair in range(heads // 2):
        cols = slice(pair * 2 * HEAD, (pair + 1) * 2 * HEAD)
        q_top = queries[:half, cols]
        q_end = jnp.concatenate([queries[half:, cols], pad], axis=0)
        k_new, v_new = keys[:, cols], values[:, cols]
        k_out = jnp.where(flagged, k_new, ck_ref[:, cols].astype(F32))
        v_out = jnp.where(flagged, v_new, cv_ref[:, cols].astype(F32))
        for odd in range(2):
            if odd:
                q_pack = jnp.where(low_q, swap_halves(q_top), q_end)
                join = lambda k, v: jnp.where(low, swap_halves(k), v)
            else:
                q_pack = jnp.where(low_q, q_top, swap_halves(q_end))
                join = lambda k, v: jnp.where(low, k, swap_halves(v))
            q_pack = q_pack.astype(BF16)
            sent = join(k_out, v_out).astype(BF16)
            head = step * heads + pair * 2 + odd
            dest = head + head // 3
            own_ref[head, :rows, :] = join(k_new, v_new).astype(BF16)
            own_ref[head, rows:, :] = q_pack
            send_ref[dest, :rows, :] = sent
            send_ref[dest, rows:, :] = q_pack

            @pl.when(head % 3 == 2)
            def _():
                send_ref[dest + 1, :rows, :] = sent
                send_ref[dest + 1, rows:, :] = q_pack


def project(flag, tokens, modulate, w_qkv, cached):
    rows, width = tokens.shape
    half = 64
    block = 256
    steps = width // block
    heads = width // HEAD
    dests = heads + heads // 3
    whole = lambda *shape: pl.BlockSpec(shape, lambda s: (0,) * len(shape))
    return pl.pallas_call(
        project_kernel,
        grid=(steps,),
        out_shape=(
            jax.ShapeDtypeStruct((dests, rows + half, 2 * HEAD), BF16),
            jax.ShapeDtypeStruct((heads, rows + half, 2 * HEAD), BF16),
        ),
        in_specs=[
            pl.BlockSpec(memory_space=pltpu.SMEM),
            whole(rows, width),
            whole(6, width),
            pl.BlockSpec((width, block), lambda s: (0, s)),
            pl.BlockSpec((width, block), lambda s: (0, s + steps)),
            pl.BlockSpec((width, block), lambda s: (0, s + 2 * steps)),
            pl.BlockSpec((rows, block), lambda s: (0, s)),
            pl.BlockSpec((rows, block), lambda s: (0, s + steps)),
        ],
        out_specs=(
            whole(dests, rows + half, 2 * HEAD),
            whole(heads, rows + half, 2 * HEAD),
        ),
        scratch_shapes=[pltpu.VMEM((rows, width), BF16)],
        compiler_params=pltpu.CompilerParams(vmem_limit_bytes=40 << 20),
        name="project",
    )(flag, tokens, modulate, w_qkv, w_qkv, w_qkv, cached, cached)


def own_kernel(live_ref, own_ref, tk_ref, tv_ref, out_ref):
    rows = out_ref.shape[1]
    texts = tk_ref.shape[0]
    half = own_ref.shape[1] - rows
    low = lane_iota((rows, 2 * HEAD)) < HEAD
    live = lane_iota((rows, rows)) < live_ref[0]
    nt = (((1,), (1,)), ((), ()))
    text_keys = tk_ref[...]
    text_values = tv_ref[...]
    for odd in range(2):
        kv = own_ref[odd, :rows, :]
        folded = own_ref[odd, rows:, :].astype(F32)
        query = jnp.concatenate([folded, swap_halves(folded)[: rows - half]], axis=0)
        query = jnp.where(low, query, 0.0)
        text_query = swap_halves(query) if odd else query
        query = query.astype(BF16)
        text_query = text_query.astype(BF16)
        s_own = lax.dot_general(query, kv, nt, preferred_element_type=F32)
        s_own = jnp.where(live, s_own, -BIG)
        s_text = lax.dot_general(text_query, text_keys, nt, preferred_element_type=F32)
        top = jnp.maximum(
            jnp.max(s_own, -1, keepdims=True), jnp.max(s_text, -1, keepdims=True)
        )
        p_own = jnp.exp(s_own - top)
        p_text = jnp.exp(s_text - top)
        total = jnp.sum(p_own, -1, keepdims=True) + jnp.sum(p_text, -1, keepdims=True)
        mixed = jnp.dot(p_own.astype(BF16), kv, preferred_element_type=F32)
        from_text = jnp.dot(p_text.astype(BF16), text_values, preferred_element_type=F32)
        if not odd:
            from_text = swap_halves(from_text)
        mixed = (mixed + from_text) / total
        out_ref[odd] = jnp.where(low, top + jnp.log(total), mixed)


def own_attend(live, own, text_rows):
    heads, packed, _ = own.shape
    rows = packed - 64
    texts, width2 = text_rows.shape
    pairs = heads // 2
    return pl.pallas_call(
        own_kernel,
        grid=(pairs,),
        out_shape=jax.ShapeDtypeStruct((heads, rows, 2 * HEAD), F32),
        in_specs=[
            pl.BlockSpec(memory_space=pltpu.SMEM),
            pl.BlockSpec((2, packed, 2 * HEAD), lambda p: (p, 0, 0)),
            pl.BlockSpec((texts, 2 * HEAD), lambda p: (0, p)),
            pl.BlockSpec((texts, 2 * HEAD), lambda p: (0, p + pairs)),
        ],
        out_specs=pl.BlockSpec((2, rows, 2 * HEAD), lambda p: (p, 0, 0)),
        compiler_params=pltpu.CompilerParams(vmem_limit_bytes=16 << 20),
        cost_estimate=pl.CostEstimate(
            flops=2 * 4 * rows * (rows + texts) * 64 * heads,
            bytes_accessed=6 << 20,
            transcendentals=rows * (rows + texts) * heads,
        ),
        name="own_attend",
    )(live, own, text_rows, text_rows)


def head_kernel(len_ref, pack_ref, out_ref, q_ref, k_ref, v_ref, kt_ref, s_ref):
    step = pl.program_id(0)
    tiles, packed, _ = pack_ref.shape
    rows = packed - 64
    total_rows = tiles * rows
    block = out_ref.shape[0]
    chunk = 256

    @pl.when(step == 0)
    def _():
        low = lane_iota((2 * rows, 2 * HEAD)) < HEAD
        feature = lane_iota((2 * rows, 2 * HEAD)) - HEAD
        second = (row_iota((2 * rows, 2 * HEAD)) >= rows).astype(jnp.int32)

        def fill(pair, carry):
            first = 2 * pair
            kv = jnp.concatenate(
                [pack_ref[first, :rows, :].astype(F32), pack_ref[first + 1, :rows, :].astype(F32)],
                axis=0,
            )
            parts = []
            for t in range(2):
                folded = pack_ref[first + t, rows:, :].astype(F32)
                parts += [folded, swap_halves(folded)[: rows - 64]]
            query = jnp.concatenate(parts, axis=0)
            tile = first + second
            masked = jnp.logical_or(feature == tile, feature == 32)
            query = jnp.where(low, query, jnp.where(masked, -BIG, 0.0))
            index = pair * 2 * rows + row_iota((2 * rows, 2 * HEAD))
            dead = jnp.logical_and(feature == 32, index >= len_ref[0])
            held = jnp.logical_or(feature == tile, dead)
            key = jnp.where(low, kv, jnp.where(held, 1.0, 0.0))
            at = pl.ds(pl.multiple_of(pair * 2 * rows, 16), 2 * rows)
            q_ref[at, :] = query.astype(BF16)
            k_ref[at, :] = key.astype(BF16)
            v_ref[at, :] = jnp.where(low, 1.0, kv).astype(BF16)
            return carry

        lax.fori_loop(0, tiles // 2, fill, 0)
        for c in range(total_rows // chunk):
            part = slice(c * chunk, (c + 1) * chunk)
            kt_ref[:, part] = jnp.transpose(k_ref[part, :].astype(F32)).astype(BF16)

    query = q_ref[pl.ds(pl.multiple_of(step * block, block), block), :]
    top = jnp.full((block, 128), -jnp.inf, F32)
    for c in range(total_rows // chunk):
        part = slice(c * chunk, (c + 1) * chunk)
        scores = jnp.dot(query, kt_ref[:, part], preferred_element_type=F32)
        s_ref[:, part] = scores
        for i in range(chunk // 128):
            top = jnp.maximum(top, scores[:, i * 128 : (i + 1) * 128])
    top = jnp.max(top, -1, keepdims=True)
    total = jnp.zeros((block, 2 * HEAD), F32)
    for c in range(total_rows // chunk):
        part = slice(c * chunk, (c + 1) * chunk)
        probs = jnp.exp(s_ref[:, part] - top).astype(BF16)
        total = total + jnp.dot(probs, v_ref[part, :], preferred_element_type=F32)
    weight = total[:, 0:1]
    lse = top + jnp.log(weight)
    high = lse.astype(BF16).astype(F32)
    lane = lane_iota((block, 2 * HEAD))
    result = jnp.where(lane < 32, high, jnp.where(lane < HEAD, lse - high, total / weight))
    out_ref[...] = result.astype(BF16)


def head_attend(length, pack):
    tiles, packed, lanes = pack.shape
    rows = packed - 64
    total_rows = tiles * rows
    block = 384
    return pl.pallas_call(
        head_kernel,
        grid=(total_rows // block,),
        out_shape=jax.ShapeDtypeStruct((total_rows, lanes), BF16),
        in_specs=[
            pl.BlockSpec(memory_space=pltpu.SMEM),
            pl.BlockSpec((tiles, packed, lanes), lambda s: (0, 0, 0)),
        ],
        out_specs=pl.BlockSpec((block, lanes), lambda s: (s, 0)),
        scratch_shapes=[
            pltpu.VMEM((total_rows, lanes), BF16),
            pltpu.VMEM((total_rows, lanes), BF16),
            pltpu.VMEM((total_rows, lanes), BF16),
            pltpu.VMEM((lanes, total_rows), BF16),
            pltpu.VMEM((block, total_rows), F32),
        ],
        compiler_params=pltpu.CompilerParams(vmem_limit_bytes=40 << 20),
        name="head_attend",
    )(length, pack)


def merge_kernel(far_ref, own_ref, out_ref):
    heads = own_ref.shape[0]
    rows = own_ref.shape[1]
    low = lane_iota((rows, 2 * HEAD)) < HEAD
    for pair in range(heads // 2):
        both = []
        for odd in range(2):
            head = 2 * pair + odd
            far = far_ref[head + head // 3].astype(F32)
            own = own_ref[head]
            far_lse = far[:, 0:1] + far[:, 32:33]
            own_lse = own[:, 0:1]
            share = 1.0 / (1.0 + jnp.exp(own_lse - far_lse))
            other = 1.0 / (1.0 + jnp.exp(far_lse - own_lse))
            both.append(share * far + other * own)
        joined = jnp.where(low, swap_halves(both[0]), both[1])
        out_ref[:, pair * 2 * HEAD : (pair + 1) * 2 * HEAD] = joined.astype(BF16)


def merge(far, own):
    heads, rows, lanes = own.shape
    return pl.pallas_call(
        merge_kernel,
        out_shape=jax.ShapeDtypeStruct((rows, heads * HEAD), BF16),
        in_specs=[pl.BlockSpec(memory_space=pltpu.VMEM)] * 2,
        out_specs=pl.BlockSpec(memory_space=pltpu.VMEM),
        compiler_params=pltpu.CompilerParams(vmem_limit_bytes=16 << 20),
        name="merge",
    )(far, own)


def swap(values, axis):
    return lax.ppermute(values, axis, [(0, 1), (1, 0)])


def per_device(
    latents, modulation, kv_cache, text_kv, lengths, refresh, w_qkv, w_out, w_up, w_down
):
    tokens = latents[0]
    rows = tokens.shape[0]
    modulate = modulation[0].astype(F32)
    tile_index = lax.axis_index(TILE)
    length = lengths[0]
    flag = jnp.any(refresh[0] == tile_index).astype(jnp.int32).reshape(1)
    all_w_out = lax.all_gather(w_out, REQ, axis=0, tiled=True)
    send, own = project(flag, tokens, modulation[0], w_qkv, kv_cache[0])
    pack = lax.all_to_all(send, TILE, split_axis=0, concat_axis=0, tiled=True)
    live = (length - tile_index * rows).reshape(1)
    own_part = own_attend(live, own, text_kv[0])
    far = head_attend(length.reshape(1), pack)
    far = lax.all_to_all(
        far.reshape(-1, rows, 2 * HEAD), TILE, split_axis=0, concat_axis=0, tiled=True
    )
    attended = merge(far, own_part)
    projected = jnp.dot(attended, all_w_out, preferred_element_type=F32)
    mixed = tokens.astype(F32) + modulate[2] * projected
    mlp_input = (layer_norm(mixed) * (1.0 + modulate[4]) + modulate[3]).astype(BF16)

    def feed(values):
        hidden = jax.nn.gelu(jnp.dot(values, w_up, preferred_element_type=F32), approximate=True)
        return jnp.dot(hidden.astype(BF16), w_down, preferred_element_type=F32)

    far_z = swap(mlp_input, "zh")
    near = swap(mlp_input, "co")
    far_both = swap(far_z, "co")
    parts_near = feed(jnp.concatenate([mlp_input, near], axis=0))
    parts_far = feed(jnp.concatenate([far_z, far_both], axis=0))
    sum_far = parts_far[:rows] + swap(parts_far[rows:].astype(BF16), "co").astype(F32)
    sum_near = parts_near[:rows] + swap(parts_near[rows:].astype(BF16), "co").astype(F32)
    mlp_out = sum_near + swap(sum_far.astype(BF16), "zh").astype(F32)
    positions = tile_index * rows + jnp.arange(rows, dtype=jnp.int32)
    live_rows = positions < length
    finished = jnp.where(live_rows[:, None], mixed + modulate[5] * mlp_out, 0.0)
    return finished.astype(BF16)[None]


def solution(mesh):
    fine = Mesh(mesh.devices.reshape(2, 2, 4, 2, 4), REQ + TILE)
    return jax.shard_map(
        per_device,
        mesh=fine,
        in_specs=(
            P(REQ, TILE, None),
            P(REQ, None, None),
            P(REQ, TILE, None),
            P(REQ, None, None),
            P(REQ),
            P(REQ, None),
            P(),
            P(REQ, None),
            P(None, REQ),
            P(REQ, None),
        ),
        out_specs=P(REQ, TILE, None),
        check_vma=False,
    )
```

time: 581 us -> 165 us (0.28)
  waiting for transfers between devices: 318 us -> 42 us
  matrix products: 110 us -> 15.9 us
  local copies, waits for them, and re-layouts: 82.4 us -> 4.52 us
  Pallas kernels: 0 us -> 57.1 us
  other arithmetic: 37.5 us -> 3.98 us
  starting transfers between devices: 0.13 us -> 25.6 us
  blocking collectives: 12.3 us -> 0 us
    all_gather x2 -> x1, waiting for transfers between devices: 255 us -> 0.02 us  [per_device(): all_w_out = lax.all_gather(w_out, REQ, axis=0, tiled=True)]
    dot_general x27 -> x3, matrix products: 110 us -> 15.9 us  [the longest x2 12.6 us: feed(): return jnp.dot(hidden.astype(BF16), w_down, preferred_element_type=F32)]
    slice x33 -> x2, local copies, waits for them, and re-layouts: 73.9 us -> 0.08 us  [the longest x1 0.04 us: per_device(): parts_far[rows:].astype(BF16)]
    reduce_scatter x2 -> x0, waiting for transfers between devices: 62.9 us -> none  [the longest x1 33.5 us: per_device(): lax.psum_scatter(jnp.dot(part_rows, w_down, preferred_element_type=jnp.fl...]
    pallas_call x0 -> x4, Pallas kernels: none -> 57.1 us  [the longest x1 34.8 us: head_attend(): pl.pallas_call(head_kernel, grid=(total_rows // block,), out_shape=jax.Sh...]
    all_to_all x0 -> x2, waiting for transfers between devices: none -> 24.2 us  [the longest x1 20 us: per_device(): pack = lax.all_to_all(send, TILE, split_axis=0, concat_axis=0, tiled=True)]
    reduce_sum x9 -> x0, other arithmetic: 21.2 us -> none  [the longest x1 13.4 us: attend(): jnp.sum(img_probs, -1, keepdims=True)]
    ppermute x0 -> x6, waiting for transfers between devices: none -> 17.1 us  [swap(): return lax.ppermute(values, axis, [(0, 1), (1, 0)])]
  transfers between devices with their start and end apart: 4 -> 9, of which waited for: 4 -> 5; matrix products, arithmetic and copies ran while one was open for 6% -> 9% of each run, Pallas kernels for 0% -> 35%
where the time goes in v1:
time: 165 us; the launch traced here: 164 us
  Pallas kernels  57.1 us (35%)
  waiting for transfers between devices  42 us (25%)
  starting transfers between devices  25.6 us (16%)
  matrix products  15.9 us (10%)
  between operations  14.9 us (9%)
  local copies, waits for them, and re-layouts  4.52 us (3%)
  other arithmetic  3.98 us (2%)
    pallas_call x1, Pallas kernels, head_attend(): pl.pallas_call(head_kernel, grid=(total_rows // block,), out_shape=jax.Sh...  34.8 us
    all_to_all x1, waiting for transfers between devices, per_device(): pack = lax.all_to_all(send, TILE, split_axis=0, concat_axis=0, tiled=True)  20 us
    ppermute x6, waiting for transfers between devices, swap(): return lax.ppermute(values, axis, [(0, 1), (1, 0)])  17.1 us
    dot_general x2, matrix products, feed(): return jnp.dot(hidden.astype(BF16), w_down, preferred_element_type=F32)  12.6 us
    ppermute x6, starting transfers between devices, swap(): return lax.ppermute(values, axis, [(0, 1), (1, 0)])  10.4 us
    pallas_call x1, Pallas kernels, project(): pl.pallas_call(project_kernel, grid=(steps,), out_shape=(jax.ShapeDtypeSt...  10.1 us
    all_to_all x1, starting transfers between devices, per_device(): pack = lax.all_to_all(send, TILE, split_axis=0, concat_axis=0, tiled=True)  9.22 us
    pallas_call x1, Pallas kernels, own_attend(): pl.pallas_call(own_kernel, grid=(pairs,), out_shape=jax.ShapeDtypeStruct(...  9.12 us
  transfers between devices with their start and end apart: 9, of which 5 were waited for; matrix products, arithmetic and copies ran while one was open for 9% of the time, Pallas kernels for 35%

profile of v1, /device:TPU:1, one launch (start us, length us, event | category | flops | bytes accessed | tf_op | source)
XLA Modules:
  0.0 164.0 jit_solution(5346130450418623718)
XLA Ops:
  6.5 0.7 all-gather.2.cloned.1.call-update
  7.3 1.3 compare_reduce_fusion
  9.2 1.0 copy-done.2
  10.2 0.7 copy-done.6
  11.0 10.1 %project.1 = (bf16[32,184,128]{2,1,0:T(8,128)(2,1)}, bf16[24,184,128]{2,1,0:T(8,128)(2,1)S(1)}) custom-call(s32[1]{0:T(128)} %bitcast.3.flag_ref, bf16[120,1536]{1,0:T(8,128)(2,1)S(1)} %bitcast.24, bf16[6,1536]{1,0:T(8,128)(2,1)S(1)} %bitcast.25, bf16[1536,4608]{1,0:T(8,128)(2,1)} %wv_ref.1, bf16[1536,4608]{1,0:T(8,128)(2,1)} %wv_ref.1, ...), custom_call_target="tpu_custom_call" | custom-call | tf_op jit(solution)/shard_map/project/pallas_call | solution.py:99
  21.1 1.0 copy-done.4
  22.1 9.2 %all-to-all-start = ((bf16[32,184,128]{2,1,0:T(8,128)(2,1)}), bf16[32,184,128]{2,1,0:T(8,128)(2,1)S(1)}, u32[]{:S(2)}, u32[]{:S(2)}) async-start(bf16[32,184,128]{2,1,0:T(8,128)(2,1)} %get-tuple-element.7), calls=%async_computation | async-start | bytes 3014656 | tf_op jit(solution)/shard_map/all_to_all | solution.py:323
  32.0 20.0 %all-to-all-done.pack_ref = bf16[32,184,128]{2,1,0:T(8,128)(2,1)S(1)} async-done(((bf16[32,184,128]{2,1,0:T(8,128)(2,1)}), bf16[32,184,128]{2,1,0:T(8,128)(2,1)S(1)}, u32[]{:S(2)}, u32[]{:S(2)}) %all-to-all-start) | async-done | bytes 1507360 | tf_op jit(solution)/shard_map/all_to_all | solution.py:323
  52.0 34.8 %head_attend.1 = bf16[3840,128]{1,0:T(8,128)(2,1)} custom-call(s32[1]{0:T(128)} %copy.11.len_ref, bf16[32,184,128]{2,1,0:T(8,128)(2,1)S(1)} %all-to-all-done.pack_ref), custom_call_target="tpu_custom_call" | custom-call | tf_op jit(solution)/shard_map/head_attend/pallas_call | solution.py:256
  86.8 6.0 %all-to-all-start.1 = ((bf16[32,120,128]{2,1,0:T(8,128)(2,1)}), bf16[32,120,128]{2,1,0:T(8,128)(2,1)S(1)}, u32[]{:S(2)}, u32[]{:S(2)}) async-start(bf16[32,120,128]{2,1,0:T(8,128)(2,1)} %bitcast.5), calls=%async_computation.1 | async-start | bytes 1966080 | tf_op jit(solution)/shard_map/all_to_all | solution.py:327
  92.8 1.2 copy-done.5
  94.1 9.1 %own_attend.1.own_ref = f32[24,120,128]{2,1,0:T(8,128)S(1)} custom-call(s32[1]{0:T(128)} %bitcast.6.live_ref, bf16[24,184,128]{2,1,0:T(8,128)(2,1)S(1)} %copy-done.5, bf16[154,3072]{1,0:T(8,128)(2,1)S(1)} %bitcast.20, bf16[154,3072]{1,0:T(8,128)(2,1)S(1)} %bitcast.21), custom_call_target="tpu_custom_call" | custom-call | flops 404029440 | bytes 6291456 | tf_op jit(solution)/shard_map/own_attend/pallas_call | solution.py:165
  103.3 0.1 slice_reduce_fusion.1
  103.3 4.2 %all-to-all-done.1.far_ref = bf16[32,120,128]{2,1,0:T(8,128)(2,1)S(1)} async-done(((bf16[32,120,128]{2,1,0:T(8,128)(2,1)}), bf16[32,120,128]{2,1,0:T(8,128)(2,1)S(1)}, u32[]{:S(2)}, u32[]{:S(2)}) %all-to-all-start.1) | async-done | bytes 983072 | tf_op jit(solution)/shard_map/all_to_all | solution.py:327
  107.5 3.0 %merge.1 = bf16[120,1536]{1,0:T(8,128)(2,1)S(1)} custom-call(bf16[32,120,128]{2,1,0:T(8,128)(2,1)S(1)} %all-to-all-done.1.far_ref, f32[24,120,128]{2,1,0:T(8,128)S(1)} %own_attend.1.own_ref), custom_call_target="tpu_custom_call" | custom-call | tf_op jit(solution)/shard_map/merge/pallas_call | solution.py:298
  110.5 0.0 all-gather.2.cloned.1.call-done
  110.5 3.2 %fusion.65 = (f32[120]{0:T(128)S(1)}, f32[120,1536]{1,0:T(8,128)S(1)}) fusion(bf16[120,1536]{1,0:T(8,128)(2,1)S(1)} %merge.1, bf16[1536,1536]{1,0:T(8,128)(2,1)} %all-gather.2.cloned.1.call-done, f32[1536]{0:T(1024)S(1)} %get-tuple-element.12, bf16[1,120,1536]{2,1,0:T(8,128)(2,1)S(1)} %copy-done.3), kind=kOutput, calls=%fused_computation.71 | convolution fusion | flops 566968192 | bytes 6199776 | tf_op jit(solution)/shard_map/dot_general | solution.py:331
  113.8 0.2 multiply_reduce_fusion
  114.0 0.2 add_convert_fusion
  114.2 3.4 %collective-permute-start.2 = (bf16[120,1536]{1,0:T(8,128)(2,1)S(1)}, bf16[120,1536]{1,0:T(8,128)(2,1)S(1)}, u32[]{:S(2)}, u32[]{:S(2)}) collective-permute-start(bf16[120,1536]{1,0:T(8,128)(2,1)S(1)} %add_convert_fusion), channel_id=1, source_target_pairs={{0,64},{64,0},{1,65},{65,1},{2,66},{66,2},{3,67},{67,3},{4,68},{68... | collective-permute-start | bytes 1105928 | tf_op jit(solution)/shard_map/ppermute | solution.py:309
  117.7 6.7 %collective-permute-done.2 = bf16[120,1536]{1,0:T(8,128)(2,1)S(1)} collective-permute-done((bf16[120,1536]{1,0:T(8,128)(2,1)S(1)}, bf16[120,1536]{1,0:T(8,128)(2,1)S(1)}, u32[]{:S(2)}, u32[]{:S(2)}) %collective-permute-start.2) | collective-permute-done | bytes 368672 | tf_op jit(solution)/shard_map/ppermute | solution.py:309
  124.4 2.8 %collective-permute-start.3 = (bf16[120,1536]{1,0:T(8,128)(2,1)S(1)}, bf16[120,1536]{1,0:T(8,128)(2,1)S(1)}, u32[]{:S(2)}, u32[]{:S(2)}) collective-permute-start(bf16[120,1536]{1,0:T(8,128)(2,1)S(1)} %collective-permute-done.2), channel_id=1, source_target_pairs={{0,32},{32,0},{1,33},{33,1},{2,34},{34,2},{3,35},{35,3},{4,36},{36... | collective-permute-start | bytes 1105928 | tf_op jit(solution)/shard_map/ppermute | solution.py:309
  127.2 1.8 %collective-permute-done.3 = bf16[120,1536]{1,0:T(8,128)(2,1)S(1)} collective-permute-done((bf16[120,1536]{1,0:T(8,128)(2,1)S(1)}, bf16[120,1536]{1,0:T(8,128)(2,1)S(1)}, u32[]{:S(2)}, u32[]{:S(2)}) %collective-permute-start.3) | collective-permute-done | bytes 368672 | tf_op jit(solution)/shard_map/ppermute | solution.py:309
  129.0 6.3 %fusion.17 = f32[240,1536]{1,0:T(8,128)S(1)} fusion(bf16[1536,1536]{1,0:T(8,128)(2,1)} %param.19, bf16[1536,1536]{1,0:T(8,128)(2,1)} %param.18, bf16[120,1536]{1,0:T(8,128)(2,1)S(1)} %collective-permute-done.3, bf16[120,1536]{1,0:T(8,128)(2,1)S(1)} %collective-permute-done.2), kind=kOutput, calls=%fused_computation.20 | convolution fusion | flops 2269716480 | bytes 11649024 | tf_op jit(solution)/shard_map/dot_general | solution.py:337
  135.4 0.6 collective-permute-start.4
  136.0 0.4 copy-done.8
  136.4 6.4 %fusion.19 = f32[240,1536]{1,0:T(8,128)S(1)} fusion(bf16[1536,1536]{1,0:T(8,128)(2,1)} %param.19, bf16[1536,1536]{1,0:T(8,128)(2,1)} %param.18, bf16[120,1536]{1,0:T(8,128)(2,1)} %collective-permute-done, bf16[120,1536]{1,0:T(8,128)(2,1)S(1)} %add_convert_fusion), kind=kOutput, calls=%fused_computation.21 | convolution fusion | flops 2269716480 | bytes 11649024 | tf_op jit(solution)/shard_map/dot_general | solution.py:337
  142.9 0.5 collective-permute-start.1
  143.3 1.2 fusion.21
  144.5 3.0 %collective-permute-start.5 = (bf16[120,1536]{1,0:T(8,128)(2,1)S(1)}, bf16[120,1536]{1,0:T(8,128)(2,1)S(1)}, u32[]{:S(2)}, u32[]{:S(2)}) collective-permute-start(bf16[120,1536]{1,0:T(8,128)(2,1)S(1)} %fusion.21), channel_id=1, source_target_pairs={{0,64},{64,0},{1,65},{65,1},{2,66},{66,2},{3,67},{67,3},{4,68},{68... | collective-permute-start | bytes 1105928 | tf_op jit(solution)/shard_map/ppermute | solution.py:309
  147.6 8.6 %collective-permute-done.5 = bf16[120,1536]{1,0:T(8,128)(2,1)S(1)} collective-permute-done((bf16[120,1536]{1,0:T(8,128)(2,1)S(1)}, bf16[120,1536]{1,0:T(8,128)(2,1)S(1)}, u32[]{:S(2)}, u32[]{:S(2)}) %collective-permute-start.5) | collective-permute-done | bytes 368672 | tf_op jit(solution)/shard_map/ppermute | solution.py:309
  156.2 1.0 fusion.51
  (24 shorter events, 0.1 us)
Async XLA Ops:
  6.5 2.7 %copy-start.1 = (bf16[1,120,3072]{2,1,0:T(8,128)(2,1)S(1)}, bf16[1,120,3072]{2,1,0:T(8,128)(2,1)}, u32[]{:S(2)}) copy-start(bf16[1,120,3072]{2,1,0:T(8,128)(2,1)} %param.12) | copy-start | bytes 2211844
  6.5 104.0 %all-gather.2.cloned.1.call-start = ((), (), s32[]{:S(2)}) async-start(), calls=%async_computation.2 | async-start | bytes 5898240 | tf_op jit(solution)/shard_map/all_gather | solution.py:321
  9.2 1.0 copy-start.2
  10.2 0.7 copy-start.6
  21.1 1.0 copy-start.4
  22.1 29.9 %all-to-all-start = ((bf16[32,184,128]{2,1,0:T(8,128)(2,1)}), bf16[32,184,128]{2,1,0:T(8,128)(2,1)S(1)}, u32[]{:S(2)}, u32[]{:S(2)}) async-start(bf16[32,184,128]{2,1,0:T(8,128)(2,1)} %get-tuple-element.7), calls=%async_computation | async-start | bytes 3014656 | tf_op jit(solution)/shard_map/all_to_all | solution.py:323
  86.8 6.0 %copy-start = (bf16[1,154,3072]{2,1,0:T(8,128)(2,1)S(1)}, bf16[1,154,3072]{2,1,0:T(8,128)(2,1)}, u32[]{:S(2)}) copy-start(bf16[1,154,3072]{2,1,0:T(8,128)(2,1)} %param.13) | copy-start | bytes 2838532
  86.8 20.7 %all-to-all-start.1 = ((bf16[32,120,128]{2,1,0:T(8,128)(2,1)}), bf16[32,120,128]{2,1,0:T(8,128)(2,1)S(1)}, u32[]{:S(2)}, u32[]{:S(2)}) async-start(bf16[32,120,128]{2,1,0:T(8,128)(2,1)} %bitcast.5), calls=%async_computation.1 | async-start | bytes 1966080 | tf_op jit(solution)/shard_map/all_to_all | solution.py:327
  92.8 1.3 copy-start.5
  94.1 9.1 %copy-start.7 = (bf16[1,6,1536]{2,1,0:T(8,128)(2,1)S(1)}, bf16[1,6,1536]{2,1,0:T(8,128)(2,1)}, u32[]{:S(2)}) copy-start(bf16[1,6,1536]{2,1,0:T(8,128)(2,1)} %param.11) | copy-start | bytes 55300
  103.2 7.3 %copy-start.3 = (bf16[1,120,1536]{2,1,0:T(8,128)(2,1)S(1)}, bf16[1,120,1536]{2,1,0:T(8,128)(2,1)}, u32[]{:S(2)}) copy-start(bf16[1,120,1536]{2,1,0:T(8,128)(2,1)} %param.10) | copy-start | bytes 1105924
  114.2 10.1 %collective-permute-start.2 = (bf16[120,1536]{1,0:T(8,128)(2,1)S(1)}, bf16[120,1536]{1,0:T(8,128)(2,1)S(1)}, u32[]{:S(2)}, u32[]{:S(2)}) collective-permute-start(bf16[120,1536]{1,0:T(8,128)(2,1)S(1)} %add_convert_fusion), channel_id=1, source_target_pairs={{0,64},{64,0},{1,65},{65,1},{2,66},{66,2},{3,67},{67,3},{4,68},{68... | collective-permute-start | bytes 1105928 | tf_op jit(solution)/shard_map/ppermute | solution.py:309
  124.4 4.7 %collective-permute-start.3 = (bf16[120,1536]{1,0:T(8,128)(2,1)S(1)}, bf16[120,1536]{1,0:T(8,128)(2,1)S(1)}, u32[]{:S(2)}, u32[]{:S(2)}) collective-permute-start(bf16[120,1536]{1,0:T(8,128)(2,1)S(1)} %collective-permute-done.2), channel_id=1, source_target_pairs={{0,32},{32,0},{1,33},{33,1},{2,34},{34,2},{3,35},{35,3},{4,36},{36... | collective-permute-start | bytes 1105928 | tf_op jit(solution)/shard_map/ppermute | solution.py:309
  127.2 9.2 %collective-permute-start = (bf16[120,1536]{1,0:T(8,128)(2,1)S(1)}, bf16[120,1536]{1,0:T(8,128)(2,1)}, u32[]{:S(2)}, u32[]{:S(2)}) collective-permute-start(bf16[120,1536]{1,0:T(8,128)(2,1)S(1)} %add_convert_fusion), channel_id=1, source_target_pairs={{0,32},{32,0},{1,33},{33,1},{2,34},{34,2},{3,35},{35,3},{4,36},{36... | collective-permute-start | bytes 1105928 | tf_op jit(solution)/shard_map/ppermute | solution.py:309
  135.3 1.1 copy-start.8
  135.4 8.0 %collective-permute-start.4 = (bf16[120,1536]{1,0:T(8,128)(2,1)S(1)}, bf16[120,1536]{1,0:T(8,128)(2,1)S(1)}, u32[]{:S(2)}, u32[]{:S(2)}) collective-permute-start(bf16[120,1536]{1,0:T(8,128)(2,1)S(1)} %slice.66), channel_id=1, source_target_pairs={{0,32},{32,0},{1,33},{33,1},{2,34},{34,2},{3,35},{35,3},{4,36},{36... | collective-permute-start | bytes 1105928 | tf_op jit(solution)/shard_map/ppermute | solution.py:309
  142.9 4.7 %collective-permute-start.1 = (bf16[120,1536]{1,0:T(8,128)(2,1)S(1)}, bf16[120,1536]{1,0:T(8,128)(2,1)S(1)}, u32[]{:S(2)}, u32[]{:S(2)}) collective-permute-start(bf16[120,1536]{1,0:T(8,128)(2,1)S(1)} %slice.67), channel_id=1, source_target_pairs={{0,32},{32,0},{1,33},{33,1},{2,34},{34,2},{3,35},{35,3},{4,36},{36... | collective-permute-start | bytes 1105928 | tf_op jit(solution)/shard_map/ppermute | solution.py:309
  144.5 11.6 %collective-permute-start.5 = (bf16[120,1536]{1,0:T(8,128)(2,1)S(1)}, bf16[120,1536]{1,0:T(8,128)(2,1)S(1)}, u32[]{:S(2)}, u32[]{:S(2)}) collective-permute-start(bf16[120,1536]{1,0:T(8,128)(2,1)S(1)} %fusion.21), channel_id=1, source_target_pairs={{0,64},{64,0},{1,65},{65,1},{2,66},{66,2},{3,67},{67,3},{4,68},{68... | collective-permute-start | bytes 1105928 | tf_op jit(solution)/shard_map/ppermute | solution.py:309
Sparse Core Ops, SparseCore 0:
  9.0 61.4 all-gather.1

commit v2 on v1

--- a/solution.py
+++ b/solution.py
@@ -1,5 +1,3 @@
-import functools
-
 import jax
 import jax.numpy as jnp
 from jax import lax
@@ -36,7 +34,18 @@
 
 
 def project_kernel(
-    flag_ref, tokens_ref, mod_ref, wq_ref, wk_ref, wv_ref, ck_ref, cv_ref, send_ref, own_ref, normed_ref
+    tile_ref,
+    refresh_ref,
+    tokens_ref,
+    mod_ref,
+    wq_ref,
+    wk_ref,
+    wv_ref,
+    ck_ref,
+    cv_ref,
+    send_ref,
+    own_ref,
+    normed_ref,
 ):
     step = pl.program_id(0)
     rows = tokens_ref.shape[0]
@@ -55,7 +64,9 @@
     queries = jnp.dot(normed, wq_ref[...], preferred_element_type=F32) * 0.125
     keys = jnp.dot(normed, wk_ref[...], preferred_element_type=F32)
     values = jnp.dot(normed, wv_ref[...], preferred_element_type=F32)
-    flagged = flag_ref[0] != 0
+    flagged = refresh_ref[0, 0] == tile_ref[0]
+    for slot in range(1, refresh_ref.shape[1]):
+        flagged = jnp.logical_or(flagged, refresh_ref[0, slot] == tile_ref[0])
     low = lane_iota((rows, 2 * HEAD)) < HEAD
     low_q = lane_iota((half, 2 * HEAD)) < HEAD
     pad = jnp.zeros((2 * half - rows, 2 * HEAD), F32)
@@ -88,7 +99,7 @@
                 send_ref[dest + 1, rows:, :] = q_pack
 
 
-def project(flag, tokens, modulate, w_qkv, cached):
+def project(tile_index, refresh, tokens, modulate, w_qkv, cached):
     rows, width = tokens.shape
     half = 64
     block = 256
@@ -105,6 +116,7 @@
         ),
         in_specs=[
             pl.BlockSpec(memory_space=pltpu.SMEM),
+            pl.BlockSpec(memory_space=pltpu.SMEM),
             whole(rows, width),
             whole(6, width),
             pl.BlockSpec((width, block), lambda s: (0, s)),
@@ -120,7 +132,7 @@
         scratch_shapes=[pltpu.VMEM((rows, width), BF16)],
         compiler_params=pltpu.CompilerParams(vmem_limit_bytes=40 << 20),
         name="project",
-    )(flag, tokens, modulate, w_qkv, w_qkv, w_qkv, cached, cached)
+    )(tile_index, refresh, tokens, modulate, w_qkv, w_qkv, w_qkv, cached, cached)
 
 
 def own_kernel(live_ref, own_ref, tk_ref, tv_ref, out_ref):
@@ -183,50 +195,44 @@
     )(live, own, text_rows, text_rows)
 
 
-def head_kernel(len_ref, pack_ref, out_ref, q_ref, k_ref, v_ref, kt_ref, s_ref):
+def head_kernel(len_ref, pack_ref, out_ref, v_ref, kt_ref, s_ref):
     step = pl.program_id(0)
-    tiles, packed, _ = pack_ref.shape
-    rows = packed - 64
+    tiles, packed, lanes = pack_ref.shape
+    rows = packed - HEAD
     total_rows = tiles * rows
-    block = out_ref.shape[0]
-    chunk = 256
+    group = out_ref.shape[0]
+    block = group * rows
+    piece = 256
+    chunk = 1920
+    low = lane_iota((1, lanes)) < HEAD
 
     @pl.when(step == 0)
     def _():
-        low = lane_iota((2 * rows, 2 * HEAD)) < HEAD
-        feature = lane_iota((2 * rows, 2 * HEAD)) - HEAD
-        second = (row_iota((2 * rows, 2 * HEAD)) >= rows).astype(jnp.int32)
-
-        def fill(pair, carry):
-            first = 2 * pair
-            kv = jnp.concatenate(
-                [pack_ref[first, :rows, :].astype(F32), pack_ref[first + 1, :rows, :].astype(F32)],
-                axis=0,
+        for pair in range(tiles // 2):
+            both = jnp.concatenate(
+                [pack_ref[2 * pair + t, :rows, :].astype(F32) for t in range(2)], axis=0
             )
-            parts = []
-            for t in range(2):
-                folded = pack_ref[first + t, rows:, :].astype(F32)
-                parts += [folded, swap_halves(folded)[: rows - 64]]
-            query = jnp.concatenate(parts, axis=0)
-            tile = first + second
-            masked = jnp.logical_or(feature == tile, feature == 32)
-            query = jnp.where(low, query, jnp.where(masked, -BIG, 0.0))
-            index = pair * 2 * rows + row_iota((2 * rows, 2 * HEAD))
-            dead = jnp.logical_and(feature == 32, index >= len_ref[0])
-            held = jnp.logical_or(feature == tile, dead)
-            key = jnp.where(low, kv, jnp.where(held, 1.0, 0.0))
-            at = pl.ds(pl.multiple_of(pair * 2 * rows, 16), 2 * rows)
-            q_ref[at, :] = query.astype(BF16)
-            k_ref[at, :] = key.astype(BF16)
-            v_ref[at, :] = jnp.where(low, 1.0, kv).astype(BF16)
-            return carry
-
-        lax.fori_loop(0, tiles // 2, fill, 0)
-        for c in range(total_rows // chunk):
-            part = slice(c * chunk, (c + 1) * chunk)
-            kt_ref[:, part] = jnp.transpose(k_ref[part, :].astype(F32)).astype(BF16)
-
-    query = q_ref[pl.ds(pl.multiple_of(step * block, block), block), :]
+            v_ref[pair * 2 * rows : (pair + 1) * 2 * rows, :] = both.astype(BF16)
+        feature = row_iota((HEAD, piece))
+        for c in range(total_rows // piece):
+            part = slice(c * piece, (c + 1) * piece)
+            kv = v_ref[part, :]
+            index = lane_iota((HEAD, piece)) + c * piece
+            own = jnp.logical_and(index >= feature * rows, index < feature * rows + rows)
+            held = jnp.logical_or(own, jnp.logical_and(feature == tiles, index >= len_ref[0]))
+            kt_ref[:HEAD, part] = jnp.transpose(kv.astype(F32))[:HEAD].astype(BF16)
+            kt_ref[HEAD:, part] = jnp.where(held, 1.0, 0.0).astype(BF16)
+            v_ref[part, :] = jnp.where(low, jnp.ones((), BF16), kv)
+
+    feature = lane_iota((1, lanes)) - HEAD
+    parts = []
+    for t in range(group):
+        tile = step * group + t
+        mask = jnp.where(jnp.logical_or(feature == tile, feature == tiles), -BIG, 0.0)
+        folded = pack_ref[tile, rows:, :].astype(F32)
+        parts.append(jnp.where(low, folded, mask))
+        parts.append(jnp.where(low, swap_halves(folded)[: rows - HEAD], mask))
+    query = jnp.concatenate(parts, axis=0).astype(BF16)
     top = jnp.full((block, 128), -jnp.inf, F32)
     for c in range(total_rows // chunk):
         part = slice(c * chunk, (c + 1) * chunk)
@@ -235,74 +241,169 @@
         for i in range(chunk // 128):
             top = jnp.maximum(top, scores[:, i * 128 : (i + 1) * 128])
     top = jnp.max(top, -1, keepdims=True)
-    total = jnp.zeros((block, 2 * HEAD), F32)
+    total = jnp.zeros((block, lanes), F32)
     for c in range(total_rows // chunk):
         part = slice(c * chunk, (c + 1) * chunk)
         probs = jnp.exp(s_ref[:, part] - top).astype(BF16)
         total = total + jnp.dot(probs, v_ref[part, :], preferred_element_type=F32)
     weight = total[:, 0:1]
-    lse = top + jnp.log(weight)
-    high = lse.astype(BF16).astype(F32)
-    lane = lane_iota((block, 2 * HEAD))
-    result = jnp.where(lane < 32, high, jnp.where(lane < HEAD, lse - high, total / weight))
-    out_ref[...] = result.astype(BF16)
+    lse = jnp.broadcast_to(top + jnp.log(weight), (block, lanes))
+    result = total / weight
+    diagonal = row_iota((HEAD, lanes)) == lane_iota((HEAD, lanes))
+    line = row_iota((8, lanes))
+    pad = jnp.zeros((2 * HEAD - rows, lanes), F32)
+    for t in range(group):
+        first = slice(t * rows, t * rows + HEAD)
+        rest = slice(t * rows + HEAD, (t + 1) * rows)
+        lse_a = jnp.sum(jnp.where(diagonal, lse[first], 0.0), 0, keepdims=True)
+        lse_b = jnp.concatenate([lse[rest], pad], axis=0)
+        lse_b = jnp.sum(jnp.where(diagonal, lse_b, 0.0), 0, keepdims=True)
+        high_a = lse_a.astype(BF16).astype(F32)
+        high_b = lse_b.astype(BF16).astype(F32)
+        stats = jnp.where(line == 2, lse_a - high_a, lse_b - high_b)
+        stats = jnp.where(line == 0, high_a, jnp.where(line == 1, high_b, stats))
+        folded = jnp.concatenate([swap_halves(result[rest]), stats], axis=0)
+        out_ref[t] = jnp.where(low, folded, result[first]).astype(BF16)
 
 
 def head_attend(length, pack):
     tiles, packed, lanes = pack.shape
-    rows = packed - 64
+    rows = packed - HEAD
     total_rows = tiles * rows
-    block = 384
+    group = 8
+    block = group * rows
     return pl.pallas_call(
         head_kernel,
-        grid=(total_rows // block,),
-        out_shape=jax.ShapeDtypeStruct((total_rows, lanes), BF16),
+        grid=(tiles // group,),
+        out_shape=jax.ShapeDtypeStruct((tiles, HEAD, lanes), BF16),
         in_specs=[
             pl.BlockSpec(memory_space=pltpu.SMEM),
             pl.BlockSpec((tiles, packed, lanes), lambda s: (0, 0, 0)),
         ],
-        out_specs=pl.BlockSpec((block, lanes), lambda s: (s, 0)),
+        out_specs=pl.BlockSpec((group, HEAD, lanes), lambda s: (s, 0, 0)),
         scratch_shapes=[
-            pltpu.VMEM((total_rows, lanes), BF16),
-            pltpu.VMEM((total_rows, lanes), BF16),
             pltpu.VMEM((total_rows, lanes), BF16),
             pltpu.VMEM((lanes, total_rows), BF16),
             pltpu.VMEM((block, total_rows), F32),
         ],
-        compiler_params=pltpu.CompilerParams(vmem_limit_bytes=40 << 20),
+        compiler_params=pltpu.CompilerParams(vmem_limit_bytes=44 << 20),
+        cost_estimate=pl.CostEstimate(
+            flops=4 * total_rows * total_rows * 128,
+            bytes_accessed=4 << 20,
+            transcendentals=total_rows * total_rows,
+        ),
         name="head_attend",
     )(length, pack)
 
 
-def merge_kernel(far_ref, own_ref, out_ref):
-    heads = own_ref.shape[0]
-    rows = own_ref.shape[1]
-    low = lane_iota((rows, 2 * HEAD)) < HEAD
+def merge_kernel(far_ref, own_ref, w_ref, tokens_ref, mod_ref, mixed_ref, input_ref, att_ref):
+    heads, rows, lanes = own_ref.shape
+    low = lane_iota((1, lanes)) < HEAD
+    diagonal = row_iota((HEAD, lanes)) == lane_iota((HEAD, lanes))
+
+    def column(line):
+        spread = jnp.where(diagonal, jnp.broadcast_to(line, (HEAD, lanes)), 0.0)
+        return jnp.sum(spread, -1, keepdims=True)
+
     for pair in range(heads // 2):
         both = []
         for odd in range(2):
             head = 2 * pair + odd
-            far = far_ref[head + head // 3].astype(F32)
+            folded = far_ref[head + head // 3].astype(F32)
+            stats = folded[rows - HEAD :]
+            first = column(stats[0:1] + stats[2:3])
+            rest = column(stats[1:2] + stats[3:4])
+            far_lse = jnp.concatenate([first, rest[: rows - HEAD]], axis=0)
+            far = jnp.concatenate([folded, swap_halves(folded)[: rows - HEAD]], axis=0)
             own = own_ref[head]
-            far_lse = far[:, 0:1] + far[:, 32:33]
-            own_lse = own[:, 0:1]
-            share = 1.0 / (1.0 + jnp.exp(own_lse - far_lse))
-            other = 1.0 / (1.0 + jnp.exp(far_lse - own_lse))
+            gap = jnp.broadcast_to(far_lse, (rows, lanes)) - own[:, 0:1]
+            share = 1.0 / (1.0 + jnp.exp(-gap))
+            other = 1.0 / (1.0 + jnp.exp(gap))
             both.append(share * far + other * own)
         joined = jnp.where(low, swap_halves(both[0]), both[1])
-        out_ref[:, pair * 2 * HEAD : (pair + 1) * 2 * HEAD] = joined.astype(BF16)
-
-
-def merge(far, own):
-    heads, rows, lanes = own.shape
+        att_ref[:, pair * lanes : (pair + 1) * lanes] = joined.astype(BF16)
+    projected = jnp.dot(att_ref[...], w_ref[...], preferred_element_type=F32)
+    mod = mod_ref[...].astype(F32)
+    mixed = tokens_ref[...].astype(F32) + mod[2:3] * projected
+    mixed_ref[...] = mixed
+    input_ref[...] = (layer_norm(mixed) * (1.0 + mod[4:5]) + mod[3:4]).astype(BF16)
+
+
+def merge(far, own, w_out, tokens, modulate):
+    rows, width = tokens.shape
     return pl.pallas_call(
         merge_kernel,
-        out_shape=jax.ShapeDtypeStruct((rows, heads * HEAD), BF16),
-        in_specs=[pl.BlockSpec(memory_space=pltpu.VMEM)] * 2,
-        out_specs=pl.BlockSpec(memory_space=pltpu.VMEM),
-        compiler_params=pltpu.CompilerParams(vmem_limit_bytes=16 << 20),
+        out_shape=(
+            jax.ShapeDtypeStruct((rows, width), F32),
+            jax.ShapeDtypeStruct((rows, width), BF16),
+        ),
+        in_specs=[pl.BlockSpec(memory_space=pltpu.VMEM)] * 5,
+        out_specs=(pl.BlockSpec(memory_space=pltpu.VMEM),) * 2,
+        scratch_shapes=[pltpu.VMEM((rows, width), BF16)],
+        compiler_params=pltpu.CompilerParams(vmem_limit_bytes=24 << 20),
         name="merge",
-    )(far, own)
+    )(far, own, w_out, tokens, modulate)
+
+
+def feed_kernel(first_ref, second_ref, up_ref, down_ref, keep_ref, pass_ref, x_ref, sum_ref):
+    step = pl.program_id(0)
+    rows = first_ref.shape[0]
+
+    @pl.when(step == 0)
+    def _():
+        both = [first_ref[...].astype(F32), second_ref[...].astype(F32)]
+        x_ref[...] = jnp.concatenate(both, axis=0).astype(BF16)
+
+    hidden = jnp.dot(x_ref[...], up_ref[...], preferred_element_type=F32)
+    hidden = jax.nn.gelu(hidden, approximate=True).astype(BF16)
+    part = jnp.dot(hidden, down_ref[...], preferred_element_type=F32)
+    last = pl.num_programs(0) - 1
+
+    @pl.when(step == 0)
+    def _():
+        sum_ref[...] = part
+
+    @pl.when(jnp.logical_and(step > 0, step < last))
+    def _():
+        sum_ref[...] += part
+
+    @pl.when(step == last)
+    def _():
+        keep_ref[...] = sum_ref[:rows] + part[:rows]
+        pass_ref[...] = (sum_ref[rows:] + part[rows:]).astype(BF16)
+
+
+def feed(first, second, w_up, w_down):
+    rows, width = first.shape
+    hidden = w_up.shape[1]
+    block = 512
+    whole = lambda *shape: pl.BlockSpec(shape, lambda s: (0,) * len(shape))
+    return pl.pallas_call(
+        feed_kernel,
+        grid=(hidden // block,),
+        out_shape=(
+            jax.ShapeDtypeStruct((rows, width), F32),
+            jax.ShapeDtypeStruct((rows, width), BF16),
+        ),
+        in_specs=[
+            whole(rows, width),
+            whole(rows, width),
+            pl.BlockSpec((width, block), lambda s: (0, s)),
+            pl.BlockSpec((block, width), lambda s: (s, 0)),
+        ],
+        out_specs=(whole(rows, width), whole(rows, width)),
+        scratch_shapes=[
+            pltpu.VMEM((2 * rows, width), BF16),
+            pltpu.VMEM((2 * rows, width), F32),
+        ],
+        compiler_params=pltpu.CompilerParams(vmem_limit_bytes=32 << 20),
+        cost_estimate=pl.CostEstimate(
+            flops=8 * rows * width * hidden,
+            bytes_accessed=4 * width * hidden,
+            transcendentals=2 * rows * hidden,
+        ),
+        name="feed",
+    )(first, second, w_up, w_down)
 
 
 def swap(values, axis):
@@ -314,39 +415,33 @@
 ):
     tokens = latents[0]
     rows = tokens.shape[0]
-    modulate = modulation[0].astype(F32)
-    tile_index = lax.axis_index(TILE)
+    tile_index = lax.axis_index(TILE).astype(jnp.int32)
     length = lengths[0]
-    flag = jnp.any(refresh[0] == tile_index).astype(jnp.int32).reshape(1)
     all_w_out = lax.all_gather(w_out, REQ, axis=0, tiled=True)
-    send, own = project(flag, tokens, modulation[0], w_qkv, kv_cache[0])
+    send, own = project(
+        tile_index.reshape(1), refresh, tokens, modulation[0], w_qkv, kv_cache[0]
+    )
     pack = lax.all_to_all(send, TILE, split_axis=0, concat_axis=0, tiled=True)
     live = (length - tile_index * rows).reshape(1)
     own_part = own_attend(live, own, text_kv[0])
-    far = head_attend(length.reshape(1), pack)
-    far = lax.all_to_all(
-        far.reshape(-1, rows, 2 * HEAD), TILE, split_axis=0, concat_axis=0, tiled=True
-    )
-    attended = merge(far, own_part)
-    projected = jnp.dot(attended, all_w_out, preferred_element_type=F32)
-    mixed = tokens.astype(F32) + modulate[2] * projected
-    mlp_input = (layer_norm(mixed) * (1.0 + modulate[4]) + modulate[3]).astype(BF16)
-
-    def feed(values):
-        hidden = jax.nn.gelu(jnp.dot(values, w_up, preferred_element_type=F32), approximate=True)
-        return jnp.dot(hidden.astype(BF16), w_down, preferred_element_type=F32)
+    pack, own_part = lax.optimization_barrier((pack, own_part))
+    far = head_attend(lengths, pack)
+    far = lax.all_to_all(far, TILE, split_axis=0, concat_axis=0, tiled=True)
+    mixed, mlp_input = merge(far, own_part, all_w_out, tokens, modulation[0])
 
     far_z = swap(mlp_input, "zh")
     near = swap(mlp_input, "co")
+    near_keep, near_pass = feed(mlp_input, near, w_up, w_down)
+    far_z, near_keep, near_pass = lax.optimization_barrier((far_z, near_keep, near_pass))
     far_both = swap(far_z, "co")
-    parts_near = feed(jnp.concatenate([mlp_input, near], axis=0))
-    parts_far = feed(jnp.concatenate([far_z, far_both], axis=0))
-    sum_far = parts_far[:rows] + swap(parts_far[rows:].astype(BF16), "co").astype(F32)
-    sum_near = parts_near[:rows] + swap(parts_near[rows:].astype(BF16), "co").astype(F32)
-    mlp_out = sum_near + swap(sum_far.astype(BF16), "zh").astype(F32)
+    far_keep, far_pass = feed(far_z, far_both, w_up, w_down)
+    sum_far = (far_keep + swap(far_pass, "co").astype(F32)).astype(BF16)
+    near_sum = near_keep + swap(near_pass, "co").astype(F32)
+    mlp_out = near_sum + swap(sum_far, "zh").astype(F32)
     positions = tile_index * rows + jnp.arange(rows, dtype=jnp.int32)
     live_rows = positions < length
-    finished = jnp.where(live_rows[:, None], mixed + modulate[5] * mlp_out, 0.0)
+    gate = modulation[0, 5].astype(F32)
+    finished = jnp.where(live_rows[:, None], mixed + gate * mlp_out, 0.0)
     return finished.astype(BF16)[None]
 
 

time: 165 us -> 140 us (0.85)
  waiting for transfers between devices: 42 us -> 21.1 us
  matrix products: 15.9 us -> 0 us
  blocking collectives: 0 us -> 15.2 us
  local copies, waits for them, and re-layouts: 4.52 us -> 16.8 us
  Pallas kernels: 57.1 us -> 51.2 us
  starting transfers between devices: 25.6 us -> 20.1 us
  other arithmetic: 3.98 us -> 1.06 us
    dot_general x3 -> x0, matrix products: 15.9 us -> none  [the longest x2 12.6 us: feed(): return jnp.dot(hidden.astype(BF16), w_down, preferred_element_type=F32)]
    all_to_all x0 -> x1, blocking collectives: none -> 15.2 us  [per_device(): far = lax.all_to_all(far, TILE, split_axis=0, concat_axis=0, tiled=True)]
    unnamed x18 -> x28, local copies, waits for them, and re-layouts: 4.44 us -> 16.8 us
    all_to_all x1, waiting for transfers between devices: 20 us -> 9.61 us  [per_device(): pack = lax.all_to_all(send, TILE, split_axis=0, concat_axis=0, tiled=True)]
    ppermute x6, waiting for transfers between devices: 17.1 us -> 10.8 us  [swap(): return lax.ppermute(values, axis, [(0, 1), (1, 0)])]
    all_to_all x1 -> x0, starting transfers between devices: 5.99 us -> none  [per_device(): lax.all_to_all(far.reshape(-1, rows, 2 * HEAD), TILE, split_axis=0, conca...]
    pallas_call x2 -> x4, Pallas kernels: 37.8 us -> 31.9 us  [the longest x1 20 us: head_attend(): pl.pallas_call(head_kernel, grid=(tiles // group,), out_shape=jax.ShapeDt...]
    all_to_all x1 -> x0, waiting for transfers between devices: 4.16 us -> none  [per_device(): lax.all_to_all(far.reshape(-1, rows, 2 * HEAD), TILE, split_axis=0, conca...]
  transfers between devices with their start and end apart: 9 -> 8, of which waited for: 5 -> 4; matrix products, arithmetic and copies ran while one was open for 9% -> 0% of each run, Pallas kernels for 35% -> 31%
where the time goes in v2:
time: 140 us
  Pallas kernels  51.2 us (37%)
  waiting for transfers between devices  21.1 us (15%)
  starting transfers between devices  20.1 us (14%)
  local copies, waits for them, and re-layouts  16.8 us (12%)
  blocking collectives  15.2 us (11%)
  between operations  14.2 us (10%)
    pallas_call x1, Pallas kernels, head_attend(): pl.pallas_call(head_kernel, grid=(tiles // group,), out_shape=jax.ShapeDt...  20 us
    unnamed x28, local copies, waits for them, and re-layouts  16.8 us
    all_to_all x1, blocking collectives, per_device(): far = lax.all_to_all(far, TILE, split_axis=0, concat_axis=0, tiled=True)  15.2 us
    ppermute x6, waiting for transfers between devices, swap(): return lax.ppermute(values, axis, [(0, 1), (1, 0)])  10.8 us
    ppermute x6, starting transfers between devices, swap(): return lax.ppermute(values, axis, [(0, 1), (1, 0)])  10.7 us
    pallas_call x1, Pallas kernels, project(): pl.pallas_call(project_kernel, grid=(steps,), out_shape=(jax.ShapeDtypeSt...  10.2 us
    all_to_all x1, waiting for transfers between devices, per_device(): pack = lax.all_to_all(send, TILE, split_axis=0, concat_axis=0, tiled=True)  9.61 us
    all_to_all x1, starting transfers between devices, per_device(): pack = lax.all_to_all(send, TILE, split_axis=0, concat_axis=0, tiled=True)  9.47 us
  transfers between devices with their start and end apart: 8, of which 4 were waited for; matrix products, arithmetic and copies ran while one was open for 0% of the time, Pallas kernels for 31%

profile of v2, /device:TPU:1, one launch (start us, length us, event | category | flops | bytes accessed | tf_op | source)
XLA Modules:
  0.0 139.7 jit_solution(16883148582311975174)
XLA Ops:
  6.5 0.7 all-gather.2.cloned.1.call-update
  7.3 0.4 copy-done.6
  7.7 1.0 copy-done.7
  8.6 0.7 copy-done.11
  9.4 0.7 copy-done.13
  10.0 10.2 %project.1 = (bf16[32,184,128]{2,1,0:T(8,128)(2,1)}, bf16[24,184,128]{2,1,0:T(8,128)(2,1)S(1)}) custom-call(s32[1]{0:T(128)} %bitcast.1.tile_ref, s32[1,4]{1,0:T(1,128)S(1)} %copy-done.13, bf16[120,1536]{1,0:T(8,128)(2,1)S(1)} %bitcast.15, bf16[6,1536]{1,0:T(8,128)(2,1)S(1)} %bitcast.17, bf16[1536,4608]{1,0:T(8,128)(2,1)} %wv_ref.1, ...), custom_call_target="tpu_custom_call" | custom-call | tf_op jit(solution)/shard_map/project/pallas_call | solution.py:110
  20.2 1.1 copy-done.9
  21.3 9.5 %all-to-all-start = ((bf16[32,184,128]{2,1,0:T(8,128)(2,1)}), bf16[32,184,128]{2,1,0:T(8,128)(2,1)}, u32[]{:S(2)}, u32[]{:S(2)}) async-start(bf16[32,184,128]{2,1,0:T(8,128)(2,1)} %get-tuple-element.18), calls=%async_computation | async-start | bytes 3014656 | tf_op jit(solution)/shard_map/all_to_all | solution.py:424
  31.4 1.2 copy-done.10
  32.7 9.1 %own_attend.1.own_ref = f32[24,120,128]{2,1,0:T(8,128)S(1)} custom-call(s32[1]{0:T(128)} %bitcast.5.live_ref, bf16[24,184,128]{2,1,0:T(8,128)(2,1)S(1)} %copy-done.10, bf16[154,3072]{1,0:T(8,128)(2,1)S(1)} %bitcast.11, bf16[154,3072]{1,0:T(8,128)(2,1)S(1)} %bitcast.12), custom_call_target="tpu_custom_call" | custom-call | flops 404029440 | bytes 6291456 | tf_op jit(solution)/shard_map/own_attend/pallas_call | solution.py:177
  41.8 9.6 %all-to-all-done.pack_ref = bf16[32,184,128]{2,1,0:T(8,128)(2,1)} async-done(((bf16[32,184,128]{2,1,0:T(8,128)(2,1)}), bf16[32,184,128]{2,1,0:T(8,128)(2,1)}, u32[]{:S(2)}, u32[]{:S(2)}) %all-to-all-start) | async-done | bytes 1507360 | tf_op jit(solution)/shard_map/all_to_all | solution.py:424
  51.4 20.0 %head_attend.1 = bf16[32,64,128]{2,1,0:T(8,128)(2,1)S(1)} custom-call(s32[1]{0:T(128)} %copy.11.len_ref, bf16[32,184,128]{2,1,0:T(8,128)(2,1)} %all-to-all-done.pack_ref), custom_call_target="tpu_custom_call" | custom-call | flops 7549747200 | bytes 4194304 | tf_op jit(solution)/shard_map/head_attend/pallas_call | solution.py:275
  71.4 15.2 %all_to_all.10.far_ref = bf16[32,64,128]{2,1,0:T(8,128)(2,1)S(1)} all-to-all(bf16[32,64,128]{2,1,0:T(8,128)(2,1)S(1)} %head_attend.1), channel_id=1, replica_groups=mesh['zh'=2,'co'=2,'y'=4,'zl'=2,'x'=4] {'y','zl','x'}, dimensions={0} | all-to-all | bytes 1048576 | tf_op jit(solution)/shard_map/all_to_all | solution.py:429
  86.7 2.3 %copy-done.4 = bf16[1536,1536]{1,0:T(8,128)(2,1)S(1)} copy-done((bf16[1536,1536]{1,0:T(8,128)(2,1)S(1)}, bf16[1536,1536]{1,0:T(8,128)(2,1)}, u32[]{:S(2)}) %copy-start.4) | copy-done | bytes 4718616
  89.0 3.8 %merge.1 = (f32[120,1536]{1,0:T(8,128)S(1)}, bf16[120,1536]{1,0:T(8,128)(2,1)S(1)}) custom-call(bf16[32,64,128]{2,1,0:T(8,128)(2,1)S(1)} %all_to_all.10.far_ref, f32[24,120,128]{2,1,0:T(8,128)S(1)} %own_attend.1.own_ref, bf16[1536,1536]{1,0:T(8,128)(2,1)S(1)} %copy-done.4, bf16[120,1536]{1,0:T(8,128)(2,1)S(1)} %bitcast.16, bf16[6,1536]{1,0:T(8,128)(2,1)S(1)} %bitcast.18), custom_call_target="tpu_custom_call" | custom-call | tf_op jit(solution)/shard_map/merge/pallas_call | solution.py:334
  92.8 3.0 %collective-permute-start.1 = (bf16[120,1536]{1,0:T(8,128)(2,1)S(1)}, bf16[120,1536]{1,0:T(8,128)(2,1)S(1)}, u32[]{:S(2)}, u32[]{:S(2)}) collective-permute-start(bf16[120,1536]{1,0:T(8,128)(2,1)S(1)} %get-tuple-element.23.first_ref), channel_id=1, source_target_pairs={{0,32},{32,0},{1,33},{33,1},{2,34},{34,2},{3,35},{35,3},{4,36},{36... | collective-permute-start | bytes 1105928 | tf_op jit(solution)/shard_map/ppermute | solution.py:410
  95.8 3.3 %collective-permute-start = (bf16[120,1536]{1,0:T(8,128)(2,1)S(1)}, bf16[120,1536]{1,0:T(8,128)(2,1)S(1)}, u32[]{:S(2)}, u32[]{:S(2)}) collective-permute-start(bf16[120,1536]{1,0:T(8,128)(2,1)S(1)} %get-tuple-element.23.first_ref), channel_id=1, source_target_pairs={{0,64},{64,0},{1,65},{65,1},{2,66},{66,2},{3,67},{67,3},{4,68},{68... | collective-permute-start | bytes 1105928 | tf_op jit(solution)/shard_map/ppermute | solution.py:410
  99.0 2.3 %copy-done = bf16[1536,1536]{1,0:T(8,128)(2,1)S(1)} copy-done((bf16[1536,1536]{1,0:T(8,128)(2,1)S(1)}, bf16[1536,1536]{1,0:T(8,128)(2,1)}, u32[]{:S(2)}) %copy-start) | copy-done | bytes 4718616
  101.4 2.3 %copy-done.2 = bf16[1536,1536]{1,0:T(8,128)(2,1)S(1)} copy-done((bf16[1536,1536]{1,0:T(8,128)(2,1)S(1)}, bf16[1536,1536]{1,0:T(8,128)(2,1)}, u32[]{:S(2)}) %copy-start.2) | copy-done | bytes 4718616
  103.7 4.1 %feed.2 = (f32[120,1536]{1,0:T(8,128)S(1)}, bf16[120,1536]{1,0:T(8,128)(2,1)S(1)}) custom-call(bf16[120,1536]{1,0:T(8,128)(2,1)S(1)} %get-tuple-element.23.first_ref, bf16[120,1536]{1,0:T(8,128)(2,1)S(1)} %collective-permute-done.1.second_ref, bf16[1536,1536]{1,0:T(8,128)(2,1)S(1)} %copy-done, bf16[1536,1536]{1,0:T(8,128)(2,1)S(1)} %copy-done.2), custom_call_target="tpu_custom_call" | custom-call | flops 2264924160 | bytes 9437184 | tf_op jit(solution)/shard_map/feed/pallas_call | solution.py:381
  107.8 0.8 collective-permute-start.3
  108.6 1.3 collective-permute-done.3.second_ref
  109.9 2.3 %copy-done.1 = bf16[1536,1536]{1,0:T(8,128)(2,1)S(1)} copy-done((bf16[1536,1536]{1,0:T(8,128)(2,1)S(1)}, bf16[1536,1536]{1,0:T(8,128)(2,1)}, u32[]{:S(2)}) %copy-start.1) | copy-done | bytes 4718616
  112.2 2.3 %copy-done.3 = bf16[1536,1536]{1,0:T(8,128)(2,1)S(1)} copy-done((bf16[1536,1536]{1,0:T(8,128)(2,1)S(1)}, bf16[1536,1536]{1,0:T(8,128)(2,1)}, u32[]{:S(2)}) %copy-start.3) | copy-done | bytes 4718616
  114.6 4.1 %feed.3 = (f32[120,1536]{1,0:T(8,128)S(1)}, bf16[120,1536]{1,0:T(8,128)(2,1)S(1)}) custom-call(bf16[120,1536]{1,0:T(8,128)(2,1)S(1)} %collective-permute-done.first_ref, bf16[120,1536]{1,0:T(8,128)(2,1)S(1)} %collective-permute-done.3.second_ref, bf16[1536,1536]{1,0:T(8,128)(2,1)S(1)} %copy-done.1, bf16[1536,1536]{1,0:T(8,128)(2,1)S(1)} %copy-done.3), custom_call_target="tpu_custom_call" | custom-call | flops 2264924160 | bytes 9437184 | tf_op jit(solution)/shard_map/feed/pallas_call | solution.py:381
  118.7 0.5 collective-permute-start.4
  119.1 0.1 collective-permute-start.2
  119.2 1.2 collective-permute-done.4
  120.4 0.1 add_convert_fusion
  120.5 3.0 %collective-permute-start.5 = (bf16[120,1536]{1,0:T(8,128)(2,1)S(1)}, bf16[120,1536]{1,0:T(8,128)(2,1)S(1)}, u32[]{:S(2)}, u32[]{:S(2)}) collective-permute-start(bf16[120,1536]{1,0:T(8,128)(2,1)S(1)} %add_convert_fusion), channel_id=1, source_target_pairs={{0,64},{64,0},{1,65},{65,1},{2,66},{66,2},{3,67},{67,3},{4,68},{68... | collective-permute-start | bytes 1105928 | tf_op jit(solution)/shard_map/ppermute | solution.py:410
  123.6 8.3 %collective-permute-done.5 = bf16[120,1536]{1,0:T(8,128)(2,1)S(1)} collective-permute-done((bf16[120,1536]{1,0:T(8,128)(2,1)S(1)}, bf16[120,1536]{1,0:T(8,128)(2,1)S(1)}, u32[]{:S(2)}, u32[]{:S(2)}) %collective-permute-start.5) | collective-permute-done | bytes 368672 | tf_op jit(solution)/shard_map/ppermute | solution.py:410
  131.9 1.0 fusion
  (24 shorter events, 0.1 us)
Async XLA Ops:
  6.5 1.1 copy-start.6
  6.5 80.1 %all-gather.2.cloned.1.call-start = ((), (), s32[]{:S(2)}) async-start(), calls=%async_computation.2 | async-start | bytes 5898240 | tf_op jit(solution)/shard_map/all_gather | solution.py:420
  7.7 1.0 copy-start.7
  8.6 0.7 copy-start.11
  9.4 0.7 copy-start.13
  20.2 1.1 copy-start.9
  21.3 10.1 %copy-start.5 = (bf16[1,154,3072]{2,1,0:T(8,128)(2,1)S(1)}, bf16[1,154,3072]{2,1,0:T(8,128)(2,1)}, u32[]{:S(2)}) copy-start(bf16[1,154,3072]{2,1,0:T(8,128)(2,1)} %param.13) | copy-start | bytes 2838532
  21.3 30.2 %all-to-all-start = ((bf16[32,184,128]{2,1,0:T(8,128)(2,1)}), bf16[32,184,128]{2,1,0:T(8,128)(2,1)}, u32[]{:S(2)}, u32[]{:S(2)}) async-start(bf16[32,184,128]{2,1,0:T(8,128)(2,1)} %get-tuple-element.18), calls=%async_computation | async-start | bytes 3014656 | tf_op jit(solution)/shard_map/all_to_all | solution.py:424
  31.4 1.3 copy-start.10
  41.8 44.9 %copy-start.8 = (bf16[1,120,1536]{2,1,0:T(8,128)(2,1)S(1)}, bf16[1,120,1536]{2,1,0:T(8,128)(2,1)}, u32[]{:S(2)}) copy-start(bf16[1,120,1536]{2,1,0:T(8,128)(2,1)} %param.10) | copy-start | bytes 1105924
  41.8 44.8 %copy-start.12 = (bf16[1,6,1536]{2,1,0:T(8,128)(2,1)S(1)}, bf16[1,6,1536]{2,1,0:T(8,128)(2,1)}, u32[]{:S(2)}) copy-start(bf16[1,6,1536]{2,1,0:T(8,128)(2,1)} %param.11) | copy-start | bytes 55300
  86.7 2.3 %copy-start.4 = (bf16[1536,1536]{1,0:T(8,128)(2,1)S(1)}, bf16[1536,1536]{1,0:T(8,128)(2,1)}, u32[]{:S(2)}) copy-start(bf16[1536,1536]{1,0:T(8,128)(2,1)} %all-gather.2.cloned.1.call-done.w_ref) | copy-start | bytes 14155780
  92.8 6.3 %collective-permute-start.1 = (bf16[120,1536]{1,0:T(8,128)(2,1)S(1)}, bf16[120,1536]{1,0:T(8,128)(2,1)S(1)}, u32[]{:S(2)}, u32[]{:S(2)}) collective-permute-start(bf16[120,1536]{1,0:T(8,128)(2,1)S(1)} %get-tuple-element.23.first_ref), channel_id=1, source_target_pairs={{0,32},{32,0},{1,33},{33,1},{2,34},{34,2},{3,35},{35,3},{4,36},{36... | collective-permute-start | bytes 1105928 | tf_op jit(solution)/shard_map/ppermute | solution.py:410
  95.8 12.0 %collective-permute-start = (bf16[120,1536]{1,0:T(8,128)(2,1)S(1)}, bf16[120,1536]{1,0:T(8,128)(2,1)S(1)}, u32[]{:S(2)}, u32[]{:S(2)}) collective-permute-start(bf16[120,1536]{1,0:T(8,128)(2,1)S(1)} %get-tuple-element.23.first_ref), channel_id=1, source_target_pairs={{0,64},{64,0},{1,65},{65,1},{2,66},{66,2},{3,67},{67,3},{4,68},{68... | collective-permute-start | bytes 1105928 | tf_op jit(solution)/shard_map/ppermute | solution.py:410
  99.0 2.3 %copy-start = (bf16[1536,1536]{1,0:T(8,128)(2,1)S(1)}, bf16[1536,1536]{1,0:T(8,128)(2,1)}, u32[]{:S(2)}) copy-start(bf16[1536,1536]{1,0:T(8,128)(2,1)} %up_ref.3) | copy-start | bytes 14155780
  101.4 2.3 %copy-start.2 = (bf16[1536,1536]{1,0:T(8,128)(2,1)S(1)}, bf16[1536,1536]{1,0:T(8,128)(2,1)}, u32[]{:S(2)}) copy-start(bf16[1536,1536]{1,0:T(8,128)(2,1)} %down_ref.3) | copy-start | bytes 14155780
  107.8 2.1 %collective-permute-start.3 = (bf16[120,1536]{1,0:T(8,128)(2,1)S(1)}, bf16[120,1536]{1,0:T(8,128)(2,1)S(1)}, u32[]{:S(2)}, u32[]{:S(2)}) collective-permute-start(bf16[120,1536]{1,0:T(8,128)(2,1)S(1)} %collective-permute-done.first_ref), channel_id=1, source_target_pairs={{0,32},{32,0},{1,33},{33,1},{2,34},{34,2},{3,35},{35,3},{4,36},{36... | collective-permute-start | bytes 1105928 | tf_op jit(solution)/shard_map/ppermute | solution.py:410
  109.9 2.3 %copy-start.1 = (bf16[1536,1536]{1,0:T(8,128)(2,1)S(1)}, bf16[1536,1536]{1,0:T(8,128)(2,1)}, u32[]{:S(2)}) copy-start(bf16[1536,1536]{1,0:T(8,128)(2,1)} %up_ref.3) | copy-start | bytes 14155780
  112.2 2.3 %copy-start.3 = (bf16[1536,1536]{1,0:T(8,128)(2,1)S(1)}, bf16[1536,1536]{1,0:T(8,128)(2,1)}, u32[]{:S(2)}) copy-start(bf16[1536,1536]{1,0:T(8,128)(2,1)} %down_ref.3) | copy-start | bytes 14155780
  118.7 1.8 %collective-permute-start.4 = (bf16[120,1536]{1,0:T(8,128)(2,1)S(1)}, bf16[120,1536]{1,0:T(8,128)(2,1)S(1)}, u32[]{:S(2)}, u32[]{:S(2)}) collective-permute-start(bf16[120,1536]{1,0:T(8,128)(2,1)S(1)} %get-tuple-element.30), channel_id=1, source_target_pairs={{0,32},{32,0},{1,33},{33,1},{2,34},{34,2},{3,35},{35,3},{4,36},{36... | collective-permute-start | bytes 1105928 | tf_op jit(solution)/shard_map/ppermute | solution.py:410
  119.1 4.5 %collective-permute-start.2 = (bf16[120,1536]{1,0:T(8,128)(2,1)S(1)}, bf16[120,1536]{1,0:T(8,128)(2,1)S(1)}, u32[]{:S(2)}, u32[]{:S(2)}) collective-permute-start(bf16[120,1536]{1,0:T(8,128)(2,1)S(1)} %get-tuple-element.27), channel_id=1, source_target_pairs={{0,32},{32,0},{1,33},{33,1},{2,34},{34,2},{3,35},{35,3},{4,36},{36... | collective-permute-start | bytes 1105928 | tf_op jit(solution)/shard_map/ppermute | solution.py:410
  120.5 11.4 %collective-permute-start.5 = (bf16[120,1536]{1,0:T(8,128)(2,1)S(1)}, bf16[120,1536]{1,0:T(8,128)(2,1)S(1)}, u32[]{:S(2)}, u32[]{:S(2)}) collective-permute-start(bf16[120,1536]{1,0:T(8,128)(2,1)S(1)} %add_convert_fusion), channel_id=1, source_target_pairs={{0,64},{64,0},{1,65},{65,1},{2,66},{66,2},{3,67},{67,3},{4,68},{68... | collective-permute-start | bytes 1105928 | tf_op jit(solution)/shard_map/ppermute | solution.py:410
Sparse Core Ops, SparseCore 0:
  9.0 61.4 all-gather.1

commit v3 on v2

--- a/solution.py
+++ b/solution.py
@@ -38,101 +38,152 @@
     refresh_ref,
     tokens_ref,
     mod_ref,
-    wq_ref,
-    wk_ref,
-    wv_ref,
-    ck_ref,
-    cv_ref,
+    w_ref,
+    cache_ref,
     send_ref,
     own_ref,
-    normed_ref,
+    picks,
+    tokens,
+    mod,
+    weights,
+    cache,
+    sent,
+    kept,
+    in_sems,
+    w_sems,
+    send_sem,
+    own_sem,
 ):
-    step = pl.program_id(0)
-    rows = tokens_ref.shape[0]
-    half = send_ref.shape[1] - rows
-
-    @pl.when(step == 0)
-    def _():
-        shift = mod_ref[0:1, :].astype(F32)
-        scale = mod_ref[1:2, :].astype(F32)
-        normed = layer_norm(tokens_ref[...].astype(F32)) * (1.0 + scale) + shift
-        normed_ref[...] = normed.astype(BF16)
-
-    normed = normed_ref[...]
-    wide = wq_ref.shape[1]
-    heads = wide // HEAD
-    queries = jnp.dot(normed, wq_ref[...], preferred_element_type=F32) * 0.125
-    keys = jnp.dot(normed, wk_ref[...], preferred_element_type=F32)
-    values = jnp.dot(normed, wv_ref[...], preferred_element_type=F32)
-    flagged = refresh_ref[0, 0] == tile_ref[0]
-    for slot in range(1, refresh_ref.shape[1]):
-        flagged = jnp.logical_or(flagged, refresh_ref[0, slot] == tile_ref[0])
-    low = lane_iota((rows, 2 * HEAD)) < HEAD
-    low_q = lane_iota((half, 2 * HEAD)) < HEAD
+    rows, width = tokens.shape
+    half = HEAD
+    blocks = w_sems.shape[0]
+    wide = width // blocks
+    inputs = (
+        (tokens_ref, tokens),
+        (mod_ref, mod),
+        (refresh_ref, picks),
+        (cache_ref, cache),
+    )
+    input_copies = [
+        pltpu.make_async_copy(src, dst, in_sems.at[i]) for i, (src, dst) in enumerate(inputs)
+    ]
+    w_copies = [
+        [
+            pltpu.make_async_copy(
+                w_ref.at[:, kind * width + b * wide : kind * width + (b + 1) * wide],
+                weights.at[:, kind * width + b * wide : kind * width + (b + 1) * wide],
+                w_sems.at[b, kind],
+            )
+            for kind in range(3)
+        ]
+        for b in range(blocks)
+    ]
+    for copy in input_copies[:3]:
+        copy.start()
+    for kind in range(3):
+        w_copies[0][kind].start()
+    input_copies[3].start()
+    for b in range(1, blocks):
+        for copy in w_copies[b]:
+            copy.start()
+    for copy in input_copies[:3]:
+        copy.wait()
+    normed = layer_norm(tokens[...].astype(F32)) * (1.0 + mod[1:2, :].astype(F32))
+    normed = (normed + mod[0:1, :].astype(F32)).astype(BF16)
+    flagged = picks[0, 0] == tile_ref[0]
+    for slot in range(1, picks.shape[1]):
+        flagged = jnp.logical_or(flagged, picks[0, slot] == tile_ref[0])
+    low = lane_iota((1, 2 * HEAD)) < HEAD
     pad = jnp.zeros((2 * half - rows, 2 * HEAD), F32)
-    for pair in range(heads // 2):
-        cols = slice(pair * 2 * HEAD, (pair + 1) * 2 * HEAD)
-        q_top = queries[:half, cols]
-        q_end = jnp.concatenate([queries[half:, cols], pad], axis=0)
-        k_new, v_new = keys[:, cols], values[:, cols]
-        k_out = jnp.where(flagged, k_new, ck_ref[:, cols].astype(F32))
-        v_out = jnp.where(flagged, v_new, cv_ref[:, cols].astype(F32))
-        for odd in range(2):
-            if odd:
-                q_pack = jnp.where(low_q, swap_halves(q_top), q_end)
-                join = lambda k, v: jnp.where(low, swap_halves(k), v)
-            else:
-                q_pack = jnp.where(low_q, q_top, swap_halves(q_end))
-                join = lambda k, v: jnp.where(low, k, swap_halves(v))
-            q_pack = q_pack.astype(BF16)
-            sent = join(k_out, v_out).astype(BF16)
-            head = step * heads + pair * 2 + odd
-            dest = head + head // 3
-            own_ref[head, :rows, :] = join(k_new, v_new).astype(BF16)
-            own_ref[head, rows:, :] = q_pack
-            send_ref[dest, :rows, :] = sent
-            send_ref[dest, rows:, :] = q_pack
-
-            @pl.when(head % 3 == 2)
-            def _():
-                send_ref[dest + 1, :rows, :] = sent
-                send_ref[dest + 1, rows:, :] = q_pack
+    input_copies[3].wait()
+    out_copies = []
+    for b in range(blocks):
+        made = []
+        for kind in range(3):
+            w_copies[b][kind].wait()
+            first = kind * width + b * wide
+            made.append(
+                jnp.dot(normed, weights[:, first : first + wide], preferred_element_type=F32)
+            )
+        queries, keys, values = made
+        queries = queries * 0.125
+        k_old = cache[:, b * wide : (b + 1) * wide].astype(F32)
+        v_old = cache[:, width + b * wide : width + (b + 1) * wide].astype(F32)
+        k_sent = jnp.where(flagged, keys, k_old)
+        v_sent = jnp.where(flagged, values, v_old)
+        for pair in range(wide // (2 * HEAD)):
+            cols = slice(pair * 2 * HEAD, (pair + 1) * 2 * HEAD)
+            q_top = queries[:half, cols]
+            q_end = jnp.concatenate([queries[half:, cols], pad], axis=0)
+            for odd in range(2):
+                if odd:
+                    q_pack = jnp.where(low, swap_halves(q_top), q_end)
+                    join = lambda k, v: jnp.where(low, swap_halves(k), v)
+                else:
+                    q_pack = jnp.where(low, q_top, swap_halves(q_end))
+                    join = lambda k, v: jnp.where(low, k, swap_halves(v))
+                q_pack = q_pack.astype(BF16)
+                out = join(k_sent[:, cols], v_sent[:, cols]).astype(BF16)
+                head = (b * wide) // HEAD + pair * 2 + odd
+                kept[head, :rows, :] = join(keys[:, cols], values[:, cols]).astype(BF16)
+                kept[head, rows:, :] = q_pack
+                dest = head + head // 3
+                for copy in range(2 if head % 3 == 2 else 1):
+                    sent[dest + copy, :rows, :] = out
+                    sent[dest + copy, rows:, :] = q_pack
+        head = (b * wide) // HEAD
+        last = (b + 1) * wide // HEAD
+        dest, dest_last = head + head // 3, last + last // 3
+        out_copies.append(
+            pltpu.make_async_copy(
+                sent.at[dest:dest_last], send_ref.at[dest:dest_last], send_sem.at[b]
+            )
+        )
+        out_copies.append(
+            pltpu.make_async_copy(kept.at[head:last], own_ref.at[head:last], own_sem.at[b])
+        )
+        out_copies[-2].start()
+        out_copies[-1].start()
+    for copy in out_copies:
+        copy.wait()
 
 
 def project(tile_index, refresh, tokens, modulate, w_qkv, cached):
     rows, width = tokens.shape
-    half = 64
-    block = 256
-    steps = width // block
+    blocks = 4
     heads = width // HEAD
     dests = heads + heads // 3
-    whole = lambda *shape: pl.BlockSpec(shape, lambda s: (0,) * len(shape))
+    packed = rows + HEAD
+    anywhere = pl.BlockSpec(memory_space=pltpu.HBM)
     return pl.pallas_call(
         project_kernel,
-        grid=(steps,),
         out_shape=(
-            jax.ShapeDtypeStruct((dests, rows + half, 2 * HEAD), BF16),
-            jax.ShapeDtypeStruct((heads, rows + half, 2 * HEAD), BF16),
-        ),
-        in_specs=[
-            pl.BlockSpec(memory_space=pltpu.SMEM),
-            pl.BlockSpec(memory_space=pltpu.SMEM),
-            whole(rows, width),
-            whole(6, width),
-            pl.BlockSpec((width, block), lambda s: (0, s)),
-            pl.BlockSpec((width, block), lambda s: (0, s + steps)),
-            pl.BlockSpec((width, block), lambda s: (0, s + 2 * steps)),
-            pl.BlockSpec((rows, block), lambda s: (0, s)),
-            pl.BlockSpec((rows, block), lambda s: (0, s + steps)),
+            pltpu.HBM((dests, packed, 2 * HEAD), BF16),
+            pltpu.HBM((heads, packed, 2 * HEAD), BF16),
+        ),
+        in_specs=[pl.BlockSpec(memory_space=pltpu.SMEM)] + [anywhere] * 5,
+        out_specs=(anywhere, anywhere),
+        scratch_shapes=[
+            pltpu.SMEM(refresh.shape, jnp.int32),
+            pltpu.VMEM(tokens.shape, BF16),
+            pltpu.VMEM(modulate.shape, BF16),
+            pltpu.VMEM(w_qkv.shape, BF16),
+            pltpu.VMEM(cached.shape, BF16),
+            pltpu.VMEM((dests, packed, 2 * HEAD), BF16),
+            pltpu.VMEM((heads, packed, 2 * HEAD), BF16),
+            pltpu.SemaphoreType.DMA((4,)),
+            pltpu.SemaphoreType.DMA((blocks, 3)),
+            pltpu.SemaphoreType.DMA((blocks,)),
+            pltpu.SemaphoreType.DMA((blocks,)),
         ],
-        out_specs=(
-            whole(dests, rows + half, 2 * HEAD),
-            whole(heads, rows + half, 2 * HEAD),
-        ),
-        scratch_shapes=[pltpu.VMEM((rows, width), BF16)],
-        compiler_params=pltpu.CompilerParams(vmem_limit_bytes=40 << 20),
+        compiler_params=pltpu.CompilerParams(vmem_limit_bytes=60 << 20),
+        cost_estimate=pl.CostEstimate(
+            flops=6 * rows * width * width,
+            bytes_accessed=6 * width * width + (4 << 20),
+            transcendentals=0,
+        ),
         name="project",
-    )(tile_index, refresh, tokens, modulate, w_qkv, w_qkv, w_qkv, cached, cached)
+    )(tile_index, refresh, tokens, modulate, w_qkv, cached)
 
 
 def own_kernel(live_ref, own_ref, tk_ref, tv_ref, out_ref):
@@ -275,7 +326,7 @@
     return pl.pallas_call(
         head_kernel,
         grid=(tiles // group,),
-        out_shape=jax.ShapeDtypeStruct((tiles, HEAD, lanes), BF16),
+        out_shape=pltpu.HBM((tiles, HEAD, lanes), BF16),
         in_specs=[
             pl.BlockSpec(memory_space=pltpu.SMEM),
             pl.BlockSpec((tiles, packed, lanes), lambda s: (0, 0, 0)),
@@ -296,8 +347,18 @@
     )(length, pack)
 
 
-def merge_kernel(far_ref, own_ref, w_ref, tokens_ref, mod_ref, mixed_ref, input_ref, att_ref):
+def join_kernel(far_ref, own_ref, w0, w1, w2, w3, att_ref, w_ref, sems):
     heads, rows, lanes = own_ref.shape
+    depth = att_ref.shape[2]
+    copies = []
+    first = 0
+    for i, part in enumerate((w0, w1, w2, w3)):
+        last = first + part.shape[0]
+        copies.append(pltpu.make_async_copy(part, w_ref.at[first:last], sems.at[i]))
+        first = last
+    for copy in copies:
+        copy.start()
+    per = depth // lanes
     low = lane_iota((1, lanes)) < HEAD
     diagonal = row_iota((HEAD, lanes)) == lane_iota((HEAD, lanes))
 
@@ -311,9 +372,9 @@
             head = 2 * pair + odd
             folded = far_ref[head + head // 3].astype(F32)
             stats = folded[rows - HEAD :]
-            first = column(stats[0:1] + stats[2:3])
+            begin = column(stats[0:1] + stats[2:3])
             rest = column(stats[1:2] + stats[3:4])
-            far_lse = jnp.concatenate([first, rest[: rows - HEAD]], axis=0)
+            far_lse = jnp.concatenate([begin, rest[: rows - HEAD]], axis=0)
             far = jnp.concatenate([folded, swap_halves(folded)[: rows - HEAD]], axis=0)
             own = own_ref[head]
             gap = jnp.broadcast_to(far_lse, (rows, lanes)) - own[:, 0:1]
@@ -321,88 +382,151 @@
             other = 1.0 / (1.0 + jnp.exp(gap))
             both.append(share * far + other * own)
         joined = jnp.where(low, swap_halves(both[0]), both[1])
-        att_ref[:, pair * lanes : (pair + 1) * lanes] = joined.astype(BF16)
-    projected = jnp.dot(att_ref[...], w_ref[...], preferred_element_type=F32)
+        at = (pair % per) * lanes
+        att_ref[pair // per, :, at : at + lanes] = joined.astype(BF16)
+    for copy in copies:
+        copy.wait()
+
+
+def join(far, own, w_parts):
+    heads, rows, _ = own.shape
+    depth, width = w_parts[0].shape
+    fetched = sum(part.shape[0] for part in w_parts)
+    local = pl.BlockSpec(memory_space=pltpu.VMEM)
+    anywhere = pl.BlockSpec(memory_space=pltpu.HBM)
+    return pl.pallas_call(
+        join_kernel,
+        out_shape=(
+            jax.ShapeDtypeStruct((width // depth, rows, depth), BF16),
+            pltpu.VMEM((fetched, width), BF16),
+        ),
+        in_specs=[local, local] + [anywhere] * 4,
+        out_specs=(local, local),
+        scratch_shapes=[pltpu.SemaphoreType.DMA((4,))],
+        compiler_params=pltpu.CompilerParams(vmem_limit_bytes=24 << 20),
+        cost_estimate=pl.CostEstimate(
+            flops=64 * heads * rows * 128, bytes_accessed=8 << 20, transcendentals=heads * rows * 256
+        ),
+        name="join",
+    )(far, own, *w_parts)
+
+
+def mix_kernel(
+    place_ref, att_ref, w_ref, w2_ref, w3_ref, tokens_ref, mod_ref, mixed_ref, input_ref
+):
+    place = place_ref[0]
+    depth = att_ref.shape[2]
+    late = w2_ref.shape[0]
+    early = depth - late
+    near = att_ref[place + 1 - 2 * (place % 2)]
+    far = att_ref[(place + 2) % 4]
+    far_near = att_ref[3 - place]
+    dot = lambda a, b: jnp.dot(a, b, preferred_element_type=F32)
+    projected = dot(att_ref[place], w_ref[:depth])
+    projected += dot(near, w_ref[depth : 2 * depth])
+    projected += dot(far[:, :early], w_ref[2 * depth : 2 * depth + early])
+    projected += dot(far_near[:, :early], w_ref[2 * depth + early :])
+    projected += dot(far[:, early:], w2_ref[...])
+    projected += dot(far_near[:, early:], w3_ref[...])
     mod = mod_ref[...].astype(F32)
     mixed = tokens_ref[...].astype(F32) + mod[2:3] * projected
     mixed_ref[...] = mixed
     input_ref[...] = (layer_norm(mixed) * (1.0 + mod[4:5]) + mod[3:4]).astype(BF16)
 
 
-def merge(far, own, w_out, tokens, modulate):
-    rows, width = tokens.shape
+def mix(place, attended, w_main, w2_late, w3_late, tokens, modulate):
+    local = pl.BlockSpec(memory_space=pltpu.VMEM)
     return pl.pallas_call(
-        merge_kernel,
+        mix_kernel,
+        out_shape=(
+            jax.ShapeDtypeStruct(tokens.shape, F32),
+            jax.ShapeDtypeStruct(tokens.shape, BF16),
+        ),
+        in_specs=[pl.BlockSpec(memory_space=pltpu.SMEM)] + [local] * 6,
+        out_specs=(local, local),
+        compiler_params=pltpu.CompilerParams(vmem_limit_bytes=24 << 20),
+        name="mix",
+    )(place, attended, w_main, w2_late, w3_late, tokens, modulate)
+
+
+def feed_blocks(first_ref, second_ref, keep_ref, pass_ref, up_ref, down_ref, ready):
+    rows = first_ref.shape[0]
+    hidden_width = up_ref.shape[1]
+    wide = 512
+    both = [first_ref[...].astype(F32), second_ref[...].astype(F32)]
+    both = jnp.concatenate(both, axis=0).astype(BF16)
+    total = None
+    for c in range(hidden_width // wide):
+        part = slice(c * wide, (c + 1) * wide)
+        ready(2 * c)
+        hidden = jnp.dot(both, up_ref[:, part], preferred_element_type=F32)
+        hidden = jax.nn.gelu(hidden, approximate=True).astype(BF16)
+        ready(2 * c + 1)
+        product = jnp.dot(hidden, down_ref[part, :], preferred_element_type=F32)
+        total = product if total is None else total + product
+    keep_ref[...] = total[:rows]
+    pass_ref[...] = total[rows:].astype(BF16)
+
+
+def feed_near_kernel(first, second, up_hbm, down_hbm, keep, passed, up, down, sems):
+    wide = 512
+    copies = []
+    for c in range(up.shape[1] // wide):
+        part = slice(c * wide, (c + 1) * wide)
+        copies.append(
+            pltpu.make_async_copy(up_hbm.at[:, part], up.at[:, part], sems.at[2 * c])
+        )
+        copies.append(
+            pltpu.make_async_copy(down_hbm.at[part], down.at[part], sems.at[2 * c + 1])
+        )
+    for copy in copies:
+        copy.start()
+    feed_blocks(first, second, keep, passed, up, down, lambda i: copies[i].wait())
+
+
+def feed_far_kernel(first, second, up, down, keep, passed):
+    feed_blocks(first, second, keep, passed, up, down, lambda i: None)
+
+
+def feed_near(first, second, w_up, w_down):
+    rows, width = first.shape
+    local = pl.BlockSpec(memory_space=pltpu.VMEM)
+    anywhere = pl.BlockSpec(memory_space=pltpu.HBM)
+    return pl.pallas_call(
+        feed_near_kernel,
         out_shape=(
             jax.ShapeDtypeStruct((rows, width), F32),
             jax.ShapeDtypeStruct((rows, width), BF16),
-        ),
-        in_specs=[pl.BlockSpec(memory_space=pltpu.VMEM)] * 5,
-        out_specs=(pl.BlockSpec(memory_space=pltpu.VMEM),) * 2,
-        scratch_shapes=[pltpu.VMEM((rows, width), BF16)],
-        compiler_params=pltpu.CompilerParams(vmem_limit_bytes=24 << 20),
-        name="merge",
-    )(far, own, w_out, tokens, modulate)
-
-
-def feed_kernel(first_ref, second_ref, up_ref, down_ref, keep_ref, pass_ref, x_ref, sum_ref):
-    step = pl.program_id(0)
-    rows = first_ref.shape[0]
-
-    @pl.when(step == 0)
-    def _():
-        both = [first_ref[...].astype(F32), second_ref[...].astype(F32)]
-        x_ref[...] = jnp.concatenate(both, axis=0).astype(BF16)
-
-    hidden = jnp.dot(x_ref[...], up_ref[...], preferred_element_type=F32)
-    hidden = jax.nn.gelu(hidden, approximate=True).astype(BF16)
-    part = jnp.dot(hidden, down_ref[...], preferred_element_type=F32)
-    last = pl.num_programs(0) - 1
-
-    @pl.when(step == 0)
-    def _():
-        sum_ref[...] = part
-
-    @pl.when(jnp.logical_and(step > 0, step < last))
-    def _():
-        sum_ref[...] += part
-
-    @pl.when(step == last)
-    def _():
-        keep_ref[...] = sum_ref[:rows] + part[:rows]
-        pass_ref[...] = (sum_ref[rows:] + part[rows:]).astype(BF16)
-
-
-def feed(first, second, w_up, w_down):
+            pltpu.VMEM(w_up.shape, BF16),
+            pltpu.VMEM(w_down.shape, BF16),
+        ),
+        in_specs=[local, local, anywhere, anywhere],
+        out_specs=(local,) * 4,
+        scratch_shapes=[pltpu.SemaphoreType.DMA((2 * (w_up.shape[1] // 512),))],
+        compiler_params=pltpu.CompilerParams(vmem_limit_bytes=32 << 20),
+        cost_estimate=pl.CostEstimate(
+            flops=8 * rows * w_up.size, bytes_accessed=4 * w_up.size, transcendentals=0
+        ),
+        name="feed_near",
+    )(first, second, w_up, w_down)
+
+
+def feed_far(first, second, w_up, w_down):
     rows, width = first.shape
-    hidden = w_up.shape[1]
-    block = 512
-    whole = lambda *shape: pl.BlockSpec(shape, lambda s: (0,) * len(shape))
+    local = pl.BlockSpec(memory_space=pltpu.VMEM)
     return pl.pallas_call(
-        feed_kernel,
-        grid=(hidden // block,),
+        feed_far_kernel,
         out_shape=(
             jax.ShapeDtypeStruct((rows, width), F32),
             jax.ShapeDtypeStruct((rows, width), BF16),
         ),
-        in_specs=[
-            whole(rows, width),
-            whole(rows, width),
-            pl.BlockSpec((width, block), lambda s: (0, s)),
-            pl.BlockSpec((block, width), lambda s: (s, 0)),
-        ],
-        out_specs=(whole(rows, width), whole(rows, width)),
-        scratch_shapes=[
-            pltpu.VMEM((2 * rows, width), BF16),
-            pltpu.VMEM((2 * rows, width), F32),
-        ],
-        compiler_params=pltpu.CompilerParams(vmem_limit_bytes=32 << 20),
+        in_specs=[local] * 4,
+        out_specs=(local,) * 2,
+        compiler_params=pltpu.CompilerParams(vmem_limit_bytes=24 << 20),
         cost_estimate=pl.CostEstimate(
-            flops=8 * rows * width * hidden,
-            bytes_accessed=4 * width * hidden,
-            transcendentals=2 * rows * hidden,
-        ),
-        name="feed",
+            flops=8 * rows * w_up.size, bytes_accessed=1 << 20, transcendentals=0
+        ),
+        name="feed_far",
     )(first, second, w_up, w_down)
 
 
@@ -417,24 +541,35 @@
     rows = tokens.shape[0]
     tile_index = lax.axis_index(TILE).astype(jnp.int32)
     length = lengths[0]
-    all_w_out = lax.all_gather(w_out, REQ, axis=0, tiled=True)
+    place = lax.axis_index(REQ).astype(jnp.int32).reshape(1)
+    part = w_out.shape[0] * 2 // 3
     send, own = project(
         tile_index.reshape(1), refresh, tokens, modulation[0], w_qkv, kv_cache[0]
     )
     pack = lax.all_to_all(send, TILE, split_axis=0, concat_axis=0, tiled=True)
     live = (length - tile_index * rows).reshape(1)
     own_part = own_attend(live, own, text_kv[0])
+    own_part, w_here = lax.optimization_barrier((own_part, w_out))
+    w2 = swap(w_here[:part], "zh")
+    w2_late = swap(w_here[part:], "zh")
     pack, own_part = lax.optimization_barrier((pack, own_part))
     far = head_attend(lengths, pack)
+    far, w2, w_here = lax.optimization_barrier((far, w2, w_here))
+    w1 = swap(w_here, "co")
+    w3 = swap(w2, "co")
     far = lax.all_to_all(far, TILE, split_axis=0, concat_axis=0, tiled=True)
-    mixed, mlp_input = merge(far, own_part, all_w_out, tokens, modulation[0])
+    far, w1, w3, w2_late = lax.optimization_barrier((far, w1, w3, w2_late))
+    w3_late = swap(w2_late, "co")
+    attended, w_main = join(far, own_part, (w_out, w1, w2, w3))
+    attended, w3_late = lax.optimization_barrier((attended, w3_late))
+    mixed, mlp_input = mix(place, attended, w_main, w2_late, w3_late, tokens, modulation[0])
 
     far_z = swap(mlp_input, "zh")
     near = swap(mlp_input, "co")
-    near_keep, near_pass = feed(mlp_input, near, w_up, w_down)
+    near_keep, near_pass, up, down = feed_near(mlp_input, near, w_up, w_down)
     far_z, near_keep, near_pass = lax.optimization_barrier((far_z, near_keep, near_pass))
     far_both = swap(far_z, "co")
-    far_keep, far_pass = feed(far_z, far_both, w_up, w_down)
+    far_keep, far_pass = feed_far(far_z, far_both, up, down)
     sum_far = (far_keep + swap(far_pass, "co").astype(F32)).astype(BF16)
     near_sum = near_keep + swap(near_pass, "co").astype(F32)
     mlp_out = near_sum + swap(sum_far, "zh").astype(F32)

time: 140 us -> 125 us (0.89)
  blocking collectives: 15.2 us -> 0 us
  between operations: 14.2 us -> 0.81 us
  waiting for transfers between devices: 21.1 us -> 31.9 us
  starting transfers between devices: 20.1 us -> 29 us
  local copies, waits for them, and re-layouts: 16.8 us -> 8.11 us
  Pallas kernels: 51.2 us -> 53.4 us
    ppermute x6 -> x11, waiting for transfers between devices: 10.8 us -> 27.7 us  [swap(): return lax.ppermute(values, axis, [(0, 1), (1, 0)])]
    all_to_all x1 -> x0, blocking collectives: 15.2 us -> none  [per_device(): far = lax.all_to_all(far, TILE, split_axis=0, concat_axis=0, tiled=True)]
    unnamed x28 -> x14, local copies, waits for them, and re-layouts: 16.8 us -> 7.14 us
    all_to_all x1, waiting for transfers between devices: 9.61 us -> 4.18 us  [per_device(): pack = lax.all_to_all(send, TILE, split_axis=0, concat_axis=0, tiled=True)]
    all_to_all x0 -> x1, starting transfers between devices: none -> 4.74 us  [per_device(): far = lax.all_to_all(far, TILE, split_axis=0, concat_axis=0, tiled=True)]
    ppermute x6 -> x11, starting transfers between devices: 10.7 us -> 14.8 us  [swap(): return lax.ppermute(values, axis, [(0, 1), (1, 0)])]
    pallas_call x5 -> x6, Pallas kernels: 42.1 us -> 44.3 us  [the longest x1 20.7 us: head_attend(): pl.pallas_call(head_kernel, grid=(tiles // group,), out_shape=pltpu.HBM((...]
  transfers between devices with their start and end apart: 8 -> 13, of which waited for: 4 -> 7; matrix products, arithmetic and copies ran while one was open for 0% -> 1% of each run, Pallas kernels for 31% -> 30%
where the time goes in v3:
time: 125 us; the launch traced here: 124 us
  Pallas kernels  53.4 us (43%)
  waiting for transfers between devices  31.9 us (26%)
  starting transfers between devices  29 us (23%)
  local copies, waits for them, and re-layouts  8.11 us (6%)
    ppermute x11, waiting for transfers between devices, swap(): return lax.ppermute(values, axis, [(0, 1), (1, 0)])  27.7 us
    pallas_call x1, Pallas kernels, head_attend(): pl.pallas_call(head_kernel, grid=(tiles // group,), out_shape=pltpu.HBM((...  20.7 us
    ppermute x11, starting transfers between devices, swap(): return lax.ppermute(values, axis, [(0, 1), (1, 0)])  14.8 us
    pallas_call x1, Pallas kernels, project(): pl.pallas_call(project_kernel, out_shape=(pltpu.HBM((dests, packed, 2 * H...  11 us
    all_to_all x1, starting transfers between devices, per_device(): pack = lax.all_to_all(send, TILE, split_axis=0, concat_axis=0, tiled=True)  9.48 us
    pallas_call x1, Pallas kernels, own_attend(): pl.pallas_call(own_kernel, grid=(pairs,), out_shape=jax.ShapeDtypeStruct(...  9.12 us
    unnamed x14, local copies, waits for them, and re-layouts  7.14 us
    all_to_all x1, starting transfers between devices, per_device(): far = lax.all_to_all(far, TILE, split_axis=0, concat_axis=0, tiled=True)  4.74 us
  transfers between devices with their start and end apart: 13, of which 7 were waited for; matrix products, arithmetic and copies ran while one was open for 1% of the time, Pallas kernels for 30%

profile of v3, /device:TPU:1, one launch (start us, length us, event | category | flops | bytes accessed | tf_op | source)
XLA Modules:
  0.0 124.3 jit_solution(4834096066394691249)
XLA Ops:
  0.0 11.0 %project.1 = (bf16[32,184,128]{2,1,0:T(8,128)(2,1)}, bf16[24,184,128]{2,1,0:T(8,128)(2,1)}) custom-call(s32[1]{0:T(128)} %bitcast.2.tile_ref, s32[1,4]{1,0:T(1,128)} %refresh_ref.1, bf16[120,1536]{1,0:T(8,128)(2,1)} %bitcast.14, bf16[6,1536]{1,0:T(8,128)(2,1)} %bitcast.16, bf16[1536,4608]{1,0:T(8,128)(2,1)} %w_ref.1, bf16[120,3072]{1,0:T(8,128)(2,1)} %bitcast.18), custom_call_target="tpu_custom_call" | custom-call | flops 1698693120 | bytes 18350080 | tf_op jit(solution)/shard_map/project/pallas_call | solution.py:158
  11.0 9.5 %all-to-all-start = ((bf16[32,184,128]{2,1,0:T(8,128)(2,1)}), bf16[32,184,128]{2,1,0:T(8,128)(2,1)}, u32[]{:S(2)}, u32[]{:S(2)}) async-start(bf16[32,184,128]{2,1,0:T(8,128)(2,1)} %get-tuple-element.33), calls=%async_computation | async-start | bytes 3014656 | tf_op jit(solution)/shard_map/all_to_all | solution.py:549
  21.2 1.2 copy-done.3
  22.4 1.3 %copy-done.5 = bf16[24,184,128]{2,1,0:T(8,128)(2,1)S(1)} copy-done((bf16[24,184,128]{2,1,0:T(8,128)(2,1)S(1)}, bf16[24,184,128]{2,1,0:T(8,128)(2,1)}, u32[]{:S(2)}) %copy-start.5) | copy-done | bytes 1130520
  23.6 9.1 %own_attend.1.own_ref = f32[24,120,128]{2,1,0:T(8,128)S(1)} custom-call(s32[1]{0:T(128)} %bitcast.6.live_ref, bf16[24,184,128]{2,1,0:T(8,128)(2,1)S(1)} %copy-done.5, bf16[154,3072]{1,0:T(8,128)(2,1)S(1)} %bitcast.12, bf16[154,3072]{1,0:T(8,128)(2,1)S(1)} %bitcast.13), custom_call_target="tpu_custom_call" | custom-call | flops 404029440 | bytes 6291456 | tf_op jit(solution)/shard_map/own_attend/pallas_call | solution.py:228
  32.8 0.9 slice.9
  33.7 3.3 %collective-permute-start = (bf16[256,1536]{1,0:T(8,128)(2,1)}, bf16[256,1536]{1,0:T(8,128)(2,1)}, u32[]{:S(2)}, u32[]{:S(2)}) collective-permute-start(bf16[256,1536]{1,0:T(8,128)(2,1)} %slice.9), channel_id=1, source_target_pairs={{0,64},{64,0},{1,65},{65,1},{2,66},{66,2},{3,67},{67,3},{4,68},{68... | collective-permute-start | bytes 2359304 | tf_op jit(solution)/shard_map/ppermute | solution.py:534
  37.0 4.2 %all-to-all-done.pack_ref = bf16[32,184,128]{2,1,0:T(8,128)(2,1)} async-done(((bf16[32,184,128]{2,1,0:T(8,128)(2,1)}), bf16[32,184,128]{2,1,0:T(8,128)(2,1)}, u32[]{:S(2)}, u32[]{:S(2)}) %all-to-all-start) | async-done | bytes 1507360 | tf_op jit(solution)/shard_map/all_to_all | solution.py:549
  41.2 20.7 %head_attend.1 = bf16[32,64,128]{2,1,0:T(8,128)(2,1)} custom-call(s32[1]{0:T(128)} %copy.11.len_ref, bf16[32,184,128]{2,1,0:T(8,128)(2,1)} %all-to-all-done.pack_ref), custom_call_target="tpu_custom_call" | custom-call | flops 7549747200 | bytes 4194304 | tf_op jit(solution)/shard_map/head_attend/pallas_call | solution.py:326
  61.9 1.6 %collective-permute-start.1 = (bf16[384,1536]{1,0:T(8,128)(2,1)S(1)}, bf16[384,1536]{1,0:T(8,128)(2,1)}, u32[]{:S(2)}, u32[]{:S(2)}) collective-permute-start(bf16[384,1536]{1,0:T(8,128)(2,1)S(1)} %copy-done.2), channel_id=1, source_target_pairs={{0,32},{32,0},{1,33},{33,1},{2,34},{34,2},{3,35},{35,3},{4,36},{36... | collective-permute-start | bytes 3538952 | tf_op jit(solution)/shard_map/ppermute | solution.py:534
  63.6 4.7 %all-to-all-start.1 = ((bf16[32,64,128]{2,1,0:T(8,128)(2,1)}), bf16[32,64,128]{2,1,0:T(8,128)(2,1)S(1)}, u32[]{:S(2)}, u32[]{:S(2)}) async-start(bf16[32,64,128]{2,1,0:T(8,128)(2,1)} %head_attend.1), calls=%async_computation.1 | async-start | bytes 1048576 | tf_op jit(solution)/shard_map/all_to_all | solution.py:560
  68.4 3.4 %collective-permute-start.3 = (bf16[128,1536]{1,0:T(8,128)(2,1)S(1)}, bf16[128,1536]{1,0:T(8,128)(2,1)}, u32[]{:S(2)}, u32[]{:S(2)}) collective-permute-start(bf16[128,1536]{1,0:T(8,128)(2,1)S(1)} %slice.10), channel_id=1, source_target_pairs={{0,64},{64,0},{1,65},{65,1},{2,66},{66,2},{3,67},{67,3},{4,68},{68... | collective-permute-start | bytes 1179656 | tf_op jit(solution)/shard_map/ppermute | solution.py:534
  71.8 14.5 %collective-permute-done.3.w2_ref = bf16[128,1536]{1,0:T(8,128)(2,1)} collective-permute-done((bf16[128,1536]{1,0:T(8,128)(2,1)S(1)}, bf16[128,1536]{1,0:T(8,128)(2,1)}, u32[]{:S(2)}, u32[]{:S(2)}) %collective-permute-start.3) | collective-permute-done | bytes 393248 | tf_op jit(solution)/shard_map/ppermute | solution.py:534
  86.2 1.3 %collective-permute-start.4 = (bf16[128,1536]{1,0:T(8,128)(2,1)}, bf16[128,1536]{1,0:T(8,128)(2,1)}, u32[]{:S(2)}, u32[]{:S(2)}) collective-permute-start(bf16[128,1536]{1,0:T(8,128)(2,1)} %collective-permute-done.3.w2_ref), channel_id=1, source_target_pairs={{0,32},{32,0},{1,33},{33,1},{2,34},{34,2},{3,35},{35,3},{4,36},{36... | collective-permute-start | bytes 1179656 | tf_op jit(solution)/shard_map/ppermute | solution.py:534
  87.6 3.3 %join.1 = (bf16[4,120,384]{2,1,0:T(8,128)(2,1)S(1)}, bf16[1280,1536]{1,0:T(8,128)(2,1)S(1)}) custom-call(bf16[32,64,128]{2,1,0:T(8,128)(2,1)S(1)} %all-to-all-done.1.far_ref, f32[24,120,128]{2,1,0:T(8,128)S(1)} %own_attend.1.own_ref, bf16[384,1536]{1,0:T(8,128)(2,1)S(1)} %copy-done.2, bf16[384,1536]{1,0:T(8,128)(2,1)} %collective-permute-done.1.w1, ...), custom_call_target="tpu_custom_call" | custom-call | flops 23592960 | bytes 8388608 | tf_op jit(solution)/shard_map/join/pallas_call | solution.py:397
  90.9 2.4 %mix.1 = (f32[120,1536]{1,0:T(8,128)S(1)}, bf16[120,1536]{1,0:T(8,128)(2,1)S(1)}) custom-call(s32[1]{0:T(128)} %bitcast.1.place_ref, bf16[4,120,384]{2,1,0:T(8,128)(2,1)S(1)} %get-tuple-element.47.att_ref, bf16[1280,1536]{1,0:T(8,128)(2,1)S(1)} %get-tuple-element.48.w_ref, bf16[128,1536]{1,0:T(8,128)(2,1)} %collective-permute-done.3.w2_ref, ...), custom_call_target="tpu_custom_call" | custom-call | tf_op jit(solution)/shard_map/mix/pallas_call | solution.py:439
  93.3 0.1 collective-permute-start.6
  93.4 1.5 %collective-permute-start.5 = (bf16[120,1536]{1,0:T(8,128)(2,1)S(1)}, bf16[120,1536]{1,0:T(8,128)(2,1)S(1)}, u32[]{:S(2)}, u32[]{:S(2)}) collective-permute-start(bf16[120,1536]{1,0:T(8,128)(2,1)S(1)} %get-tuple-element.51.first), channel_id=1, source_target_pairs={{0,64},{64,0},{1,65},{65,1},{2,66},{66,2},{3,67},{67,3},{4,68},{68... | collective-permute-start | bytes 1105928 | tf_op jit(solution)/shard_map/ppermute | solution.py:534
  95.0 0.1 collective-permute-done.6.second
  95.1 2.3 %copy-done = bf16[1536,1536]{1,0:T(8,128)(2,1)S(1)} copy-done((bf16[1536,1536]{1,0:T(8,128)(2,1)S(1)}, bf16[1536,1536]{1,0:T(8,128)(2,1)}, u32[]{:S(2)}) %copy-start) | copy-done | bytes 4718616
  97.4 2.3 %copy-done.1 = bf16[1536,1536]{1,0:T(8,128)(2,1)S(1)} copy-done((bf16[1536,1536]{1,0:T(8,128)(2,1)S(1)}, bf16[1536,1536]{1,0:T(8,128)(2,1)}, u32[]{:S(2)}) %copy-start.1) | copy-done | bytes 4718616
  99.8 4.1 %feed_near.1 = (f32[120,1536]{1,0:T(8,128)S(1)}, bf16[120,1536]{1,0:T(8,128)(2,1)S(1)}, bf16[1536,1536]{1,0:T(8,128)(2,1)S(1)}, bf16[1536,1536]{1,0:T(8,128)(2,1)S(1)}) custom-call(bf16[120,1536]{1,0:T(8,128)(2,1)S(1)} %get-tuple-element.51.first, bf16[120,1536]{1,0:T(8,128)(2,1)S(1)} %collective-permute-done.6.second, bf16[1536,1536]{1,0:T(8,128)(2,1)S(1)} %copy-done, ...), custom_call_target="tpu_custom_call" | custom-call | flops 2264924160 | bytes 9437184 | tf_op jit(solution)/shard_map/feed_near/pallas_call | solution.py:495
  103.9 0.9 collective-permute-done.5.first
  104.7 1.3 %collective-permute-start.8 = (bf16[120,1536]{1,0:T(8,128)(2,1)S(1)}, bf16[120,1536]{1,0:T(8,128)(2,1)S(1)}, u32[]{:S(2)}, u32[]{:S(2)}) collective-permute-start(bf16[120,1536]{1,0:T(8,128)(2,1)S(1)} %collective-permute-done.5.first), channel_id=1, source_target_pairs={{0,32},{32,0},{1,33},{33,1},{2,34},{34,2},{3,35},{35,3},{4,36},{36... | collective-permute-start | bytes 1105928 | tf_op jit(solution)/shard_map/ppermute | solution.py:534
  106.0 1.3 %collective-permute-done.8.second = bf16[120,1536]{1,0:T(8,128)(2,1)S(1)} collective-permute-done((bf16[120,1536]{1,0:T(8,128)(2,1)S(1)}, bf16[120,1536]{1,0:T(8,128)(2,1)S(1)}, u32[]{:S(2)}, u32[]{:S(2)}) %collective-permute-start.8) | collective-permute-done | bytes 368672 | tf_op jit(solution)/shard_map/ppermute | solution.py:534
  107.3 2.8 %feed_far.1 = (f32[120,1536]{1,0:T(8,128)S(1)}, bf16[120,1536]{1,0:T(8,128)(2,1)S(1)}) custom-call(bf16[120,1536]{1,0:T(8,128)(2,1)S(1)} %collective-permute-done.5.first, bf16[120,1536]{1,0:T(8,128)(2,1)S(1)} %collective-permute-done.8.second, bf16[1536,1536]{1,0:T(8,128)(2,1)S(1)} %get-tuple-element.57.up, bf16[1536,1536]{1,0:T(8,128)(2,1)S(1)} %get-tuple-element.58.down), custom_call_target="tpu_custom_call" | custom-call | flops 2264924160 | bytes 1048576 | tf_op jit(solution)/shard_map/feed_far/pallas_call | solution.py:517
  110.1 0.5 collective-permute-start.9
  110.5 0.1 collective-permute-start.7
  110.7 1.2 collective-permute-done.9
  111.9 1.6 %collective-permute-start.10 = (bf16[120,1536]{1,0:T(8,128)(2,1)S(1)}, bf16[120,1536]{1,0:T(8,128)(2,1)S(1)}, u32[]{:S(2)}, u32[]{:S(2)}) collective-permute-start(bf16[120,1536]{1,0:T(8,128)(2,1)S(1)} %add_convert_fusion), channel_id=1, source_target_pairs={{0,64},{64,0},{1,65},{65,1},{2,66},{66,2},{3,67},{67,3},{4,68},{68... | collective-permute-start | bytes 1105928 | tf_op jit(solution)/shard_map/ppermute | solution.py:534
  113.5 9.8 %collective-permute-done.10 = bf16[120,1536]{1,0:T(8,128)(2,1)S(1)} collective-permute-done((bf16[120,1536]{1,0:T(8,128)(2,1)S(1)}, bf16[120,1536]{1,0:T(8,128)(2,1)S(1)}, u32[]{:S(2)}, u32[]{:S(2)}) %collective-permute-start.10) | collective-permute-done | bytes 368672 | tf_op jit(solution)/shard_map/ppermute | solution.py:534
  123.3 1.0 fusion
  (21 shorter events, 0.3 us)
Async XLA Ops:
  11.0 21.7 %copy-start.2 = (bf16[384,1536]{1,0:T(8,128)(2,1)S(1)}, bf16[384,1536]{1,0:T(8,128)(2,1)}, u32[]{:S(2)}) copy-start(bf16[384,1536]{1,0:T(8,128)(2,1)} %w0.1) | copy-start | bytes 3538948
  11.0 30.2 %all-to-all-start = ((bf16[32,184,128]{2,1,0:T(8,128)(2,1)}), bf16[32,184,128]{2,1,0:T(8,128)(2,1)}, u32[]{:S(2)}, u32[]{:S(2)}) async-start(bf16[32,184,128]{2,1,0:T(8,128)(2,1)} %get-tuple-element.33), calls=%async_computation | async-start | bytes 3014656 | tf_op jit(solution)/shard_map/all_to_all | solution.py:549
  21.2 1.2 copy-start.3
  22.4 1.3 %copy-start.5 = (bf16[24,184,128]{2,1,0:T(8,128)(2,1)S(1)}, bf16[24,184,128]{2,1,0:T(8,128)(2,1)}, u32[]{:S(2)}) copy-start(bf16[24,184,128]{2,1,0:T(8,128)(2,1)} %get-tuple-element.34.own_ref) | copy-start | bytes 3391492
  33.7 28.2 %collective-permute-start = (bf16[256,1536]{1,0:T(8,128)(2,1)}, bf16[256,1536]{1,0:T(8,128)(2,1)}, u32[]{:S(2)}, u32[]{:S(2)}) collective-permute-start(bf16[256,1536]{1,0:T(8,128)(2,1)} %slice.9), channel_id=1, source_target_pairs={{0,64},{64,0},{1,65},{65,1},{2,66},{66,2},{3,67},{67,3},{4,68},{68... | collective-permute-start | bytes 2359304 | tf_op jit(solution)/shard_map/ppermute | solution.py:534
  61.9 29.0 %copy-start.4 = (bf16[1,120,1536]{2,1,0:T(8,128)(2,1)S(1)}, bf16[1,120,1536]{2,1,0:T(8,128)(2,1)}, u32[]{:S(2)}) copy-start(bf16[1,120,1536]{2,1,0:T(8,128)(2,1)} %param.10) | copy-start | bytes 1105924
  61.9 24.4 %collective-permute-start.1 = (bf16[384,1536]{1,0:T(8,128)(2,1)S(1)}, bf16[384,1536]{1,0:T(8,128)(2,1)}, u32[]{:S(2)}, u32[]{:S(2)}) collective-permute-start(bf16[384,1536]{1,0:T(8,128)(2,1)S(1)} %copy-done.2), channel_id=1, source_target_pairs={{0,32},{32,0},{1,33},{33,1},{2,34},{34,2},{3,35},{35,3},{4,36},{36... | collective-permute-start | bytes 3538952 | tf_op jit(solution)/shard_map/ppermute | solution.py:534
  63.5 22.7 %collective-permute-start.2 = (bf16[256,1536]{1,0:T(8,128)(2,1)}, bf16[256,1536]{1,0:T(8,128)(2,1)}, u32[]{:S(2)}, u32[]{:S(2)}) collective-permute-start(bf16[256,1536]{1,0:T(8,128)(2,1)} %collective-permute-done.w2), channel_id=1, source_target_pairs={{0,32},{32,0},{1,33},{33,1},{2,34},{34,2},{3,35},{35,3},{4,36},{36... | collective-permute-start | bytes 2359304 | tf_op jit(solution)/shard_map/ppermute | solution.py:534
  63.6 22.6 %all-to-all-start.1 = ((bf16[32,64,128]{2,1,0:T(8,128)(2,1)}), bf16[32,64,128]{2,1,0:T(8,128)(2,1)S(1)}, u32[]{:S(2)}, u32[]{:S(2)}) async-start(bf16[32,64,128]{2,1,0:T(8,128)(2,1)} %head_attend.1), calls=%async_computation.1 | async-start | bytes 1048576 | tf_op jit(solution)/shard_map/all_to_all | solution.py:560
  68.4 17.8 %collective-permute-start.3 = (bf16[128,1536]{1,0:T(8,128)(2,1)S(1)}, bf16[128,1536]{1,0:T(8,128)(2,1)}, u32[]{:S(2)}, u32[]{:S(2)}) collective-permute-start(bf16[128,1536]{1,0:T(8,128)(2,1)S(1)} %slice.10), channel_id=1, source_target_pairs={{0,64},{64,0},{1,65},{65,1},{2,66},{66,2},{3,67},{67,3},{4,68},{68... | collective-permute-start | bytes 1179656 | tf_op jit(solution)/shard_map/ppermute | solution.py:534
  86.2 4.7 %collective-permute-start.4 = (bf16[128,1536]{1,0:T(8,128)(2,1)}, bf16[128,1536]{1,0:T(8,128)(2,1)}, u32[]{:S(2)}, u32[]{:S(2)}) collective-permute-start(bf16[128,1536]{1,0:T(8,128)(2,1)} %collective-permute-done.3.w2_ref), channel_id=1, source_target_pairs={{0,32},{32,0},{1,33},{33,1},{2,34},{34,2},{3,35},{35,3},{4,36},{36... | collective-permute-start | bytes 1179656 | tf_op jit(solution)/shard_map/ppermute | solution.py:534
  87.6 3.3 %copy-start.6 = (bf16[1,6,1536]{2,1,0:T(8,128)(2,1)S(1)}, bf16[1,6,1536]{2,1,0:T(8,128)(2,1)}, u32[]{:S(2)}) copy-start(bf16[1,6,1536]{2,1,0:T(8,128)(2,1)} %param.11) | copy-start | bytes 55300
  93.3 1.8 %collective-permute-start.6 = (bf16[120,1536]{1,0:T(8,128)(2,1)S(1)}, bf16[120,1536]{1,0:T(8,128)(2,1)S(1)}, u32[]{:S(2)}, u32[]{:S(2)}) collective-permute-start(bf16[120,1536]{1,0:T(8,128)(2,1)S(1)} %get-tuple-element.51.first), channel_id=1, source_target_pairs={{0,32},{32,0},{1,33},{33,1},{2,34},{34,2},{3,35},{35,3},{4,36},{36... | collective-permute-start | bytes 1105928 | tf_op jit(solution)/shard_map/ppermute | solution.py:534
  93.4 11.3 %collective-permute-start.5 = (bf16[120,1536]{1,0:T(8,128)(2,1)S(1)}, bf16[120,1536]{1,0:T(8,128)(2,1)S(1)}, u32[]{:S(2)}, u32[]{:S(2)}) collective-permute-start(bf16[120,1536]{1,0:T(8,128)(2,1)S(1)} %get-tuple-element.51.first), channel_id=1, source_target_pairs={{0,64},{64,0},{1,65},{65,1},{2,66},{66,2},{3,67},{67,3},{4,68},{68... | collective-permute-start | bytes 1105928 | tf_op jit(solution)/shard_map/ppermute | solution.py:534
  95.1 2.3 %copy-start = (bf16[1536,1536]{1,0:T(8,128)(2,1)S(1)}, bf16[1536,1536]{1,0:T(8,128)(2,1)}, u32[]{:S(2)}) copy-start(bf16[1536,1536]{1,0:T(8,128)(2,1)} %up_hbm.1) | copy-start | bytes 14155780
  97.4 2.3 %copy-start.1 = (bf16[1536,1536]{1,0:T(8,128)(2,1)S(1)}, bf16[1536,1536]{1,0:T(8,128)(2,1)}, u32[]{:S(2)}) copy-start(bf16[1536,1536]{1,0:T(8,128)(2,1)} %down_hbm.1) | copy-start | bytes 14155780
  104.7 2.6 %collective-permute-start.8 = (bf16[120,1536]{1,0:T(8,128)(2,1)S(1)}, bf16[120,1536]{1,0:T(8,128)(2,1)S(1)}, u32[]{:S(2)}, u32[]{:S(2)}) collective-permute-start(bf16[120,1536]{1,0:T(8,128)(2,1)S(1)} %collective-permute-done.5.first), channel_id=1, source_target_pairs={{0,32},{32,0},{1,33},{33,1},{2,34},{34,2},{3,35},{35,3},{4,36},{36... | collective-permute-start | bytes 1105928 | tf_op jit(solution)/shard_map/ppermute | solution.py:534
  110.1 1.8 %collective-permute-start.9 = (bf16[120,1536]{1,0:T(8,128)(2,1)S(1)}, bf16[120,1536]{1,0:T(8,128)(2,1)S(1)}, u32[]{:S(2)}, u32[]{:S(2)}) collective-permute-start(bf16[120,1536]{1,0:T(8,128)(2,1)S(1)} %get-tuple-element.60), channel_id=1, source_target_pairs={{0,32},{32,0},{1,33},{33,1},{2,34},{34,2},{3,35},{35,3},{4,36},{36... | collective-permute-start | bytes 1105928 | tf_op jit(solution)/shard_map/ppermute | solution.py:534
  110.5 3.0 %collective-permute-start.7 = (bf16[120,1536]{1,0:T(8,128)(2,1)S(1)}, bf16[120,1536]{1,0:T(8,128)(2,1)S(1)}, u32[]{:S(2)}, u32[]{:S(2)}) collective-permute-start(bf16[120,1536]{1,0:T(8,128)(2,1)S(1)} %get-tuple-element.55), channel_id=1, source_target_pairs={{0,32},{32,0},{1,33},{33,1},{2,34},{34,2},{3,35},{35,3},{4,36},{36... | collective-permute-start | bytes 1105928 | tf_op jit(solution)/shard_map/ppermute | solution.py:534
  111.9 11.4 %collective-permute-start.10 = (bf16[120,1536]{1,0:T(8,128)(2,1)S(1)}, bf16[120,1536]{1,0:T(8,128)(2,1)S(1)}, u32[]{:S(2)}, u32[]{:S(2)}) collective-permute-start(bf16[120,1536]{1,0:T(8,128)(2,1)S(1)} %add_convert_fusion), channel_id=1, source_target_pairs={{0,64},{64,0},{1,65},{65,1},{2,66},{66,2},{3,67},{67,3},{4,68},{68... | collective-permute-start | bytes 1105928 | tf_op jit(solution)/shard_map/ppermute | solution.py:534

commit v4 on v3

v4 whole, which is shorter than its diff:
```python
import jax
import jax.numpy as jnp
from jax import lax
from jax.experimental import pallas as pl
from jax.experimental.pallas import tpu as pltpu
from jax.sharding import Mesh
from jax.sharding import PartitionSpec as P

REQ = ("zh", "co")
TILE = ("y", "zl", "x")
HEAD = 64
BIG = 1e30
BLOCKS = ((0, 768), (768, 1152), (1152, 1536))
F32 = jnp.float32
BF16 = jnp.bfloat16


def layer_norm(values):
    average = jnp.mean(values, -1, keepdims=True)
    centred = values - average
    spread = jnp.mean(centred * centred, -1, keepdims=True)
    return centred * lax.rsqrt(spread + 1e-06)


def lane_iota(shape):
    return lax.broadcasted_iota(jnp.int32, shape, len(shape) - 1)


def row_iota(shape):
    return lax.broadcasted_iota(jnp.int32, shape, len(shape) - 2)


def swap_halves(values):
    return pltpu.roll(values, HEAD, axis=1)


def project_kernel(
    tile_ref,
    refresh_ref,
    tokens_ref,
    mod_ref,
    w_ref,
    cache_ref,
    send_ref,
    own_ref,
    picks,
    tokens,
    mod,
    weights,
    cache,
    in_sems,
    w_sems,
):
    rows, width = tokens.shape
    half = HEAD
    inputs = (
        (tokens_ref, tokens),
        (mod_ref, mod),
        (refresh_ref, picks),
        (cache_ref, cache),
    )
    input_copies = [
        pltpu.make_async_copy(src, dst, in_sems.at[i]) for i, (src, dst) in enumerate(inputs)
    ]
    w_copies = [
        [
            pltpu.make_async_copy(
                w_ref.at[:, kind * width + low : kind * width + high],
                weights.at[:, kind * width + low : kind * width + high],
                w_sems.at[b, kind],
            )
            for kind in range(3)
        ]
        for b, (low, high) in enumerate(BLOCKS)
    ]
    for copy in input_copies:
        copy.start()
    for copies in w_copies:
        for copy in copies:
            copy.start()
    low = lane_iota((1, 2 * HEAD)) < HEAD
    pad = jnp.zeros((2 * half - rows, 2 * HEAD), F32)

    def joined(keys, values, odd):
        if odd:
            return jnp.where(low, swap_halves(keys), values).astype(BF16)
        return jnp.where(low, keys, swap_halves(values)).astype(BF16)

    def store(head, at, block):
        dest = head + head // 3
        for copy in range(2 if head % 3 == 2 else 1):
            send_ref[dest + copy, at] = block

    for copy in input_copies:
        copy.wait()
    normed = layer_norm(tokens[...].astype(F32)) * (1.0 + mod[1:2, :].astype(F32))
    normed = (normed + mod[0:1, :].astype(F32)).astype(BF16)
    flagged = picks[0, 0] == tile_ref[0]
    for slot in range(1, picks.shape[1]):
        flagged = jnp.logical_or(flagged, picks[0, slot] == tile_ref[0])
    above, below = slice(0, half), slice(half, half + rows)

    @pl.when(jnp.logical_not(flagged))
    def _():
        for head in range(width // HEAD):
            first = head // 2 * 2 * HEAD
            k_old = cache[:, first : first + 2 * HEAD].astype(F32)
            v_old = cache[:, width + first : width + first + 2 * HEAD].astype(F32)
            store(head, below, joined(k_old, v_old, head % 2))

    for b, (start, end) in enumerate(BLOCKS):
        made = []
        for kind in range(3):
            w_copies[b][kind].wait()
            made.append(
                jnp.dot(
                    normed,
                    weights[:, kind * width + start : kind * width + end],
                    preferred_element_type=F32,
                )
            )
        queries, keys, values = made
        queries = queries * 0.125
        for pair in range((end - start) // (2 * HEAD)):
            cols = slice(pair * 2 * HEAD, (pair + 1) * 2 * HEAD)
            q_top = queries[:half, cols]
            q_end = jnp.concatenate([queries[half:, cols], pad], axis=0)
            for odd in range(2):
                head = start // HEAD + pair * 2 + odd
                q_pack = joined(q_top, q_end, odd)
                own_ref[head, above] = q_pack
                own_ref[head, below] = joined(keys[:, cols], values[:, cols], odd)
                store(head, above, q_pack)
        head, last = start // HEAD, end // HEAD

        @pl.when(flagged)
        def _():
            for h in range(head, last):
                store(h, below, own_ref[h, below])


def project(tile_index, refresh, tokens, modulate, w_qkv, cached):
    rows, width = tokens.shape
    blocks = len(BLOCKS)
    heads = width // HEAD
    dests = heads + heads // 3
    packed = rows + HEAD
    anywhere = pl.BlockSpec(memory_space=pltpu.HBM)
    return pl.pallas_call(
        project_kernel,
        out_shape=(
            jax.ShapeDtypeStruct((dests, packed, 2 * HEAD), BF16),
            jax.ShapeDtypeStruct((heads, packed, 2 * HEAD), BF16),
        ),
        in_specs=[pl.BlockSpec(memory_space=pltpu.SMEM)] + [anywhere] * 5,
        out_specs=(pl.BlockSpec(memory_space=pltpu.VMEM),) * 2,
        scratch_shapes=[
            pltpu.SMEM(refresh.shape, jnp.int32),
            pltpu.VMEM(tokens.shape, BF16),
            pltpu.VMEM(modulate.shape, BF16),
            pltpu.VMEM(w_qkv.shape, BF16),
            pltpu.VMEM(cached.shape, BF16),
            pltpu.SemaphoreType.DMA((4,)),
            pltpu.SemaphoreType.DMA((blocks, 3)),
        ],
        compiler_params=pltpu.CompilerParams(vmem_limit_bytes=36 << 20),
        cost_estimate=pl.CostEstimate(
            flops=6 * rows * width * width,
            bytes_accessed=6 * width * width + (4 << 20),
            transcendentals=0,
        ),
        name="project",
    )(tile_index, refresh, tokens, modulate, w_qkv, cached)


def own_kernel(live_ref, own_ref, tk_ref, tv_ref, out_ref):
    heads, rows, lanes = out_ref.shape
    low = lane_iota((1, lanes)) < HEAD
    live = lane_iota((rows, rows)) < live_ref[0]
    nt = (((1,), (1,)), ((), ()))
    scores = []
    for head in range(heads):
        cols = slice(head // 2 * lanes, (head // 2 + 1) * lanes)
        folded = own_ref[head, :HEAD, :].astype(F32)
        query = jnp.concatenate([folded, swap_halves(folded)[: rows - HEAD]], axis=0)
        query = jnp.where(low, query, 0.0)
        text_query = swap_halves(query) if head % 2 else query
        s_own = lax.dot_general(
            query.astype(BF16), own_ref[head, HEAD:, :], nt, preferred_element_type=F32
        )
        s_text = lax.dot_general(
            text_query.astype(BF16), tk_ref[:, cols], nt, preferred_element_type=F32
        )
        scores.append((jnp.where(live, s_own, -BIG), s_text))
    probs = []
    for s_own, s_text in scores:
        top = jnp.maximum(
            jnp.max(s_own, -1, keepdims=True), jnp.max(s_text, -1, keepdims=True)
        )
        p_own = jnp.exp(s_own - top)
        p_text = jnp.exp(s_text - top)
        total = jnp.sum(p_own, -1, keepdims=True) + jnp.sum(p_text, -1, keepdims=True)
        probs.append((p_own.astype(BF16), p_text.astype(BF16), top, total))
    for head, (p_own, p_text, top, total) in enumerate(probs):
        cols = slice(head // 2 * lanes, (head // 2 + 1) * lanes)
        mixed = jnp.dot(p_own, own_ref[head, HEAD:, :], preferred_element_type=F32)
        from_text = jnp.dot(p_text, tv_ref[:, cols], preferred_element_type=F32)
        if head % 2 == 0:
            from_text = swap_halves(from_text)
        out_ref[head] = jnp.where(low, top + jnp.log(total), (mixed + from_text) / total)


def own_attend(live, own, text_rows):
    heads, packed, lanes = own.shape
    rows = packed - HEAD
    texts = text_rows.shape[0]
    group = 8
    steps = heads // group
    return pl.pallas_call(
        own_kernel,
        grid=(steps,),
        out_shape=jax.ShapeDtypeStruct((heads, rows, lanes), F32),
        in_specs=[
            pl.BlockSpec(memory_space=pltpu.SMEM),
            pl.BlockSpec((group, packed, lanes), lambda p: (p, 0, 0)),
            pl.BlockSpec((texts, group * HEAD), lambda p: (0, p)),
            pl.BlockSpec((texts, group * HEAD), lambda p: (0, p + steps)),
        ],
        out_specs=pl.BlockSpec((group, rows, lanes), lambda p: (p, 0, 0)),
        compiler_params=pltpu.CompilerParams(vmem_limit_bytes=24 << 20),
        cost_estimate=pl.CostEstimate(
            flops=2 * 4 * rows * (rows + texts) * 64 * heads,
            bytes_accessed=6 << 20,
            transcendentals=rows * (rows + texts) * heads,
        ),
        name="own_attend",
    )(live, own, text_rows, text_rows)


def head_kernel(len_ref, pack_ref, out_ref, v_ref, kt_ref, s_ref):
    step = pl.program_id(0)
    tiles, packed, lanes = pack_ref.shape
    rows = packed - HEAD
    total_rows = tiles * rows
    group = out_ref.shape[0]
    block = group * rows
    piece = 256
    chunk = 1920
    low = lane_iota((1, lanes)) < HEAD

    @pl.when(step == 0)
    def _():
        for pair in range(tiles // 2):
            both = jnp.concatenate(
                [pack_ref[2 * pair + t, HEAD:, :].astype(F32) for t in range(2)], axis=0
            )
            v_ref[pair * 2 * rows : (pair + 1) * 2 * rows, :] = both.astype(BF16)
        feature = row_iota((HEAD, piece))
        for c in range(total_rows // piece):
            part = slice(c * piece, (c + 1) * piece)
            kv = v_ref[part, :]
            index = lane_iota((HEAD, piece)) + c * piece
            own = jnp.logical_and(index >= feature * rows, index < feature * rows + rows)
            held = jnp.logical_or(own, jnp.logical_and(feature == tiles, index >= len_ref[0]))
            kt_ref[:HEAD, part] = jnp.transpose(kv.astype(F32))[:HEAD].astype(BF16)
            kt_ref[HEAD:, part] = jnp.where(held, 1.0, 0.0).astype(BF16)
            v_ref[part, :] = jnp.where(low, jnp.ones((), BF16), kv)

    feature = lane_iota((1, lanes)) - HEAD
    parts = []
    for t in range(group):
        tile = step * group + t
        mask = jnp.where(jnp.logical_or(feature == tile, feature == tiles), -BIG, 0.0)
        folded = pack_ref[tile, :HEAD, :].astype(F32)
        parts.append(jnp.where(low, folded, mask))
        parts.append(jnp.where(low, swap_halves(folded)[: rows - HEAD], mask))
    query = jnp.concatenate(parts, axis=0).astype(BF16)
    top = jnp.full((block, 128), -jnp.inf, F32)
    for c in range(total_rows // chunk):
        part = slice(c * chunk, (c + 1) * chunk)
        scores = jnp.dot(query, kt_ref[:, part], preferred_element_type=F32)
        s_ref[:, part] = scores
        for i in range(chunk // 128):
            top = jnp.maximum(top, scores[:, i * 128 : (i + 1) * 128])
    top = jnp.max(top, -1, keepdims=True)
    total = jnp.zeros((block, lanes), F32)
    for c in range(total_rows // chunk):
        part = slice(c * chunk, (c + 1) * chunk)
        probs = jnp.exp(s_ref[:, part] - top).astype(BF16)
        total = total + jnp.dot(probs, v_ref[part, :], preferred_element_type=F32)
    weight = total[:, 0:1]
    lse = jnp.broadcast_to(top + jnp.log(weight), (block, lanes))
    result = total / weight
    diagonal = row_iota((HEAD, lanes)) == lane_iota((HEAD, lanes))
    line = row_iota((8, lanes))
    pad = jnp.zeros((2 * HEAD - rows, lanes), F32)
    for t in range(group):
        first = slice(t * rows, t * rows + HEAD)
        rest = slice(t * rows + HEAD, (t + 1) * rows)
        lse_a = jnp.sum(jnp.where(diagonal, lse[first], 0.0), 0, keepdims=True)
        lse_b = jnp.concatenate([lse[rest], pad], axis=0)
        lse_b = jnp.sum(jnp.where(diagonal, lse_b, 0.0), 0, keepdims=True)
        high_a = lse_a.astype(BF16).astype(F32)
        high_b = lse_b.astype(BF16).astype(F32)
        stats = jnp.where(line == 2, lse_a - high_a, lse_b - high_b)
        stats = jnp.where(line == 0, high_a, jnp.where(line == 1, high_b, stats))
        folded = jnp.concatenate([swap_halves(result[rest]), stats], axis=0)
        out_ref[t] = jnp.where(low, folded, result[first]).astype(BF16)


def head_attend(length, pack):
    tiles, packed, lanes = pack.shape
    rows = packed - HEAD
    total_rows = tiles * rows
    group = 8
    block = group * rows
    return pl.pallas_call(
        head_kernel,
        grid=(tiles // group,),
        out_shape=pltpu.HBM((tiles, HEAD, lanes), BF16),
        in_specs=[
            pl.BlockSpec(memory_space=pltpu.SMEM),
            pl.BlockSpec((tiles, packed, lanes), lambda s: (0, 0, 0)),
        ],
        out_specs=pl.BlockSpec((group, HEAD, lanes), lambda s: (s, 0, 0)),
        scratch_shapes=[
            pltpu.VMEM((total_rows, lanes), BF16),
            pltpu.VMEM((lanes, total_rows), BF16),
            pltpu.VMEM((block, total_rows), F32),
        ],
        compiler_params=pltpu.CompilerParams(vmem_limit_bytes=44 << 20),
        cost_estimate=pl.CostEstimate(
            flops=4 * total_rows * total_rows * 128,
            bytes_accessed=4 << 20,
            transcendentals=total_rows * total_rows,
        ),
        name="head_attend",
    )(length, pack)


def join_kernel(far_ref, own_ref, w0, w1, w2a, w2b, w3a, w3b, att_ref, w_ref, sems):
    heads, rows, lanes = own_ref.shape
    depth = att_ref.shape[2]
    copies = []
    first = 0
    for i, part in enumerate((w0, w1, w2a, w2b, w3a, w3b)):
        last = first + part.shape[0]
        copies.append(pltpu.make_async_copy(part, w_ref.at[first:last], sems.at[i]))
        first = last
    for copy in copies:
        copy.start()
    per = depth // lanes
    low = lane_iota((1, lanes)) < HEAD
    diagonal = row_iota((HEAD, lanes)) == lane_iota((HEAD, lanes))

    def column(line):
        spread = jnp.where(diagonal, jnp.broadcast_to(line, (HEAD, lanes)), 0.0)
        return jnp.sum(spread, -1, keepdims=True)

    for pair in range(heads // 2):
        both = []
        for odd in range(2):
            head = 2 * pair + odd
            folded = far_ref[head + head // 3].astype(F32)
            stats = folded[rows - HEAD :]
            begin = column(stats[0:1] + stats[2:3])
            rest = column(stats[1:2] + stats[3:4])
            far_lse = jnp.concatenate([begin, rest[: rows - HEAD]], axis=0)
            far = jnp.concatenate([folded, swap_halves(folded)[: rows - HEAD]], axis=0)
            own = own_ref[head]
            gap = jnp.broadcast_to(far_lse, (rows, lanes)) - own[:, 0:1]
            share = 1.0 / (1.0 + jnp.exp(-gap))
            other = 1.0 / (1.0 + jnp.exp(gap))
            both.append(share * far + other * own)
        joined = jnp.where(low, swap_halves(both[0]), both[1])
        at = (pair % per) * lanes
        att_ref[pair // per, :, at : at + lanes] = joined.astype(BF16)
    for copy in copies:
        copy.wait()


def join(far, own, w_parts):
    heads, rows, _ = own.shape
    depth, width = w_parts[0].shape
    fetched = sum(part.shape[0] for part in w_parts)
    local = pl.BlockSpec(memory_space=pltpu.VMEM)
    anywhere = pl.BlockSpec(memory_space=pl.ANY)
    return pl.pallas_call(
        join_kernel,
        out_shape=(
            jax.ShapeDtypeStruct((width // depth, rows, depth), BF16),
            pltpu.VMEM((fetched, width), BF16),
        ),
        in_specs=[local, local] + [anywhere] * 6,
        out_specs=(local, local),
        scratch_shapes=[pltpu.SemaphoreType.DMA((6,))],
        compiler_params=pltpu.CompilerParams(vmem_limit_bytes=24 << 20),
        cost_estimate=pl.CostEstimate(
            flops=64 * heads * rows * 128, bytes_accessed=8 << 20, transcendentals=heads * rows * 256
        ),
        name="join",
    )(far, own, *w_parts)


def mix_kernel(
    place_ref, att_ref, w_ref, w2_ref, w3_ref, tokens_ref, mod_ref, mixed_ref, top_ref, end_ref
):
    place = place_ref[0]
    depth = att_ref.shape[2]
    late = w2_ref.shape[0]
    early = depth - late
    far = att_ref[(place + 2) % 4]
    far_near = att_ref[3 - place]
    dot = lambda a, b: jnp.dot(a, b, preferred_element_type=F32)
    projected = dot(att_ref[place], w_ref[:depth])
    projected += dot(att_ref[place + 1 - 2 * (place % 2)], w_ref[depth : 2 * depth])
    projected += dot(far[:, :early], w_ref[2 * depth : 2 * depth + early])
    projected += dot(far_near[:, :early], w_ref[2 * depth + early :])
    projected += dot(far[:, early:], w2_ref[...])
    projected += dot(far_near[:, early:], w3_ref[...])
    mod = mod_ref[...].astype(F32)
    mixed = tokens_ref[...].astype(F32) + mod[2:3] * projected
    mixed_ref[...] = mixed
    normed = layer_norm(mixed) * (1.0 + mod[4:5]) + mod[3:4]
    top_ref[...] = normed[: top_ref.shape[0]].astype(BF16)
    end_ref[...] = normed[top_ref.shape[0] :].astype(BF16)


def mix(place, attended, w_main, w2_late, w3_late, tokens, modulate):
    rows, width = tokens.shape
    local = pl.BlockSpec(memory_space=pltpu.VMEM)
    return pl.pallas_call(
        mix_kernel,
        out_shape=(
            jax.ShapeDtypeStruct((rows, width), F32),
            jax.ShapeDtypeStruct((HEAD, width), BF16),
            jax.ShapeDtypeStruct((rows - HEAD, width), BF16),
        ),
        in_specs=[pl.BlockSpec(memory_space=pltpu.SMEM)] + [local] * 6,
        out_specs=(local,) * 3,
        compiler_params=pltpu.CompilerParams(vmem_limit_bytes=24 << 20),
        name="mix",
    )(place, attended, w_main, w2_late, w3_late, tokens, modulate)


def feed_blocks(pieces, outs, up_ref, down_ref, ready):
    hidden_width = up_ref.shape[1]
    wide = 512
    both = jnp.concatenate([piece[...].astype(F32) for piece in pieces], axis=0).astype(BF16)
    total = None
    for c in range(hidden_width // wide):
        part = slice(c * wide, (c + 1) * wide)
        ready(2 * c)
        hidden = jnp.dot(both, up_ref[:, part], preferred_element_type=F32)
        hidden = jax.nn.gelu(hidden, approximate=True).astype(BF16)
        ready(2 * c + 1)
        product = jnp.dot(hidden, down_ref[part, :], preferred_element_type=F32)
        total = product if total is None else total + product
    first = 0
    for out in outs:
        last = first + out.shape[0]
        out[...] = total[first:last].astype(out.dtype)
        first = last


def feed_near_kernel(a, b, c, d, up_hbm, down_hbm, keep_a, keep_b, pass_a, pass_b, up, down, sems):
    wide = 512
    copies = []
    for i in range(up.shape[1] // wide):
        part = slice(i * wide, (i + 1) * wide)
        copies.append(
            pltpu.make_async_copy(up_hbm.at[:, part], up.at[:, part], sems.at[2 * i])
        )
        copies.append(
            pltpu.make_async_copy(down_hbm.at[part], down.at[part], sems.at[2 * i + 1])
        )
    for copy in copies:
        copy.start()
    outs = (keep_a, keep_b, pass_a, pass_b)
    feed_blocks((a, b, c, d), outs, up, down, lambda i: copies[i].wait())


def feed_far_kernel(a, b, c, d, up, down, keep_a, keep_b, pass_a, pass_b):
    feed_blocks((a, b, c, d), (keep_a, keep_b, pass_a, pass_b), up, down, lambda i: None)


def feed_outs(pieces):
    kinds = (F32, F32, BF16, BF16)
    return tuple(jax.ShapeDtypeStruct(p.shape, k) for p, k in zip(pieces, kinds))


def feed_near(pieces, w_up, w_down):
    rows = sum(piece.shape[0] for piece in pieces)
    local = pl.BlockSpec(memory_space=pltpu.VMEM)
    anywhere = pl.BlockSpec(memory_space=pltpu.HBM)
    return pl.pallas_call(
        feed_near_kernel,
        out_shape=feed_outs(pieces) + (pltpu.VMEM(w_up.shape, BF16), pltpu.VMEM(w_down.shape, BF16)),
        in_specs=[local] * 4 + [anywhere] * 2,
        out_specs=(local,) * 6,
        scratch_shapes=[pltpu.SemaphoreType.DMA((2 * (w_up.shape[1] // 512),))],
        compiler_params=pltpu.CompilerParams(vmem_limit_bytes=32 << 20),
        cost_estimate=pl.CostEstimate(
            flops=4 * rows * w_up.size, bytes_accessed=4 * w_up.size, transcendentals=0
        ),
        name="feed_near",
    )(*pieces, w_up, w_down)


def feed_far(pieces, w_up, w_down):
    rows = sum(piece.shape[0] for piece in pieces)
    local = pl.BlockSpec(memory_space=pltpu.VMEM)
    return pl.pallas_call(
        feed_far_kernel,
        out_shape=feed_outs(pieces),
        in_specs=[local] * 6,
        out_specs=(local,) * 4,
        compiler_params=pltpu.CompilerParams(vmem_limit_bytes=24 << 20),
        cost_estimate=pl.CostEstimate(
            flops=4 * rows * w_up.size, bytes_accessed=1 << 20, transcendentals=0
        ),
        name="feed_far",
    )(*pieces, w_up, w_down)


def final_kernel(
    live_ref, mixed_ref, mod_ref, near_a, near_b, core_a, core_b, far_a, far_b, out_ref
):
    gate = mod_ref[...].astype(F32)[5:6]
    cut = near_a.shape[0]
    for rows, near, core, far in (
        (slice(0, cut), near_a, core_a, far_a),
        (slice(cut, mixed_ref.shape[0]), near_b, core_b, far_b),
    ):
        total = near[...] + core[...].astype(F32) + far[...].astype(F32)
        result = mixed_ref[rows] + gate * total
        position = row_iota(result.shape) + rows.start
        out_ref[rows] = jnp.where(position < live_ref[0], result, 0.0).astype(BF16)


def final(live, mixed, modulate, *pieces):
    local = pl.BlockSpec(memory_space=pltpu.VMEM)
    return pl.pallas_call(
        final_kernel,
        out_shape=jax.ShapeDtypeStruct(mixed.shape, BF16),
        in_specs=[pl.BlockSpec(memory_space=pltpu.SMEM)] + [local] * 8,
        out_specs=local,
        compiler_params=pltpu.CompilerParams(vmem_limit_bytes=16 << 20),
        name="final",
    )(live, mixed, modulate, *pieces)


def swap(values, axis):
    return lax.ppermute(values, axis, [(0, 1), (1, 0)])


def per_device(
    latents, modulation, kv_cache, text_kv, lengths, refresh, w_qkv, w_out, w_up, w_down
):
    tokens = latents[0]
    rows = tokens.shape[0]
    tile_index = lax.axis_index(TILE).astype(jnp.int32)
    length = lengths[0]
    place = lax.axis_index(REQ).astype(jnp.int32).reshape(1)
    send, own = project(
        tile_index.reshape(1), refresh, tokens, modulation[0], w_qkv, kv_cache[0]
    )
    live = (length - tile_index * rows).reshape(1)
    own_part = own_attend(live, own, text_kv[0])
    send, own_part = lax.optimization_barrier((send, own_part))
    pack = lax.all_to_all(send, TILE, split_axis=0, concat_axis=0, tiled=True)
    pack, w_here = lax.optimization_barrier((pack, w_out))
    third = w_out.shape[0] // 3
    w2 = [swap(w_here[i * third : (i + 1) * third], "zh") for i in range(3)]
    w1 = swap(w_here, "co")
    far = head_attend(lengths, pack)
    far, w1, w2a, w2b = lax.optimization_barrier((far, w1, w2[0], w2[1]))
    w3a, w3b = swap(w2a, "co"), swap(w2b, "co")
    far = lax.all_to_all(far, TILE, split_axis=0, concat_axis=0, tiled=True)
    far, w3a, w3b, w2c = lax.optimization_barrier((far, w3a, w3b, w2[2]))
    w3c = swap(w2c, "co")
    attended, w_main = join(far, own_part, (w_out, w1, w2a, w2b, w3a, w3b))
    attended, w3c = lax.optimization_barrier((attended, w3c))
    mixed, *mlp_input = mix(place, attended, w_main, w2c, w3c, tokens, modulation[0])

    far_z = [swap(piece, "zh") for piece in mlp_input]
    near = [swap(piece, "co") for piece in mlp_input]
    *near_parts, up, down = feed_near((*mlp_input, *near), w_up, w_down)
    far_z, near_parts = lax.optimization_barrier((far_z, near_parts))
    far_both = [swap(piece, "co") for piece in far_z]
    far_parts = feed_far((*far_z, *far_both), up, down)
    far_core = [swap(piece, "co") for piece in far_parts[2:]]
    far_sums = [
        (keep + core.astype(F32)).astype(BF16) for keep, core in zip(far_parts[:2], far_core)
    ]
    far_back = [swap(piece, "zh") for piece in far_sums]
    near_core = [swap(piece, "co") for piece in near_parts[2:]]
    out = final(live, mixed, modulation[0], *near_parts[:2], *near_core, *far_back)
    return out[None]


def solution(mesh):
    fine = Mesh(mesh.devices.reshape(2, 2, 4, 2, 4), REQ + TILE)
    return jax.shard_map(
        per_device,
        mesh=fine,
        in_specs=(
            P(REQ, TILE, None),
            P(REQ, None, None),
            P(REQ, TILE, None),
            P(REQ, None, None),
            P(REQ),
            P(REQ, None),
            P(),
            P(REQ, None),
            P(None, REQ),
            P(REQ, None),
        ),
        out_specs=P(REQ, TILE, None),
        check_vma=False,
    )
```

time: 125 us -> 146 us (1.17)
  blocking collectives: 0 us -> 29.8 us
  local copies, waits for them, and re-layouts: 8.11 us -> 24.1 us
  Pallas kernels: 53.4 us -> 43.1 us
  waiting for transfers between devices: 31.9 us -> 23.6 us
  starting transfers between devices: 29 us -> 23.8 us
    all_to_all x0 -> x1, blocking collectives: none -> 29.8 us  [per_device(): pack = lax.all_to_all(send, TILE, split_axis=0, concat_axis=0, tiled=True)]
    unnamed x14 -> x46, local copies, waits for them, and re-layouts: 7.14 us -> 23.2 us
    pallas_call x5 -> x6, Pallas kernels: 29.4 us -> 19.5 us  [the longest x1 6.46 us: project(): pl.pallas_call(project_kernel, out_shape=(jax.ShapeDtypeStruct((dests, pa...]
    all_to_all x1 -> x0, starting transfers between devices: 9.48 us -> none  [per_device(): pack = lax.all_to_all(send, TILE, split_axis=0, concat_axis=0, tiled=True)]
    ppermute x11 -> x19, starting transfers between devices: 14.8 us -> 20 us  [swap(): return lax.ppermute(values, axis, [(0, 1), (1, 0)])]
    all_to_all x1 -> x0, waiting for transfers between devices: 4.18 us -> none  [per_device(): pack = lax.all_to_all(send, TILE, split_axis=0, concat_axis=0, tiled=True)]
    ppermute x11 -> x19, waiting for transfers between devices: 27.7 us -> 23.6 us  [swap(): return lax.ppermute(values, axis, [(0, 1), (1, 0)])]
  transfers between devices with their start and end apart: 13 -> 20, of which waited for: 7 -> 4; matrix products, arithmetic and copies ran while one was open for 1% -> 1% of each run, Pallas kernels for 30% -> 19%
where the time goes in v4:
time: 146 us; the launch traced here: 145 us
  Pallas kernels  43.1 us (30%)
  blocking collectives  29.8 us (20%)
  local copies, waits for them, and re-layouts  24.1 us (17%)
  starting transfers between devices  23.8 us (16%)
  waiting for transfers between devices  23.6 us (16%)
    all_to_all x1, blocking collectives, per_device(): pack = lax.all_to_all(send, TILE, split_axis=0, concat_axis=0, tiled=True)  29.8 us
    ppermute x19, waiting for transfers between devices, swap(): return lax.ppermute(values, axis, [(0, 1), (1, 0)])  23.6 us
    unnamed x46, local copies, waits for them, and re-layouts  23.2 us
    ppermute x19, starting transfers between devices, swap(): return lax.ppermute(values, axis, [(0, 1), (1, 0)])  20 us
    pallas_call x1, Pallas kernels, head_attend(): pl.pallas_call(head_kernel, grid=(tiles // group,), out_shape=pltpu.HBM((...  19.3 us
    pallas_call x1, Pallas kernels, project(): pl.pallas_call(project_kernel, out_shape=(jax.ShapeDtypeStruct((dests, pa...  6.46 us
    pallas_call x1, Pallas kernels, join(): pl.pallas_call(join_kernel, out_shape=(jax.ShapeDtypeStruct((width // dep...  4.31 us
    pallas_call x1, Pallas kernels, feed_near(): pl.pallas_call(feed_near_kernel, out_shape=feed_outs(pieces) + (pltpu.VME...  4.13 us
  transfers between devices with their start and end apart: 20, of which 4 were waited for; matrix products, arithmetic and copies ran while one was open for 1% of the time, Pallas kernels for 19%

profile of v4, /device:TPU:1, one launch (start us, length us, event | category | flops | bytes accessed | tf_op | source)
XLA Modules:
  0.0 145.4 jit_solution(8463929607250170910)
XLA Ops:
  0.7 5.0 %copy-done = bf16[1536,4608]{1,0:T(8,128)(2,1)S(1)} copy-done((bf16[1536,4608]{1,0:T(8,128)(2,1)S(1)}, bf16[1536,4608]{1,0:T(8,128)(2,1)}, u32[]{:S(2)}) %copy-start) | copy-done | bytes 14155800
  5.7 1.0 copy-done.5
  6.7 1.1 copy-done.9
  9.2 6.5 %project.1 = (bf16[32,184,128]{2,1,0:T(8,128)(2,1)S(1)}, bf16[24,184,128]{2,1,0:T(8,128)(2,1)S(1)}) custom-call(s32[1]{0:T(128)} %bitcast.3.tile_ref, s32[1,4]{1,0:T(1,128)S(1)} %copy-done.22, bf16[120,1536]{1,0:T(8,128)(2,1)S(1)} %bitcast.12, bf16[6,1536]{1,0:T(8,128)(2,1)S(1)} %bitcast.15, bf16[1536,4608]{1,0:T(8,128)(2,1)S(1)} %copy-done, ...), custom_call_target="tpu_custom_call" | custom-call | flops 1698693120 | bytes 18350080 | tf_op jit(solution)/shard_map/project/pallas_call | solution.py:149
  15.7 3.0 %own_attend.1.own_ref = f32[24,120,128]{2,1,0:T(8,128)S(1)} custom-call(s32[1]{0:T(128)} %bitcast.1.live_ref, bf16[24,184,128]{2,1,0:T(8,128)(2,1)S(1)} %get-tuple-element.43.own_ref, bf16[154,3072]{1,0:T(8,128)(2,1)S(1)} %bitcast.10, bf16[154,3072]{1,0:T(8,128)(2,1)S(1)} %bitcast.11), custom_call_target="tpu_custom_call" | custom-call | flops 404029440 | bytes 6291456 | tf_op jit(solution)/shard_map/own_attend/pallas_call | solution.py:219
  18.7 29.8 %all_to_all.10.pack_ref = bf16[32,184,128]{2,1,0:T(8,128)(2,1)S(1)} all-to-all(bf16[32,184,128]{2,1,0:T(8,128)(2,1)S(1)} %get-tuple-element.44), channel_id=1, replica_groups=mesh['zh'=2,'co'=2,'y'=4,'zl'=2,'x'=4] {'y','zl','x'}, dimensions={0} | all-to-all | bytes 3014656 | tf_op jit(solution)/shard_map/all_to_all | solution.py:571
  48.5 2.7 %collective-permute-start = (bf16[384,1536]{1,0:T(8,128)(2,1)S(1)}, bf16[384,1536]{1,0:T(8,128)(2,1)S(1)}, u32[]{:S(2)}, u32[]{:S(2)}) collective-permute-start(bf16[384,1536]{1,0:T(8,128)(2,1)S(1)} %copy-done.3), channel_id=1, source_target_pairs={{0,32},{32,0},{1,33},{33,1},{2,34},{34,2},{3,35},{35,3},{4,36},{36... | collective-permute-start | bytes 3538952 | tf_op jit(solution)/shard_map/ppermute | solution.py:554
  52.1 3.3 %collective-permute-start.2 = (bf16[128,1536]{1,0:T(8,128)(2,1)S(1)}, bf16[128,1536]{1,0:T(8,128)(2,1)S(1)}, u32[]{:S(2)}, u32[]{:S(2)}) collective-permute-start(bf16[128,1536]{1,0:T(8,128)(2,1)S(1)} %get-tuple-element.80), channel_id=1, source_target_pairs={{0,64},{64,0},{1,65},{65,1},{2,66},{66,2},{3,67},{67,3},{4,68},{68... | collective-permute-start | bytes 1179656 | tf_op jit(solution)/shard_map/ppermute | solution.py:554
  55.4 19.3 %head_attend.1 = bf16[32,64,128]{2,1,0:T(8,128)(2,1)} custom-call(s32[1]{0:T(128)} %copy.11.len_ref, bf16[32,184,128]{2,1,0:T(8,128)(2,1)S(1)} %all_to_all.10.pack_ref), custom_call_target="tpu_custom_call" | custom-call | flops 7549747200 | bytes 4194304 | tf_op jit(solution)/shard_map/head_attend/pallas_call | solution.py:317
  76.2 1.1 copy-done.7
  77.3 3.9 %all-to-all-start.1 = ((bf16[32,64,128]{2,1,0:T(8,128)(2,1)}), bf16[32,64,128]{2,1,0:T(8,128)(2,1)S(1)}, u32[]{:S(2)}, u32[]{:S(2)}) async-start(bf16[32,64,128]{2,1,0:T(8,128)(2,1)} %head_attend.1), calls=%async_computation.1 | async-start | bytes 1048576 | tf_op jit(solution)/shard_map/all_to_all | solution.py:579
  81.2 3.0 %collective-permute-start.5 = (bf16[128,1536]{1,0:T(8,128)(2,1)}, bf16[128,1536]{1,0:T(8,128)(2,1)S(1)}, u32[]{:S(2)}, u32[]{:S(2)}) collective-permute-start(bf16[128,1536]{1,0:T(8,128)(2,1)} %get-tuple-element.79), channel_id=1, source_target_pairs={{0,64},{64,0},{1,65},{65,1},{2,66},{66,2},{3,67},{67,3},{4,68},{68... | collective-permute-start | bytes 1179656 | tf_op jit(solution)/shard_map/ppermute | solution.py:554
  84.2 1.1 collective-permute-start.3
  85.3 13.5 %collective-permute-done.5.w2_ref = bf16[128,1536]{1,0:T(8,128)(2,1)S(1)} collective-permute-done((bf16[128,1536]{1,0:T(8,128)(2,1)}, bf16[128,1536]{1,0:T(8,128)(2,1)S(1)}, u32[]{:S(2)}, u32[]{:S(2)}) %collective-permute-start.5) | collective-permute-done | bytes 393248 | tf_op jit(solution)/shard_map/ppermute | solution.py:554
  101.0 1.2 collective-permute-start.6
  102.2 1.3 copy-done.8
  103.5 1.0 copy-done.11
  104.5 1.0 copy-done.13
  105.5 1.0 copy-done.17
  106.5 1.0 copy-done.19
  107.5 4.3 %join.1 = (bf16[4,120,384]{2,1,0:T(8,128)(2,1)S(1)}, bf16[1280,1536]{1,0:T(8,128)(2,1)S(1)}) custom-call(bf16[32,64,128]{2,1,0:T(8,128)(2,1)S(1)} %all-to-all-done.1.far_ref, f32[24,120,128]{2,1,0:T(8,128)S(1)} %own_attend.1.own_ref, bf16[384,1536]{1,0:T(8,128)(2,1)S(1)} %copy-done.3, bf16[384,1536]{1,0:T(8,128)(2,1)S(1)} %copy-done.8, ...), custom_call_target="tpu_custom_call" | custom-call | flops 23592960 | bytes 8388608 | tf_op jit(solution)/shard_map/join/pallas_call | solution.py:388
  111.8 2.2 %mix.1 = (f32[120,1536]{1,0:T(8,128)S(1)}, bf16[64,1536]{1,0:T(8,128)(2,1)S(1)}, bf16[56,1536]{1,0:T(8,128)(2,1)S(1)}) custom-call(s32[1]{0:T(128)} %bitcast.2.place_ref, bf16[4,120,384]{2,1,0:T(8,128)(2,1)S(1)} %get-tuple-element.57.att_ref, bf16[1280,1536]{1,0:T(8,128)(2,1)S(1)} %get-tuple-element.58.w_ref, bf16[128,1536]{1,0:T(8,128)(2,1)S(1)} %copy-done.15, ...), custom_call_target="tpu_custom_call" | custom-call | tf_op jit(solution)/shard_map/mix/pallas_call | solution.py:432
  114.7 1.7 %collective-permute-start.8 = (bf16[56,1536]{1,0:T(8,128)(2,1)S(1)}, bf16[56,1536]{1,0:T(8,128)(2,1)S(1)}, u32[]{:S(2)}, u32[]{:S(2)}) collective-permute-start(bf16[56,1536]{1,0:T(8,128)(2,1)S(1)} %get-tuple-element.62.b), channel_id=1, source_target_pairs={{0,64},{64,0},{1,65},{65,1},{2,66},{66,2},{3,67},{67,3},{4,68},{68... | collective-permute-start | bytes 516104 | tf_op jit(solution)/shard_map/ppermute | solution.py:554
  116.4 1.3 collective-permute-start.7
  117.7 2.3 %copy-done.1 = bf16[1536,1536]{1,0:T(8,128)(2,1)S(1)} copy-done((bf16[1536,1536]{1,0:T(8,128)(2,1)S(1)}, bf16[1536,1536]{1,0:T(8,128)(2,1)}, u32[]{:S(2)}) %copy-start.1) | copy-done | bytes 4718616
  120.0 2.3 %copy-done.2 = bf16[1536,1536]{1,0:T(8,128)(2,1)S(1)} copy-done((bf16[1536,1536]{1,0:T(8,128)(2,1)S(1)}, bf16[1536,1536]{1,0:T(8,128)(2,1)}, u32[]{:S(2)}) %copy-start.2) | copy-done | bytes 4718616
  122.3 4.1 %feed_near.1 = (f32[64,1536]{1,0:T(8,128)S(1)}, f32[56,1536]{1,0:T(8,128)S(1)}, bf16[64,1536]{1,0:T(8,128)(2,1)S(1)}, bf16[56,1536]{1,0:T(8,128)(2,1)S(1)}, bf16...) custom-call(bf16[64,1536]{1,0:T(8,128)(2,1)S(1)} %get-tuple-element.61.a, ...), custom_call_target="tpu_custom_call" | custom-call | flops 2264924160 | bytes 9437184 | tf_op jit(solution)/shard_map/feed_near/pallas_call | solution.py:496
  127.3 1.3 collective-permute-done.14.d
  128.6 2.8 %feed_far.1 = (f32[64,1536]{1,0:T(8,128)S(1)}, f32[56,1536]{1,0:T(8,128)S(1)}, bf16[64,1536]{1,0:T(8,128)(2,1)S(1)}, bf16[56,1536]{1,0:T(8,128)(2,1)S(1)}) custom-call(bf16[64,1536]{1,0:T(8,128)(2,1)S(1)} %collective-permute-done.7.a, bf16[56,1536]{1,0:T(8,128)(2,1)S(1)} %collective-permute-done.8.b, bf16[64,1536]{1,0:T(8,128)(2,1)S(1)} %collective-permute-done.13.c, ...), custom_call_target="tpu_custom_call" | custom-call | flops 2264924160 | bytes 1048576 | tf_op jit(solution)/shard_map/feed_far/pallas_call | solution.py:513
  133.0 1.8 %collective-permute-start.16 = (bf16[64,1536]{1,0:T(8,128)(2,1)S(1)}, bf16[64,1536]{1,0:T(8,128)(2,1)S(1)}, u32[]{:S(2)}, u32[]{:S(2)}) collective-permute-start(bf16[64,1536]{1,0:T(8,128)(2,1)S(1)} %add_convert_fusion), channel_id=1, source_target_pairs={{0,64},{64,0},{1,65},{65,1},{2,66},{66,2},{3,67},{67,3},{4,68},{68... | collective-permute-start | bytes 589832 | tf_op jit(solution)/shard_map/ppermute | solution.py:554
  134.8 1.4 collective-permute-start.18
  136.1 8.3 %collective-permute-done.18.far_b = bf16[56,1536]{1,0:T(8,128)(2,1)S(1)} collective-permute-done((bf16[56,1536]{1,0:T(8,128)(2,1)S(1)}, bf16[56,1536]{1,0:T(8,128)(2,1)S(1)}, u32[]{:S(2)}, u32[]{:S(2)}) %collective-permute-start.18) | collective-permute-done | bytes 172064 | tf_op jit(solution)/shard_map/ppermute | solution.py:554
  (66 shorter events, 10.0 us)
Async XLA Ops:
  0.7 5.0 %copy-start = (bf16[1536,4608]{1,0:T(8,128)(2,1)S(1)}, bf16[1536,4608]{1,0:T(8,128)(2,1)}, u32[]{:S(2)}) copy-start(bf16[1536,4608]{1,0:T(8,128)(2,1)} %w_ref.1) | copy-start | bytes 42467332
  6.7 1.1 copy-start.9
  9.2 6.5 %copy-start.4 = (bf16[1,154,3072]{2,1,0:T(8,128)(2,1)S(1)}, bf16[1,154,3072]{2,1,0:T(8,128)(2,1)}, u32[]{:S(2)}) copy-start(bf16[1,154,3072]{2,1,0:T(8,128)(2,1)} %param.13) | copy-start | bytes 2838532
  18.7 29.8 %copy-start.3 = (bf16[384,1536]{1,0:T(8,128)(2,1)S(1)}, bf16[384,1536]{1,0:T(8,128)(2,1)}, u32[]{:S(2)}) copy-start(bf16[384,1536]{1,0:T(8,128)(2,1)} %w0.1) | copy-start | bytes 3538948
  48.5 27.7 %collective-permute-start = (bf16[384,1536]{1,0:T(8,128)(2,1)S(1)}, bf16[384,1536]{1,0:T(8,128)(2,1)S(1)}, u32[]{:S(2)}, u32[]{:S(2)}) collective-permute-start(bf16[384,1536]{1,0:T(8,128)(2,1)S(1)} %copy-done.3), channel_id=1, source_target_pairs={{0,32},{32,0},{1,33},{33,1},{2,34},{34,2},{3,35},{35,3},{4,36},{36... | collective-permute-start | bytes 3538952 | tf_op jit(solution)/shard_map/ppermute | solution.py:554
  52.1 22.6 %collective-permute-start.2 = (bf16[128,1536]{1,0:T(8,128)(2,1)S(1)}, bf16[128,1536]{1,0:T(8,128)(2,1)S(1)}, u32[]{:S(2)}, u32[]{:S(2)}) collective-permute-start(bf16[128,1536]{1,0:T(8,128)(2,1)S(1)} %get-tuple-element.80), channel_id=1, source_target_pairs={{0,64},{64,0},{1,65},{65,1},{2,66},{66,2},{3,67},{67,3},{4,68},{68... | collective-permute-start | bytes 1179656 | tf_op jit(solution)/shard_map/ppermute | solution.py:554
  55.4 20.1 %collective-permute-start.1 = (bf16[128,1536]{1,0:T(8,128)(2,1)S(1)}, bf16[128,1536]{1,0:T(8,128)(2,1)S(1)}, u32[]{:S(2)}, u32[]{:S(2)}) collective-permute-start(bf16[128,1536]{1,0:T(8,128)(2,1)S(1)} %get-tuple-element.81), channel_id=1, source_target_pairs={{0,64},{64,0},{1,65},{65,1},{2,66},{66,2},{3,67},{67,3},{4,68},{68... | collective-permute-start | bytes 1179656 | tf_op jit(solution)/shard_map/ppermute | solution.py:554
  76.2 1.1 copy-start.7
  77.3 23.7 %all-to-all-start.1 = ((bf16[32,64,128]{2,1,0:T(8,128)(2,1)}), bf16[32,64,128]{2,1,0:T(8,128)(2,1)S(1)}, u32[]{:S(2)}, u32[]{:S(2)}) async-start(bf16[32,64,128]{2,1,0:T(8,128)(2,1)} %head_attend.1), calls=%async_computation.1 | async-start | bytes 1048576 | tf_op jit(solution)/shard_map/all_to_all | solution.py:579
  81.2 17.6 %collective-permute-start.5 = (bf16[128,1536]{1,0:T(8,128)(2,1)}, bf16[128,1536]{1,0:T(8,128)(2,1)S(1)}, u32[]{:S(2)}, u32[]{:S(2)}) collective-permute-start(bf16[128,1536]{1,0:T(8,128)(2,1)} %get-tuple-element.79), channel_id=1, source_target_pairs={{0,64},{64,0},{1,65},{65,1},{2,66},{66,2},{3,67},{67,3},{4,68},{68... | collective-permute-start | bytes 1179656 | tf_op jit(solution)/shard_map/ppermute | solution.py:554
  84.2 14.6 %collective-permute-start.3 = (bf16[128,1536]{1,0:T(8,128)(2,1)}, bf16[128,1536]{1,0:T(8,128)(2,1)S(1)}, u32[]{:S(2)}, u32[]{:S(2)}) collective-permute-start(bf16[128,1536]{1,0:T(8,128)(2,1)} %copy-done.12), channel_id=1, source_target_pairs={{0,32},{32,0},{1,33},{33,1},{2,34},{34,2},{3,35},{35,3},{4,36},{36... | collective-permute-start | bytes 1179656 | tf_op jit(solution)/shard_map/ppermute | solution.py:554
  85.3 15.0 %collective-permute-start.4 = (bf16[128,1536]{1,0:T(8,128)(2,1)}, bf16[128,1536]{1,0:T(8,128)(2,1)S(1)}, u32[]{:S(2)}, u32[]{:S(2)}) collective-permute-start(bf16[128,1536]{1,0:T(8,128)(2,1)} %copy-done.10), channel_id=1, source_target_pairs={{0,32},{32,0},{1,33},{33,1},{2,34},{34,2},{3,35},{35,3},{4,36},{36... | collective-permute-start | bytes 1179656 | tf_op jit(solution)/shard_map/ppermute | solution.py:554
  101.0 10.8 %collective-permute-start.6 = (bf16[128,1536]{1,0:T(8,128)(2,1)}, bf16[128,1536]{1,0:T(8,128)(2,1)}, u32[]{:S(2)}, u32[]{:S(2)}) collective-permute-start(bf16[128,1536]{1,0:T(8,128)(2,1)} %copy-done.14), channel_id=1, source_target_pairs={{0,32},{32,0},{1,33},{33,1},{2,34},{34,2},{3,35},{35,3},{4,36},{36... | collective-permute-start | bytes 1179656 | tf_op jit(solution)/shard_map/ppermute | solution.py:554
  102.2 1.3 copy-start.8
  104.5 1.0 copy-start.13
  107.4 4.3 %copy-start.6 = (bf16[1,120,1536]{2,1,0:T(8,128)(2,1)S(1)}, bf16[1,120,1536]{2,1,0:T(8,128)(2,1)}, u32[]{:S(2)}) copy-start(bf16[1,120,1536]{2,1,0:T(8,128)(2,1)} %param.10) | copy-start | bytes 1105924
  107.4 4.3 %copy-start.15 = (bf16[128,1536]{1,0:T(8,128)(2,1)S(1)}, bf16[128,1536]{1,0:T(8,128)(2,1)}, u32[]{:S(2)}) copy-start(bf16[128,1536]{1,0:T(8,128)(2,1)} %copy-done.14) | copy-start | bytes 1179652
  107.4 4.4 %copy-start.21 = (bf16[1,6,1536]{2,1,0:T(8,128)(2,1)S(1)}, bf16[1,6,1536]{2,1,0:T(8,128)(2,1)}, u32[]{:S(2)}) copy-start(bf16[1,6,1536]{2,1,0:T(8,128)(2,1)} %param.11) | copy-start | bytes 55300
  114.1 3.6 %collective-permute-start.9 = (bf16[64,1536]{1,0:T(8,128)(2,1)S(1)}, bf16[64,1536]{1,0:T(8,128)(2,1)S(1)}, u32[]{:S(2)}, u32[]{:S(2)}) collective-permute-start(bf16[64,1536]{1,0:T(8,128)(2,1)S(1)} %get-tuple-element.61.a), channel_id=1, source_target_pairs={{0,32},{32,0},{1,33},{33,1},{2,34},{34,2},{3,35},{35,3},{4,36},{36... | collective-permute-start | bytes 589832 | tf_op jit(solution)/shard_map/ppermute | solution.py:554
  114.2 3.5 %collective-permute-start.10 = (bf16[56,1536]{1,0:T(8,128)(2,1)S(1)}, bf16[56,1536]{1,0:T(8,128)(2,1)S(1)}, u32[]{:S(2)}, u32[]{:S(2)}) collective-permute-start(bf16[56,1536]{1,0:T(8,128)(2,1)S(1)} %get-tuple-element.62.b), channel_id=1, source_target_pairs={{0,32},{32,0},{1,33},{33,1},{2,34},{34,2},{3,35},{35,3},{4,36},{36... | collective-permute-start | bytes 516104 | tf_op jit(solution)/shard_map/ppermute | solution.py:554
  114.7 11.8 %collective-permute-start.8 = (bf16[56,1536]{1,0:T(8,128)(2,1)S(1)}, bf16[56,1536]{1,0:T(8,128)(2,1)S(1)}, u32[]{:S(2)}, u32[]{:S(2)}) collective-permute-start(bf16[56,1536]{1,0:T(8,128)(2,1)S(1)} %get-tuple-element.62.b), channel_id=1, source_target_pairs={{0,64},{64,0},{1,65},{65,1},{2,66},{66,2},{3,67},{67,3},{4,68},{68... | collective-permute-start | bytes 516104 | tf_op jit(solution)/shard_map/ppermute | solution.py:554
  116.4 10.1 %collective-permute-start.7 = (bf16[64,1536]{1,0:T(8,128)(2,1)S(1)}, bf16[64,1536]{1,0:T(8,128)(2,1)S(1)}, u32[]{:S(2)}, u32[]{:S(2)}) collective-permute-start(bf16[64,1536]{1,0:T(8,128)(2,1)S(1)} %get-tuple-element.61.a), channel_id=1, source_target_pairs={{0,64},{64,0},{1,65},{65,1},{2,66},{66,2},{3,67},{67,3},{4,68},{68... | collective-permute-start | bytes 589832 | tf_op jit(solution)/shard_map/ppermute | solution.py:554
  117.6 2.3 %copy-start.1 = (bf16[1536,1536]{1,0:T(8,128)(2,1)S(1)}, bf16[1536,1536]{1,0:T(8,128)(2,1)}, u32[]{:S(2)}) copy-start(bf16[1536,1536]{1,0:T(8,128)(2,1)} %up_hbm.1) | copy-start | bytes 14155780
  120.0 2.3 %copy-start.2 = (bf16[1536,1536]{1,0:T(8,128)(2,1)S(1)}, bf16[1536,1536]{1,0:T(8,128)(2,1)}, u32[]{:S(2)}) copy-start(bf16[1536,1536]{1,0:T(8,128)(2,1)} %down_hbm.1) | copy-start | bytes 14155780
  126.5 2.1 %collective-permute-start.13 = (bf16[64,1536]{1,0:T(8,128)(2,1)S(1)}, bf16[64,1536]{1,0:T(8,128)(2,1)S(1)}, u32[]{:S(2)}, u32[]{:S(2)}) collective-permute-start(bf16[64,1536]{1,0:T(8,128)(2,1)S(1)} %collective-permute-done.7.a), channel_id=1, source_target_pairs={{0,32},{32,0},{1,33},{33,1},{2,34},{34,2},{3,35},{35,3},{4,36},{36... | collective-permute-start | bytes 589832 | tf_op jit(solution)/shard_map/ppermute | solution.py:554
  127.2 1.4 collective-permute-start.14
  131.4 1.5 %collective-permute-start.15 = (bf16[64,1536]{1,0:T(8,128)(2,1)S(1)}, bf16[64,1536]{1,0:T(8,128)(2,1)S(1)}, u32[]{:S(2)}, u32[]{:S(2)}) collective-permute-start(bf16[64,1536]{1,0:T(8,128)(2,1)S(1)} %get-tuple-element.76), channel_id=1, source_target_pairs={{0,32},{32,0},{1,33},{33,1},{2,34},{34,2},{3,35},{35,3},{4,36},{36... | collective-permute-start | bytes 589832 | tf_op jit(solution)/shard_map/ppermute | solution.py:554
  131.7 4.4 %collective-permute-start.12 = (bf16[56,1536]{1,0:T(8,128)(2,1)S(1)}, bf16[56,1536]{1,0:T(8,128)(2,1)S(1)}, u32[]{:S(2)}, u32[]{:S(2)}) collective-permute-start(bf16[56,1536]{1,0:T(8,128)(2,1)S(1)} %get-tuple-element.70), channel_id=1, source_target_pairs={{0,32},{32,0},{1,33},{33,1},{2,34},{34,2},{3,35},{35,3},{4,36},{36... | collective-permute-start | bytes 516104 | tf_op jit(solution)/shard_map/ppermute | solution.py:554
  132.0 4.2 %collective-permute-start.11 = (bf16[64,1536]{1,0:T(8,128)(2,1)S(1)}, bf16[64,1536]{1,0:T(8,128)(2,1)S(1)}, u32[]{:S(2)}, u32[]{:S(2)}) collective-permute-start(bf16[64,1536]{1,0:T(8,128)(2,1)S(1)} %get-tuple-element.69), channel_id=1, source_target_pairs={{0,32},{32,0},{1,33},{33,1},{2,34},{34,2},{3,35},{35,3},{4,36},{36... | collective-permute-start | bytes 589832 | tf_op jit(solution)/shard_map/ppermute | solution.py:554
  132.3 2.5 %collective-permute-start.17 = (bf16[56,1536]{1,0:T(8,128)(2,1)S(1)}, bf16[56,1536]{1,0:T(8,128)(2,1)S(1)}, u32[]{:S(2)}, u32[]{:S(2)}) collective-permute-start(bf16[56,1536]{1,0:T(8,128)(2,1)S(1)} %get-tuple-element.78), channel_id=1, source_target_pairs={{0,32},{32,0},{1,33},{33,1},{2,34},{34,2},{3,35},{35,3},{4,36},{36... | collective-permute-start | bytes 516104 | tf_op jit(solution)/shard_map/ppermute | solution.py:554
  133.0 11.5 %collective-permute-start.16 = (bf16[64,1536]{1,0:T(8,128)(2,1)S(1)}, bf16[64,1536]{1,0:T(8,128)(2,1)S(1)}, u32[]{:S(2)}, u32[]{:S(2)}) collective-permute-start(bf16[64,1536]{1,0:T(8,128)(2,1)S(1)} %add_convert_fusion), channel_id=1, source_target_pairs={{0,64},{64,0},{1,65},{65,1},{2,66},{66,2},{3,67},{67,3},{4,68},{68... | collective-permute-start | bytes 589832 | tf_op jit(solution)/shard_map/ppermute | solution.py:554
  134.8 9.7 %collective-permute-start.18 = (bf16[56,1536]{1,0:T(8,128)(2,1)S(1)}, bf16[56,1536]{1,0:T(8,128)(2,1)S(1)}, u32[]{:S(2)}, u32[]{:S(2)}) collective-permute-start(bf16[56,1536]{1,0:T(8,128)(2,1)S(1)} %add_convert_fusion.1), channel_id=1, source_target_pairs={{0,64},{64,0},{1,65},{65,1},{2,66},{66,2},{3,67},{67,3},{4,68},{68... | collective-permute-start | bytes 516104 | tf_op jit(solution)/shard_map/ppermute | solution.py:554
  (11 other events, 9.1 us)

commit v5 on v4

--- a/solution.py
+++ b/solution.py
@@ -163,7 +163,7 @@
             pltpu.SemaphoreType.DMA((4,)),
             pltpu.SemaphoreType.DMA((blocks, 3)),
         ],
-        compiler_params=pltpu.CompilerParams(vmem_limit_bytes=36 << 20),
+        compiler_params=pltpu.CompilerParams(vmem_limit_bytes=60 << 20),
         cost_estimate=pl.CostEstimate(
             flops=6 * rows * width * width,
             bytes_accessed=6 * width * width + (4 << 20),
@@ -338,12 +338,12 @@
     )(length, pack)
 
 
-def join_kernel(far_ref, own_ref, w0, w1, w2a, w2b, w3a, w3b, att_ref, w_ref, sems):
+def join_kernel(far_ref, own_ref, w0, w1, w2, att_ref, w_ref, sems):
     heads, rows, lanes = own_ref.shape
     depth = att_ref.shape[2]
     copies = []
     first = 0
-    for i, part in enumerate((w0, w1, w2a, w2b, w3a, w3b)):
+    for i, part in enumerate((w0, w1, w2)):
         last = first + part.shape[0]
         copies.append(pltpu.make_async_copy(part, w_ref.at[first:last], sems.at[i]))
         first = last
@@ -370,8 +370,7 @@
             own = own_ref[head]
             gap = jnp.broadcast_to(far_lse, (rows, lanes)) - own[:, 0:1]
             share = 1.0 / (1.0 + jnp.exp(-gap))
-            other = 1.0 / (1.0 + jnp.exp(gap))
-            both.append(share * far + other * own)
+            both.append(share * far + (1.0 - share) * own)
         joined = jnp.where(low, swap_halves(both[0]), both[1])
         at = (pair % per) * lanes
         att_ref[pair // per, :, at : at + lanes] = joined.astype(BF16)
@@ -384,16 +383,16 @@
     depth, width = w_parts[0].shape
     fetched = sum(part.shape[0] for part in w_parts)
     local = pl.BlockSpec(memory_space=pltpu.VMEM)
-    anywhere = pl.BlockSpec(memory_space=pl.ANY)
+    anywhere = pl.BlockSpec(memory_space=pltpu.HBM)
     return pl.pallas_call(
         join_kernel,
         out_shape=(
             jax.ShapeDtypeStruct((width // depth, rows, depth), BF16),
             pltpu.VMEM((fetched, width), BF16),
         ),
-        in_specs=[local, local] + [anywhere] * 6,
+        in_specs=[local, local] + [anywhere] * 3,
         out_specs=(local, local),
-        scratch_shapes=[pltpu.SemaphoreType.DMA((6,))],
+        scratch_shapes=[pltpu.SemaphoreType.DMA((3,))],
         compiler_params=pltpu.CompilerParams(vmem_limit_bytes=24 << 20),
         cost_estimate=pl.CostEstimate(
             flops=64 * heads * rows * 128, bytes_accessed=8 << 20, transcendentals=heads * rows * 256
@@ -402,51 +401,41 @@
     )(far, own, *w_parts)
 
 
-def mix_kernel(
-    place_ref, att_ref, w_ref, w2_ref, w3_ref, tokens_ref, mod_ref, mixed_ref, top_ref, end_ref
-):
+def mix_kernel(place_ref, att_ref, w_ref, last_ref, tokens_ref, mod_ref, mixed_ref, input_ref):
     place = place_ref[0]
     depth = att_ref.shape[2]
-    late = w2_ref.shape[0]
-    early = depth - late
-    far = att_ref[(place + 2) % 4]
-    far_near = att_ref[3 - place]
-    dot = lambda a, b: jnp.dot(a, b, preferred_element_type=F32)
-    projected = dot(att_ref[place], w_ref[:depth])
-    projected += dot(att_ref[place + 1 - 2 * (place % 2)], w_ref[depth : 2 * depth])
-    projected += dot(far[:, :early], w_ref[2 * depth : 2 * depth + early])
-    projected += dot(far_near[:, :early], w_ref[2 * depth + early :])
-    projected += dot(far[:, early:], w2_ref[...])
-    projected += dot(far_near[:, early:], w3_ref[...])
+    owners = (place, place + 1 - 2 * (place % 2), (place + 2) % 4)
+    projected = jnp.dot(att_ref[3 - place], last_ref[...], preferred_element_type=F32)
+    for i, owner in enumerate(owners):
+        part = w_ref[i * depth : (i + 1) * depth]
+        projected += jnp.dot(att_ref[owner], part, preferred_element_type=F32)
     mod = mod_ref[...].astype(F32)
     mixed = tokens_ref[...].astype(F32) + mod[2:3] * projected
     mixed_ref[...] = mixed
-    normed = layer_norm(mixed) * (1.0 + mod[4:5]) + mod[3:4]
-    top_ref[...] = normed[: top_ref.shape[0]].astype(BF16)
-    end_ref[...] = normed[top_ref.shape[0] :].astype(BF16)
-
-
-def mix(place, attended, w_main, w2_late, w3_late, tokens, modulate):
-    rows, width = tokens.shape
+    input_ref[...] = (layer_norm(mixed) * (1.0 + mod[4:5]) + mod[3:4]).astype(BF16)
+
+
+def mix(place, attended, w_main, w_last, tokens, modulate):
     local = pl.BlockSpec(memory_space=pltpu.VMEM)
     return pl.pallas_call(
         mix_kernel,
         out_shape=(
-            jax.ShapeDtypeStruct((rows, width), F32),
-            jax.ShapeDtypeStruct((HEAD, width), BF16),
-            jax.ShapeDtypeStruct((rows - HEAD, width), BF16),
-        ),
-        in_specs=[pl.BlockSpec(memory_space=pltpu.SMEM)] + [local] * 6,
-        out_specs=(local,) * 3,
+            jax.ShapeDtypeStruct(tokens.shape, F32),
+            jax.ShapeDtypeStruct(tokens.shape, BF16),
+        ),
+        in_specs=[pl.BlockSpec(memory_space=pltpu.SMEM)] + [local] * 5,
+        out_specs=(local, local),
         compiler_params=pltpu.CompilerParams(vmem_limit_bytes=24 << 20),
         name="mix",
-    )(place, attended, w_main, w2_late, w3_late, tokens, modulate)
-
-
-def feed_blocks(pieces, outs, up_ref, down_ref, ready):
+    )(place, attended, w_main, w_last, tokens, modulate)
+
+
+def feed_blocks(first_ref, second_ref, keep_ref, pass_ref, up_ref, down_ref, ready):
+    rows = first_ref.shape[0]
     hidden_width = up_ref.shape[1]
     wide = 512
-    both = jnp.concatenate([piece[...].astype(F32) for piece in pieces], axis=0).astype(BF16)
+    both = [first_ref[...].astype(F32), second_ref[...].astype(F32)]
+    both = jnp.concatenate(both, axis=0).astype(BF16)
     total = None
     for c in range(hidden_width // wide):
         part = slice(c * wide, (c + 1) * wide)
@@ -456,98 +445,70 @@
         ready(2 * c + 1)
         product = jnp.dot(hidden, down_ref[part, :], preferred_element_type=F32)
         total = product if total is None else total + product
-    first = 0
-    for out in outs:
-        last = first + out.shape[0]
-        out[...] = total[first:last].astype(out.dtype)
-        first = last
-
-
-def feed_near_kernel(a, b, c, d, up_hbm, down_hbm, keep_a, keep_b, pass_a, pass_b, up, down, sems):
+    keep_ref[...] = total[:rows]
+    pass_ref[...] = total[rows:].astype(BF16)
+
+
+def feed_near_kernel(first, second, up_hbm, down_hbm, keep, passed, up, down, sems):
     wide = 512
     copies = []
-    for i in range(up.shape[1] // wide):
-        part = slice(i * wide, (i + 1) * wide)
+    for c in range(up.shape[1] // wide):
+        part = slice(c * wide, (c + 1) * wide)
         copies.append(
-            pltpu.make_async_copy(up_hbm.at[:, part], up.at[:, part], sems.at[2 * i])
+            pltpu.make_async_copy(up_hbm.at[:, part], up.at[:, part], sems.at[2 * c])
         )
         copies.append(
-            pltpu.make_async_copy(down_hbm.at[part], down.at[part], sems.at[2 * i + 1])
+            pltpu.make_async_copy(down_hbm.at[part], down.at[part], sems.at[2 * c + 1])
         )
     for copy in copies:
         copy.start()
-    outs = (keep_a, keep_b, pass_a, pass_b)
-    feed_blocks((a, b, c, d), outs, up, down, lambda i: copies[i].wait())
-
-
-def feed_far_kernel(a, b, c, d, up, down, keep_a, keep_b, pass_a, pass_b):
-    feed_blocks((a, b, c, d), (keep_a, keep_b, pass_a, pass_b), up, down, lambda i: None)
-
-
-def feed_outs(pieces):
-    kinds = (F32, F32, BF16, BF16)
-    return tuple(jax.ShapeDtypeStruct(p.shape, k) for p, k in zip(pieces, kinds))
-
-
-def feed_near(pieces, w_up, w_down):
-    rows = sum(piece.shape[0] for piece in pieces)
+    feed_blocks(first, second, keep, passed, up, down, lambda i: copies[i].wait())
+
+
+def feed_far_kernel(first, second, up, down, keep, passed):
+    feed_blocks(first, second, keep, passed, up, down, lambda i: None)
+
+
+def feed_near(first, second, w_up, w_down):
+    rows, width = first.shape
     local = pl.BlockSpec(memory_space=pltpu.VMEM)
     anywhere = pl.BlockSpec(memory_space=pltpu.HBM)
     return pl.pallas_call(
         feed_near_kernel,
-        out_shape=feed_outs(pieces) + (pltpu.VMEM(w_up.shape, BF16), pltpu.VMEM(w_down.shape, BF16)),
-        in_specs=[local] * 4 + [anywhere] * 2,
-        out_specs=(local,) * 6,
+        out_shape=(
+            jax.ShapeDtypeStruct((rows, width), F32),
+            jax.ShapeDtypeStruct((rows, width), BF16),
+            pltpu.VMEM(w_up.shape, BF16),
+            pltpu.VMEM(w_down.shape, BF16),
+        ),
+        in_specs=[local, local, anywhere, anywhere],
+        out_specs=(local,) * 4,
         scratch_shapes=[pltpu.SemaphoreType.DMA((2 * (w_up.shape[1] // 512),))],
         compiler_params=pltpu.CompilerParams(vmem_limit_bytes=32 << 20),
         cost_estimate=pl.CostEstimate(
-            flops=4 * rows * w_up.size, bytes_accessed=4 * w_up.size, transcendentals=0
+            flops=8 * rows * w_up.size, bytes_accessed=4 * w_up.size, transcendentals=0
         ),
         name="feed_near",
-    )(*pieces, w_up, w_down)
-
-
-def feed_far(pieces, w_up, w_down):
-    rows = sum(piece.shape[0] for piece in pieces)
+    )(first, second, w_up, w_down)
+
+
+def feed_far(first, second, w_up, w_down):
+    rows, width = first.shape
     local = pl.BlockSpec(memory_space=pltpu.VMEM)
     return pl.pallas_call(
         feed_far_kernel,
-        out_shape=feed_outs(pieces),
-        in_specs=[local] * 6,
-        out_specs=(local,) * 4,
+        out_shape=(
+            jax.ShapeDtypeStruct((rows, width), F32),
+            jax.ShapeDtypeStruct((rows, width), BF16),
+        ),
+        in_specs=[local] * 4,
+        out_specs=(local,) * 2,
         compiler_params=pltpu.CompilerParams(vmem_limit_bytes=24 << 20),
         cost_estimate=pl.CostEstimate(
-            flops=4 * rows * w_up.size, bytes_accessed=1 << 20, transcendentals=0
+            flops=8 * rows * w_up.size, bytes_accessed=1 << 20, transcendentals=0
         ),
         name="feed_far",
-    )(*pieces, w_up, w_down)
-
-
-def final_kernel(
-    live_ref, mixed_ref, mod_ref, near_a, near_b, core_a, core_b, far_a, far_b, out_ref
-):
-    gate = mod_ref[...].astype(F32)[5:6]
-    cut = near_a.shape[0]
-    for rows, near, core, far in (
-        (slice(0, cut), near_a, core_a, far_a),
-        (slice(cut, mixed_ref.shape[0]), near_b, core_b, far_b),
-    ):
-        total = near[...] + core[...].astype(F32) + far[...].astype(F32)
-        result = mixed_ref[rows] + gate * total
-        position = row_iota(result.shape) + rows.start
-        out_ref[rows] = jnp.where(position < live_ref[0], result, 0.0).astype(BF16)
-
-
-def final(live, mixed, modulate, *pieces):
-    local = pl.BlockSpec(memory_space=pltpu.VMEM)
-    return pl.pallas_call(
-        final_kernel,
-        out_shape=jax.ShapeDtypeStruct(mixed.shape, BF16),
-        in_specs=[pl.BlockSpec(memory_space=pltpu.SMEM)] + [local] * 8,
-        out_specs=local,
-        compiler_params=pltpu.CompilerParams(vmem_limit_bytes=16 << 20),
-        name="final",
-    )(live, mixed, modulate, *pieces)
+    )(first, second, w_up, w_down)
 
 
 def swap(values, axis):
@@ -565,38 +526,35 @@
     send, own = project(
         tile_index.reshape(1), refresh, tokens, modulation[0], w_qkv, kv_cache[0]
     )
+    pack = lax.all_to_all(send, TILE, split_axis=0, concat_axis=0, tiled=True)
     live = (length - tile_index * rows).reshape(1)
     own_part = own_attend(live, own, text_kv[0])
-    send, own_part = lax.optimization_barrier((send, own_part))
-    pack = lax.all_to_all(send, TILE, split_axis=0, concat_axis=0, tiled=True)
-    pack, w_here = lax.optimization_barrier((pack, w_out))
-    third = w_out.shape[0] // 3
-    w2 = [swap(w_here[i * third : (i + 1) * third], "zh") for i in range(3)]
+    own_part, w_here = lax.optimization_barrier((own_part, w_out))
+    w2 = swap(w_here, "zh")
+    pack, own_part = lax.optimization_barrier((pack, own_part))
+    far = head_attend(lengths, pack)
+    far, w2, w_here = lax.optimization_barrier((far, w2, w_here))
     w1 = swap(w_here, "co")
-    far = head_attend(lengths, pack)
-    far, w1, w2a, w2b = lax.optimization_barrier((far, w1, w2[0], w2[1]))
-    w3a, w3b = swap(w2a, "co"), swap(w2b, "co")
+    w3 = swap(w2, "co")
     far = lax.all_to_all(far, TILE, split_axis=0, concat_axis=0, tiled=True)
-    far, w3a, w3b, w2c = lax.optimization_barrier((far, w3a, w3b, w2[2]))
-    w3c = swap(w2c, "co")
-    attended, w_main = join(far, own_part, (w_out, w1, w2a, w2b, w3a, w3b))
-    attended, w3c = lax.optimization_barrier((attended, w3c))
-    mixed, *mlp_input = mix(place, attended, w_main, w2c, w3c, tokens, modulation[0])
-
-    far_z = [swap(piece, "zh") for piece in mlp_input]
-    near = [swap(piece, "co") for piece in mlp_input]
-    *near_parts, up, down = feed_near((*mlp_input, *near), w_up, w_down)
-    far_z, near_parts = lax.optimization_barrier((far_z, near_parts))
-    far_both = [swap(piece, "co") for piece in far_z]
-    far_parts = feed_far((*far_z, *far_both), up, down)
-    far_core = [swap(piece, "co") for piece in far_parts[2:]]
-    far_sums = [
-        (keep + core.astype(F32)).astype(BF16) for keep, core in zip(far_parts[:2], far_core)
-    ]
-    far_back = [swap(piece, "zh") for piece in far_sums]
-    near_core = [swap(piece, "co") for piece in near_parts[2:]]
-    out = final(live, mixed, modulation[0], *near_parts[:2], *near_core, *far_back)
-    return out[None]
+    far, w1, w3 = lax.optimization_barrier((far, w1, w3))
+    attended, w_main = join(far, own_part, (w_out, w1, w2))
+    mixed, mlp_input = mix(place, attended, w_main, w3, tokens, modulation[0])
+
+    far_z = swap(mlp_input, "zh")
+    near = swap(mlp_input, "co")
+    near_keep, near_pass, up, down = feed_near(mlp_input, near, w_up, w_down)
+    far_z, near_keep, near_pass = lax.optimization_barrier((far_z, near_keep, near_pass))
+    far_both = swap(far_z, "co")
+    far_keep, far_pass = feed_far(far_z, far_both, up, down)
+    sum_far = (far_keep + swap(far_pass, "co").astype(F32)).astype(BF16)
+    near_sum = near_keep + swap(near_pass, "co").astype(F32)
+    mlp_out = near_sum + swap(sum_far, "zh").astype(F32)
+    positions = tile_index * rows + jnp.arange(rows, dtype=jnp.int32)
+    live_rows = positions < length
+    gate = modulation[0, 5].astype(F32)
+    finished = jnp.where(live_rows[:, None], mixed + gate * mlp_out, 0.0)
+    return finished.astype(BF16)[None]
 
 
 def solution(mesh):

time: 146 us -> 124 us (0.85)
  blocking collectives: 29.8 us -> 0 us
  waiting for transfers between devices: 23.6 us -> 43 us
  local copies, waits for them, and re-layouts: 24.1 us -> 5.94 us
  Pallas kernels: 43.1 us -> 47.8 us
    all_to_all x1 -> x0, blocking collectives: 29.8 us -> none  [per_device(): pack = lax.all_to_all(send, TILE, split_axis=0, concat_axis=0, tiled=True)]
    unnamed x46 -> x12, local copies, waits for them, and re-layouts: 23.2 us -> 5.94 us
    all_to_all x0 -> x1, waiting for transfers between devices: none -> 11.8 us  [per_device(): pack = lax.all_to_all(send, TILE, split_axis=0, concat_axis=0, tiled=True)]
    ppermute x19 -> x9, starting transfers between devices: 20 us -> 9.64 us  [swap(): return lax.ppermute(values, axis, [(0, 1), (1, 0)])]
    all_to_all x1, waiting for transfers between devices: 0.01 us -> 9.99 us  [per_device(): far = lax.all_to_all(far, TILE, split_axis=0, concat_axis=0, tiled=True)]
    all_to_all x0 -> x1, starting transfers between devices: none -> 9.3 us  [per_device(): pack = lax.all_to_all(send, TILE, split_axis=0, concat_axis=0, tiled=True)]
    pallas_call x1, Pallas kernels: 6.46 us -> 11.6 us  [project(): pl.pallas_call(project_kernel, out_shape=(jax.ShapeDtypeStruct((dests, pa...]
    ppermute x19 -> x9, waiting for transfers between devices: 23.6 us -> 21.3 us  [swap(): return lax.ppermute(values, axis, [(0, 1), (1, 0)])]
  transfers between devices with their start and end apart: 20 -> 11, of which waited for: 4 -> 8; matrix products, arithmetic and copies ran while one was open for 1% -> 0% of each run, Pallas kernels for 19% -> 22%
where the time goes in v5:
time: 124 us
  Pallas kernels  47.8 us (39%)
  waiting for transfers between devices  43 us (35%)
  starting transfers between devices  25.1 us (20%)
  local copies, waits for them, and re-layouts  5.94 us (5%)
    ppermute x9, waiting for transfers between devices, swap(): return lax.ppermute(values, axis, [(0, 1), (1, 0)])  21.3 us
    pallas_call x1, Pallas kernels, head_attend(): pl.pallas_call(head_kernel, grid=(tiles // group,), out_shape=pltpu.HBM((...  20.7 us
    all_to_all x1, waiting for transfers between devices, per_device(): pack = lax.all_to_all(send, TILE, split_axis=0, concat_axis=0, tiled=True)  11.8 us
    pallas_call x1, Pallas kernels, project(): pl.pallas_call(project_kernel, out_shape=(jax.ShapeDtypeStruct((dests, pa...  11.6 us
    all_to_all x1, waiting for transfers between devices, per_device(): far = lax.all_to_all(far, TILE, split_axis=0, concat_axis=0, tiled=True)  9.99 us
    ppermute x9, starting transfers between devices, swap(): return lax.ppermute(values, axis, [(0, 1), (1, 0)])  9.64 us
    all_to_all x1, starting transfers between devices, per_device(): pack = lax.all_to_all(send, TILE, split_axis=0, concat_axis=0, tiled=True)  9.3 us
    all_to_all x1, starting transfers between devices, per_device(): far = lax.all_to_all(far, TILE, split_axis=0, concat_axis=0, tiled=True)  6.16 us
  transfers between devices with their start and end apart: 11, of which 8 were waited for; matrix products, arithmetic and copies ran while one was open for 0% of the time, Pallas kernels for 22%

profile of v5, /device:TPU:1, one launch (start us, length us, event | category | flops | bytes accessed | tf_op | source)
XLA Modules:
  0.0 123.8 jit_solution(9556538125493095593)
XLA Ops:
  0.0 11.6 %project.1 = (bf16[32,184,128]{2,1,0:T(8,128)(2,1)}, bf16[24,184,128]{2,1,0:T(8,128)(2,1)}) custom-call(s32[1]{0:T(128)} %bitcast.2.tile_ref, s32[1,4]{1,0:T(1,128)} %refresh_ref.1, bf16[120,1536]{1,0:T(8,128)(2,1)} %bitcast.14, bf16[6,1536]{1,0:T(8,128)(2,1)} %bitcast.16, bf16[1536,4608]{1,0:T(8,128)(2,1)} %w_ref.1, bf16[120,3072]{1,0:T(8,128)(2,1)} %bitcast.18), custom_call_target="tpu_custom_call" | custom-call | flops 1698693120 | bytes 18350080 | tf_op jit(solution)/shard_map/project/pallas_call | solution.py:149
  11.6 9.3 %all-to-all-start = ((bf16[32,184,128]{2,1,0:T(8,128)(2,1)}), bf16[32,184,128]{2,1,0:T(8,128)(2,1)}, u32[]{:S(2)}, u32[]{:S(2)}) async-start(bf16[32,184,128]{2,1,0:T(8,128)(2,1)} %get-tuple-element.30), calls=%async_computation | async-start | bytes 3014656 | tf_op jit(solution)/shard_map/all_to_all | solution.py:529
  21.6 1.2 %copy-done.4 = bf16[24,184,128]{2,1,0:T(8,128)(2,1)S(1)} copy-done((bf16[24,184,128]{2,1,0:T(8,128)(2,1)S(1)}, bf16[24,184,128]{2,1,0:T(8,128)(2,1)}, u32[]{:S(2)}) %copy-start.4) | copy-done | bytes 1130520
  22.8 3.0 %own_attend.1.own_ref = f32[24,120,128]{2,1,0:T(8,128)S(1)} custom-call(s32[1]{0:T(128)} %bitcast.6.live_ref, bf16[24,184,128]{2,1,0:T(8,128)(2,1)S(1)} %copy-done.4, bf16[154,3072]{1,0:T(8,128)(2,1)S(1)} %bitcast.12, bf16[154,3072]{1,0:T(8,128)(2,1)S(1)} %bitcast.13), custom_call_target="tpu_custom_call" | custom-call | flops 404029440 | bytes 6291456 | tf_op jit(solution)/shard_map/own_attend/pallas_call | solution.py:219
  25.8 3.6 %collective-permute-start = (bf16[384,1536]{1,0:T(8,128)(2,1)}, bf16[384,1536]{1,0:T(8,128)(2,1)S(1)}, u32[]{:S(2)}, u32[]{:S(2)}) collective-permute-start(bf16[384,1536]{1,0:T(8,128)(2,1)} %w0.1), channel_id=1, source_target_pairs={{0,64},{64,0},{1,65},{65,1},{2,66},{66,2},{3,67},{67,3},{4,68},{68... | collective-permute-start | bytes 3538952 | tf_op jit(solution)/shard_map/ppermute | solution.py:515
  29.4 11.8 %all-to-all-done.pack_ref = bf16[32,184,128]{2,1,0:T(8,128)(2,1)} async-done(((bf16[32,184,128]{2,1,0:T(8,128)(2,1)}), bf16[32,184,128]{2,1,0:T(8,128)(2,1)}, u32[]{:S(2)}, u32[]{:S(2)}) %all-to-all-start) | async-done | bytes 1507360 | tf_op jit(solution)/shard_map/all_to_all | solution.py:529
  41.2 20.7 %head_attend.1 = bf16[32,64,128]{2,1,0:T(8,128)(2,1)} custom-call(s32[1]{0:T(128)} %copy.11.len_ref, bf16[32,184,128]{2,1,0:T(8,128)(2,1)} %all-to-all-done.pack_ref), custom_call_target="tpu_custom_call" | custom-call | flops 7549747200 | bytes 4194304 | tf_op jit(solution)/shard_map/head_attend/pallas_call | solution.py:317
  61.8 6.1 %collective-permute-done.w2 = bf16[384,1536]{1,0:T(8,128)(2,1)S(1)} collective-permute-done((bf16[384,1536]{1,0:T(8,128)(2,1)}, bf16[384,1536]{1,0:T(8,128)(2,1)S(1)}, u32[]{:S(2)}, u32[]{:S(2)}) %collective-permute-start) | collective-permute-done | bytes 1179680 | tf_op jit(solution)/shard_map/ppermute | solution.py:515
  67.9 0.5 collective-permute-start.1
  68.4 0.0 collective-permute-start.2
  68.4 6.2 %all-to-all-start.1 = ((bf16[32,64,128]{2,1,0:T(8,128)(2,1)}), bf16[32,64,128]{2,1,0:T(8,128)(2,1)S(1)}, u32[]{:S(2)}, u32[]{:S(2)}) async-start(bf16[32,64,128]{2,1,0:T(8,128)(2,1)} %head_attend.1), calls=%async_computation.1 | async-start | bytes 1048576 | tf_op jit(solution)/shard_map/all_to_all | solution.py:539
  74.6 0.0 copy-start.3
  74.6 10.0 %all-to-all-done.1.far_ref = bf16[32,64,128]{2,1,0:T(8,128)(2,1)S(1)} async-done(((bf16[32,64,128]{2,1,0:T(8,128)(2,1)}), bf16[32,64,128]{2,1,0:T(8,128)(2,1)S(1)}, u32[]{:S(2)}, u32[]{:S(2)}) %all-to-all-start.1) | async-done | bytes 524320 | tf_op jit(solution)/shard_map/all_to_all | solution.py:539
  84.6 3.2 %join.1 = (bf16[4,120,384]{2,1,0:T(8,128)(2,1)S(1)}, bf16[1152,1536]{1,0:T(8,128)(2,1)S(1)}) custom-call(bf16[32,64,128]{2,1,0:T(8,128)(2,1)S(1)} %all-to-all-done.1.far_ref, f32[24,120,128]{2,1,0:T(8,128)S(1)} %own_attend.1.own_ref, bf16[384,1536]{1,0:T(8,128)(2,1)} %w0.1, bf16[384,1536]{1,0:T(8,128)(2,1)} %collective-permute-done.1.w1, ...), custom_call_target="tpu_custom_call" | custom-call | flops 23592960 | bytes 8388608 | tf_op jit(solution)/shard_map/join/pallas_call | solution.py:387
  87.8 2.5 %mix.1 = (f32[120,1536]{1,0:T(8,128)S(1)}, bf16[120,1536]{1,0:T(8,128)(2,1)S(1)}) custom-call(s32[1]{0:T(128)} %bitcast.1.place_ref, bf16[4,120,384]{2,1,0:T(8,128)(2,1)S(1)} %get-tuple-element.41.att_ref, bf16[1152,1536]{1,0:T(8,128)(2,1)S(1)} %get-tuple-element.42.w_ref, bf16[384,1536]{1,0:T(8,128)(2,1)} %collective-permute-done.2.last_ref, ...), custom_call_target="tpu_custom_call" | custom-call | tf_op jit(solution)/shard_map/mix/pallas_call | solution.py:420
  90.3 2.6 %collective-permute-start.4 = (bf16[120,1536]{1,0:T(8,128)(2,1)S(1)}, bf16[120,1536]{1,0:T(8,128)(2,1)S(1)}, u32[]{:S(2)}, u32[]{:S(2)}) collective-permute-start(bf16[120,1536]{1,0:T(8,128)(2,1)S(1)} %get-tuple-element.45.first), channel_id=1, source_target_pairs={{0,32},{32,0},{1,33},{33,1},{2,34},{34,2},{3,35},{35,3},{4,36},{36... | collective-permute-start | bytes 1105928 | tf_op jit(solution)/shard_map/ppermute | solution.py:515
  93.0 0.7 collective-permute-start.3
  93.7 0.6 collective-permute-done.4.second
  94.3 2.3 %copy-done = bf16[1536,1536]{1,0:T(8,128)(2,1)S(1)} copy-done((bf16[1536,1536]{1,0:T(8,128)(2,1)S(1)}, bf16[1536,1536]{1,0:T(8,128)(2,1)}, u32[]{:S(2)}) %copy-start) | copy-done | bytes 4718616
  96.6 2.3 %copy-done.1 = bf16[1536,1536]{1,0:T(8,128)(2,1)S(1)} copy-done((bf16[1536,1536]{1,0:T(8,128)(2,1)S(1)}, bf16[1536,1536]{1,0:T(8,128)(2,1)}, u32[]{:S(2)}) %copy-start.1) | copy-done | bytes 4718616
  99.0 4.1 %feed_near.1 = (f32[120,1536]{1,0:T(8,128)S(1)}, bf16[120,1536]{1,0:T(8,128)(2,1)S(1)}, bf16[1536,1536]{1,0:T(8,128)(2,1)S(1)}, bf16[1536,1536]{1,0:T(8,128)(2,1)S(1)}) custom-call(bf16[120,1536]{1,0:T(8,128)(2,1)S(1)} %get-tuple-element.45.first, bf16[120,1536]{1,0:T(8,128)(2,1)S(1)} %collective-permute-done.4.second, bf16[1536,1536]{1,0:T(8,128)(2,1)S(1)} %copy-done, ...), custom_call_target="tpu_custom_call" | custom-call | flops 2264924160 | bytes 9437184 | tf_op jit(solution)/shard_map/feed_near/pallas_call | solution.py:476
  103.1 1.5 %collective-permute-done.3.first = bf16[120,1536]{1,0:T(8,128)(2,1)S(1)} collective-permute-done((bf16[120,1536]{1,0:T(8,128)(2,1)S(1)}, bf16[120,1536]{1,0:T(8,128)(2,1)S(1)}, u32[]{:S(2)}, u32[]{:S(2)}) %collective-permute-start.3) | collective-permute-done | bytes 368672 | tf_op jit(solution)/shard_map/ppermute | solution.py:515
  104.6 0.9 collective-permute-start.6
  105.5 1.3 %collective-permute-done.6.second = bf16[120,1536]{1,0:T(8,128)(2,1)S(1)} collective-permute-done((bf16[120,1536]{1,0:T(8,128)(2,1)S(1)}, bf16[120,1536]{1,0:T(8,128)(2,1)S(1)}, u32[]{:S(2)}, u32[]{:S(2)}) %collective-permute-start.6) | collective-permute-done | bytes 368672 | tf_op jit(solution)/shard_map/ppermute | solution.py:515
  106.8 2.8 %feed_far.1 = (f32[120,1536]{1,0:T(8,128)S(1)}, bf16[120,1536]{1,0:T(8,128)(2,1)S(1)}) custom-call(bf16[120,1536]{1,0:T(8,128)(2,1)S(1)} %collective-permute-done.3.first, bf16[120,1536]{1,0:T(8,128)(2,1)S(1)} %collective-permute-done.6.second, bf16[1536,1536]{1,0:T(8,128)(2,1)S(1)} %get-tuple-element.51.up, bf16[1536,1536]{1,0:T(8,128)(2,1)S(1)} %get-tuple-element.52.down), custom_call_target="tpu_custom_call" | custom-call | flops 2264924160 | bytes 1048576 | tf_op jit(solution)/shard_map/feed_far/pallas_call | solution.py:498
  109.6 0.5 collective-permute-start.7
  110.0 0.1 collective-permute-start.5
  110.2 1.2 collective-permute-done.7
  111.4 0.1 add_convert_fusion
  111.4 0.8 collective-permute-start.8
  112.3 10.6 %collective-permute-done.8 = bf16[120,1536]{1,0:T(8,128)(2,1)S(1)} collective-permute-done((bf16[120,1536]{1,0:T(8,128)(2,1)S(1)}, bf16[120,1536]{1,0:T(8,128)(2,1)S(1)}, u32[]{:S(2)}, u32[]{:S(2)}) %collective-permute-start.8) | collective-permute-done | bytes 368672 | tf_op jit(solution)/shard_map/ppermute | solution.py:515
  122.8 1.0 fusion
  (13 shorter events, 0.1 us)
Async XLA Ops:
  11.6 10.0 %copy-start.2 = (bf16[1,154,3072]{2,1,0:T(8,128)(2,1)S(1)}, bf16[1,154,3072]{2,1,0:T(8,128)(2,1)}, u32[]{:S(2)}) copy-start(bf16[1,154,3072]{2,1,0:T(8,128)(2,1)} %param.13) | copy-start | bytes 2838532
  11.6 29.6 %all-to-all-start = ((bf16[32,184,128]{2,1,0:T(8,128)(2,1)}), bf16[32,184,128]{2,1,0:T(8,128)(2,1)}, u32[]{:S(2)}, u32[]{:S(2)}) async-start(bf16[32,184,128]{2,1,0:T(8,128)(2,1)} %get-tuple-element.30), calls=%async_computation | async-start | bytes 3014656 | tf_op jit(solution)/shard_map/all_to_all | solution.py:529
  21.6 1.3 %copy-start.4 = (bf16[24,184,128]{2,1,0:T(8,128)(2,1)S(1)}, bf16[24,184,128]{2,1,0:T(8,128)(2,1)}, u32[]{:S(2)}) copy-start(bf16[24,184,128]{2,1,0:T(8,128)(2,1)} %get-tuple-element.31.own_ref) | copy-start | bytes 3391492
  25.8 42.1 %collective-permute-start = (bf16[384,1536]{1,0:T(8,128)(2,1)}, bf16[384,1536]{1,0:T(8,128)(2,1)S(1)}, u32[]{:S(2)}, u32[]{:S(2)}) collective-permute-start(bf16[384,1536]{1,0:T(8,128)(2,1)} %w0.1), channel_id=1, source_target_pairs={{0,64},{64,0},{1,65},{65,1},{2,66},{66,2},{3,67},{67,3},{4,68},{68... | collective-permute-start | bytes 3538952 | tf_op jit(solution)/shard_map/ppermute | solution.py:515
  67.9 16.7 %collective-permute-start.1 = (bf16[384,1536]{1,0:T(8,128)(2,1)}, bf16[384,1536]{1,0:T(8,128)(2,1)}, u32[]{:S(2)}, u32[]{:S(2)}) collective-permute-start(bf16[384,1536]{1,0:T(8,128)(2,1)} %w0.1), channel_id=1, source_target_pairs={{0,32},{32,0},{1,33},{33,1},{2,34},{34,2},{3,35},{35,3},{4,36},{36... | collective-permute-start | bytes 3538952 | tf_op jit(solution)/shard_map/ppermute | solution.py:515
  68.4 16.2 %collective-permute-start.2 = (bf16[384,1536]{1,0:T(8,128)(2,1)S(1)}, bf16[384,1536]{1,0:T(8,128)(2,1)}, u32[]{:S(2)}, u32[]{:S(2)}) collective-permute-start(bf16[384,1536]{1,0:T(8,128)(2,1)S(1)} %collective-permute-done.w2), channel_id=1, source_target_pairs={{0,32},{32,0},{1,33},{33,1},{2,34},{34,2},{3,35},{35,3},{4,36},{36... | collective-permute-start | bytes 3538952 | tf_op jit(solution)/shard_map/ppermute | solution.py:515
  68.4 16.2 %all-to-all-start.1 = ((bf16[32,64,128]{2,1,0:T(8,128)(2,1)}), bf16[32,64,128]{2,1,0:T(8,128)(2,1)S(1)}, u32[]{:S(2)}, u32[]{:S(2)}) async-start(bf16[32,64,128]{2,1,0:T(8,128)(2,1)} %head_attend.1), calls=%async_computation.1 | async-start | bytes 1048576 | tf_op jit(solution)/shard_map/all_to_all | solution.py:539
  74.6 13.2 %copy-start.3 = (bf16[1,120,1536]{2,1,0:T(8,128)(2,1)S(1)}, bf16[1,120,1536]{2,1,0:T(8,128)(2,1)}, u32[]{:S(2)}) copy-start(bf16[1,120,1536]{2,1,0:T(8,128)(2,1)} %param.10) | copy-start | bytes 1105924
  84.6 3.2 %copy-start.5 = (bf16[1,6,1536]{2,1,0:T(8,128)(2,1)S(1)}, bf16[1,6,1536]{2,1,0:T(8,128)(2,1)}, u32[]{:S(2)}) copy-start(bf16[1,6,1536]{2,1,0:T(8,128)(2,1)} %param.11) | copy-start | bytes 55300
  90.3 3.9 %collective-permute-start.4 = (bf16[120,1536]{1,0:T(8,128)(2,1)S(1)}, bf16[120,1536]{1,0:T(8,128)(2,1)S(1)}, u32[]{:S(2)}, u32[]{:S(2)}) collective-permute-start(bf16[120,1536]{1,0:T(8,128)(2,1)S(1)} %get-tuple-element.45.first), channel_id=1, source_target_pairs={{0,32},{32,0},{1,33},{33,1},{2,34},{34,2},{3,35},{35,3},{4,36},{36... | collective-permute-start | bytes 1105928 | tf_op jit(solution)/shard_map/ppermute | solution.py:515
  93.0 11.6 %collective-permute-start.3 = (bf16[120,1536]{1,0:T(8,128)(2,1)S(1)}, bf16[120,1536]{1,0:T(8,128)(2,1)S(1)}, u32[]{:S(2)}, u32[]{:S(2)}) collective-permute-start(bf16[120,1536]{1,0:T(8,128)(2,1)S(1)} %get-tuple-element.45.first), channel_id=1, source_target_pairs={{0,64},{64,0},{1,65},{65,1},{2,66},{66,2},{3,67},{67,3},{4,68},{68... | collective-permute-start | bytes 1105928 | tf_op jit(solution)/shard_map/ppermute | solution.py:515
  94.3 2.3 %copy-start = (bf16[1536,1536]{1,0:T(8,128)(2,1)S(1)}, bf16[1536,1536]{1,0:T(8,128)(2,1)}, u32[]{:S(2)}) copy-start(bf16[1536,1536]{1,0:T(8,128)(2,1)} %up_hbm.1) | copy-start | bytes 14155780
  96.6 2.3 %copy-start.1 = (bf16[1536,1536]{1,0:T(8,128)(2,1)S(1)}, bf16[1536,1536]{1,0:T(8,128)(2,1)}, u32[]{:S(2)}) copy-start(bf16[1536,1536]{1,0:T(8,128)(2,1)} %down_hbm.1) | copy-start | bytes 14155780
  104.6 2.2 %collective-permute-start.6 = (bf16[120,1536]{1,0:T(8,128)(2,1)S(1)}, bf16[120,1536]{1,0:T(8,128)(2,1)S(1)}, u32[]{:S(2)}, u32[]{:S(2)}) collective-permute-start(bf16[120,1536]{1,0:T(8,128)(2,1)S(1)} %collective-permute-done.3.first), channel_id=1, source_target_pairs={{0,32},{32,0},{1,33},{33,1},{2,34},{34,2},{3,35},{35,3},{4,36},{36... | collective-permute-start | bytes 1105928 | tf_op jit(solution)/shard_map/ppermute | solution.py:515
  109.6 1.8 %collective-permute-start.7 = (bf16[120,1536]{1,0:T(8,128)(2,1)S(1)}, bf16[120,1536]{1,0:T(8,128)(2,1)S(1)}, u32[]{:S(2)}, u32[]{:S(2)}) collective-permute-start(bf16[120,1536]{1,0:T(8,128)(2,1)S(1)} %get-tuple-element.54), channel_id=1, source_target_pairs={{0,32},{32,0},{1,33},{33,1},{2,34},{34,2},{3,35},{35,3},{4,36},{36... | collective-permute-start | bytes 1105928 | tf_op jit(solution)/shard_map/ppermute | solution.py:515
  110.0 2.2 %collective-permute-start.5 = (bf16[120,1536]{1,0:T(8,128)(2,1)S(1)}, bf16[120,1536]{1,0:T(8,128)(2,1)S(1)}, u32[]{:S(2)}, u32[]{:S(2)}) collective-permute-start(bf16[120,1536]{1,0:T(8,128)(2,1)S(1)} %get-tuple-element.49), channel_id=1, source_target_pairs={{0,32},{32,0},{1,33},{33,1},{2,34},{34,2},{3,35},{35,3},{4,36},{36... | collective-permute-start | bytes 1105928 | tf_op jit(solution)/shard_map/ppermute | solution.py:515
  111.4 11.4 %collective-permute-start.8 = (bf16[120,1536]{1,0:T(8,128)(2,1)S(1)}, bf16[120,1536]{1,0:T(8,128)(2,1)S(1)}, u32[]{:S(2)}, u32[]{:S(2)}) collective-permute-start(bf16[120,1536]{1,0:T(8,128)(2,1)S(1)} %add_convert_fusion), channel_id=1, source_target_pairs={{0,64},{64,0},{1,65},{65,1},{2,66},{66,2},{3,67},{67,3},{4,68},{68... | collective-permute-start | bytes 1105928 | tf_op jit(solution)/shard_map/ppermute | solution.py:515

commit v6 on v5

--- a/solution.py
+++ b/solution.py
@@ -10,7 +10,8 @@
 TILE = ("y", "zl", "x")
 HEAD = 64
 BIG = 1e30
-BLOCKS = ((0, 768), (768, 1152), (1152, 1536))
+BLOCKS = ((0, 512), (512, 1024), (1024, 1536))
+AHEAD = 2
 F32 = jnp.float32
 BF16 = jnp.bfloat16
 
@@ -75,7 +76,7 @@
     ]
     for copy in input_copies:
         copy.start()
-    for copies in w_copies:
+    for copies in w_copies[:AHEAD]:
         for copy in copies:
             copy.start()
     low = lane_iota((1, 2 * HEAD)) < HEAD
@@ -108,18 +109,24 @@
             v_old = cache[:, width + first : width + first + 2 * HEAD].astype(F32)
             store(head, below, joined(k_old, v_old, head % 2))
 
-    for b, (start, end) in enumerate(BLOCKS):
-        made = []
-        for kind in range(3):
-            w_copies[b][kind].wait()
-            made.append(
-                jnp.dot(
-                    normed,
-                    weights[:, kind * width + start : kind * width + end],
-                    preferred_element_type=F32,
-                )
+    def multiply(b):
+        start, end = BLOCKS[b]
+        for copy in w_copies[b]:
+            copy.wait()
+        if b + AHEAD < len(BLOCKS):
+            for copy in w_copies[b + AHEAD]:
+                copy.start()
+        return [
+            jnp.dot(
+                normed,
+                weights[:, kind * width + start : kind * width + end],
+                preferred_element_type=F32,
             )
-        queries, keys, values = made
+            for kind in range(3)
+        ]
+
+    def pack(b, queries, keys, values):
+        start, end = BLOCKS[b]
         queries = queries * 0.125
         for pair in range((end - start) // (2 * HEAD)):
             cols = slice(pair * 2 * HEAD, (pair + 1) * 2 * HEAD)
@@ -131,12 +138,18 @@
                 own_ref[head, above] = q_pack
                 own_ref[head, below] = joined(keys[:, cols], values[:, cols], odd)
                 store(head, above, q_pack)
-        head, last = start // HEAD, end // HEAD
-
-        @pl.when(flagged)
-        def _():
-            for h in range(head, last):
-                store(h, below, own_ref[h, below])
+
+    made = multiply(0)
+    for b in range(1, len(BLOCKS)):
+        following = multiply(b)
+        pack(b - 1, *made)
+        made = following
+    pack(len(BLOCKS) - 1, *made)
+
+    @pl.when(flagged)
+    def _():
+        for head in range(width // HEAD):
+            store(head, below, own_ref[head, below])
 
 
 def project(tile_index, refresh, tokens, modulate, w_qkv, cached):
@@ -227,7 +240,7 @@
             pl.BlockSpec((texts, group * HEAD), lambda p: (0, p + steps)),
         ],
         out_specs=pl.BlockSpec((group, rows, lanes), lambda p: (p, 0, 0)),
-        compiler_params=pltpu.CompilerParams(vmem_limit_bytes=24 << 20),
+        compiler_params=pltpu.CompilerParams(vmem_limit_bytes=14 << 20),
         cost_estimate=pl.CostEstimate(
             flops=2 * 4 * rows * (rows + texts) * 64 * heads,
             bytes_accessed=6 << 20,
@@ -338,12 +351,12 @@
     )(length, pack)
 
 
-def join_kernel(far_ref, own_ref, w0, w1, w2, att_ref, w_ref, sems):
+def join_kernel(far_ref, own_ref, w0, w1, w2, w3, att_ref, w_ref, sems):
     heads, rows, lanes = own_ref.shape
     depth = att_ref.shape[2]
     copies = []
     first = 0
-    for i, part in enumerate((w0, w1, w2)):
+    for i, part in enumerate((w0, w1, w2, w3)):
         last = first + part.shape[0]
         copies.append(pltpu.make_async_copy(part, w_ref.at[first:last], sems.at[i]))
         first = last
@@ -390,9 +403,9 @@
             jax.ShapeDtypeStruct((width // depth, rows, depth), BF16),
             pltpu.VMEM((fetched, width), BF16),
         ),
-        in_specs=[local, local] + [anywhere] * 3,
+        in_specs=[local, local] + [anywhere] * 4,
         out_specs=(local, local),
-        scratch_shapes=[pltpu.SemaphoreType.DMA((3,))],
+        scratch_shapes=[pltpu.SemaphoreType.DMA((4,))],
         compiler_params=pltpu.CompilerParams(vmem_limit_bytes=24 << 20),
         cost_estimate=pl.CostEstimate(
             flops=64 * heads * rows * 128, bytes_accessed=8 << 20, transcendentals=heads * rows * 256
@@ -401,21 +414,29 @@
     )(far, own, *w_parts)
 
 
-def mix_kernel(place_ref, att_ref, w_ref, last_ref, tokens_ref, mod_ref, mixed_ref, input_ref):
+def mix_kernel(
+    place_ref, att_ref, w_ref, w2_ref, w3_ref, tokens_ref, mod_ref, mixed_ref, input_ref
+):
     place = place_ref[0]
     depth = att_ref.shape[2]
-    owners = (place, place + 1 - 2 * (place % 2), (place + 2) % 4)
-    projected = jnp.dot(att_ref[3 - place], last_ref[...], preferred_element_type=F32)
-    for i, owner in enumerate(owners):
-        part = w_ref[i * depth : (i + 1) * depth]
-        projected += jnp.dot(att_ref[owner], part, preferred_element_type=F32)
+    late = w2_ref.shape[0]
+    early = depth - late
+    far = att_ref[(place + 2) % 4]
+    far_near = att_ref[3 - place]
+    dot = lambda a, b: jnp.dot(a, b, preferred_element_type=F32)
+    projected = dot(att_ref[place], w_ref[:depth])
+    projected += dot(att_ref[place + 1 - 2 * (place % 2)], w_ref[depth : 2 * depth])
+    projected += dot(far[:, :early], w_ref[2 * depth : 2 * depth + early])
+    projected += dot(far_near[:, :early], w_ref[2 * depth + early :])
+    projected += dot(far[:, early:], w2_ref[...])
+    projected += dot(far_near[:, early:], w3_ref[...])
     mod = mod_ref[...].astype(F32)
     mixed = tokens_ref[...].astype(F32) + mod[2:3] * projected
     mixed_ref[...] = mixed
     input_ref[...] = (layer_norm(mixed) * (1.0 + mod[4:5]) + mod[3:4]).astype(BF16)
 
 
-def mix(place, attended, w_main, w_last, tokens, modulate):
+def mix(place, attended, w_main, w2_late, w3_late, tokens, modulate):
     local = pl.BlockSpec(memory_space=pltpu.VMEM)
     return pl.pallas_call(
         mix_kernel,
@@ -423,11 +444,11 @@
             jax.ShapeDtypeStruct(tokens.shape, F32),
             jax.ShapeDtypeStruct(tokens.shape, BF16),
         ),
-        in_specs=[pl.BlockSpec(memory_space=pltpu.SMEM)] + [local] * 5,
+        in_specs=[pl.BlockSpec(memory_space=pltpu.SMEM)] + [local] * 6,
         out_specs=(local, local),
         compiler_params=pltpu.CompilerParams(vmem_limit_bytes=24 << 20),
         name="mix",
-    )(place, attended, w_main, w_last, tokens, modulate)
+    )(place, attended, w_main, w2_late, w3_late, tokens, modulate)
 
 
 def feed_blocks(first_ref, second_ref, keep_ref, pass_ref, up_ref, down_ref, ready):
@@ -530,16 +551,20 @@
     live = (length - tile_index * rows).reshape(1)
     own_part = own_attend(live, own, text_kv[0])
     own_part, w_here = lax.optimization_barrier((own_part, w_out))
-    w2 = swap(w_here, "zh")
+    early = w_out.shape[0] * 5 // 6
+    w2 = swap(w_here[:early], "zh")
+    w2_late = swap(w_here[early:], "zh")
     pack, own_part = lax.optimization_barrier((pack, own_part))
     far = head_attend(lengths, pack)
     far, w2, w_here = lax.optimization_barrier((far, w2, w_here))
     w1 = swap(w_here, "co")
     w3 = swap(w2, "co")
     far = lax.all_to_all(far, TILE, split_axis=0, concat_axis=0, tiled=True)
-    far, w1, w3 = lax.optimization_barrier((far, w1, w3))
-    attended, w_main = join(far, own_part, (w_out, w1, w2))
-    mixed, mlp_input = mix(place, attended, w_main, w3, tokens, modulation[0])
+    far, w1, w3, w2_late = lax.optimization_barrier((far, w1, w3, w2_late))
+    w3_late = swap(w2_late, "co")
+    attended, w_main = join(far, own_part, (w_out, w1, w2, w3))
+    attended, w3_late = lax.optimization_barrier((attended, w3_late))
+    mixed, mlp_input = mix(place, attended, w_main, w2_late, w3_late, tokens, modulation[0])
 
     far_z = swap(mlp_input, "zh")
     near = swap(mlp_input, "co")

time: 124 us -> 120 us (0.968)
  waiting for transfers between devices: 43 us -> 35.5 us
  starting transfers between devices: 25.1 us -> 28.4 us
  Pallas kernels: 47.8 us -> 45.3 us
  local copies, waits for them, and re-layouts: 5.94 us -> 8.16 us
    all_to_all x1, waiting for transfers between devices: 9.99 us -> 0.01 us  [per_device(): far = lax.all_to_all(far, TILE, split_axis=0, concat_axis=0, tiled=True)]
    ppermute x9 -> x11, waiting for transfers between devices: 21.3 us -> 25.3 us  [swap(): return lax.ppermute(values, axis, [(0, 1), (1, 0)])]
    ppermute x9 -> x11, starting transfers between devices: 9.64 us -> 12.7 us  [swap(): return lax.ppermute(values, axis, [(0, 1), (1, 0)])]
    pallas_call x1, Pallas kernels: 11.6 us -> 9.07 us  [project(): pl.pallas_call(project_kernel, out_shape=(jax.ShapeDtypeStruct((dests, pa...]
    all_to_all x1, waiting for transfers between devices: 11.8 us -> 10.3 us  [per_device(): pack = lax.all_to_all(send, TILE, split_axis=0, concat_axis=0, tiled=True)]
    unnamed x12 -> x14, local copies, waits for them, and re-layouts: 5.94 us -> 7.14 us
  transfers between devices with their start and end apart: 11 -> 13, of which waited for: 8 -> 7; matrix products, arithmetic and copies ran while one was open for 0% -> 1% of each run, Pallas kernels for 22% -> 26%
where the time goes in v6:
time: 120 us; the launch traced here: 119 us
  Pallas kernels  45.3 us (38%)
  waiting for transfers between devices  35.5 us (30%)
  starting transfers between devices  28.4 us (24%)
  local copies, waits for them, and re-layouts  8.16 us (7%)
    ppermute x11, waiting for transfers between devices, swap(): return lax.ppermute(values, axis, [(0, 1), (1, 0)])  25.3 us
    pallas_call x1, Pallas kernels, head_attend(): pl.pallas_call(head_kernel, grid=(tiles // group,), out_shape=pltpu.HBM((...  20.7 us
    ppermute x11, starting transfers between devices, swap(): return lax.ppermute(values, axis, [(0, 1), (1, 0)])  12.7 us
    all_to_all x1, waiting for transfers between devices, per_device(): pack = lax.all_to_all(send, TILE, split_axis=0, concat_axis=0, tiled=True)  10.3 us
    all_to_all x1, starting transfers between devices, per_device(): pack = lax.all_to_all(send, TILE, split_axis=0, concat_axis=0, tiled=True)  9.48 us
    pallas_call x1, Pallas kernels, project(): pl.pallas_call(project_kernel, out_shape=(jax.ShapeDtypeStruct((dests, pa...  9.07 us
    unnamed x14, local copies, waits for them, and re-layouts  7.14 us
    all_to_all x1, starting transfers between devices, per_device(): far = lax.all_to_all(far, TILE, split_axis=0, concat_axis=0, tiled=True)  6.16 us
  transfers between devices with their start and end apart: 13, of which 7 were waited for; matrix products, arithmetic and copies ran while one was open for 1% of the time, Pallas kernels for 26%

profile of v6, /device:TPU:1, one launch (start us, length us, event | category | flops | bytes accessed | tf_op | source)
XLA Modules:
  0.0 119.2 jit_solution(6691474413188776837)
XLA Ops:
  0.0 9.1 %project.1 = (bf16[32,184,128]{2,1,0:T(8,128)(2,1)}, bf16[24,184,128]{2,1,0:T(8,128)(2,1)}) custom-call(s32[1]{0:T(128)} %bitcast.2.tile_ref, s32[1,4]{1,0:T(1,128)} %refresh_ref.1, bf16[120,1536]{1,0:T(8,128)(2,1)} %bitcast.14, bf16[6,1536]{1,0:T(8,128)(2,1)} %bitcast.16, bf16[1536,4608]{1,0:T(8,128)(2,1)} %w_ref.1, bf16[120,3072]{1,0:T(8,128)(2,1)} %bitcast.18), custom_call_target="tpu_custom_call" | custom-call | flops 1698693120 | bytes 18350080 | tf_op jit(solution)/shard_map/project/pallas_call | solution.py:162
  9.1 9.5 %all-to-all-start = ((bf16[32,184,128]{2,1,0:T(8,128)(2,1)}), bf16[32,184,128]{2,1,0:T(8,128)(2,1)}, u32[]{:S(2)}, u32[]{:S(2)}) async-start(bf16[32,184,128]{2,1,0:T(8,128)(2,1)} %get-tuple-element.33), calls=%async_computation | async-start | bytes 3014656 | tf_op jit(solution)/shard_map/all_to_all | solution.py:550
  19.2 1.2 %copy-done.3 = bf16[1,154,3072]{2,1,0:T(8,128)(2,1)S(1)} copy-done((bf16[1,154,3072]{2,1,0:T(8,128)(2,1)S(1)}, bf16[1,154,3072]{2,1,0:T(8,128)(2,1)}, u32[]{:S(2)}) %copy-start.3) | copy-done | bytes 946200
  20.4 1.3 %copy-done.5 = bf16[24,184,128]{2,1,0:T(8,128)(2,1)S(1)} copy-done((bf16[24,184,128]{2,1,0:T(8,128)(2,1)S(1)}, bf16[24,184,128]{2,1,0:T(8,128)(2,1)}, u32[]{:S(2)}) %copy-start.5) | copy-done | bytes 1130520
  21.7 3.0 %own_attend.1.own_ref = f32[24,120,128]{2,1,0:T(8,128)S(1)} custom-call(s32[1]{0:T(128)} %bitcast.6.live_ref, bf16[24,184,128]{2,1,0:T(8,128)(2,1)S(1)} %copy-done.5, bf16[154,3072]{1,0:T(8,128)(2,1)S(1)} %bitcast.12, bf16[154,3072]{1,0:T(8,128)(2,1)S(1)} %bitcast.13), custom_call_target="tpu_custom_call" | custom-call | flops 404029440 | bytes 6291456 | tf_op jit(solution)/shard_map/own_attend/pallas_call | solution.py:232
  24.7 1.0 slice.9
  25.7 3.3 %collective-permute-start = (bf16[320,1536]{1,0:T(8,128)(2,1)}, bf16[320,1536]{1,0:T(8,128)(2,1)}, u32[]{:S(2)}, u32[]{:S(2)}) collective-permute-start(bf16[320,1536]{1,0:T(8,128)(2,1)} %slice.9), channel_id=1, source_target_pairs={{0,64},{64,0},{1,65},{65,1},{2,66},{66,2},{3,67},{67,3},{4,68},{68... | collective-permute-start | bytes 2949128 | tf_op jit(solution)/shard_map/ppermute | solution.py:536
  29.0 10.3 %all-to-all-done.pack_ref = bf16[32,184,128]{2,1,0:T(8,128)(2,1)} async-done(((bf16[32,184,128]{2,1,0:T(8,128)(2,1)}), bf16[32,184,128]{2,1,0:T(8,128)(2,1)}, u32[]{:S(2)}, u32[]{:S(2)}) %all-to-all-start) | async-done | bytes 1507360 | tf_op jit(solution)/shard_map/all_to_all | solution.py:550
  39.3 20.7 %head_attend.1 = bf16[32,64,128]{2,1,0:T(8,128)(2,1)} custom-call(s32[1]{0:T(128)} %copy.11.len_ref, bf16[32,184,128]{2,1,0:T(8,128)(2,1)} %all-to-all-done.pack_ref), custom_call_target="tpu_custom_call" | custom-call | flops 7549747200 | bytes 4194304 | tf_op jit(solution)/shard_map/head_attend/pallas_call | solution.py:330
  59.9 1.3 %collective-permute-done.w2 = bf16[320,1536]{1,0:T(8,128)(2,1)} collective-permute-done((bf16[320,1536]{1,0:T(8,128)(2,1)}, bf16[320,1536]{1,0:T(8,128)(2,1)}, u32[]{:S(2)}, u32[]{:S(2)}) %collective-permute-start) | collective-permute-done | bytes 983072 | tf_op jit(solution)/shard_map/ppermute | solution.py:536
  61.3 0.5 collective-permute-start.1
  61.8 6.2 %all-to-all-start.1 = ((bf16[32,64,128]{2,1,0:T(8,128)(2,1)}), bf16[32,64,128]{2,1,0:T(8,128)(2,1)S(1)}, u32[]{:S(2)}, u32[]{:S(2)}) async-start(bf16[32,64,128]{2,1,0:T(8,128)(2,1)} %head_attend.1), calls=%async_computation.1 | async-start | bytes 1048576 | tf_op jit(solution)/shard_map/all_to_all | solution.py:562
  68.0 1.8 %collective-permute-start.3 = (bf16[64,1536]{1,0:T(8,128)(2,1)S(1)}, bf16[64,1536]{1,0:T(8,128)(2,1)}, u32[]{:S(2)}, u32[]{:S(2)}) collective-permute-start(bf16[64,1536]{1,0:T(8,128)(2,1)S(1)} %slice.10), channel_id=1, source_target_pairs={{0,64},{64,0},{1,65},{65,1},{2,66},{66,2},{3,67},{67,3},{4,68},{68... | collective-permute-start | bytes 589832 | tf_op jit(solution)/shard_map/ppermute | solution.py:536
  69.8 10.9 %collective-permute-done.3.w2_ref = bf16[64,1536]{1,0:T(8,128)(2,1)} collective-permute-done((bf16[64,1536]{1,0:T(8,128)(2,1)S(1)}, bf16[64,1536]{1,0:T(8,128)(2,1)}, u32[]{:S(2)}, u32[]{:S(2)}) %collective-permute-start.3) | collective-permute-done | bytes 196640 | tf_op jit(solution)/shard_map/ppermute | solution.py:536
  80.7 1.8 %collective-permute-start.4 = (bf16[64,1536]{1,0:T(8,128)(2,1)}, bf16[64,1536]{1,0:T(8,128)(2,1)}, u32[]{:S(2)}, u32[]{:S(2)}) collective-permute-start(bf16[64,1536]{1,0:T(8,128)(2,1)} %collective-permute-done.3.w2_ref), channel_id=1, source_target_pairs={{0,32},{32,0},{1,33},{33,1},{2,34},{34,2},{3,35},{35,3},{4,36},{36... | collective-permute-start | bytes 589832 | tf_op jit(solution)/shard_map/ppermute | solution.py:536
  82.5 3.2 %join.1 = (bf16[4,120,384]{2,1,0:T(8,128)(2,1)S(1)}, bf16[1408,1536]{1,0:T(8,128)(2,1)S(1)}) custom-call(bf16[32,64,128]{2,1,0:T(8,128)(2,1)S(1)} %all-to-all-done.1.far_ref, f32[24,120,128]{2,1,0:T(8,128)S(1)} %own_attend.1.own_ref, bf16[384,1536]{1,0:T(8,128)(2,1)S(1)} %copy-done.2, bf16[384,1536]{1,0:T(8,128)(2,1)} %collective-permute-done.1.w1, ...), custom_call_target="tpu_custom_call" | custom-call | flops 23592960 | bytes 8388608 | tf_op jit(solution)/shard_map/join/pallas_call | solution.py:400
  85.7 2.5 %mix.1 = (f32[120,1536]{1,0:T(8,128)S(1)}, bf16[120,1536]{1,0:T(8,128)(2,1)S(1)}) custom-call(s32[1]{0:T(128)} %bitcast.1.place_ref, bf16[4,120,384]{2,1,0:T(8,128)(2,1)S(1)} %get-tuple-element.47.att_ref, bf16[1408,1536]{1,0:T(8,128)(2,1)S(1)} %get-tuple-element.48.w_ref, bf16[64,1536]{1,0:T(8,128)(2,1)} %collective-permute-done.3.w2_ref, ...), custom_call_target="tpu_custom_call" | custom-call | tf_op jit(solution)/shard_map/mix/pallas_call | solution.py:441
  88.2 0.1 collective-permute-start.6
  88.4 1.6 %collective-permute-start.5 = (bf16[120,1536]{1,0:T(8,128)(2,1)S(1)}, bf16[120,1536]{1,0:T(8,128)(2,1)S(1)}, u32[]{:S(2)}, u32[]{:S(2)}) collective-permute-start(bf16[120,1536]{1,0:T(8,128)(2,1)S(1)} %get-tuple-element.51.first), channel_id=1, source_target_pairs={{0,64},{64,0},{1,65},{65,1},{2,66},{66,2},{3,67},{67,3},{4,68},{68... | collective-permute-start | bytes 1105928 | tf_op jit(solution)/shard_map/ppermute | solution.py:536
  90.0 2.3 %copy-done = bf16[1536,1536]{1,0:T(8,128)(2,1)S(1)} copy-done((bf16[1536,1536]{1,0:T(8,128)(2,1)S(1)}, bf16[1536,1536]{1,0:T(8,128)(2,1)}, u32[]{:S(2)}) %copy-start) | copy-done | bytes 4718616
  92.3 2.3 %copy-done.1 = bf16[1536,1536]{1,0:T(8,128)(2,1)S(1)} copy-done((bf16[1536,1536]{1,0:T(8,128)(2,1)S(1)}, bf16[1536,1536]{1,0:T(8,128)(2,1)}, u32[]{:S(2)}) %copy-start.1) | copy-done | bytes 4718616
  94.7 4.1 %feed_near.1 = (f32[120,1536]{1,0:T(8,128)S(1)}, bf16[120,1536]{1,0:T(8,128)(2,1)S(1)}, bf16[1536,1536]{1,0:T(8,128)(2,1)S(1)}, bf16[1536,1536]{1,0:T(8,128)(2,1)S(1)}) custom-call(bf16[120,1536]{1,0:T(8,128)(2,1)S(1)} %get-tuple-element.51.first, bf16[120,1536]{1,0:T(8,128)(2,1)S(1)} %collective-permute-done.6.second, bf16[1536,1536]{1,0:T(8,128)(2,1)S(1)} %copy-done, ...), custom_call_target="tpu_custom_call" | custom-call | flops 2264924160 | bytes 9437184 | tf_op jit(solution)/shard_map/feed_near/pallas_call | solution.py:497
  98.8 0.9 collective-permute-done.5.first
  99.7 1.3 %collective-permute-start.8 = (bf16[120,1536]{1,0:T(8,128)(2,1)S(1)}, bf16[120,1536]{1,0:T(8,128)(2,1)S(1)}, u32[]{:S(2)}, u32[]{:S(2)}) collective-permute-start(bf16[120,1536]{1,0:T(8,128)(2,1)S(1)} %collective-permute-done.5.first), channel_id=1, source_target_pairs={{0,32},{32,0},{1,33},{33,1},{2,34},{34,2},{3,35},{35,3},{4,36},{36... | collective-permute-start | bytes 1105928 | tf_op jit(solution)/shard_map/ppermute | solution.py:536
  100.9 1.3 %collective-permute-done.8.second = bf16[120,1536]{1,0:T(8,128)(2,1)S(1)} collective-permute-done((bf16[120,1536]{1,0:T(8,128)(2,1)S(1)}, bf16[120,1536]{1,0:T(8,128)(2,1)S(1)}, u32[]{:S(2)}, u32[]{:S(2)}) %collective-permute-start.8) | collective-permute-done | bytes 368672 | tf_op jit(solution)/shard_map/ppermute | solution.py:536
  102.2 2.8 %feed_far.1 = (f32[120,1536]{1,0:T(8,128)S(1)}, bf16[120,1536]{1,0:T(8,128)(2,1)S(1)}) custom-call(bf16[120,1536]{1,0:T(8,128)(2,1)S(1)} %collective-permute-done.5.first, bf16[120,1536]{1,0:T(8,128)(2,1)S(1)} %collective-permute-done.8.second, bf16[1536,1536]{1,0:T(8,128)(2,1)S(1)} %get-tuple-element.57.up, bf16[1536,1536]{1,0:T(8,128)(2,1)S(1)} %get-tuple-element.58.down), custom_call_target="tpu_custom_call" | custom-call | flops 2264924160 | bytes 1048576 | tf_op jit(solution)/shard_map/feed_far/pallas_call | solution.py:519
  105.0 0.5 collective-permute-start.9
  105.5 0.1 collective-permute-start.7
  105.6 1.2 collective-permute-done.9
  106.9 1.7 %collective-permute-start.10 = (bf16[120,1536]{1,0:T(8,128)(2,1)S(1)}, bf16[120,1536]{1,0:T(8,128)(2,1)S(1)}, u32[]{:S(2)}, u32[]{:S(2)}) collective-permute-start(bf16[120,1536]{1,0:T(8,128)(2,1)S(1)} %add_convert_fusion), channel_id=1, source_target_pairs={{0,64},{64,0},{1,65},{65,1},{2,66},{66,2},{3,67},{67,3},{4,68},{68... | collective-permute-start | bytes 1105928 | tf_op jit(solution)/shard_map/ppermute | solution.py:536
  108.6 9.7 %collective-permute-done.10 = bf16[120,1536]{1,0:T(8,128)(2,1)S(1)} collective-permute-done((bf16[120,1536]{1,0:T(8,128)(2,1)S(1)}, bf16[120,1536]{1,0:T(8,128)(2,1)S(1)}, u32[]{:S(2)}, u32[]{:S(2)}) %collective-permute-start.10) | collective-permute-done | bytes 368672 | tf_op jit(solution)/shard_map/ppermute | solution.py:536
  118.2 1.0 fusion
  (21 shorter events, 0.2 us)
Async XLA Ops:
  9.1 15.6 %copy-start.2 = (bf16[384,1536]{1,0:T(8,128)(2,1)S(1)}, bf16[384,1536]{1,0:T(8,128)(2,1)}, u32[]{:S(2)}) copy-start(bf16[384,1536]{1,0:T(8,128)(2,1)} %w0.1) | copy-start | bytes 3538948
  9.1 30.2 %all-to-all-start = ((bf16[32,184,128]{2,1,0:T(8,128)(2,1)}), bf16[32,184,128]{2,1,0:T(8,128)(2,1)}, u32[]{:S(2)}, u32[]{:S(2)}) async-start(bf16[32,184,128]{2,1,0:T(8,128)(2,1)} %get-tuple-element.33), calls=%async_computation | async-start | bytes 3014656 | tf_op jit(solution)/shard_map/all_to_all | solution.py:550
  19.2 1.2 %copy-start.3 = (bf16[1,154,3072]{2,1,0:T(8,128)(2,1)S(1)}, bf16[1,154,3072]{2,1,0:T(8,128)(2,1)}, u32[]{:S(2)}) copy-start(bf16[1,154,3072]{2,1,0:T(8,128)(2,1)} %param.13) | copy-start | bytes 2838532
  20.4 1.3 %copy-start.5 = (bf16[24,184,128]{2,1,0:T(8,128)(2,1)S(1)}, bf16[24,184,128]{2,1,0:T(8,128)(2,1)}, u32[]{:S(2)}) copy-start(bf16[24,184,128]{2,1,0:T(8,128)(2,1)} %get-tuple-element.34.own_ref) | copy-start | bytes 3391492
  25.7 35.6 %collective-permute-start = (bf16[320,1536]{1,0:T(8,128)(2,1)}, bf16[320,1536]{1,0:T(8,128)(2,1)}, u32[]{:S(2)}, u32[]{:S(2)}) collective-permute-start(bf16[320,1536]{1,0:T(8,128)(2,1)} %slice.9), channel_id=1, source_target_pairs={{0,64},{64,0},{1,65},{65,1},{2,66},{66,2},{3,67},{67,3},{4,68},{68... | collective-permute-start | bytes 2949128 | tf_op jit(solution)/shard_map/ppermute | solution.py:536
  59.9 25.8 %copy-start.4 = (bf16[1,120,1536]{2,1,0:T(8,128)(2,1)S(1)}, bf16[1,120,1536]{2,1,0:T(8,128)(2,1)}, u32[]{:S(2)}) copy-start(bf16[1,120,1536]{2,1,0:T(8,128)(2,1)} %param.10) | copy-start | bytes 1105924
  61.3 19.5 %collective-permute-start.1 = (bf16[384,1536]{1,0:T(8,128)(2,1)S(1)}, bf16[384,1536]{1,0:T(8,128)(2,1)}, u32[]{:S(2)}, u32[]{:S(2)}) collective-permute-start(bf16[384,1536]{1,0:T(8,128)(2,1)S(1)} %copy-done.2), channel_id=1, source_target_pairs={{0,32},{32,0},{1,33},{33,1},{2,34},{34,2},{3,35},{35,3},{4,36},{36... | collective-permute-start | bytes 3538952 | tf_op jit(solution)/shard_map/ppermute | solution.py:536
  61.8 19.0 %collective-permute-start.2 = (bf16[320,1536]{1,0:T(8,128)(2,1)}, bf16[320,1536]{1,0:T(8,128)(2,1)}, u32[]{:S(2)}, u32[]{:S(2)}) collective-permute-start(bf16[320,1536]{1,0:T(8,128)(2,1)} %collective-permute-done.w2), channel_id=1, source_target_pairs={{0,32},{32,0},{1,33},{33,1},{2,34},{34,2},{3,35},{35,3},{4,36},{36... | collective-permute-start | bytes 2949128 | tf_op jit(solution)/shard_map/ppermute | solution.py:536
  61.8 18.9 %all-to-all-start.1 = ((bf16[32,64,128]{2,1,0:T(8,128)(2,1)}), bf16[32,64,128]{2,1,0:T(8,128)(2,1)S(1)}, u32[]{:S(2)}, u32[]{:S(2)}) async-start(bf16[32,64,128]{2,1,0:T(8,128)(2,1)} %head_attend.1), calls=%async_computation.1 | async-start | bytes 1048576 | tf_op jit(solution)/shard_map/all_to_all | solution.py:562
  68.0 12.7 %collective-permute-start.3 = (bf16[64,1536]{1,0:T(8,128)(2,1)S(1)}, bf16[64,1536]{1,0:T(8,128)(2,1)}, u32[]{:S(2)}, u32[]{:S(2)}) collective-permute-start(bf16[64,1536]{1,0:T(8,128)(2,1)S(1)} %slice.10), channel_id=1, source_target_pairs={{0,64},{64,0},{1,65},{65,1},{2,66},{66,2},{3,67},{67,3},{4,68},{68... | collective-permute-start | bytes 589832 | tf_op jit(solution)/shard_map/ppermute | solution.py:536
  80.7 5.0 %collective-permute-start.4 = (bf16[64,1536]{1,0:T(8,128)(2,1)}, bf16[64,1536]{1,0:T(8,128)(2,1)}, u32[]{:S(2)}, u32[]{:S(2)}) collective-permute-start(bf16[64,1536]{1,0:T(8,128)(2,1)} %collective-permute-done.3.w2_ref), channel_id=1, source_target_pairs={{0,32},{32,0},{1,33},{33,1},{2,34},{34,2},{3,35},{35,3},{4,36},{36... | collective-permute-start | bytes 589832 | tf_op jit(solution)/shard_map/ppermute | solution.py:536
  82.5 3.2 %copy-start.6 = (bf16[1,6,1536]{2,1,0:T(8,128)(2,1)S(1)}, bf16[1,6,1536]{2,1,0:T(8,128)(2,1)}, u32[]{:S(2)}) copy-start(bf16[1,6,1536]{2,1,0:T(8,128)(2,1)} %param.11) | copy-start | bytes 55300
  88.2 1.8 %collective-permute-start.6 = (bf16[120,1536]{1,0:T(8,128)(2,1)S(1)}, bf16[120,1536]{1,0:T(8,128)(2,1)S(1)}, u32[]{:S(2)}, u32[]{:S(2)}) collective-permute-start(bf16[120,1536]{1,0:T(8,128)(2,1)S(1)} %get-tuple-element.51.first), channel_id=1, source_target_pairs={{0,32},{32,0},{1,33},{33,1},{2,34},{34,2},{3,35},{35,3},{4,36},{36... | collective-permute-start | bytes 1105928 | tf_op jit(solution)/shard_map/ppermute | solution.py:536
  88.4 11.3 %collective-permute-start.5 = (bf16[120,1536]{1,0:T(8,128)(2,1)S(1)}, bf16[120,1536]{1,0:T(8,128)(2,1)S(1)}, u32[]{:S(2)}, u32[]{:S(2)}) collective-permute-start(bf16[120,1536]{1,0:T(8,128)(2,1)S(1)} %get-tuple-element.51.first), channel_id=1, source_target_pairs={{0,64},{64,0},{1,65},{65,1},{2,66},{66,2},{3,67},{67,3},{4,68},{68... | collective-permute-start | bytes 1105928 | tf_op jit(solution)/shard_map/ppermute | solution.py:536
  90.0 2.3 %copy-start = (bf16[1536,1536]{1,0:T(8,128)(2,1)S(1)}, bf16[1536,1536]{1,0:T(8,128)(2,1)}, u32[]{:S(2)}) copy-start(bf16[1536,1536]{1,0:T(8,128)(2,1)} %up_hbm.1) | copy-start | bytes 14155780
  92.3 2.3 %copy-start.1 = (bf16[1536,1536]{1,0:T(8,128)(2,1)S(1)}, bf16[1536,1536]{1,0:T(8,128)(2,1)}, u32[]{:S(2)}) copy-start(bf16[1536,1536]{1,0:T(8,128)(2,1)} %down_hbm.1) | copy-start | bytes 14155780
  99.7 2.6 %collective-permute-start.8 = (bf16[120,1536]{1,0:T(8,128)(2,1)S(1)}, bf16[120,1536]{1,0:T(8,128)(2,1)S(1)}, u32[]{:S(2)}, u32[]{:S(2)}) collective-permute-start(bf16[120,1536]{1,0:T(8,128)(2,1)S(1)} %collective-permute-done.5.first), channel_id=1, source_target_pairs={{0,32},{32,0},{1,33},{33,1},{2,34},{34,2},{3,35},{35,3},{4,36},{36... | collective-permute-start | bytes 1105928 | tf_op jit(solution)/shard_map/ppermute | solution.py:536
  105.0 1.8 %collective-permute-start.9 = (bf16[120,1536]{1,0:T(8,128)(2,1)S(1)}, bf16[120,1536]{1,0:T(8,128)(2,1)S(1)}, u32[]{:S(2)}, u32[]{:S(2)}) collective-permute-start(bf16[120,1536]{1,0:T(8,128)(2,1)S(1)} %get-tuple-element.60), channel_id=1, source_target_pairs={{0,32},{32,0},{1,33},{33,1},{2,34},{34,2},{3,35},{35,3},{4,36},{36... | collective-permute-start | bytes 1105928 | tf_op jit(solution)/shard_map/ppermute | solution.py:536
  105.5 3.1 %collective-permute-start.7 = (bf16[120,1536]{1,0:T(8,128)(2,1)S(1)}, bf16[120,1536]{1,0:T(8,128)(2,1)S(1)}, u32[]{:S(2)}, u32[]{:S(2)}) collective-permute-start(bf16[120,1536]{1,0:T(8,128)(2,1)S(1)} %get-tuple-element.55), channel_id=1, source_target_pairs={{0,32},{32,0},{1,33},{33,1},{2,34},{34,2},{3,35},{35,3},{4,36},{36... | collective-permute-start | bytes 1105928 | tf_op jit(solution)/shard_map/ppermute | solution.py:536
  106.9 11.4 %collective-permute-start.10 = (bf16[120,1536]{1,0:T(8,128)(2,1)S(1)}, bf16[120,1536]{1,0:T(8,128)(2,1)S(1)}, u32[]{:S(2)}, u32[]{:S(2)}) collective-permute-start(bf16[120,1536]{1,0:T(8,128)(2,1)S(1)} %add_convert_fusion), channel_id=1, source_target_pairs={{0,64},{64,0},{1,65},{65,1},{2,66},{66,2},{3,67},{67,3},{4,68},{68... | collective-permute-start | bytes 1105928 | tf_op jit(solution)/shard_map/ppermute | solution.py:536

commit v7 on v6

--- a/solution.py
+++ b/solution.py
@@ -351,12 +351,12 @@
     )(length, pack)
 
 
-def join_kernel(far_ref, own_ref, w0, w1, w2, w3, att_ref, w_ref, sems):
+def join_kernel(far_ref, own_ref, w0, w1, w2a, w2b, w3a, w3b, att_ref, w_ref, sems):
     heads, rows, lanes = own_ref.shape
     depth = att_ref.shape[2]
     copies = []
     first = 0
-    for i, part in enumerate((w0, w1, w2, w3)):
+    for i, part in enumerate((w0, w1, w2a, w2b, w3a, w3b)):
         last = first + part.shape[0]
         copies.append(pltpu.make_async_copy(part, w_ref.at[first:last], sems.at[i]))
         first = last
@@ -403,9 +403,9 @@
             jax.ShapeDtypeStruct((width // depth, rows, depth), BF16),
             pltpu.VMEM((fetched, width), BF16),
         ),
-        in_specs=[local, local] + [anywhere] * 4,
+        in_specs=[local, local] + [anywhere] * 6,
         out_specs=(local, local),
-        scratch_shapes=[pltpu.SemaphoreType.DMA((4,))],
+        scratch_shapes=[pltpu.SemaphoreType.DMA((6,))],
         compiler_params=pltpu.CompilerParams(vmem_limit_bytes=24 << 20),
         cost_estimate=pl.CostEstimate(
             flops=64 * heads * rows * 128, bytes_accessed=8 << 20, transcendentals=heads * rows * 256
@@ -414,29 +414,21 @@
     )(far, own, *w_parts)
 
 
-def mix_kernel(
-    place_ref, att_ref, w_ref, w2_ref, w3_ref, tokens_ref, mod_ref, mixed_ref, input_ref
-):
+def mix_kernel(place_ref, att_ref, w_ref, tokens_ref, mod_ref, mixed_ref, input_ref):
     place = place_ref[0]
     depth = att_ref.shape[2]
-    late = w2_ref.shape[0]
-    early = depth - late
-    far = att_ref[(place + 2) % 4]
-    far_near = att_ref[3 - place]
-    dot = lambda a, b: jnp.dot(a, b, preferred_element_type=F32)
-    projected = dot(att_ref[place], w_ref[:depth])
-    projected += dot(att_ref[place + 1 - 2 * (place % 2)], w_ref[depth : 2 * depth])
-    projected += dot(far[:, :early], w_ref[2 * depth : 2 * depth + early])
-    projected += dot(far_near[:, :early], w_ref[2 * depth + early :])
-    projected += dot(far[:, early:], w2_ref[...])
-    projected += dot(far_near[:, early:], w3_ref[...])
+    projected = jnp.zeros(mixed_ref.shape, F32)
+    owners = (place, place + 1 - 2 * (place % 2), (place + 2) % 4, 3 - place)
+    for i, owner in enumerate(owners):
+        part = w_ref[i * depth : (i + 1) * depth]
+        projected += jnp.dot(att_ref[owner], part, preferred_element_type=F32)
     mod = mod_ref[...].astype(F32)
     mixed = tokens_ref[...].astype(F32) + mod[2:3] * projected
     mixed_ref[...] = mixed
     input_ref[...] = (layer_norm(mixed) * (1.0 + mod[4:5]) + mod[3:4]).astype(BF16)
 
 
-def mix(place, attended, w_main, w2_late, w3_late, tokens, modulate):
+def mix(place, attended, w_main, tokens, modulate):
     local = pl.BlockSpec(memory_space=pltpu.VMEM)
     return pl.pallas_call(
         mix_kernel,
@@ -444,11 +436,11 @@
             jax.ShapeDtypeStruct(tokens.shape, F32),
             jax.ShapeDtypeStruct(tokens.shape, BF16),
         ),
-        in_specs=[pl.BlockSpec(memory_space=pltpu.SMEM)] + [local] * 6,
+        in_specs=[pl.BlockSpec(memory_space=pltpu.SMEM)] + [local] * 4,
         out_specs=(local, local),
         compiler_params=pltpu.CompilerParams(vmem_limit_bytes=24 << 20),
         name="mix",
-    )(place, attended, w_main, w2_late, w3_late, tokens, modulate)
+    )(place, attended, w_main, tokens, modulate)
 
 
 def feed_blocks(first_ref, second_ref, keep_ref, pass_ref, up_ref, down_ref, ready):
@@ -544,27 +536,27 @@
     tile_index = lax.axis_index(TILE).astype(jnp.int32)
     length = lengths[0]
     place = lax.axis_index(REQ).astype(jnp.int32).reshape(1)
+    w2_first = swap(w_out[: w_out.shape[0] // 6], "zh")
     send, own = project(
         tile_index.reshape(1), refresh, tokens, modulation[0], w_qkv, kv_cache[0]
     )
+    send, own, w2_first = lax.optimization_barrier((send, own, w2_first))
     pack = lax.all_to_all(send, TILE, split_axis=0, concat_axis=0, tiled=True)
     live = (length - tile_index * rows).reshape(1)
     own_part = own_attend(live, own, text_kv[0])
     own_part, w_here = lax.optimization_barrier((own_part, w_out))
-    early = w_out.shape[0] * 5 // 6
-    w2 = swap(w_here[:early], "zh")
-    w2_late = swap(w_here[early:], "zh")
+    early = w_out.shape[0] // 6
+    w1 = swap(w_here, "co")
+    w2 = swap(w_here[early:], "zh")
     pack, own_part = lax.optimization_barrier((pack, own_part))
     far = head_attend(lengths, pack)
-    far, w2, w_here = lax.optimization_barrier((far, w2, w_here))
-    w1 = swap(w_here, "co")
+    far, w1, w2 = lax.optimization_barrier((far, w1, w2))
     w3 = swap(w2, "co")
+    w3_first = swap(w2_first, "co")
     far = lax.all_to_all(far, TILE, split_axis=0, concat_axis=0, tiled=True)
-    far, w1, w3, w2_late = lax.optimization_barrier((far, w1, w3, w2_late))
-    w3_late = swap(w2_late, "co")
-    attended, w_main = join(far, own_part, (w_out, w1, w2, w3))
-    attended, w3_late = lax.optimization_barrier((attended, w3_late))
-    mixed, mlp_input = mix(place, attended, w_main, w2_late, w3_late, tokens, modulation[0])
+    far, w3, w3_first = lax.optimization_barrier((far, w3, w3_first))
+    attended, w_main = join(far, own_part, (w_out, w1, w2_first, w2, w3_first, w3))
+    mixed, mlp_input = mix(place, attended, w_main, tokens, modulation[0])
 
     far_z = swap(mlp_input, "zh")
     near = swap(mlp_input, "co")

time: 120 us -> 120 us (level)
  waiting for transfers between devices: 35.5 us -> 32.5 us
  starting transfers between devices: 28.4 us -> 30.6 us
  local copies, waits for them, and re-layouts: 8.16 us -> 10.1 us
    ppermute x11, waiting for transfers between devices: 25.3 us -> 13.3 us  [swap(): return lax.ppermute(values, axis, [(0, 1), (1, 0)])]
    all_to_all x1, waiting for transfers between devices: 0.01 us -> 8.49 us  [per_device(): far = lax.all_to_all(far, TILE, split_axis=0, concat_axis=0, tiled=True)]
    ppermute x11, starting transfers between devices: 12.7 us -> 18 us  [swap(): return lax.ppermute(values, axis, [(0, 1), (1, 0)])]
    all_to_all x1, starting transfers between devices: 9.48 us -> 7.93 us  [per_device(): pack = lax.all_to_all(send, TILE, split_axis=0, concat_axis=0, tiled=True)]
    all_to_all x1, starting transfers between devices: 6.16 us -> 4.65 us  [per_device(): far = lax.all_to_all(far, TILE, split_axis=0, concat_axis=0, tiled=True)]
    pallas_call x1, Pallas kernels: 2.47 us -> 1.24 us  [mix(): pl.pallas_call(mix_kernel, out_shape=(jax.ShapeDtypeStruct(tokens.shape,...]
    unnamed x14 -> x18, local copies, waits for them, and re-layouts: 7.14 us -> 8.07 us
  transfers between devices with their start and end apart: 13 -> 13, of which waited for: 7 -> 7; matrix products, arithmetic and copies ran while one was open for 1% -> 1% of each run, Pallas kernels for 26% -> 31%
where the time goes in v7:
time: 120 us; the launch traced here: 119 us
  Pallas kernels  44.1 us (37%)
  waiting for transfers between devices  32.5 us (27%)
  starting transfers between devices  30.6 us (26%)
  local copies, waits for them, and re-layouts  10.1 us (8%)
    pallas_call x1, Pallas kernels, head_attend(): pl.pallas_call(head_kernel, grid=(tiles // group,), out_shape=pltpu.HBM((...  20.7 us
    ppermute x11, starting transfers between devices, swap(): return lax.ppermute(values, axis, [(0, 1), (1, 0)])  18 us
    ppermute x11, waiting for transfers between devices, swap(): return lax.ppermute(values, axis, [(0, 1), (1, 0)])  13.3 us
    all_to_all x1, waiting for transfers between devices, per_device(): pack = lax.all_to_all(send, TILE, split_axis=0, concat_axis=0, tiled=True)  10.7 us
    pallas_call x1, Pallas kernels, project(): pl.pallas_call(project_kernel, out_shape=(jax.ShapeDtypeStruct((dests, pa...  8.89 us
    all_to_all x1, waiting for transfers between devices, per_device(): far = lax.all_to_all(far, TILE, split_axis=0, concat_axis=0, tiled=True)  8.49 us
    unnamed x18, local copies, waits for them, and re-layouts  8.07 us
    all_to_all x1, starting transfers between devices, per_device(): pack = lax.all_to_all(send, TILE, split_axis=0, concat_axis=0, tiled=True)  7.93 us
  transfers between devices with their start and end apart: 13, of which 7 were waited for; matrix products, arithmetic and copies ran while one was open for 1% of the time, Pallas kernels for 31%

profile of v7, /device:TPU:1, one launch (start us, length us, event | category | flops | bytes accessed | tf_op | source)
XLA Modules:
  0.0 119.1 jit_solution(9506651261040037302)
XLA Ops:
  0.0 0.9 slice.9
  0.9 4.5 %collective-permute-start = (bf16[64,1536]{1,0:T(8,128)(2,1)S(1)}, bf16[64,1536]{1,0:T(8,128)(2,1)S(1)}, u32[]{:S(2)}, u32[]{:S(2)}) collective-permute-start(bf16[64,1536]{1,0:T(8,128)(2,1)S(1)} %slice.9), channel_id=1, source_target_pairs={{0,64},{64,0},{1,65},{65,1},{2,66},{66,2},{3,67},{67,3},{4,68},{68... | collective-permute-start | bytes 589832 | tf_op jit(solution)/shard_map/ppermute | solution.py:528
  5.4 8.9 %project.1 = (bf16[32,184,128]{2,1,0:T(8,128)(2,1)}, bf16[24,184,128]{2,1,0:T(8,128)(2,1)}) custom-call(s32[1]{0:T(128)} %bitcast.2.tile_ref, s32[1,4]{1,0:T(1,128)} %refresh_ref.1, bf16[120,1536]{1,0:T(8,128)(2,1)} %bitcast.14, bf16[6,1536]{1,0:T(8,128)(2,1)} %bitcast.16, bf16[1536,4608]{1,0:T(8,128)(2,1)} %w_ref.1, bf16[120,3072]{1,0:T(8,128)(2,1)} %bitcast.18), custom_call_target="tpu_custom_call" | custom-call | flops 1698693120 | bytes 18350080 | tf_op jit(solution)/shard_map/project/pallas_call | solution.py:162
  14.4 7.9 %all-to-all-start = ((bf16[32,184,128]{2,1,0:T(8,128)(2,1)}), bf16[32,184,128]{2,1,0:T(8,128)(2,1)}, u32[]{:S(2)}, u32[]{:S(2)}) async-start(bf16[32,184,128]{2,1,0:T(8,128)(2,1)} %get-tuple-element.35), calls=%async_computation | async-start | bytes 3014656 | tf_op jit(solution)/shard_map/all_to_all | solution.py:544
  23.0 1.2 %copy-done.3 = bf16[1,154,3072]{2,1,0:T(8,128)(2,1)S(1)} copy-done((bf16[1,154,3072]{2,1,0:T(8,128)(2,1)S(1)}, bf16[1,154,3072]{2,1,0:T(8,128)(2,1)}, u32[]{:S(2)}) %copy-start.3) | copy-done | bytes 946200
  24.2 1.3 %copy-done.5 = bf16[24,184,128]{2,1,0:T(8,128)(2,1)S(1)} copy-done((bf16[24,184,128]{2,1,0:T(8,128)(2,1)S(1)}, bf16[24,184,128]{2,1,0:T(8,128)(2,1)}, u32[]{:S(2)}) %copy-start.5) | copy-done | bytes 1130520
  25.4 3.0 %own_attend.1.own_ref = f32[24,120,128]{2,1,0:T(8,128)S(1)} custom-call(s32[1]{0:T(128)} %bitcast.6.live_ref, bf16[24,184,128]{2,1,0:T(8,128)(2,1)S(1)} %copy-done.5, bf16[154,3072]{1,0:T(8,128)(2,1)S(1)} %bitcast.12, bf16[154,3072]{1,0:T(8,128)(2,1)S(1)} %bitcast.13), custom_call_target="tpu_custom_call" | custom-call | flops 404029440 | bytes 6291456 | tf_op jit(solution)/shard_map/own_attend/pallas_call | solution.py:232
  28.4 1.3 %collective-permute-start.1 = (bf16[384,1536]{1,0:T(8,128)(2,1)S(1)}, bf16[384,1536]{1,0:T(8,128)(2,1)}, u32[]{:S(2)}, u32[]{:S(2)}) collective-permute-start(bf16[384,1536]{1,0:T(8,128)(2,1)S(1)} %copy-done.2), channel_id=1, source_target_pairs={{0,32},{32,0},{1,33},{33,1},{2,34},{34,2},{3,35},{35,3},{4,36},{36... | collective-permute-start | bytes 3538952 | tf_op jit(solution)/shard_map/ppermute | solution.py:528
  29.8 1.0 slice.10
  30.8 0.9 collective-permute-start.2
  31.7 10.7 %all-to-all-done.pack_ref = bf16[32,184,128]{2,1,0:T(8,128)(2,1)} async-done(((bf16[32,184,128]{2,1,0:T(8,128)(2,1)}), bf16[32,184,128]{2,1,0:T(8,128)(2,1)}, u32[]{:S(2)}, u32[]{:S(2)}) %all-to-all-start) | async-done | bytes 1507360 | tf_op jit(solution)/shard_map/all_to_all | solution.py:544
  42.4 20.7 %head_attend.1 = bf16[32,64,128]{2,1,0:T(8,128)(2,1)} custom-call(s32[1]{0:T(128)} %copy.11.len_ref, bf16[32,184,128]{2,1,0:T(8,128)(2,1)} %all-to-all-done.pack_ref), custom_call_target="tpu_custom_call" | custom-call | flops 7549747200 | bytes 4194304 | tf_op jit(solution)/shard_map/head_attend/pallas_call | solution.py:330
  63.0 2.5 %collective-permute-start.3 = (bf16[320,1536]{1,0:T(8,128)(2,1)}, bf16[320,1536]{1,0:T(8,128)(2,1)}, u32[]{:S(2)}, u32[]{:S(2)}) collective-permute-start(bf16[320,1536]{1,0:T(8,128)(2,1)} %collective-permute-done.2.w2b), channel_id=1, source_target_pairs={{0,32},{32,0},{1,33},{33,1},{2,34},{34,2},{3,35},{35,3},{4,36},{36... | collective-permute-start | bytes 2949128 | tf_op jit(solution)/shard_map/ppermute | solution.py:528
  65.5 4.6 %all-to-all-start.1 = ((bf16[32,64,128]{2,1,0:T(8,128)(2,1)}), bf16[32,64,128]{2,1,0:T(8,128)(2,1)S(1)}, u32[]{:S(2)}, u32[]{:S(2)}) async-start(bf16[32,64,128]{2,1,0:T(8,128)(2,1)} %head_attend.1), calls=%async_computation.1 | async-start | bytes 1048576 | tf_op jit(solution)/shard_map/all_to_all | solution.py:556
  70.2 0.6 collective-permute-start.4
  70.7 1.5 %collective-permute-done.4.w3a = bf16[64,1536]{1,0:T(8,128)(2,1)} collective-permute-done((bf16[64,1536]{1,0:T(8,128)(2,1)}, bf16[64,1536]{1,0:T(8,128)(2,1)}, u32[]{:S(2)}, u32[]{:S(2)}) %collective-permute-start.4) | collective-permute-done | bytes 196640 | tf_op jit(solution)/shard_map/ppermute | solution.py:528
  72.2 8.5 %all-to-all-done.1.far_ref = bf16[32,64,128]{2,1,0:T(8,128)(2,1)S(1)} async-done(((bf16[32,64,128]{2,1,0:T(8,128)(2,1)}), bf16[32,64,128]{2,1,0:T(8,128)(2,1)S(1)}, u32[]{:S(2)}, u32[]{:S(2)}) %all-to-all-start.1) | async-done | bytes 524320 | tf_op jit(solution)/shard_map/all_to_all | solution.py:556
  80.7 0.9 copy-done.7
  81.6 3.5 %join.1 = (bf16[4,120,384]{2,1,0:T(8,128)(2,1)S(1)}, bf16[1536,1536]{1,0:T(8,128)(2,1)S(1)}) custom-call(bf16[32,64,128]{2,1,0:T(8,128)(2,1)S(1)} %all-to-all-done.1.far_ref, f32[24,120,128]{2,1,0:T(8,128)S(1)} %own_attend.1.own_ref, bf16[384,1536]{1,0:T(8,128)(2,1)S(1)} %copy-done.2, bf16[384,1536]{1,0:T(8,128)(2,1)} %collective-permute-done.1.w1, ...), custom_call_target="tpu_custom_call" | custom-call | flops 23592960 | bytes 8388608 | tf_op jit(solution)/shard_map/join/pallas_call | solution.py:400
  85.1 1.2 %mix.1 = (f32[120,1536]{1,0:T(8,128)S(1)}, bf16[120,1536]{1,0:T(8,128)(2,1)S(1)}) custom-call(s32[1]{0:T(128)} %bitcast.1.place_ref, bf16[4,120,384]{2,1,0:T(8,128)(2,1)S(1)} %get-tuple-element.48.att_ref, bf16[1536,1536]{1,0:T(8,128)(2,1)S(1)} %get-tuple-element.49.w_ref, bf16[120,1536]{1,0:T(8,128)(2,1)S(1)} %bitcast.15, bf16[6,1536]{1,0:T(8,128)(2,1)S(1)} %bitcast.17), custom_call_target="tpu_custom_call" | custom-call | tf_op jit(solution)/shard_map/mix/pallas_call | solution.py:433
  86.4 1.9 %collective-permute-start.6 = (bf16[120,1536]{1,0:T(8,128)(2,1)S(1)}, bf16[120,1536]{1,0:T(8,128)(2,1)S(1)}, u32[]{:S(2)}, u32[]{:S(2)}) collective-permute-start(bf16[120,1536]{1,0:T(8,128)(2,1)S(1)} %get-tuple-element.51.first), channel_id=1, source_target_pairs={{0,32},{32,0},{1,33},{33,1},{2,34},{34,2},{3,35},{35,3},{4,36},{36... | collective-permute-start | bytes 1105928 | tf_op jit(solution)/shard_map/ppermute | solution.py:528
  88.3 2.4 %collective-permute-start.5 = (bf16[120,1536]{1,0:T(8,128)(2,1)S(1)}, bf16[120,1536]{1,0:T(8,128)(2,1)S(1)}, u32[]{:S(2)}, u32[]{:S(2)}) collective-permute-start(bf16[120,1536]{1,0:T(8,128)(2,1)S(1)} %get-tuple-element.51.first), channel_id=1, source_target_pairs={{0,64},{64,0},{1,65},{65,1},{2,66},{66,2},{3,67},{67,3},{4,68},{68... | collective-permute-start | bytes 1105928 | tf_op jit(solution)/shard_map/ppermute | solution.py:528
  90.7 2.3 %copy-done = bf16[1536,1536]{1,0:T(8,128)(2,1)S(1)} copy-done((bf16[1536,1536]{1,0:T(8,128)(2,1)S(1)}, bf16[1536,1536]{1,0:T(8,128)(2,1)}, u32[]{:S(2)}) %copy-start) | copy-done | bytes 4718616
  93.0 2.3 %copy-done.1 = bf16[1536,1536]{1,0:T(8,128)(2,1)S(1)} copy-done((bf16[1536,1536]{1,0:T(8,128)(2,1)S(1)}, bf16[1536,1536]{1,0:T(8,128)(2,1)}, u32[]{:S(2)}) %copy-start.1) | copy-done | bytes 4718616
  95.4 4.1 %feed_near.1 = (f32[120,1536]{1,0:T(8,128)S(1)}, bf16[120,1536]{1,0:T(8,128)(2,1)S(1)}, bf16[1536,1536]{1,0:T(8,128)(2,1)S(1)}, bf16[1536,1536]{1,0:T(8,128)(2,1)S(1)}) custom-call(bf16[120,1536]{1,0:T(8,128)(2,1)S(1)} %get-tuple-element.51.first, bf16[120,1536]{1,0:T(8,128)(2,1)S(1)} %collective-permute-done.6.second, bf16[1536,1536]{1,0:T(8,128)(2,1)S(1)} %copy-done, ...), custom_call_target="tpu_custom_call" | custom-call | flops 2264924160 | bytes 9437184 | tf_op jit(solution)/shard_map/feed_near/pallas_call | solution.py:489
  100.0 0.9 collective-permute-start.8
  100.8 1.3 %collective-permute-done.8.second = bf16[120,1536]{1,0:T(8,128)(2,1)S(1)} collective-permute-done((bf16[120,1536]{1,0:T(8,128)(2,1)S(1)}, bf16[120,1536]{1,0:T(8,128)(2,1)S(1)}, u32[]{:S(2)}, u32[]{:S(2)}) %collective-permute-start.8) | collective-permute-done | bytes 368672 | tf_op jit(solution)/shard_map/ppermute | solution.py:528
  102.1 2.8 %feed_far.1 = (f32[120,1536]{1,0:T(8,128)S(1)}, bf16[120,1536]{1,0:T(8,128)(2,1)S(1)}) custom-call(bf16[120,1536]{1,0:T(8,128)(2,1)S(1)} %collective-permute-done.5.first, bf16[120,1536]{1,0:T(8,128)(2,1)S(1)} %collective-permute-done.8.second, bf16[1536,1536]{1,0:T(8,128)(2,1)S(1)} %get-tuple-element.57.up, bf16[1536,1536]{1,0:T(8,128)(2,1)S(1)} %get-tuple-element.58.down), custom_call_target="tpu_custom_call" | custom-call | flops 2264924160 | bytes 1048576 | tf_op jit(solution)/shard_map/feed_far/pallas_call | solution.py:511
  105.5 1.2 collective-permute-done.9
  106.8 2.5 %collective-permute-start.10 = (bf16[120,1536]{1,0:T(8,128)(2,1)S(1)}, bf16[120,1536]{1,0:T(8,128)(2,1)S(1)}, u32[]{:S(2)}, u32[]{:S(2)}) collective-permute-start(bf16[120,1536]{1,0:T(8,128)(2,1)S(1)} %add_convert_fusion), channel_id=1, source_target_pairs={{0,64},{64,0},{1,65},{65,1},{2,66},{66,2},{3,67},{67,3},{4,68},{68... | collective-permute-start | bytes 1105928 | tf_op jit(solution)/shard_map/ppermute | solution.py:528
  109.3 8.9 %collective-permute-done.10 = bf16[120,1536]{1,0:T(8,128)(2,1)S(1)} collective-permute-done((bf16[120,1536]{1,0:T(8,128)(2,1)S(1)}, bf16[120,1536]{1,0:T(8,128)(2,1)S(1)}, u32[]{:S(2)}, u32[]{:S(2)}) %collective-permute-start.10) | collective-permute-done | bytes 368672 | tf_op jit(solution)/shard_map/ppermute | solution.py:528
  118.2 1.0 fusion
  (25 shorter events, 1.2 us)
Async XLA Ops:
  0.9 13.4 %collective-permute-start = (bf16[64,1536]{1,0:T(8,128)(2,1)S(1)}, bf16[64,1536]{1,0:T(8,128)(2,1)S(1)}, u32[]{:S(2)}, u32[]{:S(2)}) collective-permute-start(bf16[64,1536]{1,0:T(8,128)(2,1)S(1)} %slice.9), channel_id=1, source_target_pairs={{0,64},{64,0},{1,65},{65,1},{2,66},{66,2},{3,67},{67,3},{4,68},{68... | collective-permute-start | bytes 589832 | tf_op jit(solution)/shard_map/ppermute | solution.py:528
  14.3 14.1 %copy-start.2 = (bf16[384,1536]{1,0:T(8,128)(2,1)S(1)}, bf16[384,1536]{1,0:T(8,128)(2,1)}, u32[]{:S(2)}) copy-start(bf16[384,1536]{1,0:T(8,128)(2,1)} %w0.1) | copy-start | bytes 3538948
  14.4 8.6 %copy-start.6 = (bf16[64,1536]{1,0:T(8,128)(2,1)}, bf16[64,1536]{1,0:T(8,128)(2,1)S(1)}, u32[]{:S(2)}) copy-start(bf16[64,1536]{1,0:T(8,128)(2,1)S(1)} %collective-permute-done.w2a) | copy-start | bytes 589828
  14.4 28.0 %all-to-all-start = ((bf16[32,184,128]{2,1,0:T(8,128)(2,1)}), bf16[32,184,128]{2,1,0:T(8,128)(2,1)}, u32[]{:S(2)}, u32[]{:S(2)}) async-start(bf16[32,184,128]{2,1,0:T(8,128)(2,1)} %get-tuple-element.35), calls=%async_computation | async-start | bytes 3014656 | tf_op jit(solution)/shard_map/all_to_all | solution.py:544
  23.0 1.2 %copy-start.3 = (bf16[1,154,3072]{2,1,0:T(8,128)(2,1)S(1)}, bf16[1,154,3072]{2,1,0:T(8,128)(2,1)}, u32[]{:S(2)}) copy-start(bf16[1,154,3072]{2,1,0:T(8,128)(2,1)} %param.13) | copy-start | bytes 2838532
  24.2 1.3 %copy-start.5 = (bf16[24,184,128]{2,1,0:T(8,128)(2,1)S(1)}, bf16[24,184,128]{2,1,0:T(8,128)(2,1)}, u32[]{:S(2)}) copy-start(bf16[24,184,128]{2,1,0:T(8,128)(2,1)} %get-tuple-element.36.own_ref) | copy-start | bytes 3391492
  28.4 34.6 %collective-permute-start.1 = (bf16[384,1536]{1,0:T(8,128)(2,1)S(1)}, bf16[384,1536]{1,0:T(8,128)(2,1)}, u32[]{:S(2)}, u32[]{:S(2)}) collective-permute-start(bf16[384,1536]{1,0:T(8,128)(2,1)S(1)} %copy-done.2), channel_id=1, source_target_pairs={{0,32},{32,0},{1,33},{33,1},{2,34},{34,2},{3,35},{35,3},{4,36},{36... | collective-permute-start | bytes 3538952 | tf_op jit(solution)/shard_map/ppermute | solution.py:528
  30.8 32.2 %collective-permute-start.2 = (bf16[320,1536]{1,0:T(8,128)(2,1)}, bf16[320,1536]{1,0:T(8,128)(2,1)}, u32[]{:S(2)}, u32[]{:S(2)}) collective-permute-start(bf16[320,1536]{1,0:T(8,128)(2,1)} %slice.10), channel_id=1, source_target_pairs={{0,64},{64,0},{1,65},{65,1},{2,66},{66,2},{3,67},{67,3},{4,68},{68... | collective-permute-start | bytes 2949128 | tf_op jit(solution)/shard_map/ppermute | solution.py:528
  63.0 22.1 %copy-start.4 = (bf16[1,120,1536]{2,1,0:T(8,128)(2,1)S(1)}, bf16[1,120,1536]{2,1,0:T(8,128)(2,1)}, u32[]{:S(2)}) copy-start(bf16[1,120,1536]{2,1,0:T(8,128)(2,1)} %param.10) | copy-start | bytes 1105924
  63.0 17.7 %collective-permute-start.3 = (bf16[320,1536]{1,0:T(8,128)(2,1)}, bf16[320,1536]{1,0:T(8,128)(2,1)}, u32[]{:S(2)}, u32[]{:S(2)}) collective-permute-start(bf16[320,1536]{1,0:T(8,128)(2,1)} %collective-permute-done.2.w2b), channel_id=1, source_target_pairs={{0,32},{32,0},{1,33},{33,1},{2,34},{34,2},{3,35},{35,3},{4,36},{36... | collective-permute-start | bytes 2949128 | tf_op jit(solution)/shard_map/ppermute | solution.py:528
  65.5 15.2 %all-to-all-start.1 = ((bf16[32,64,128]{2,1,0:T(8,128)(2,1)}), bf16[32,64,128]{2,1,0:T(8,128)(2,1)S(1)}, u32[]{:S(2)}, u32[]{:S(2)}) async-start(bf16[32,64,128]{2,1,0:T(8,128)(2,1)} %head_attend.1), calls=%async_computation.1 | async-start | bytes 1048576 | tf_op jit(solution)/shard_map/all_to_all | solution.py:556
  70.2 2.0 %collective-permute-start.4 = (bf16[64,1536]{1,0:T(8,128)(2,1)}, bf16[64,1536]{1,0:T(8,128)(2,1)}, u32[]{:S(2)}, u32[]{:S(2)}) collective-permute-start(bf16[64,1536]{1,0:T(8,128)(2,1)} %copy-done.6), channel_id=1, source_target_pairs={{0,32},{32,0},{1,33},{33,1},{2,34},{34,2},{3,35},{35,3},{4,36},{36... | collective-permute-start | bytes 589832 | tf_op jit(solution)/shard_map/ppermute | solution.py:528
  80.7 0.9 copy-start.7
  81.6 3.5 %copy-start.8 = (bf16[1,6,1536]{2,1,0:T(8,128)(2,1)S(1)}, bf16[1,6,1536]{2,1,0:T(8,128)(2,1)}, u32[]{:S(2)}) copy-start(bf16[1,6,1536]{2,1,0:T(8,128)(2,1)} %param.11) | copy-start | bytes 55300
  86.4 4.3 %collective-permute-start.6 = (bf16[120,1536]{1,0:T(8,128)(2,1)S(1)}, bf16[120,1536]{1,0:T(8,128)(2,1)S(1)}, u32[]{:S(2)}, u32[]{:S(2)}) collective-permute-start(bf16[120,1536]{1,0:T(8,128)(2,1)S(1)} %get-tuple-element.51.first), channel_id=1, source_target_pairs={{0,32},{32,0},{1,33},{33,1},{2,34},{34,2},{3,35},{35,3},{4,36},{36... | collective-permute-start | bytes 1105928 | tf_op jit(solution)/shard_map/ppermute | solution.py:528
  88.3 11.6 %collective-permute-start.5 = (bf16[120,1536]{1,0:T(8,128)(2,1)S(1)}, bf16[120,1536]{1,0:T(8,128)(2,1)S(1)}, u32[]{:S(2)}, u32[]{:S(2)}) collective-permute-start(bf16[120,1536]{1,0:T(8,128)(2,1)S(1)} %get-tuple-element.51.first), channel_id=1, source_target_pairs={{0,64},{64,0},{1,65},{65,1},{2,66},{66,2},{3,67},{67,3},{4,68},{68... | collective-permute-start | bytes 1105928 | tf_op jit(solution)/shard_map/ppermute | solution.py:528
  90.7 2.3 %copy-start = (bf16[1536,1536]{1,0:T(8,128)(2,1)S(1)}, bf16[1536,1536]{1,0:T(8,128)(2,1)}, u32[]{:S(2)}) copy-start(bf16[1536,1536]{1,0:T(8,128)(2,1)} %up_hbm.1) | copy-start | bytes 14155780
  93.0 2.3 %copy-start.1 = (bf16[1536,1536]{1,0:T(8,128)(2,1)S(1)}, bf16[1536,1536]{1,0:T(8,128)(2,1)}, u32[]{:S(2)}) copy-start(bf16[1536,1536]{1,0:T(8,128)(2,1)} %down_hbm.1) | copy-start | bytes 14155780
  100.0 2.2 %collective-permute-start.8 = (bf16[120,1536]{1,0:T(8,128)(2,1)S(1)}, bf16[120,1536]{1,0:T(8,128)(2,1)S(1)}, u32[]{:S(2)}, u32[]{:S(2)}) collective-permute-start(bf16[120,1536]{1,0:T(8,128)(2,1)S(1)} %collective-permute-done.5.first), channel_id=1, source_target_pairs={{0,32},{32,0},{1,33},{33,1},{2,34},{34,2},{3,35},{35,3},{4,36},{36... | collective-permute-start | bytes 1105928 | tf_op jit(solution)/shard_map/ppermute | solution.py:528
  104.9 1.8 %collective-permute-start.9 = (bf16[120,1536]{1,0:T(8,128)(2,1)S(1)}, bf16[120,1536]{1,0:T(8,128)(2,1)S(1)}, u32[]{:S(2)}, u32[]{:S(2)}) collective-permute-start(bf16[120,1536]{1,0:T(8,128)(2,1)S(1)} %get-tuple-element.60), channel_id=1, source_target_pairs={{0,32},{32,0},{1,33},{33,1},{2,34},{34,2},{3,35},{35,3},{4,36},{36... | collective-permute-start | bytes 1105928 | tf_op jit(solution)/shard_map/ppermute | solution.py:528
  105.4 3.9 %collective-permute-start.7 = (bf16[120,1536]{1,0:T(8,128)(2,1)S(1)}, bf16[120,1536]{1,0:T(8,128)(2,1)S(1)}, u32[]{:S(2)}, u32[]{:S(2)}) collective-permute-start(bf16[120,1536]{1,0:T(8,128)(2,1)S(1)} %get-tuple-element.55), channel_id=1, source_target_pairs={{0,32},{32,0},{1,33},{33,1},{2,34},{34,2},{3,35},{35,3},{4,36},{36... | collective-permute-start | bytes 1105928 | tf_op jit(solution)/shard_map/ppermute | solution.py:528
  106.8 11.4 %collective-permute-start.10 = (bf16[120,1536]{1,0:T(8,128)(2,1)S(1)}, bf16[120,1536]{1,0:T(8,128)(2,1)S(1)}, u32[]{:S(2)}, u32[]{:S(2)}) collective-permute-start(bf16[120,1536]{1,0:T(8,128)(2,1)S(1)} %add_convert_fusion), channel_id=1, source_target_pairs={{0,64},{64,0},{1,65},{65,1},{2,66},{66,2},{3,67},{67,3},{4,68},{68... | collective-permute-start | bytes 1105928 | tf_op jit(solution)/shard_map/ppermute | solution.py:528

commit v8 on v7

--- a/solution.py
+++ b/solution.py
@@ -1,3 +1,5 @@
+import functools
+
 import jax
 import jax.numpy as jnp
 from jax import lax
@@ -351,24 +353,16 @@
     )(length, pack)
 
 
-def join_kernel(far_ref, own_ref, w0, w1, w2a, w2b, w3a, w3b, att_ref, w_ref, sems):
+def mix_rows(
+    second, place_ref, far_ref, own_ref, w_ref, tokens_ref, mod_ref, mixed_ref, input_ref, att_ref, ready
+):
     heads, rows, lanes = own_ref.shape
+    count, width = mixed_ref.shape
     depth = att_ref.shape[2]
-    copies = []
-    first = 0
-    for i, part in enumerate((w0, w1, w2a, w2b, w3a, w3b)):
-        last = first + part.shape[0]
-        copies.append(pltpu.make_async_copy(part, w_ref.at[first:last], sems.at[i]))
-        first = last
-    for copy in copies:
-        copy.start()
     per = depth // lanes
+    here = slice(HEAD, rows) if second else slice(0, HEAD)
     low = lane_iota((1, lanes)) < HEAD
-    diagonal = row_iota((HEAD, lanes)) == lane_iota((HEAD, lanes))
-
-    def column(line):
-        spread = jnp.where(diagonal, jnp.broadcast_to(line, (HEAD, lanes)), 0.0)
-        return jnp.sum(spread, -1, keepdims=True)
+    diagonal = row_iota((count, lanes)) == lane_iota((count, lanes))
 
     for pair in range(heads // 2):
         both = []
@@ -376,152 +370,140 @@
             head = 2 * pair + odd
             folded = far_ref[head + head // 3].astype(F32)
             stats = folded[rows - HEAD :]
-            begin = column(stats[0:1] + stats[2:3])
-            rest = column(stats[1:2] + stats[3:4])
-            far_lse = jnp.concatenate([begin, rest[: rows - HEAD]], axis=0)
-            far = jnp.concatenate([folded, swap_halves(folded)[: rows - HEAD]], axis=0)
-            own = own_ref[head]
-            gap = jnp.broadcast_to(far_lse, (rows, lanes)) - own[:, 0:1]
+            line = stats[1:2] + stats[3:4] if second else stats[0:1] + stats[2:3]
+            spread = jnp.where(diagonal, jnp.broadcast_to(line, (count, lanes)), 0.0)
+            far_lse = jnp.sum(spread, -1, keepdims=True)
+            far = swap_halves(folded)[:count] if second else folded
+            own = own_ref[head, here]
+            gap = jnp.broadcast_to(far_lse, (count, lanes)) - own[:, 0:1]
             share = 1.0 / (1.0 + jnp.exp(-gap))
             both.append(share * far + (1.0 - share) * own)
         joined = jnp.where(low, swap_halves(both[0]), both[1])
         at = (pair % per) * lanes
         att_ref[pair // per, :, at : at + lanes] = joined.astype(BF16)
-    for copy in copies:
-        copy.wait()
-
-
-def join(far, own, w_parts):
-    heads, rows, _ = own.shape
-    depth, width = w_parts[0].shape
-    fetched = sum(part.shape[0] for part in w_parts)
-    local = pl.BlockSpec(memory_space=pltpu.VMEM)
-    anywhere = pl.BlockSpec(memory_space=pltpu.HBM)
-    return pl.pallas_call(
-        join_kernel,
-        out_shape=(
-            jax.ShapeDtypeStruct((width // depth, rows, depth), BF16),
-            pltpu.VMEM((fetched, width), BF16),
-        ),
-        in_specs=[local, local] + [anywhere] * 6,
-        out_specs=(local, local),
-        scratch_shapes=[pltpu.SemaphoreType.DMA((6,))],
-        compiler_params=pltpu.CompilerParams(vmem_limit_bytes=24 << 20),
-        cost_estimate=pl.CostEstimate(
-            flops=64 * heads * rows * 128, bytes_accessed=8 << 20, transcendentals=heads * rows * 256
-        ),
-        name="join",
-    )(far, own, *w_parts)
-
-
-def mix_kernel(place_ref, att_ref, w_ref, tokens_ref, mod_ref, mixed_ref, input_ref):
+    ready()
     place = place_ref[0]
-    depth = att_ref.shape[2]
-    projected = jnp.zeros(mixed_ref.shape, F32)
+    projected = jnp.zeros((count, width), F32)
     owners = (place, place + 1 - 2 * (place % 2), (place + 2) % 4, 3 - place)
     for i, owner in enumerate(owners):
         part = w_ref[i * depth : (i + 1) * depth]
         projected += jnp.dot(att_ref[owner], part, preferred_element_type=F32)
     mod = mod_ref[...].astype(F32)
-    mixed = tokens_ref[...].astype(F32) + mod[2:3] * projected
+    mixed = tokens_ref[here].astype(F32) + mod[2:3] * projected
     mixed_ref[...] = mixed
     input_ref[...] = (layer_norm(mixed) * (1.0 + mod[4:5]) + mod[3:4]).astype(BF16)
 
 
-def mix(place, attended, w_main, tokens, modulate):
+def mix_a_kernel(
+    place, far, own, w0, w1, w2, w3, tokens, mod, mixed, out, w_ref, att, sems
+):
+    copies = []
+    first = 0
+    for i, part in enumerate((w0, w1, w2, w3)):
+        last = first + part.shape[0]
+        copies.append(pltpu.make_async_copy(part, w_ref.at[first:last], sems.at[i]))
+        first = last
+    for copy in copies:
+        copy.start()
+
+    def ready():
+        for copy in copies:
+            copy.wait()
+
+    mix_rows(False, place, far, own, w_ref, tokens, mod, mixed, out, att, ready)
+
+
+def mix_b_kernel(place, far, own, w_ref, tokens, mod, mixed, out, att):
+    mix_rows(True, place, far, own, w_ref, tokens, mod, mixed, out, att, lambda: None)
+
+
+def mix(second, place, far, own, weights, tokens, modulate):
+    rows, width = tokens.shape
+    count = rows - HEAD if second else HEAD
+    owners = 4
+    local = pl.BlockSpec(memory_space=pltpu.VMEM)
+    outs = [
+        jax.ShapeDtypeStruct((count, width), F32),
+        jax.ShapeDtypeStruct((count, width), BF16),
+    ]
+    scratch = [pltpu.VMEM((owners, count, width // owners), BF16)]
+    if not second:
+        outs.append(pltpu.VMEM((width, width), BF16))
+        scratch.append(pltpu.SemaphoreType.DMA((owners,)))
+    weight_spec = local if second else pl.BlockSpec(memory_space=pl.ANY)
+    return pl.pallas_call(
+        mix_b_kernel if second else mix_a_kernel,
+        out_shape=tuple(outs),
+        in_specs=[pl.BlockSpec(memory_space=pltpu.SMEM), local, local]
+        + [weight_spec] * len(weights)
+        + [local, local],
+        out_specs=(local,) * len(outs),
+        scratch_shapes=scratch,
+        compiler_params=pltpu.CompilerParams(vmem_limit_bytes=20 << 20),
+        name="mix_b" if second else "mix_a",
+    )(place, far, own, *weights, tokens, modulate)
+
+
+def feed_kernel(count, *refs):
+    pieces, (up_ref, down_ref), outs = refs[:count], refs[count : count + 2], refs[count + 2 :]
+    both = jnp.concatenate([piece[...].astype(F32) for piece in pieces], axis=0).astype(BF16)
+    wide = 512
+    total = None
+    for c in range(up_ref.shape[1] // wide):
+        part = slice(c * wide, (c + 1) * wide)
+        hidden = jnp.dot(both, up_ref[:, part], preferred_element_type=F32)
+        hidden = jax.nn.gelu(hidden, approximate=True).astype(BF16)
+        product = jnp.dot(hidden, down_ref[part, :], preferred_element_type=F32)
+        total = product if total is None else total + product
+    first = 0
+    for out in outs:
+        last = first + out.shape[0]
+        out[...] = total[first:last].astype(out.dtype)
+        first = last
+
+
+def feed(name, pieces, w_up, w_down):
+    count = len(pieces)
+    kinds = [F32] * (count // 2) + [BF16] * (count // 2)
     local = pl.BlockSpec(memory_space=pltpu.VMEM)
     return pl.pallas_call(
-        mix_kernel,
-        out_shape=(
-            jax.ShapeDtypeStruct(tokens.shape, F32),
-            jax.ShapeDtypeStruct(tokens.shape, BF16),
-        ),
-        in_specs=[pl.BlockSpec(memory_space=pltpu.SMEM)] + [local] * 4,
-        out_specs=(local, local),
-        compiler_params=pltpu.CompilerParams(vmem_limit_bytes=24 << 20),
-        name="mix",
-    )(place, attended, w_main, tokens, modulate)
-
-
-def feed_blocks(first_ref, second_ref, keep_ref, pass_ref, up_ref, down_ref, ready):
-    rows = first_ref.shape[0]
-    hidden_width = up_ref.shape[1]
-    wide = 512
-    both = [first_ref[...].astype(F32), second_ref[...].astype(F32)]
-    both = jnp.concatenate(both, axis=0).astype(BF16)
-    total = None
-    for c in range(hidden_width // wide):
-        part = slice(c * wide, (c + 1) * wide)
-        ready(2 * c)
-        hidden = jnp.dot(both, up_ref[:, part], preferred_element_type=F32)
-        hidden = jax.nn.gelu(hidden, approximate=True).astype(BF16)
-        ready(2 * c + 1)
-        product = jnp.dot(hidden, down_ref[part, :], preferred_element_type=F32)
-        total = product if total is None else total + product
-    keep_ref[...] = total[:rows]
-    pass_ref[...] = total[rows:].astype(BF16)
-
-
-def feed_near_kernel(first, second, up_hbm, down_hbm, keep, passed, up, down, sems):
-    wide = 512
-    copies = []
-    for c in range(up.shape[1] // wide):
-        part = slice(c * wide, (c + 1) * wide)
-        copies.append(
-            pltpu.make_async_copy(up_hbm.at[:, part], up.at[:, part], sems.at[2 * c])
-        )
-        copies.append(
-            pltpu.make_async_copy(down_hbm.at[part], down.at[part], sems.at[2 * c + 1])
-        )
-    for copy in copies:
-        copy.start()
-    feed_blocks(first, second, keep, passed, up, down, lambda i: copies[i].wait())
-
-
-def feed_far_kernel(first, second, up, down, keep, passed):
-    feed_blocks(first, second, keep, passed, up, down, lambda i: None)
-
-
-def feed_near(first, second, w_up, w_down):
-    rows, width = first.shape
-    local = pl.BlockSpec(memory_space=pltpu.VMEM)
-    anywhere = pl.BlockSpec(memory_space=pltpu.HBM)
-    return pl.pallas_call(
-        feed_near_kernel,
-        out_shape=(
-            jax.ShapeDtypeStruct((rows, width), F32),
-            jax.ShapeDtypeStruct((rows, width), BF16),
-            pltpu.VMEM(w_up.shape, BF16),
-            pltpu.VMEM(w_down.shape, BF16),
-        ),
-        in_specs=[local, local, anywhere, anywhere],
-        out_specs=(local,) * 4,
-        scratch_shapes=[pltpu.SemaphoreType.DMA((2 * (w_up.shape[1] // 512),))],
-        compiler_params=pltpu.CompilerParams(vmem_limit_bytes=32 << 20),
-        cost_estimate=pl.CostEstimate(
-            flops=8 * rows * w_up.size, bytes_accessed=4 * w_up.size, transcendentals=0
-        ),
-        name="feed_near",
-    )(first, second, w_up, w_down)
-
-
-def feed_far(first, second, w_up, w_down):
-    rows, width = first.shape
+        functools.partial(feed_kernel, count),
+        out_shape=tuple(jax.ShapeDtypeStruct(p.shape, k) for p, k in zip(pieces, kinds)),
+        in_specs=[local] * (count + 2),
+        out_specs=(local,) * count,
+        compiler_params=pltpu.CompilerParams(vmem_limit_bytes=20 << 20),
+        name=name,
+    )(*pieces, w_up, w_down)
+
+
+def final_kernel(
+    live_ref, mod_ref, mix_a, mix_b, near_a, near_b, core_a, core_b, far_a, far_b, out_ref
+):
+    gate = mod_ref[...].astype(F32)[5:6]
+    first = 0
+    for mixed, near, core, far in (
+        (mix_a, near_a, core_a, far_a),
+        (mix_b, near_b, core_b, far_b),
+    ):
+        total = near[...] + core[...].astype(F32) + far[...].astype(F32)
+        result = mixed[...] + gate * total
+        position = row_iota(result.shape) + first
+        last = first + mixed.shape[0]
+        out_ref[first:last] = jnp.where(position < live_ref[0], result, 0.0).astype(BF16)
+        first = last
+
+
+def final(live, modulate, *pieces):
+    rows = sum(piece.shape[0] for piece in pieces[:2])
     local = pl.BlockSpec(memory_space=pltpu.VMEM)
     return pl.pallas_call(
-        feed_far_kernel,
-        out_shape=(
-            jax.ShapeDtypeStruct((rows, width), F32),
-            jax.ShapeDtypeStruct((rows, width), BF16),
-        ),
-        in_specs=[local] * 4,
-        out_specs=(local,) * 2,
-        compiler_params=pltpu.CompilerParams(vmem_limit_bytes=24 << 20),
-        cost_estimate=pl.CostEstimate(
-            flops=8 * rows * w_up.size, bytes_accessed=1 << 20, transcendentals=0
-        ),
-        name="feed_far",
-    )(first, second, w_up, w_down)
+        final_kernel,
+        out_shape=jax.ShapeDtypeStruct((rows, modulate.shape[1]), BF16),
+        in_specs=[pl.BlockSpec(memory_space=pltpu.SMEM)] + [local] * 9,
+        out_specs=local,
+        compiler_params=pltpu.CompilerParams(vmem_limit_bytes=16 << 20),
+        name="final",
+    )(live, modulate, *pieces)
 
 
 def swap(values, axis):
@@ -536,42 +518,39 @@
     tile_index = lax.axis_index(TILE).astype(jnp.int32)
     length = lengths[0]
     place = lax.axis_index(REQ).astype(jnp.int32).reshape(1)
-    w2_first = swap(w_out[: w_out.shape[0] // 6], "zh")
     send, own = project(
         tile_index.reshape(1), refresh, tokens, modulation[0], w_qkv, kv_cache[0]
     )
-    send, own, w2_first = lax.optimization_barrier((send, own, w2_first))
+    send, own, w_here = lax.optimization_barrier((send, own, w_out))
     pack = lax.all_to_all(send, TILE, split_axis=0, concat_axis=0, tiled=True)
+    w2 = swap(w_here, "zh")
+    w1 = swap(w_here, "co")
     live = (length - tile_index * rows).reshape(1)
     own_part = own_attend(live, own, text_kv[0])
-    own_part, w_here = lax.optimization_barrier((own_part, w_out))
-    early = w_out.shape[0] // 6
-    w1 = swap(w_here, "co")
-    w2 = swap(w_here[early:], "zh")
     pack, own_part = lax.optimization_barrier((pack, own_part))
     far = head_attend(lengths, pack)
     far, w1, w2 = lax.optimization_barrier((far, w1, w2))
     w3 = swap(w2, "co")
-    w3_first = swap(w2_first, "co")
     far = lax.all_to_all(far, TILE, split_axis=0, concat_axis=0, tiled=True)
-    far, w3, w3_first = lax.optimization_barrier((far, w3, w3_first))
-    attended, w_main = join(far, own_part, (w_out, w1, w2_first, w2, w3_first, w3))
-    mixed, mlp_input = mix(place, attended, w_main, tokens, modulation[0])
-
-    far_z = swap(mlp_input, "zh")
-    near = swap(mlp_input, "co")
-    near_keep, near_pass, up, down = feed_near(mlp_input, near, w_up, w_down)
-    far_z, near_keep, near_pass = lax.optimization_barrier((far_z, near_keep, near_pass))
-    far_both = swap(far_z, "co")
-    far_keep, far_pass = feed_far(far_z, far_both, up, down)
-    sum_far = (far_keep + swap(far_pass, "co").astype(F32)).astype(BF16)
-    near_sum = near_keep + swap(near_pass, "co").astype(F32)
-    mlp_out = near_sum + swap(sum_far, "zh").astype(F32)
-    positions = tile_index * rows + jnp.arange(rows, dtype=jnp.int32)
-    live_rows = positions < length
-    gate = modulation[0, 5].astype(F32)
-    finished = jnp.where(live_rows[:, None], mixed + gate * mlp_out, 0.0)
-    return finished.astype(BF16)[None]
+    far, w3 = lax.optimization_barrier((far, w3))
+
+    w_parts = (w_out, w1, w2, w3)
+    mixed_a, input_a, w_main = mix(False, place, far, own_part, w_parts, tokens, modulation[0])
+    z_a, core_a = swap(input_a, "zh"), swap(input_a, "co")
+    mixed_b, input_b = mix(True, place, far, own_part, (w_main,), tokens, modulation[0])
+    z_b, core_b = swap(input_b, "zh"), swap(input_b, "co")
+    near = feed("feed_near", (input_a, input_b, core_a, core_b), w_up, w_down)
+    z_a, z_b, near = lax.optimization_barrier((z_a, z_b, near))
+    far_a = feed("feed_a", (z_a, swap(z_a, "co")), w_up, w_down)
+    sum_a = (far_a[0] + swap(far_a[1], "co").astype(F32)).astype(BF16)
+    z_b, sum_a = lax.optimization_barrier((z_b, sum_a))
+    back_a = swap(sum_a, "zh")
+    far_b = feed("feed_b", (z_b, swap(z_b, "co")), w_up, w_down)
+    sum_b = (far_b[0] + swap(far_b[1], "co").astype(F32)).astype(BF16)
+    back_b = swap(sum_b, "zh")
+    near_a, near_b = swap(near[2], "co"), swap(near[3], "co")
+    pieces = (mixed_a, mixed_b, near[0], near[1], near_a, near_b, back_a, back_b)
+    return final(live, modulation[0], *pieces)[None]
 
 
 def solution(mesh):

time: 120 us -> 124 us (1.033)
  local copies, waits for them, and re-layouts: 10.1 us -> 3.61 us
  waiting for transfers between devices: 32.5 us -> 37.6 us
  starting transfers between devices: 30.6 us -> 34.4 us
  Pallas kernels: 44.1 us -> 46.7 us
    unnamed x18 -> x14, local copies, waits for them, and re-layouts: 8.07 us -> 3.61 us
    ppermute x11 -> x15, waiting for transfers between devices: 13.3 us -> 16.1 us  [swap(): return lax.ppermute(values, axis, [(0, 1), (1, 0)])]
    all_to_all x1, starting transfers between devices: 4.65 us -> 7.43 us  [per_device(): far = lax.all_to_all(far, TILE, split_axis=0, concat_axis=0, tiled=True)]
    pallas_call x4 -> x6, Pallas kernels: 11.6 us -> 14.1 us  [the longest x2 6.93 us: mix(): pl.pallas_call(mix_b_kernel if second else mix_a_kernel, out_shape=tuple(...]
    slice x2 -> x0, local copies, waits for them, and re-layouts: 1.99 us -> none  [the longest x1 1.05 us: per_device(): w2 = swap(w_here[early:], 'zh')]
    all_to_all x1, waiting for transfers between devices: 8.49 us -> 10.4 us  [per_device(): far = lax.all_to_all(far, TILE, split_axis=0, concat_axis=0, tiled=True)]
    all_to_all x1, starting transfers between devices: 7.93 us -> 9.66 us  [per_device(): pack = lax.all_to_all(send, TILE, split_axis=0, concat_axis=0, tiled=True)]
    ppermute x11 -> x15, starting transfers between devices: 18 us -> 17.3 us  [swap(): return lax.ppermute(values, axis, [(0, 1), (1, 0)])]
  transfers between devices with their start and end apart: 13 -> 17, of which waited for: 7 -> 9; matrix products, arithmetic and copies ran while one was open for 1% -> 0% of each run, Pallas kernels for 31% -> 23%
where the time goes in v8:
time: 124 us; the launch traced here: 123 us
  Pallas kernels  46.7 us (38%)
  waiting for transfers between devices  37.6 us (30%)
  starting transfers between devices  34.4 us (28%)
  local copies, waits for them, and re-layouts  3.61 us (3%)
    pallas_call x1, Pallas kernels, head_attend(): pl.pallas_call(head_kernel, grid=(tiles // group,), out_shape=pltpu.HBM((...  20.7 us
    ppermute x15, starting transfers between devices, swap(): return lax.ppermute(values, axis, [(0, 1), (1, 0)])  17.3 us
    ppermute x15, waiting for transfers between devices, swap(): return lax.ppermute(values, axis, [(0, 1), (1, 0)])  16.1 us
    all_to_all x1, waiting for transfers between devices, per_device(): pack = lax.all_to_all(send, TILE, split_axis=0, concat_axis=0, tiled=True)  11.1 us
    all_to_all x1, waiting for transfers between devices, per_device(): far = lax.all_to_all(far, TILE, split_axis=0, concat_axis=0, tiled=True)  10.4 us
    all_to_all x1, starting transfers between devices, per_device(): pack = lax.all_to_all(send, TILE, split_axis=0, concat_axis=0, tiled=True)  9.66 us
    pallas_call x1, Pallas kernels, project(): pl.pallas_call(project_kernel, out_shape=(jax.ShapeDtypeStruct((dests, pa...  8.92 us
    all_to_all x1, starting transfers between devices, per_device(): far = lax.all_to_all(far, TILE, split_axis=0, concat_axis=0, tiled=True)  7.43 us
  transfers between devices with their start and end apart: 17, of which 9 were waited for; matrix products, arithmetic and copies ran while one was open for 0% of the time, Pallas kernels for 23%

profile of v8, /device:TPU:1, one launch (start us, length us, event | category | flops | bytes accessed | tf_op | source)
XLA Modules:
  0.0 123.2 jit_solution(2362537237307060473)
XLA Ops:
  0.0 8.9 %project.1 = (bf16[32,184,128]{2,1,0:T(8,128)(2,1)}, bf16[24,184,128]{2,1,0:T(8,128)(2,1)}) custom-call(s32[1]{0:T(128)} %bitcast.4.tile_ref, s32[1,4]{1,0:T(1,128)} %refresh_ref.1, bf16[120,1536]{1,0:T(8,128)(2,1)} %bitcast.14, bf16[6,1536]{1,0:T(8,128)(2,1)} %bitcast.17, bf16[1536,4608]{1,0:T(8,128)(2,1)} %w_ref.1, bf16[120,3072]{1,0:T(8,128)(2,1)} %bitcast.21), custom_call_target="tpu_custom_call" | custom-call | flops 1698693120 | bytes 18350080 | tf_op jit(solution)/shard_map/project/pallas_call | solution.py:164
  8.9 9.7 %all-to-all-start = ((bf16[32,184,128]{2,1,0:T(8,128)(2,1)}), bf16[32,184,128]{2,1,0:T(8,128)(2,1)}, u32[]{:S(2)}, u32[]{:S(2)}) async-start(bf16[32,184,128]{2,1,0:T(8,128)(2,1)} %get-tuple-element.40), calls=%async_computation | async-start | bytes 3014656 | tf_op jit(solution)/shard_map/all_to_all | solution.py:525
  18.6 3.4 %collective-permute-start.1 = (bf16[384,1536]{1,0:T(8,128)(2,1)}, bf16[384,1536]{1,0:T(8,128)(2,1)}, u32[]{:S(2)}, u32[]{:S(2)}) collective-permute-start(bf16[384,1536]{1,0:T(8,128)(2,1)} %w0.1), channel_id=1, source_target_pairs={{0,64},{64,0},{1,65},{65,1},{2,66},{66,2},{3,67},{67,3},{4,68},{68... | collective-permute-start | bytes 3538952 | tf_op jit(solution)/shard_map/ppermute | solution.py:510
  22.0 1.2 %collective-permute-start = (bf16[384,1536]{1,0:T(8,128)(2,1)}, bf16[384,1536]{1,0:T(8,128)(2,1)}, u32[]{:S(2)}, u32[]{:S(2)}) collective-permute-start(bf16[384,1536]{1,0:T(8,128)(2,1)} %w0.1), channel_id=1, source_target_pairs={{0,32},{32,0},{1,33},{33,1},{2,34},{34,2},{3,35},{35,3},{4,36},{36... | collective-permute-start | bytes 3538952 | tf_op jit(solution)/shard_map/ppermute | solution.py:510
  23.9 1.2 %copy-done.3 = bf16[24,184,128]{2,1,0:T(8,128)(2,1)S(1)} copy-done((bf16[24,184,128]{2,1,0:T(8,128)(2,1)S(1)}, bf16[24,184,128]{2,1,0:T(8,128)(2,1)}, u32[]{:S(2)}) %copy-start.3) | copy-done | bytes 1130520
  25.1 3.0 %own_attend.1.own = f32[24,120,128]{2,1,0:T(8,128)S(1)} custom-call(s32[1]{0:T(128)} %bitcast.1.live_ref, bf16[24,184,128]{2,1,0:T(8,128)(2,1)S(1)} %copy-done.3, bf16[154,3072]{1,0:T(8,128)(2,1)S(1)} %bitcast.12, bf16[154,3072]{1,0:T(8,128)(2,1)S(1)} %bitcast.13), custom_call_target="tpu_custom_call" | custom-call | flops 404029440 | bytes 6291456 | tf_op jit(solution)/shard_map/own_attend/pallas_call | solution.py:234
  28.2 11.1 %all-to-all-done.pack_ref = bf16[32,184,128]{2,1,0:T(8,128)(2,1)} async-done(((bf16[32,184,128]{2,1,0:T(8,128)(2,1)}), bf16[32,184,128]{2,1,0:T(8,128)(2,1)}, u32[]{:S(2)}, u32[]{:S(2)}) %all-to-all-start) | async-done | bytes 1507360 | tf_op jit(solution)/shard_map/all_to_all | solution.py:525
  39.3 20.7 %head_attend.1 = bf16[32,64,128]{2,1,0:T(8,128)(2,1)} custom-call(s32[1]{0:T(128)} %copy.11.len_ref, bf16[32,184,128]{2,1,0:T(8,128)(2,1)} %all-to-all-done.pack_ref), custom_call_target="tpu_custom_call" | custom-call | flops 7549747200 | bytes 4194304 | tf_op jit(solution)/shard_map/head_attend/pallas_call | solution.py:332
  60.0 3.5 %collective-permute-done.1.w2 = bf16[384,1536]{1,0:T(8,128)(2,1)} collective-permute-done((bf16[384,1536]{1,0:T(8,128)(2,1)}, bf16[384,1536]{1,0:T(8,128)(2,1)}, u32[]{:S(2)}, u32[]{:S(2)}) %collective-permute-start.1) | collective-permute-done | bytes 1179680 | tf_op jit(solution)/shard_map/ppermute | solution.py:510
  63.5 1.6 %collective-permute-start.2 = (bf16[384,1536]{1,0:T(8,128)(2,1)}, bf16[384,1536]{1,0:T(8,128)(2,1)}, u32[]{:S(2)}, u32[]{:S(2)}) collective-permute-start(bf16[384,1536]{1,0:T(8,128)(2,1)} %collective-permute-done.1.w2), channel_id=1, source_target_pairs={{0,32},{32,0},{1,33},{33,1},{2,34},{34,2},{3,35},{35,3},{4,36},{36... | collective-permute-start | bytes 3538952 | tf_op jit(solution)/shard_map/ppermute | solution.py:510
  65.1 7.4 %all-to-all-start.1 = ((bf16[32,64,128]{2,1,0:T(8,128)(2,1)}), bf16[32,64,128]{2,1,0:T(8,128)(2,1)S(1)}, u32[]{:S(2)}, u32[]{:S(2)}) async-start(bf16[32,64,128]{2,1,0:T(8,128)(2,1)} %head_attend.1), calls=%async_computation.1 | async-start | bytes 1048576 | tf_op jit(solution)/shard_map/all_to_all | solution.py:534
  72.5 10.4 %all-to-all-done.1.far = bf16[32,64,128]{2,1,0:T(8,128)(2,1)S(1)} async-done(((bf16[32,64,128]{2,1,0:T(8,128)(2,1)}), bf16[32,64,128]{2,1,0:T(8,128)(2,1)S(1)}, u32[]{:S(2)}, u32[]{:S(2)}) %all-to-all-start.1) | async-done | bytes 524320 | tf_op jit(solution)/shard_map/all_to_all | solution.py:534
  82.9 4.8 %mix_a.1 = (f32[64,1536]{1,0:T(8,128)S(1)}, bf16[64,1536]{1,0:T(8,128)(2,1)S(1)}, bf16[1536,1536]{1,0:T(8,128)(2,1)S(1)}) custom-call(s32[1]{0:T(128)} %bitcast.3.place, bf16[32,64,128]{2,1,0:T(8,128)(2,1)S(1)} %all-to-all-done.1.far, f32[24,120,128]{2,1,0:T(8,128)S(1)} %own_attend.1.own, bf16[384,1536]{1,0:T(8,128)(2,1)} %w0.1, ...), custom_call_target="tpu_custom_call" | custom-call | tf_op jit(solution)/shard_map/mix_a/pallas_call | solution.py:434
  87.8 1.9 %collective-permute-start.5 = (bf16[64,1536]{1,0:T(8,128)(2,1)S(1)}, bf16[64,1536]{1,0:T(8,128)(2,1)S(1)}, u32[]{:S(2)}, u32[]{:S(2)}) collective-permute-start(bf16[64,1536]{1,0:T(8,128)(2,1)S(1)} %get-tuple-element.53.refs_0_), channel_id=1, source_target_pairs={{0,32},{32,0},{1,33},{33,1},{2,34},{34,2},{3,35},{35,3},{4,36},{36... | collective-permute-start | bytes 589832 | tf_op jit(solution)/shard_map/ppermute | solution.py:510
  89.7 0.9 collective-permute-start.3
  90.6 2.1 %mix_b.1 = (f32[56,1536]{1,0:T(8,128)S(1)}, bf16[56,1536]{1,0:T(8,128)(2,1)S(1)}) custom-call(s32[1]{0:T(128)} %bitcast.3.place, bf16[32,64,128]{2,1,0:T(8,128)(2,1)S(1)} %all-to-all-done.1.far, f32[24,120,128]{2,1,0:T(8,128)S(1)} %own_attend.1.own, bf16[1536,1536]{1,0:T(8,128)(2,1)S(1)} %get-tuple-element.51.w_ref, bf16[120,1536]{1,0:T(8,128)(2,1)S(1)} %bitcast.16, ...), custom_call_target="tpu_custom_call" | custom-call | tf_op jit(solution)/shard_map/mix_b/pallas_call | solution.py:434
  92.6 0.4 collective-permute-start.6
  93.1 2.1 %collective-permute-start.4 = (bf16[56,1536]{1,0:T(8,128)(2,1)S(1)}, bf16[56,1536]{1,0:T(8,128)(2,1)S(1)}, u32[]{:S(2)}, u32[]{:S(2)}) collective-permute-start(bf16[56,1536]{1,0:T(8,128)(2,1)S(1)} %get-tuple-element.54.refs_1_), channel_id=1, source_target_pairs={{0,64},{64,0},{1,65},{65,1},{2,66},{66,2},{3,67},{67,3},{4,68},{68... | collective-permute-start | bytes 516104 | tf_op jit(solution)/shard_map/ppermute | solution.py:510
  95.2 2.3 %copy-done = bf16[1536,1536]{1,0:T(8,128)(2,1)S(1)} copy-done((bf16[1536,1536]{1,0:T(8,128)(2,1)S(1)}, bf16[1536,1536]{1,0:T(8,128)(2,1)}, u32[]{:S(2)}) %copy-start) | copy-done | bytes 4718616
  97.6 2.8 %feed_near.1 = (f32[64,1536]{1,0:T(8,128)S(1)}, f32[56,1536]{1,0:T(8,128)S(1)}, bf16[64,1536]{1,0:T(8,128)(2,1)S(1)}, bf16[56,1536]{1,0:T(8,128)(2,1)S(1)}) custom-call(bf16[64,1536]{1,0:T(8,128)(2,1)S(1)} %get-tuple-element.53.refs_0_, bf16[56,1536]{1,0:T(8,128)(2,1)S(1)} %get-tuple-element.54.refs_1_, bf16[64,1536]{1,0:T(8,128)(2,1)S(1)} %collective-permute-done.5.refs_2_, ...), custom_call_target="tpu_custom_call" | custom-call | tf_op jit(solution)/shard_map/feed_near/pallas_call | solution.py:469
  100.3 1.0 collective-permute-done.4.refs_0_
  101.3 0.9 collective-permute-start.9
  102.2 1.1 collective-permute-done.9.refs_1_
  103.3 1.7 %feed_a.1 = (f32[64,1536]{1,0:T(8,128)S(1)}, bf16[64,1536]{1,0:T(8,128)(2,1)S(1)}) custom-call(bf16[64,1536]{1,0:T(8,128)(2,1)S(1)} %collective-permute-done.3.refs_0_, bf16[64,1536]{1,0:T(8,128)(2,1)S(1)} %collective-permute-done.9.refs_1_, bf16[1536,1536]{1,0:T(8,128)(2,1)S(1)} %bitcast.11, bf16[1536,1536]{1,0:T(8,128)(2,1)S(1)} %copy-done), custom_call_target="tpu_custom_call" | custom-call | tf_op jit(solution)/shard_map/feed_a/pallas_call | solution.py:469
  105.4 1.1 collective-permute-done.10
  107.0 1.0 collective-permute-done.12.refs_1_
  108.0 1.7 %feed_b.1 = (f32[56,1536]{1,0:T(8,128)S(1)}, bf16[56,1536]{1,0:T(8,128)(2,1)S(1)}) custom-call(bf16[56,1536]{1,0:T(8,128)(2,1)S(1)} %collective-permute-done.4.refs_0_, bf16[56,1536]{1,0:T(8,128)(2,1)S(1)} %collective-permute-done.12.refs_1_, bf16[1536,1536]{1,0:T(8,128)(2,1)S(1)} %bitcast.11, bf16[1536,1536]{1,0:T(8,128)(2,1)S(1)} %copy-done), custom_call_target="tpu_custom_call" | custom-call | tf_op jit(solution)/shard_map/feed_b/pallas_call | solution.py:469
  110.7 1.3 %collective-permute-start.11 = (bf16[64,1536]{1,0:T(8,128)(2,1)S(1)}, bf16[64,1536]{1,0:T(8,128)(2,1)S(1)}, u32[]{:S(2)}, u32[]{:S(2)}) collective-permute-start(bf16[64,1536]{1,0:T(8,128)(2,1)S(1)} %add_convert_fusion), channel_id=1, source_target_pairs={{0,64},{64,0},{1,65},{65,1},{2,66},{66,2},{3,67},{67,3},{4,68},{68... | collective-permute-start | bytes 589832 | tf_op jit(solution)/shard_map/ppermute | solution.py:510
  112.1 1.7 %collective-permute-start.14 = (bf16[56,1536]{1,0:T(8,128)(2,1)S(1)}, bf16[56,1536]{1,0:T(8,128)(2,1)S(1)}, u32[]{:S(2)}, u32[]{:S(2)}) collective-permute-start(bf16[56,1536]{1,0:T(8,128)(2,1)S(1)} %add_convert_fusion.1), channel_id=1, source_target_pairs={{0,64},{64,0},{1,65},{65,1},{2,66},{66,2},{3,67},{67,3},{4,68},{68... | collective-permute-start | bytes 516104 | tf_op jit(solution)/shard_map/ppermute | solution.py:510
  113.8 4.8 %collective-permute-done.11.far_a = bf16[64,1536]{1,0:T(8,128)(2,1)S(1)} collective-permute-done((bf16[64,1536]{1,0:T(8,128)(2,1)S(1)}, bf16[64,1536]{1,0:T(8,128)(2,1)S(1)}, u32[]{:S(2)}, u32[]{:S(2)}) %collective-permute-start.11) | collective-permute-done | bytes 196640 | tf_op jit(solution)/shard_map/ppermute | solution.py:510
  118.6 3.7 %collective-permute-done.14.far_b = bf16[56,1536]{1,0:T(8,128)(2,1)S(1)} collective-permute-done((bf16[56,1536]{1,0:T(8,128)(2,1)S(1)}, bf16[56,1536]{1,0:T(8,128)(2,1)S(1)}, u32[]{:S(2)}, u32[]{:S(2)}) %collective-permute-start.14) | collective-permute-done | bytes 172064 | tf_op jit(solution)/shard_map/ppermute | solution.py:510
  122.3 0.9 final.1
  (28 shorter events, 2.0 us)
Async XLA Ops:
  8.9 15.0 %copy-start.1 = (bf16[1,154,3072]{2,1,0:T(8,128)(2,1)S(1)}, bf16[1,154,3072]{2,1,0:T(8,128)(2,1)}, u32[]{:S(2)}) copy-start(bf16[1,154,3072]{2,1,0:T(8,128)(2,1)} %param.13) | copy-start | bytes 2838532
  8.9 30.3 %all-to-all-start = ((bf16[32,184,128]{2,1,0:T(8,128)(2,1)}), bf16[32,184,128]{2,1,0:T(8,128)(2,1)}, u32[]{:S(2)}, u32[]{:S(2)}) async-start(bf16[32,184,128]{2,1,0:T(8,128)(2,1)} %get-tuple-element.40), calls=%async_computation | async-start | bytes 3014656 | tf_op jit(solution)/shard_map/all_to_all | solution.py:525
  18.6 44.9 %collective-permute-start.1 = (bf16[384,1536]{1,0:T(8,128)(2,1)}, bf16[384,1536]{1,0:T(8,128)(2,1)}, u32[]{:S(2)}, u32[]{:S(2)}) collective-permute-start(bf16[384,1536]{1,0:T(8,128)(2,1)} %w0.1), channel_id=1, source_target_pairs={{0,64},{64,0},{1,65},{65,1},{2,66},{66,2},{3,67},{67,3},{4,68},{68... | collective-permute-start | bytes 3538952 | tf_op jit(solution)/shard_map/ppermute | solution.py:510
  22.0 41.5 %collective-permute-start = (bf16[384,1536]{1,0:T(8,128)(2,1)}, bf16[384,1536]{1,0:T(8,128)(2,1)}, u32[]{:S(2)}, u32[]{:S(2)}) collective-permute-start(bf16[384,1536]{1,0:T(8,128)(2,1)} %w0.1), channel_id=1, source_target_pairs={{0,32},{32,0},{1,33},{33,1},{2,34},{34,2},{3,35},{35,3},{4,36},{36... | collective-permute-start | bytes 3538952 | tf_op jit(solution)/shard_map/ppermute | solution.py:510
  23.9 1.3 %copy-start.3 = (bf16[24,184,128]{2,1,0:T(8,128)(2,1)S(1)}, bf16[24,184,128]{2,1,0:T(8,128)(2,1)}, u32[]{:S(2)}) copy-start(bf16[24,184,128]{2,1,0:T(8,128)(2,1)} %get-tuple-element.41.own_ref) | copy-start | bytes 3391492
  28.2 54.7 %copy-start.2 = (bf16[1,120,1536]{2,1,0:T(8,128)(2,1)S(1)}, bf16[1,120,1536]{2,1,0:T(8,128)(2,1)}, u32[]{:S(2)}) copy-start(bf16[1,120,1536]{2,1,0:T(8,128)(2,1)} %param.10) | copy-start | bytes 1105924
  28.2 54.7 %copy-start.4 = (bf16[1,6,1536]{2,1,0:T(8,128)(2,1)S(1)}, bf16[1,6,1536]{2,1,0:T(8,128)(2,1)}, u32[]{:S(2)}) copy-start(bf16[1,6,1536]{2,1,0:T(8,128)(2,1)} %param.11) | copy-start | bytes 55300
  63.5 19.4 %collective-permute-start.2 = (bf16[384,1536]{1,0:T(8,128)(2,1)}, bf16[384,1536]{1,0:T(8,128)(2,1)}, u32[]{:S(2)}, u32[]{:S(2)}) collective-permute-start(bf16[384,1536]{1,0:T(8,128)(2,1)} %collective-permute-done.1.w2), channel_id=1, source_target_pairs={{0,32},{32,0},{1,33},{33,1},{2,34},{34,2},{3,35},{35,3},{4,36},{36... | collective-permute-start | bytes 3538952 | tf_op jit(solution)/shard_map/ppermute | solution.py:510
  65.1 30.1 %slice-start = ((s8[4718592]{0:T(1024)(128)(4,1)}), s8[524288]{0:T(1024)(128)(4,1)S(1)}, s32[]{:S(2)}) async-start(s8[4718592]{0:T(1024)(128)(4,1)} %bitcast.10), calls=%async_computation.2 | async-start | bytes 1048576
  65.1 17.8 %all-to-all-start.1 = ((bf16[32,64,128]{2,1,0:T(8,128)(2,1)}), bf16[32,64,128]{2,1,0:T(8,128)(2,1)S(1)}, u32[]{:S(2)}, u32[]{:S(2)}) async-start(bf16[32,64,128]{2,1,0:T(8,128)(2,1)} %head_attend.1), calls=%async_computation.1 | async-start | bytes 1048576 | tf_op jit(solution)/shard_map/all_to_all | solution.py:534
  82.9 12.3 %slice-start.1 = ((s8[4718592]{0:T(1024)(128)(4,1)}), s8[4194304]{0:T(1024)(128)(4,1)S(1)}, s32[]{:S(2)}) async-start(s8[4718592]{0:T(1024)(128)(4,1)} %bitcast.10), calls=%async_computation.3 | async-start | bytes 8388608
  87.8 7.4 %collective-permute-start.5 = (bf16[64,1536]{1,0:T(8,128)(2,1)S(1)}, bf16[64,1536]{1,0:T(8,128)(2,1)S(1)}, u32[]{:S(2)}, u32[]{:S(2)}) collective-permute-start(bf16[64,1536]{1,0:T(8,128)(2,1)S(1)} %get-tuple-element.53.refs_0_), channel_id=1, source_target_pairs={{0,32},{32,0},{1,33},{33,1},{2,34},{34,2},{3,35},{35,3},{4,36},{36... | collective-permute-start | bytes 589832 | tf_op jit(solution)/shard_map/ppermute | solution.py:510
  89.7 11.7 %collective-permute-start.3 = (bf16[64,1536]{1,0:T(8,128)(2,1)S(1)}, bf16[64,1536]{1,0:T(8,128)(2,1)S(1)}, u32[]{:S(2)}, u32[]{:S(2)}) collective-permute-start(bf16[64,1536]{1,0:T(8,128)(2,1)S(1)} %get-tuple-element.53.refs_0_), channel_id=1, source_target_pairs={{0,64},{64,0},{1,65},{65,1},{2,66},{66,2},{3,67},{67,3},{4,68},{68... | collective-permute-start | bytes 589832 | tf_op jit(solution)/shard_map/ppermute | solution.py:510
  92.6 2.6 %collective-permute-start.6 = (bf16[56,1536]{1,0:T(8,128)(2,1)S(1)}, bf16[56,1536]{1,0:T(8,128)(2,1)S(1)}, u32[]{:S(2)}, u32[]{:S(2)}) collective-permute-start(bf16[56,1536]{1,0:T(8,128)(2,1)S(1)} %get-tuple-element.54.refs_1_), channel_id=1, source_target_pairs={{0,32},{32,0},{1,33},{33,1},{2,34},{34,2},{3,35},{35,3},{4,36},{36... | collective-permute-start | bytes 516104 | tf_op jit(solution)/shard_map/ppermute | solution.py:510
  93.1 8.2 %collective-permute-start.4 = (bf16[56,1536]{1,0:T(8,128)(2,1)S(1)}, bf16[56,1536]{1,0:T(8,128)(2,1)S(1)}, u32[]{:S(2)}, u32[]{:S(2)}) collective-permute-start(bf16[56,1536]{1,0:T(8,128)(2,1)S(1)} %get-tuple-element.54.refs_1_), channel_id=1, source_target_pairs={{0,64},{64,0},{1,65},{65,1},{2,66},{66,2},{3,67},{67,3},{4,68},{68... | collective-permute-start | bytes 516104 | tf_op jit(solution)/shard_map/ppermute | solution.py:510
  95.2 2.3 %copy-start = (bf16[1536,1536]{1,0:T(8,128)(2,1)S(1)}, bf16[1536,1536]{1,0:T(8,128)(2,1)}, u32[]{:S(2)}) copy-start(bf16[1536,1536]{1,0:T(8,128)(2,1)} %refs_3_.3) | copy-start | bytes 14155780
  101.3 1.9 %collective-permute-start.9 = (bf16[64,1536]{1,0:T(8,128)(2,1)S(1)}, bf16[64,1536]{1,0:T(8,128)(2,1)S(1)}, u32[]{:S(2)}, u32[]{:S(2)}) collective-permute-start(bf16[64,1536]{1,0:T(8,128)(2,1)S(1)} %collective-permute-done.3.refs_0_), channel_id=1, source_target_pairs={{0,32},{32,0},{1,33},{33,1},{2,34},{34,2},{3,35},{35,3},{4,36},{36... | collective-permute-start | bytes 589832 | tf_op jit(solution)/shard_map/ppermute | solution.py:510
  105.0 1.5 %collective-permute-start.10 = (bf16[64,1536]{1,0:T(8,128)(2,1)S(1)}, bf16[64,1536]{1,0:T(8,128)(2,1)S(1)}, u32[]{:S(2)}, u32[]{:S(2)}) collective-permute-start(bf16[64,1536]{1,0:T(8,128)(2,1)S(1)} %get-tuple-element.66), channel_id=1, source_target_pairs={{0,32},{32,0},{1,33},{33,1},{2,34},{34,2},{3,35},{35,3},{4,36},{36... | collective-permute-start | bytes 589832 | tf_op jit(solution)/shard_map/ppermute | solution.py:510
  106.5 1.5 %collective-permute-start.12 = (bf16[56,1536]{1,0:T(8,128)(2,1)S(1)}, bf16[56,1536]{1,0:T(8,128)(2,1)S(1)}, u32[]{:S(2)}, u32[]{:S(2)}) collective-permute-start(bf16[56,1536]{1,0:T(8,128)(2,1)S(1)} %collective-permute-done.4.refs_0_), channel_id=1, source_target_pairs={{0,32},{32,0},{1,33},{33,1},{2,34},{34,2},{3,35},{35,3},{4,36},{36... | collective-permute-start | bytes 516104 | tf_op jit(solution)/shard_map/ppermute | solution.py:510
  109.8 2.3 %collective-permute-start.13 = (bf16[56,1536]{1,0:T(8,128)(2,1)S(1)}, bf16[56,1536]{1,0:T(8,128)(2,1)S(1)}, u32[]{:S(2)}, u32[]{:S(2)}) collective-permute-start(bf16[56,1536]{1,0:T(8,128)(2,1)S(1)} %get-tuple-element.70), channel_id=1, source_target_pairs={{0,32},{32,0},{1,33},{33,1},{2,34},{34,2},{3,35},{35,3},{4,36},{36... | collective-permute-start | bytes 516104 | tf_op jit(solution)/shard_map/ppermute | solution.py:510
  110.2 3.6 %collective-permute-start.8 = (bf16[56,1536]{1,0:T(8,128)(2,1)S(1)}, bf16[56,1536]{1,0:T(8,128)(2,1)S(1)}, u32[]{:S(2)}, u32[]{:S(2)}) collective-permute-start(bf16[56,1536]{1,0:T(8,128)(2,1)S(1)} %get-tuple-element.62), channel_id=1, source_target_pairs={{0,32},{32,0},{1,33},{33,1},{2,34},{34,2},{3,35},{35,3},{4,36},{36... | collective-permute-start | bytes 516104 | tf_op jit(solution)/shard_map/ppermute | solution.py:510
  110.4 3.5 %collective-permute-start.7 = (bf16[64,1536]{1,0:T(8,128)(2,1)S(1)}, bf16[64,1536]{1,0:T(8,128)(2,1)S(1)}, u32[]{:S(2)}, u32[]{:S(2)}) collective-permute-start(bf16[64,1536]{1,0:T(8,128)(2,1)S(1)} %get-tuple-element.61), channel_id=1, source_target_pairs={{0,32},{32,0},{1,33},{33,1},{2,34},{34,2},{3,35},{35,3},{4,36},{36... | collective-permute-start | bytes 589832 | tf_op jit(solution)/shard_map/ppermute | solution.py:510
  110.7 7.9 %collective-permute-start.11 = (bf16[64,1536]{1,0:T(8,128)(2,1)S(1)}, bf16[64,1536]{1,0:T(8,128)(2,1)S(1)}, u32[]{:S(2)}, u32[]{:S(2)}) collective-permute-start(bf16[64,1536]{1,0:T(8,128)(2,1)S(1)} %add_convert_fusion), channel_id=1, source_target_pairs={{0,64},{64,0},{1,65},{65,1},{2,66},{66,2},{3,67},{67,3},{4,68},{68... | collective-permute-start | bytes 589832 | tf_op jit(solution)/shard_map/ppermute | solution.py:510
  112.1 10.2 %collective-permute-start.14 = (bf16[56,1536]{1,0:T(8,128)(2,1)S(1)}, bf16[56,1536]{1,0:T(8,128)(2,1)S(1)}, u32[]{:S(2)}, u32[]{:S(2)}) collective-permute-start(bf16[56,1536]{1,0:T(8,128)(2,1)S(1)} %add_convert_fusion.1), channel_id=1, source_target_pairs={{0,64},{64,0},{1,65},{65,1},{2,66},{66,2},{3,67},{67,3},{4,68},{68... | collective-permute-start | bytes 516104 | tf_op jit(solution)/shard_map/ppermute | solution.py:510

commit v9 on v7

--- a/solution.py
+++ b/solution.py
@@ -49,8 +49,11 @@
     mod,
     weights,
     cache,
+    sent,
+    kept,
     in_sems,
     w_sems,
+    out_sems,
 ):
     rows, width = tokens.shape
     half = HEAD
@@ -90,7 +93,7 @@
     def store(head, at, block):
         dest = head + head // 3
         for copy in range(2 if head % 3 == 2 else 1):
-            send_ref[dest + copy, at] = block
+            sent[dest + copy, at] = block
 
     for copy in input_copies:
         copy.wait()
@@ -135,21 +138,39 @@
             for odd in range(2):
                 head = start // HEAD + pair * 2 + odd
                 q_pack = joined(q_top, q_end, odd)
-                own_ref[head, above] = q_pack
-                own_ref[head, below] = joined(keys[:, cols], values[:, cols], odd)
+                kept[head, above] = q_pack
+                kept[head, below] = joined(keys[:, cols], values[:, cols], odd)
                 store(head, above, q_pack)
+
+    out_copies = []
+
+    def hand_out(b):
+        head, last = (edge // HEAD for edge in BLOCKS[b])
+
+        @pl.when(flagged)
+        def _():
+            for h in range(head, last):
+                store(h, below, kept[h, below])
+
+        dest, dest_last = head + head // 3, last + last // 3
+        for i, (src, dst, part) in enumerate(
+            ((sent, send_ref, slice(dest, dest_last)), (kept, own_ref, slice(head, last)))
+        ):
+            out_copies.append(
+                pltpu.make_async_copy(src.at[part], dst.at[part], out_sems.at[b, i])
+            )
+            out_copies[-1].start()
 
     made = multiply(0)
     for b in range(1, len(BLOCKS)):
         following = multiply(b)
         pack(b - 1, *made)
+        hand_out(b - 1)
         made = following
     pack(len(BLOCKS) - 1, *made)
-
-    @pl.when(flagged)
-    def _():
-        for head in range(width // HEAD):
-            store(head, below, own_ref[head, below])
+    hand_out(len(BLOCKS) - 1)
+    for copy in out_copies:
+        copy.wait()
 
 
 def project(tile_index, refresh, tokens, modulate, w_qkv, cached):
@@ -162,19 +183,22 @@
     return pl.pallas_call(
         project_kernel,
         out_shape=(
-            jax.ShapeDtypeStruct((dests, packed, 2 * HEAD), BF16),
-            jax.ShapeDtypeStruct((heads, packed, 2 * HEAD), BF16),
+            pltpu.HBM((dests, packed, 2 * HEAD), BF16),
+            pltpu.HBM((heads, packed, 2 * HEAD), BF16),
         ),
         in_specs=[pl.BlockSpec(memory_space=pltpu.SMEM)] + [anywhere] * 5,
-        out_specs=(pl.BlockSpec(memory_space=pltpu.VMEM),) * 2,
+        out_specs=(anywhere, anywhere),
         scratch_shapes=[
             pltpu.SMEM(refresh.shape, jnp.int32),
             pltpu.VMEM(tokens.shape, BF16),
             pltpu.VMEM(modulate.shape, BF16),
             pltpu.VMEM(w_qkv.shape, BF16),
             pltpu.VMEM(cached.shape, BF16),
+            pltpu.VMEM((dests, packed, 2 * HEAD), BF16),
+            pltpu.VMEM((heads, packed, 2 * HEAD), BF16),
             pltpu.SemaphoreType.DMA((4,)),
             pltpu.SemaphoreType.DMA((blocks, 3)),
+            pltpu.SemaphoreType.DMA((blocks, 2)),
         ],
         compiler_params=pltpu.CompilerParams(vmem_limit_bytes=60 << 20),
         cost_estimate=pl.CostEstimate(
@@ -396,14 +420,15 @@
     depth, width = w_parts[0].shape
     fetched = sum(part.shape[0] for part in w_parts)
     local = pl.BlockSpec(memory_space=pltpu.VMEM)
-    anywhere = pl.BlockSpec(memory_space=pltpu.HBM)
+    anywhere = pl.BlockSpec(memory_space=pl.ANY)
+    fixed = pl.BlockSpec(memory_space=pltpu.HBM)
     return pl.pallas_call(
         join_kernel,
         out_shape=(
             jax.ShapeDtypeStruct((width // depth, rows, depth), BF16),
             pltpu.VMEM((fetched, width), BF16),
         ),
-        in_specs=[local, local] + [anywhere] * 6,
+        in_specs=[local, local, fixed, anywhere, fixed] + [anywhere] * 3,
         out_specs=(local, local),
         scratch_shapes=[pltpu.SemaphoreType.DMA((6,))],
         compiler_params=pltpu.CompilerParams(vmem_limit_bytes=24 << 20),
@@ -536,7 +561,7 @@
     tile_index = lax.axis_index(TILE).astype(jnp.int32)
     length = lengths[0]
     place = lax.axis_index(REQ).astype(jnp.int32).reshape(1)
-    w2_first = swap(w_out[: w_out.shape[0] // 6], "zh")
+    w2_first = swap(w_out[: w_out.shape[0] // 4], "zh")
     send, own = project(
         tile_index.reshape(1), refresh, tokens, modulation[0], w_qkv, kv_cache[0]
     )
@@ -545,7 +570,7 @@
     live = (length - tile_index * rows).reshape(1)
     own_part = own_attend(live, own, text_kv[0])
     own_part, w_here = lax.optimization_barrier((own_part, w_out))
-    early = w_out.shape[0] // 6
+    early = w_out.shape[0] // 4
     w1 = swap(w_here, "co")
     w2 = swap(w_here[early:], "zh")
     pack, own_part = lax.optimization_barrier((pack, own_part))

time: 120 us -> 119 us (level)
  starting transfers between devices: 30.6 us -> 28.8 us
  waiting for transfers between devices: 32.5 us -> 34.2 us
    ppermute x11, waiting for transfers between devices: 13.3 us -> 15.8 us  [swap(): return lax.ppermute(values, axis, [(0, 1), (1, 0)])]
    ppermute x11, starting transfers between devices: 18 us -> 16.3 us  [swap(): return lax.ppermute(values, axis, [(0, 1), (1, 0)])]
  transfers between devices with their start and end apart: 13 -> 13, of which waited for: 7 -> 8; matrix products, arithmetic and copies ran while one was open for 1% -> 1% of each run, Pallas kernels for 31% -> 31%
where the time goes in v9:
time: 119 us
  Pallas kernels  43.8 us (37%)
  waiting for transfers between devices  34.2 us (29%)
  starting transfers between devices  28.8 us (24%)
  local copies, waits for them, and re-layouts  10.1 us (8%)
    pallas_call x1, Pallas kernels, head_attend(): pl.pallas_call(head_kernel, grid=(tiles // group,), out_shape=pltpu.HBM((...  20.7 us
    ppermute x11, starting transfers between devices, swap(): return lax.ppermute(values, axis, [(0, 1), (1, 0)])  16.3 us
    ppermute x11, waiting for transfers between devices, swap(): return lax.ppermute(values, axis, [(0, 1), (1, 0)])  15.8 us
    all_to_all x1, waiting for transfers between devices, per_device(): pack = lax.all_to_all(send, TILE, split_axis=0, concat_axis=0, tiled=True)  9.97 us
    pallas_call x1, Pallas kernels, project(): pl.pallas_call(project_kernel, out_shape=(pltpu.HBM((dests, packed, 2 * H...  8.78 us
    all_to_all x1, waiting for transfers between devices, per_device(): far = lax.all_to_all(far, TILE, split_axis=0, concat_axis=0, tiled=True)  8.35 us
    unnamed x18, local copies, waits for them, and re-layouts  8.1 us
    all_to_all x1, starting transfers between devices, per_device(): pack = lax.all_to_all(send, TILE, split_axis=0, concat_axis=0, tiled=True)  7.76 us
  transfers between devices with their start and end apart: 13, of which 8 were waited for; matrix products, arithmetic and copies ran while one was open for 1% of the time, Pallas kernels for 31%

profile of v9, /device:TPU:1, one launch (start us, length us, event | category | flops | bytes accessed | tf_op | source)
XLA Modules:
  0.0 118.7 jit_solution(15367273907721155092)
XLA Ops:
  0.0 1.0 slice.9
  1.0 4.5 %collective-permute-start = (bf16[96,1536]{1,0:T(8,128)(2,1)S(1)}, bf16[96,1536]{1,0:T(8,128)(2,1)S(1)}, u32[]{:S(2)}, u32[]{:S(2)}) collective-permute-start(bf16[96,1536]{1,0:T(8,128)(2,1)S(1)} %slice.9), channel_id=1, source_target_pairs={{0,64},{64,0},{1,65},{65,1},{2,66},{66,2},{3,67},{67,3},{4,68},{68... | collective-permute-start | bytes 884744 | tf_op jit(solution)/shard_map/ppermute | solution.py:553
  5.5 8.8 %project.1 = (bf16[32,184,128]{2,1,0:T(8,128)(2,1)}, bf16[24,184,128]{2,1,0:T(8,128)(2,1)}) custom-call(s32[1]{0:T(128)} %bitcast.2.tile_ref, s32[1,4]{1,0:T(1,128)} %refresh_ref.1, bf16[120,1536]{1,0:T(8,128)(2,1)} %bitcast.14, bf16[6,1536]{1,0:T(8,128)(2,1)} %bitcast.16, bf16[1536,4608]{1,0:T(8,128)(2,1)} %w_ref.1, bf16[120,3072]{1,0:T(8,128)(2,1)} %bitcast.18), custom_call_target="tpu_custom_call" | custom-call | flops 1698693120 | bytes 18350080 | tf_op jit(solution)/shard_map/project/pallas_call | solution.py:183
  14.3 7.8 %all-to-all-start = ((bf16[32,184,128]{2,1,0:T(8,128)(2,1)}), bf16[32,184,128]{2,1,0:T(8,128)(2,1)}, u32[]{:S(2)}, u32[]{:S(2)}) async-start(bf16[32,184,128]{2,1,0:T(8,128)(2,1)} %get-tuple-element.35), calls=%async_computation | async-start | bytes 3014656 | tf_op jit(solution)/shard_map/all_to_all | solution.py:569
  22.8 1.2 %copy-done.3 = bf16[1,154,3072]{2,1,0:T(8,128)(2,1)S(1)} copy-done((bf16[1,154,3072]{2,1,0:T(8,128)(2,1)S(1)}, bf16[1,154,3072]{2,1,0:T(8,128)(2,1)}, u32[]{:S(2)}) %copy-start.3) | copy-done | bytes 946200
  23.9 1.3 %copy-done.5 = bf16[24,184,128]{2,1,0:T(8,128)(2,1)S(1)} copy-done((bf16[24,184,128]{2,1,0:T(8,128)(2,1)S(1)}, bf16[24,184,128]{2,1,0:T(8,128)(2,1)}, u32[]{:S(2)}) %copy-start.5) | copy-done | bytes 1130520
  25.2 3.0 %own_attend.1.own_ref = f32[24,120,128]{2,1,0:T(8,128)S(1)} custom-call(s32[1]{0:T(128)} %bitcast.6.live_ref, bf16[24,184,128]{2,1,0:T(8,128)(2,1)S(1)} %copy-done.5, bf16[154,3072]{1,0:T(8,128)(2,1)S(1)} %bitcast.12, bf16[154,3072]{1,0:T(8,128)(2,1)S(1)} %bitcast.13), custom_call_target="tpu_custom_call" | custom-call | flops 404029440 | bytes 6291456 | tf_op jit(solution)/shard_map/own_attend/pallas_call | solution.py:256
  28.2 1.3 %collective-permute-start.1 = (bf16[384,1536]{1,0:T(8,128)(2,1)S(1)}, bf16[384,1536]{1,0:T(8,128)(2,1)}, u32[]{:S(2)}, u32[]{:S(2)}) collective-permute-start(bf16[384,1536]{1,0:T(8,128)(2,1)S(1)} %copy-done.2), channel_id=1, source_target_pairs={{0,32},{32,0},{1,33},{33,1},{2,34},{34,2},{3,35},{35,3},{4,36},{36... | collective-permute-start | bytes 3538952 | tf_op jit(solution)/shard_map/ppermute | solution.py:553
  29.5 1.0 slice.10
  30.5 1.6 %collective-permute-start.2 = (bf16[288,1536]{1,0:T(8,128)(2,1)}, bf16[288,1536]{1,0:T(8,128)(2,1)}, u32[]{:S(2)}, u32[]{:S(2)}) collective-permute-start(bf16[288,1536]{1,0:T(8,128)(2,1)} %slice.10), channel_id=1, source_target_pairs={{0,64},{64,0},{1,65},{65,1},{2,66},{66,2},{3,67},{67,3},{4,68},{68... | collective-permute-start | bytes 2654216 | tf_op jit(solution)/shard_map/ppermute | solution.py:553
  32.1 10.0 %all-to-all-done.pack_ref = bf16[32,184,128]{2,1,0:T(8,128)(2,1)} async-done(((bf16[32,184,128]{2,1,0:T(8,128)(2,1)}), bf16[32,184,128]{2,1,0:T(8,128)(2,1)}, u32[]{:S(2)}, u32[]{:S(2)}) %all-to-all-start) | async-done | bytes 1507360 | tf_op jit(solution)/shard_map/all_to_all | solution.py:569
  42.1 20.7 %head_attend.1 = bf16[32,64,128]{2,1,0:T(8,128)(2,1)} custom-call(s32[1]{0:T(128)} %copy.11.len_ref, bf16[32,184,128]{2,1,0:T(8,128)(2,1)} %all-to-all-done.pack_ref), custom_call_target="tpu_custom_call" | custom-call | flops 7549747200 | bytes 4194304 | tf_op jit(solution)/shard_map/head_attend/pallas_call | solution.py:354
  62.8 2.5 %collective-permute-start.3 = (bf16[288,1536]{1,0:T(8,128)(2,1)}, bf16[288,1536]{1,0:T(8,128)(2,1)}, u32[]{:S(2)}, u32[]{:S(2)}) collective-permute-start(bf16[288,1536]{1,0:T(8,128)(2,1)} %collective-permute-done.2.w2b), channel_id=1, source_target_pairs={{0,32},{32,0},{1,33},{33,1},{2,34},{34,2},{3,35},{35,3},{4,36},{36... | collective-permute-start | bytes 2654216 | tf_op jit(solution)/shard_map/ppermute | solution.py:553
  65.3 4.7 %all-to-all-start.1 = ((bf16[32,64,128]{2,1,0:T(8,128)(2,1)}), bf16[32,64,128]{2,1,0:T(8,128)(2,1)S(1)}, u32[]{:S(2)}, u32[]{:S(2)}) async-start(bf16[32,64,128]{2,1,0:T(8,128)(2,1)} %head_attend.1), calls=%async_computation.1 | async-start | bytes 1048576 | tf_op jit(solution)/shard_map/all_to_all | solution.py:581
  70.5 1.6 %collective-permute-done.4.w3a = bf16[96,1536]{1,0:T(8,128)(2,1)} collective-permute-done((bf16[96,1536]{1,0:T(8,128)(2,1)}, bf16[96,1536]{1,0:T(8,128)(2,1)}, u32[]{:S(2)}, u32[]{:S(2)}) %collective-permute-start.4) | collective-permute-done | bytes 294944 | tf_op jit(solution)/shard_map/ppermute | solution.py:553
  72.1 8.4 %all-to-all-done.1.far_ref = bf16[32,64,128]{2,1,0:T(8,128)(2,1)S(1)} async-done(((bf16[32,64,128]{2,1,0:T(8,128)(2,1)}), bf16[32,64,128]{2,1,0:T(8,128)(2,1)S(1)}, u32[]{:S(2)}, u32[]{:S(2)}) %all-to-all-start.1) | async-done | bytes 524320 | tf_op jit(solution)/shard_map/all_to_all | solution.py:581
  80.5 1.0 copy-done.7
  81.4 3.3 %join.1 = (bf16[4,120,384]{2,1,0:T(8,128)(2,1)S(1)}, bf16[1536,1536]{1,0:T(8,128)(2,1)S(1)}) custom-call(bf16[32,64,128]{2,1,0:T(8,128)(2,1)S(1)} %all-to-all-done.1.far_ref, f32[24,120,128]{2,1,0:T(8,128)S(1)} %own_attend.1.own_ref, bf16[384,1536]{1,0:T(8,128)(2,1)S(1)} %copy-done.2, bf16[384,1536]{1,0:T(8,128)(2,1)} %collective-permute-done.1.w1, ...), custom_call_target="tpu_custom_call" | custom-call | flops 23592960 | bytes 8388608 | tf_op jit(solution)/shard_map/join/pallas_call | solution.py:425
  84.7 1.2 %mix.1 = (f32[120,1536]{1,0:T(8,128)S(1)}, bf16[120,1536]{1,0:T(8,128)(2,1)S(1)}) custom-call(s32[1]{0:T(128)} %bitcast.1.place_ref, bf16[4,120,384]{2,1,0:T(8,128)(2,1)S(1)} %get-tuple-element.48.att_ref, bf16[1536,1536]{1,0:T(8,128)(2,1)S(1)} %get-tuple-element.49.w_ref, bf16[120,1536]{1,0:T(8,128)(2,1)S(1)} %bitcast.15, bf16[6,1536]{1,0:T(8,128)(2,1)S(1)} %bitcast.17), custom_call_target="tpu_custom_call" | custom-call | tf_op jit(solution)/shard_map/mix/pallas_call | solution.py:458
  86.0 1.9 %collective-permute-start.6 = (bf16[120,1536]{1,0:T(8,128)(2,1)S(1)}, bf16[120,1536]{1,0:T(8,128)(2,1)S(1)}, u32[]{:S(2)}, u32[]{:S(2)}) collective-permute-start(bf16[120,1536]{1,0:T(8,128)(2,1)S(1)} %get-tuple-element.51.first), channel_id=1, source_target_pairs={{0,32},{32,0},{1,33},{33,1},{2,34},{34,2},{3,35},{35,3},{4,36},{36... | collective-permute-start | bytes 1105928 | tf_op jit(solution)/shard_map/ppermute | solution.py:553
  87.9 1.2 %collective-permute-start.5 = (bf16[120,1536]{1,0:T(8,128)(2,1)S(1)}, bf16[120,1536]{1,0:T(8,128)(2,1)S(1)}, u32[]{:S(2)}, u32[]{:S(2)}) collective-permute-start(bf16[120,1536]{1,0:T(8,128)(2,1)S(1)} %get-tuple-element.51.first), channel_id=1, source_target_pairs={{0,64},{64,0},{1,65},{65,1},{2,66},{66,2},{3,67},{67,3},{4,68},{68... | collective-permute-start | bytes 1105928 | tf_op jit(solution)/shard_map/ppermute | solution.py:553
  89.2 2.3 %copy-done = bf16[1536,1536]{1,0:T(8,128)(2,1)S(1)} copy-done((bf16[1536,1536]{1,0:T(8,128)(2,1)S(1)}, bf16[1536,1536]{1,0:T(8,128)(2,1)}, u32[]{:S(2)}) %copy-start) | copy-done | bytes 4718616
  91.6 2.3 %copy-done.1 = bf16[1536,1536]{1,0:T(8,128)(2,1)S(1)} copy-done((bf16[1536,1536]{1,0:T(8,128)(2,1)S(1)}, bf16[1536,1536]{1,0:T(8,128)(2,1)}, u32[]{:S(2)}) %copy-start.1) | copy-done | bytes 4718616
  93.9 4.1 %feed_near.1 = (f32[120,1536]{1,0:T(8,128)S(1)}, bf16[120,1536]{1,0:T(8,128)(2,1)S(1)}, bf16[1536,1536]{1,0:T(8,128)(2,1)S(1)}, bf16[1536,1536]{1,0:T(8,128)(2,1)S(1)}) custom-call(bf16[120,1536]{1,0:T(8,128)(2,1)S(1)} %get-tuple-element.51.first, bf16[120,1536]{1,0:T(8,128)(2,1)S(1)} %collective-permute-done.6.second, bf16[1536,1536]{1,0:T(8,128)(2,1)S(1)} %copy-done, ...), custom_call_target="tpu_custom_call" | custom-call | flops 2264924160 | bytes 9437184 | tf_op jit(solution)/shard_map/feed_near/pallas_call | solution.py:514
  98.0 1.5 %collective-permute-done.5.first = bf16[120,1536]{1,0:T(8,128)(2,1)S(1)} collective-permute-done((bf16[120,1536]{1,0:T(8,128)(2,1)S(1)}, bf16[120,1536]{1,0:T(8,128)(2,1)S(1)}, u32[]{:S(2)}, u32[]{:S(2)}) %collective-permute-start.5) | collective-permute-done | bytes 368672 | tf_op jit(solution)/shard_map/ppermute | solution.py:553
  99.6 0.9 collective-permute-start.8
  100.4 1.3 %collective-permute-done.8.second = bf16[120,1536]{1,0:T(8,128)(2,1)S(1)} collective-permute-done((bf16[120,1536]{1,0:T(8,128)(2,1)S(1)}, bf16[120,1536]{1,0:T(8,128)(2,1)S(1)}, u32[]{:S(2)}, u32[]{:S(2)}) %collective-permute-start.8) | collective-permute-done | bytes 368672 | tf_op jit(solution)/shard_map/ppermute | solution.py:553
  101.8 2.8 %feed_far.1 = (f32[120,1536]{1,0:T(8,128)S(1)}, bf16[120,1536]{1,0:T(8,128)(2,1)S(1)}) custom-call(bf16[120,1536]{1,0:T(8,128)(2,1)S(1)} %collective-permute-done.5.first, bf16[120,1536]{1,0:T(8,128)(2,1)S(1)} %collective-permute-done.8.second, bf16[1536,1536]{1,0:T(8,128)(2,1)S(1)} %get-tuple-element.57.up, bf16[1536,1536]{1,0:T(8,128)(2,1)S(1)} %get-tuple-element.58.down), custom_call_target="tpu_custom_call" | custom-call | flops 2264924160 | bytes 1048576 | tf_op jit(solution)/shard_map/feed_far/pallas_call | solution.py:536
  105.1 1.2 collective-permute-done.9
  106.4 1.3 %collective-permute-start.10 = (bf16[120,1536]{1,0:T(8,128)(2,1)S(1)}, bf16[120,1536]{1,0:T(8,128)(2,1)S(1)}, u32[]{:S(2)}, u32[]{:S(2)}) collective-permute-start(bf16[120,1536]{1,0:T(8,128)(2,1)S(1)} %add_convert_fusion), channel_id=1, source_target_pairs={{0,64},{64,0},{1,65},{65,1},{2,66},{66,2},{3,67},{67,3},{4,68},{68... | collective-permute-start | bytes 1105928 | tf_op jit(solution)/shard_map/ppermute | solution.py:553
  107.7 10.1 %collective-permute-done.10 = bf16[120,1536]{1,0:T(8,128)(2,1)S(1)} collective-permute-done((bf16[120,1536]{1,0:T(8,128)(2,1)S(1)}, bf16[120,1536]{1,0:T(8,128)(2,1)S(1)}, u32[]{:S(2)}, u32[]{:S(2)}) %collective-permute-start.10) | collective-permute-done | bytes 368672 | tf_op jit(solution)/shard_map/ppermute | solution.py:553
  117.8 1.0 fusion
  (25 shorter events, 1.4 us)
Async XLA Ops:
  1.0 13.3 %collective-permute-start = (bf16[96,1536]{1,0:T(8,128)(2,1)S(1)}, bf16[96,1536]{1,0:T(8,128)(2,1)S(1)}, u32[]{:S(2)}, u32[]{:S(2)}) collective-permute-start(bf16[96,1536]{1,0:T(8,128)(2,1)S(1)} %slice.9), channel_id=1, source_target_pairs={{0,64},{64,0},{1,65},{65,1},{2,66},{66,2},{3,67},{67,3},{4,68},{68... | collective-permute-start | bytes 884744 | tf_op jit(solution)/shard_map/ppermute | solution.py:553
  14.3 13.9 %copy-start.2 = (bf16[384,1536]{1,0:T(8,128)(2,1)S(1)}, bf16[384,1536]{1,0:T(8,128)(2,1)}, u32[]{:S(2)}) copy-start(bf16[384,1536]{1,0:T(8,128)(2,1)} %w0.1) | copy-start | bytes 3538948
  14.3 8.4 %copy-start.6 = (bf16[96,1536]{1,0:T(8,128)(2,1)}, bf16[96,1536]{1,0:T(8,128)(2,1)S(1)}, u32[]{:S(2)}) copy-start(bf16[96,1536]{1,0:T(8,128)(2,1)S(1)} %collective-permute-done.w2a) | copy-start | bytes 884740
  14.3 27.8 %all-to-all-start = ((bf16[32,184,128]{2,1,0:T(8,128)(2,1)}), bf16[32,184,128]{2,1,0:T(8,128)(2,1)}, u32[]{:S(2)}, u32[]{:S(2)}) async-start(bf16[32,184,128]{2,1,0:T(8,128)(2,1)} %get-tuple-element.35), calls=%async_computation | async-start | bytes 3014656 | tf_op jit(solution)/shard_map/all_to_all | solution.py:569
  22.7 1.2 %copy-start.3 = (bf16[1,154,3072]{2,1,0:T(8,128)(2,1)S(1)}, bf16[1,154,3072]{2,1,0:T(8,128)(2,1)}, u32[]{:S(2)}) copy-start(bf16[1,154,3072]{2,1,0:T(8,128)(2,1)} %param.13) | copy-start | bytes 2838532
  23.9 1.3 %copy-start.5 = (bf16[24,184,128]{2,1,0:T(8,128)(2,1)S(1)}, bf16[24,184,128]{2,1,0:T(8,128)(2,1)}, u32[]{:S(2)}) copy-start(bf16[24,184,128]{2,1,0:T(8,128)(2,1)} %get-tuple-element.36.own_ref) | copy-start | bytes 3391492
  28.2 34.6 %collective-permute-start.1 = (bf16[384,1536]{1,0:T(8,128)(2,1)S(1)}, bf16[384,1536]{1,0:T(8,128)(2,1)}, u32[]{:S(2)}, u32[]{:S(2)}) collective-permute-start(bf16[384,1536]{1,0:T(8,128)(2,1)S(1)} %copy-done.2), channel_id=1, source_target_pairs={{0,32},{32,0},{1,33},{33,1},{2,34},{34,2},{3,35},{35,3},{4,36},{36... | collective-permute-start | bytes 3538952 | tf_op jit(solution)/shard_map/ppermute | solution.py:553
  30.5 32.3 %collective-permute-start.2 = (bf16[288,1536]{1,0:T(8,128)(2,1)}, bf16[288,1536]{1,0:T(8,128)(2,1)}, u32[]{:S(2)}, u32[]{:S(2)}) collective-permute-start(bf16[288,1536]{1,0:T(8,128)(2,1)} %slice.10), channel_id=1, source_target_pairs={{0,64},{64,0},{1,65},{65,1},{2,66},{66,2},{3,67},{67,3},{4,68},{68... | collective-permute-start | bytes 2654216 | tf_op jit(solution)/shard_map/ppermute | solution.py:553
  62.8 21.9 %copy-start.4 = (bf16[1,120,1536]{2,1,0:T(8,128)(2,1)S(1)}, bf16[1,120,1536]{2,1,0:T(8,128)(2,1)}, u32[]{:S(2)}) copy-start(bf16[1,120,1536]{2,1,0:T(8,128)(2,1)} %param.10) | copy-start | bytes 1105924
  62.8 17.7 %collective-permute-start.3 = (bf16[288,1536]{1,0:T(8,128)(2,1)}, bf16[288,1536]{1,0:T(8,128)(2,1)}, u32[]{:S(2)}, u32[]{:S(2)}) collective-permute-start(bf16[288,1536]{1,0:T(8,128)(2,1)} %collective-permute-done.2.w2b), channel_id=1, source_target_pairs={{0,32},{32,0},{1,33},{33,1},{2,34},{34,2},{3,35},{35,3},{4,36},{36... | collective-permute-start | bytes 2654216 | tf_op jit(solution)/shard_map/ppermute | solution.py:553
  65.3 15.2 %all-to-all-start.1 = ((bf16[32,64,128]{2,1,0:T(8,128)(2,1)}), bf16[32,64,128]{2,1,0:T(8,128)(2,1)S(1)}, u32[]{:S(2)}, u32[]{:S(2)}) async-start(bf16[32,64,128]{2,1,0:T(8,128)(2,1)} %head_attend.1), calls=%async_computation.1 | async-start | bytes 1048576 | tf_op jit(solution)/shard_map/all_to_all | solution.py:581
  69.9 2.2 %collective-permute-start.4 = (bf16[96,1536]{1,0:T(8,128)(2,1)}, bf16[96,1536]{1,0:T(8,128)(2,1)}, u32[]{:S(2)}, u32[]{:S(2)}) collective-permute-start(bf16[96,1536]{1,0:T(8,128)(2,1)} %copy-done.6), channel_id=1, source_target_pairs={{0,32},{32,0},{1,33},{33,1},{2,34},{34,2},{3,35},{35,3},{4,36},{36... | collective-permute-start | bytes 884744 | tf_op jit(solution)/shard_map/ppermute | solution.py:553
  80.5 1.0 copy-start.7
  81.4 3.3 %copy-start.8 = (bf16[1,6,1536]{2,1,0:T(8,128)(2,1)S(1)}, bf16[1,6,1536]{2,1,0:T(8,128)(2,1)}, u32[]{:S(2)}) copy-start(bf16[1,6,1536]{2,1,0:T(8,128)(2,1)} %param.11) | copy-start | bytes 55300
  86.0 3.3 %collective-permute-start.6 = (bf16[120,1536]{1,0:T(8,128)(2,1)S(1)}, bf16[120,1536]{1,0:T(8,128)(2,1)S(1)}, u32[]{:S(2)}, u32[]{:S(2)}) collective-permute-start(bf16[120,1536]{1,0:T(8,128)(2,1)S(1)} %get-tuple-element.51.first), channel_id=1, source_target_pairs={{0,32},{32,0},{1,33},{33,1},{2,34},{34,2},{3,35},{35,3},{4,36},{36... | collective-permute-start | bytes 1105928 | tf_op jit(solution)/shard_map/ppermute | solution.py:553
  87.9 11.6 %collective-permute-start.5 = (bf16[120,1536]{1,0:T(8,128)(2,1)S(1)}, bf16[120,1536]{1,0:T(8,128)(2,1)S(1)}, u32[]{:S(2)}, u32[]{:S(2)}) collective-permute-start(bf16[120,1536]{1,0:T(8,128)(2,1)S(1)} %get-tuple-element.51.first), channel_id=1, source_target_pairs={{0,64},{64,0},{1,65},{65,1},{2,66},{66,2},{3,67},{67,3},{4,68},{68... | collective-permute-start | bytes 1105928 | tf_op jit(solution)/shard_map/ppermute | solution.py:553
  89.2 2.3 %copy-start = (bf16[1536,1536]{1,0:T(8,128)(2,1)S(1)}, bf16[1536,1536]{1,0:T(8,128)(2,1)}, u32[]{:S(2)}) copy-start(bf16[1536,1536]{1,0:T(8,128)(2,1)} %up_hbm.1) | copy-start | bytes 14155780
  91.6 2.3 %copy-start.1 = (bf16[1536,1536]{1,0:T(8,128)(2,1)S(1)}, bf16[1536,1536]{1,0:T(8,128)(2,1)}, u32[]{:S(2)}) copy-start(bf16[1536,1536]{1,0:T(8,128)(2,1)} %down_hbm.1) | copy-start | bytes 14155780
  99.6 2.2 %collective-permute-start.8 = (bf16[120,1536]{1,0:T(8,128)(2,1)S(1)}, bf16[120,1536]{1,0:T(8,128)(2,1)S(1)}, u32[]{:S(2)}, u32[]{:S(2)}) collective-permute-start(bf16[120,1536]{1,0:T(8,128)(2,1)S(1)} %collective-permute-done.5.first), channel_id=1, source_target_pairs={{0,32},{32,0},{1,33},{33,1},{2,34},{34,2},{3,35},{35,3},{4,36},{36... | collective-permute-start | bytes 1105928 | tf_op jit(solution)/shard_map/ppermute | solution.py:553
  104.5 1.8 %collective-permute-start.9 = (bf16[120,1536]{1,0:T(8,128)(2,1)S(1)}, bf16[120,1536]{1,0:T(8,128)(2,1)S(1)}, u32[]{:S(2)}, u32[]{:S(2)}) collective-permute-start(bf16[120,1536]{1,0:T(8,128)(2,1)S(1)} %get-tuple-element.60), channel_id=1, source_target_pairs={{0,32},{32,0},{1,33},{33,1},{2,34},{34,2},{3,35},{35,3},{4,36},{36... | collective-permute-start | bytes 1105928 | tf_op jit(solution)/shard_map/ppermute | solution.py:553
  105.0 2.7 %collective-permute-start.7 = (bf16[120,1536]{1,0:T(8,128)(2,1)S(1)}, bf16[120,1536]{1,0:T(8,128)(2,1)S(1)}, u32[]{:S(2)}, u32[]{:S(2)}) collective-permute-start(bf16[120,1536]{1,0:T(8,128)(2,1)S(1)} %get-tuple-element.55), channel_id=1, source_target_pairs={{0,32},{32,0},{1,33},{33,1},{2,34},{34,2},{3,35},{35,3},{4,36},{36... | collective-permute-start | bytes 1105928 | tf_op jit(solution)/shard_map/ppermute | solution.py:553
  106.4 11.4 %collective-permute-start.10 = (bf16[120,1536]{1,0:T(8,128)(2,1)S(1)}, bf16[120,1536]{1,0:T(8,128)(2,1)S(1)}, u32[]{:S(2)}, u32[]{:S(2)}) collective-permute-start(bf16[120,1536]{1,0:T(8,128)(2,1)S(1)} %add_convert_fusion), channel_id=1, source_target_pairs={{0,64},{64,0},{1,65},{65,1},{2,66},{66,2},{3,67},{67,3},{4,68},{68... | collective-permute-start | bytes 1105928 | tf_op jit(solution)/shard_map/ppermute | solution.py:553
